TPU v7x, 256 devices: a whole 4x4x8 slice. The times are simulated.
256 devices in a mesh: gx: 4 (over y), gy: 16 (over x, z_hi, core), gz: 4 (over z_lo).
Axes of the slice: x: 4, y: 4, z: 8 (z_hi: 2, z_lo: 4; z = z_hi * 4 + z_lo), core: 2. Of those that a mesh axis runs over, the one named last changes fastest.
Arguments:
- features: bfloat16 [8, 16, 16, 128, 128], P('gx', 'gy', 'gz'), may hold values from -6 to 6
- msg_weight: bfloat16 [128, 128], replicated, may hold values from -0.5 to 0.5
- self_weight: bfloat16 [128, 128], replicated, may hold values from -0.5 to 0.5
- charge_weight: bfloat16 [128], replicated, may hold values from -0.5 to 0.5
- spline_corner: int32 [8, 16, 16, 3, 128], P('gx', 'gy', 'gz'), may hold values from 0 to 12
- spline_fraction: float32 [8, 16, 16, 3, 128], P('gx', 'gy', 'gz'), may hold values from 0 to 1
Outputs:
- feature_grad: float32 [8, 16, 16, 128, 128], P('gx', 'gy', 'gz')
- atom_potential: float32 [8, 16, 16, 128], P('gx', 'gy', 'gz')
- energy_per_atom: float32 [], replicated
All inputs are finite; a program needn't handle non-finite values.
Results may differ from a plain program's by a relative error of at most 0.0095.
Values may be sent and summed in bfloat16 or wider, within the bound.
No kernel may reach another device: no remote copies, remote signals or barrier semaphores. Data moves between devices by JAX's collectives and lax.ppermute only.
A program may use at most 64 MiB of HBM per device.

v0:
```python
import functools
import math

import jax
import jax.numpy as jnp
import numpy as np
from jax import lax
from jax.experimental import pallas as pl
from jax.experimental.pallas import tpu as pltpu
from jax.sharding import PartitionSpec as P

PC = 16
pair_scale = 0.1
coupling = 0.125
spread_width = 0.0625
f32 = jnp.float32
bf16 = jnp.bfloat16
plane = ("gx", "gz")
everyone = ("gx", "gy", "gz")


def dot(a, b):
    return jnp.dot(a, b, preferred_element_type=f32)


def dot_t(a, b, precision=None):
    return lax.dot_general(
        a, b, (((1,), (1,)), ((), ())), preferred_element_type=f32, precision=precision
    )


def whole(shape):
    zeros = (0,) * len(shape)
    return pl.BlockSpec(shape, lambda *_: zeros)


VM = pl.BlockSpec(memory_space=pltpu.VMEM)
ANY = pl.BlockSpec(memory_space=pl.ANY)
SMALL = pltpu.CompilerParams(vmem_limit_bytes=20 << 20)
LARGE = pltpu.CompilerParams(vmem_limit_bytes=50 << 20)
MIDDLE = pltpu.CompilerParams(vmem_limit_bytes=36 << 20)


def cas(rows, columns, size):
    turns = np.outer(rows, columns) % size
    angle = 2.0 * np.pi / size * turns
    return np.cos(angle) + np.sin(angle)


def moved(value, axis, step):
    count = lax.axis_size(axis)
    pairs = [(i, (i + step) % count) for i in range(count)]
    return lax.ppermute(value.reshape(-1, 128), axis, pairs).reshape(value.shape)


def halo_yz(own):
    last = own.shape[1] - 1
    sides = [moved(own, "gy", 1), moved(own, "gy", -1)]
    rows = [sides[0], own, sides[1]]
    ends = [
        moved(jnp.stack([row[:, last:] for row in rows]), "gz", 1),
        moved(jnp.stack([row[:, :1] for row in rows]), "gz", -1),
    ]
    return sides + ends


def halo_x(own, near):
    below, above, left, right = near
    last = own.shape[0] - 1
    rows = (below, own, above)

    def slab(at):
        return jnp.stack(
            [
                jnp.concatenate(
                    [left[i, at : at + 1], row[at : at + 1], right[i, at : at + 1]], axis=1
                )
                for i, row in enumerate(rows)
            ]
        )

    return [moved(slab(last), "gx", 1), moved(slab(0), "gx", -1)]


def project_kernel(features_ref, weight_ref, corner_ref, fraction_ref, out_ref):
    value = dot(features_ref[...].reshape(1024, 128), weight_ref[...]).astype(bf16)
    out_ref[:, :128, :] = value.reshape(8, 128, 128)
    place = corner_ref[...].astype(f32) + 1.0 + fraction_ref[...]
    high = place.astype(bf16).astype(f32)
    rest = place - high
    middle = rest.astype(bf16).astype(f32)
    low = rest - middle
    two = jnp.zeros((8, 2, 128), f32)
    five = jnp.zeros((8, 5, 128), f32)
    out_ref[:, 128:, :] = jnp.concatenate([high, low, two, middle, five], axis=1).astype(bf16)


def project(features, weight, corner, fraction):
    return pl.pallas_call(
        project_kernel,
        grid=(1,),
        in_specs=[whole((8, 128, 128)), whole((128, 128)), whole((8, 3, 128)), whole((8, 3, 128))],
        out_specs=whole((8, 144, 128)),
        out_shape=jax.ShapeDtypeStruct((8, 144, 128), bf16),
        compiler_params=SMALL,
        name="project",
    )(features, weight, corner, fraction)


def place_of(rows):
    rows = rows.astype(f32)
    return rows[0:8] + rows[8:16] + pltpu.roll(rows[0:8], 5, 0)


BLOCKS = ((0, 0), (0, 1), (1, 0), (1, 1), (1, 2), (1, 3), (2, 2), (2, 3))
SPANS = ((0, 2, 0, 2), (2, 6, 0, 4), (6, 8, 2, 2))
ORDER_Y = (0, 2, 1)


def weigh(centres, a, shift, near, store):
    for c in range(4):
        columns = jnp.transpose(centres[a, c])
        centre_x = jnp.broadcast_to(columns[:, 0:1], (128, 128))
        centre_y = jnp.broadcast_to(columns[:, 1:2], (128, 128))
        centre_z = jnp.broadcast_to(columns[:, 2:3], (128, 128))
        for block, (pair, owner) in enumerate(BLOCKS):
            if owner != c:
                continue
            for at, dy in enumerate(ORDER_Y):
                for half in range(2):
                    dz = 2 * pair + half - c - 1
                    if abs(dz) > 1:
                        tile = jnp.zeros((128, 128), bf16)
                    else:
                        row = near(dy, 2 * pair + half)
                        gap_x = (row[0:1] + shift) - centre_x
                        gap_y = (row[1:2] + (dy - 1.0)) - centre_y
                        gap_z = (row[2:3] + float(dz)) - centre_z
                        squared = gap_x * gap_x + gap_y * gap_y + gap_z * gap_z
                        inside = jnp.maximum(1.0 - squared, 0.0)
                        tile = (pair_scale * inside * inside).astype(bf16)
                    store(block, (at * 2 + half) * 128, tile)


def inner_kernel(
    own_ref, below_ref, above_ref, left_ref, right_ref, features_ref, self_ref,
    weight_out, total_ref, place_ref, weight_ref, position_ref, sems
):
    refs = (below_ref, own_ref, above_ref)

    def cell(dy, x, z):
        if z == 0:
            return left_ref.at[dy, x, 0]
        if z == 5:
            return right_ref.at[dy, x, 0]
        return refs[dy].at[x, z - 1]

    def places(x, carry):
        for dy in range(3):
            for z in range(6):
                place = place_of(cell(dy, x, z)[128:144, :])
                place_ref[dy, x, z] = place
                position_ref[dy, x, z] = (place * (1.0 / PC)).astype(bf16).astype(f32)
        return carry

    lax.fori_loop(0, 2, places, 0)

    def copy_out(t):
        return pltpu.make_async_copy(weight_ref.at[t], weight_out.at[t], sems.at[t])

    total_ref[...] = dot(features_ref[...].reshape(1024, 128), self_ref[...]).reshape(
        2, 4, 128, 128
    )

    def combination(t, carry):
        x, a = t // 2, t % 2

        def store(block, lane, tile):
            weight_ref[t, block, :, lane : lane + 128] = tile

        weigh(
            position_ref.at[1, :, 1:5],
            a,
            (x - a).astype(f32),
            lambda dy, z: position_ref[dy, x, z],
            store,
        )
        copy_out(t).start()
        for pair, (start, stop, first, width) in enumerate(SPANS):
            near = jnp.concatenate(
                [
                    cell(dy, x, 2 * pair + half)[0:128, :]
                    for dy in ORDER_Y
                    for half in range(2)
                ],
                axis=0,
            )
            part = dot(weight_ref[t, start:stop].reshape(width * 128, 768), near)
            total_ref[a, first : first + width] += part.reshape(width, 128, 128)
        return carry

    lax.fori_loop(0, 4, combination, 0)
    for t in range(4):
        copy_out(t).wait()


def inner_pairs(own, near, features, self_weight):
    return pl.pallas_call(
        inner_kernel,
        in_specs=[VM] * 7,
        out_specs=[ANY, VM, VM],
        out_shape=[
            jax.ShapeDtypeStruct((6, 8, 128, 768), bf16),
            jax.ShapeDtypeStruct((2, 4, 128, 128), f32),
            jax.ShapeDtypeStruct((3, 2, 6, 8, 128), f32),
        ],
        scratch_shapes=[
            pltpu.VMEM((4, 8, 128, 768), bf16),
            pltpu.VMEM((3, 2, 6, 8, 128), f32),
            pltpu.SemaphoreType.DMA((4,)),
        ],
        cost_estimate=pl.CostEstimate(
            flops=9000000000, bytes_accessed=9000000, transcendentals=0
        ),
        compiler_params=LARGE,
        name="inner_pairs",
    )(own, *near, features, self_weight)


def spline_row(place):
    point = lax.broadcasted_iota(jnp.int32, (PC, 128), 0).astype(f32)
    away = jnp.abs(point - place)
    near = (4.0 - 6.0 * away * away + 3.0 * away * away * away) * (1.0 / 6.0)
    rest = 2.0 - away
    far = rest * rest * rest * (1.0 / 6.0)
    return jnp.where(away < 1.0, near, jnp.where(away < 2.0, far, 0.0))


def message_kernel(
    before_ref, after_ref, part_ref, place_ref, read_ref, _,
    weight_out, slope_ref, mesh_ref, row_place_ref,
    weight_ref, position_ref, centre_ref, total_ref, high_ref, low_ref, charge_ref, left_ref,
    right_ref, sems
):
    refs = (before_ref, after_ref)

    def position(place):
        return (place * (1.0 / PC)).astype(bf16).astype(f32)

    def places(dy, carry):
        for side in range(2):
            for z in range(6):
                place = place_of(refs[side][dy, 0, z, 128:144, :])
                position_ref[side, dy, z] = position(place)

                @pl.when(dy == 1)
                def _():
                    row_place_ref[3 * side, z] = place

        return carry

    lax.fori_loop(0, 3, places, 0)
    for x in range(2):
        for z in range(6):
            place = place_ref[1, x, z]
            row_place_ref[1 + x, z] = place
            if 1 <= z <= 4:
                centre_ref[x, z - 1] = position(place)

    def copy_out(t):
        return pltpu.make_async_copy(weight_ref.at[t], weight_out.at[4 + t], sems.at[t])

    def combination(t, carry):
        def store(block, lane, tile):
            weight_ref[t, block, :, lane : lane + 128] = tile

        weigh(
            centre_ref,
            t,
            (2 * t - 1).astype(f32),
            lambda dy, z: position_ref[t, dy, z],
            store,
        )
        copy_out(t).start()
        return carry

    lax.fori_loop(0, 2, combination, 0)
    total_ref[...] = part_ref[...]
    for t in range(2):
        for pair, (start, stop, first, width) in enumerate(SPANS):
            near = jnp.concatenate(
                [
                    refs[t][dy, 0, 2 * pair + half, 0:128, :]
                    for dy in ORDER_Y
                    for half in range(2)
                ],
                axis=0,
            )
            part = dot(weight_ref[t, start:stop].reshape(width * 128, 768), near)
            total_ref[t, first : first + width] += part.reshape(width, 128, 128)
    read = read_ref[...].astype(f32)

    def finish(cell, carry):
        a, c = cell // 4, cell % 4
        preact = total_ref[a, c]
        sigma = 0.5 + 0.5 * jnp.tanh(0.5 * preact)
        slope_ref[a, c] = (read * (sigma * (1.0 + preact * (1.0 - sigma)))).astype(bf16)
        silu = preact * sigma
        high = silu.astype(bf16)
        high_ref[cell] = high
        low_ref[cell] = (silu - high.astype(f32)).astype(bf16)
        return carry

    lax.fori_loop(0, 8, finish, 0)
    wide = jnp.broadcast_to(read_ref[...], (16, 128))
    charge_ref[...] = dot_t(wide, high_ref[...].reshape(1024, 128)) + dot_t(
        wide, low_ref[...].reshape(1024, 128)
    )
    block = lax.broadcasted_iota(jnp.int32, (128, 128), 0) // PC

    def spread(cell, carry):
        lanes = pl.ds(pl.multiple_of(cell * 128, 128), 128)
        place = place_ref[1, cell // 4, cell % 4 + 1]
        row_x = spline_row(place[0:1])
        row_y = spline_row(place[1:2]) * charge_ref[0:1, lanes]
        row_z = spline_row(place[2:3])
        left_ref[:, lanes] = (
            (row_y[:, None, :] * row_x[None, :, :]).reshape(PC * PC, 128).astype(bf16)
        )
        right_ref[:, lanes] = jnp.where(block == cell, jnp.tile(row_z, (8, 1)), 0.0).astype(bf16)
        return carry

    lax.fori_loop(0, 8, spread, 0)
    mesh_ref[...] = dot_t(left_ref[...], right_ref[...]).reshape(PC, PC, 128).astype(bf16)
    for t in range(2):
        copy_out(t).wait()


def message_layer(ends, part, place, read, weights):
    return pl.pallas_call(
        message_kernel,
        in_specs=[VM] * 5 + [ANY],
        out_specs=[ANY, VM, VM, VM],
        input_output_aliases={5: 0},
        out_shape=[
            jax.ShapeDtypeStruct((6, 8, 128, 768), bf16),
            jax.ShapeDtypeStruct((2, 4, 128, 128), bf16),
            jax.ShapeDtypeStruct((PC, PC, 128), bf16),
            jax.ShapeDtypeStruct((4, 6, 8, 128), f32),
        ],
        scratch_shapes=[
            pltpu.VMEM((2, 8, 128, 768), bf16),
            pltpu.VMEM((2, 3, 6, 8, 128), f32),
            pltpu.VMEM((2, 4, 8, 128), f32),
            pltpu.VMEM((2, 4, 128, 128), f32),
            pltpu.VMEM((8, 128, 128), bf16),
            pltpu.VMEM((8, 128, 128), bf16),
            pltpu.VMEM((16, 1024), f32),
            pltpu.VMEM((PC * PC, 1024), bf16),
            pltpu.VMEM((128, 1024), bf16),
            pltpu.SemaphoreType.DMA((2,)),
        ],
        cost_estimate=pl.CostEstimate(
            flops=5000000000, bytes_accessed=6000000, transcendentals=8 * 16384
        ),
        compiler_params=LARGE,
        name="message",
    )(*ends, part, place, read, weights)


def forward_kernel(mesh_ref, along_z_ref, along_x_ref, out_ref):
    total = jnp.zeros((64, 512), f32)
    for g in range(4):
        total = total + dot(mesh_ref[:, g].reshape(64, 128), along_z_ref[g])
    lines = jnp.concatenate([total[:, :256], total[:, 256:]], axis=0).astype(bf16)
    waves = dot(along_x_ref[...], lines)
    out_ref[0:128, :] = waves[:, :128]
    out_ref[128:256, :] = waves[:, 128:]


def forward_xz(mesh, along_z, along_x):
    return pl.pallas_call(
        forward_kernel,
        in_specs=[VM] * 3,
        out_specs=VM,
        compiler_params=SMALL,
        out_shape=jax.ShapeDtypeStruct((256, 128), f32),
        cost_estimate=pl.CostEstimate(
            flops=2 * 64 * 512 * 512, bytes_accessed=800000, transcendentals=0
        ),
        name="forward_xz",
    )(mesh, along_z, along_x)


def filter_kernel(lines_ref, into_ref, back_ref, influence_ref, out_ref):
    waves = dot(into_ref[...], lines_ref[...].astype(bf16))
    scaled = influence_ref[...] * waves
    power = jnp.sum(jnp.sum(scaled * waves, axis=0, keepdims=True), axis=1, keepdims=True)
    out_ref[pl.ds(0, 256, stride=2), :] = dot(back_ref[...], scaled.astype(bf16))
    out_ref[pl.ds(1, 256, stride=2), :] = jnp.broadcast_to(power, (256, 128))


def filter_y(lines, into, back, influence):
    return pl.pallas_call(
        filter_kernel,
        in_specs=[VM] * 4,
        out_specs=VM,
        compiler_params=SMALL,
        out_shape=jax.ShapeDtypeStruct((512, 128), f32),
        cost_estimate=pl.CostEstimate(
            flops=4 * 256 * 256 * 128, bytes_accessed=700000, transcendentals=0
        ),
        name="filter_y",
    )(lines, into, back, influence)


def inverse_kernel(energy_scale, lines_ref, along_x_ref, along_z_ref, out_ref, energy_ref):
    waves = jnp.concatenate(
        [lines_ref[pl.ds(0, 128, stride=2), :], lines_ref[pl.ds(256, 128, stride=2), :]], axis=1
    ).astype(bf16)
    half = dot(along_x_ref[...], waves).astype(bf16)
    field = dot(half, along_z_ref[...]).astype(bf16)
    for gx in range(4):
        for gz in range(4):
            out_ref[gx, gz] = field[gx * 64 : (gx + 1) * 64, gz * 128 : (gz + 1) * 128]
    power = jnp.sum(lines_ref[pl.ds(1, 256, stride=2), :], axis=0, keepdims=True)
    energy_ref[...] = jnp.broadcast_to(power * energy_scale, (8, 128))


def inverse_xz(lines, along_x, along_z, energy_scale):
    return pl.pallas_call(
        functools.partial(inverse_kernel, energy_scale),
        in_specs=[VM] * 3,
        out_specs=[VM, VM],
        compiler_params=SMALL,
        out_shape=[
            jax.ShapeDtypeStruct((4, 4, 64, 128), bf16),
            jax.ShapeDtypeStruct((8, 128), f32),
        ],
        cost_estimate=pl.CostEstimate(
            flops=2 * 256 * 256 * 640, bytes_accessed=900000, transcendentals=0
        ),
        name="inverse_xz",
    )(lines, along_x, along_z)


def interpolate_kernel(field_scale, field_ref, place_ref, out_ref, own_ref):
    block = lax.broadcasted_iota(jnp.int32, (128, 128), 0) // PC

    def gather(cell, carry):
        ax, cz = cell // 6, cell % 6
        field = field_ref[:, pl.ds(pl.multiple_of(ax * PC, PC), PC), :].reshape(PC * PC, 128)
        place = place_ref[cell]
        row_x = spline_row(place[0:1])
        row_y = spline_row(place[1:2])
        row_z = spline_row(place[2:3])
        right = jnp.where(block == cz + 1, jnp.tile(row_z, (8, 1)), 0.0).astype(bf16)
        partial = dot(field, right)
        left = (row_y[:, None, :] * row_x[None, :, :]).reshape(PC * PC, 128)
        out_ref[pl.ds(cell, 1), :] = jnp.sum(partial * left, axis=0, keepdims=True) * field_scale
        return carry

    lax.fori_loop(0, 24, gather, 0)
    own_ref[0:4, :] = out_ref[7:11, :]
    own_ref[4:8, :] = out_ref[13:17, :]


def interpolate(field, place, field_scale):
    return pl.pallas_call(
        functools.partial(interpolate_kernel, field_scale),
        in_specs=[VM] * 2,
        out_specs=[VM, VM],
        compiler_params=SMALL,
        out_shape=[
            jax.ShapeDtypeStruct((24, 128), f32),
            jax.ShapeDtypeStruct((8, 128), f32),
        ],
        cost_estimate=pl.CostEstimate(
            flops=24 * 2 * 256 * 128 * 128, bytes_accessed=400000, transcendentals=0
        ),
        name="interpolate",
    )(field, place)


def combination_of(t):
    return jnp.where(t < 4, 1 + t // 2, 3 * (t - 4)), t % 2


def scaled(columns, cell, slope):
    return (columns[:, cell : cell + 1] * slope.astype(f32)).astype(bf16)


def beside_kernel(
    stored_ref, own_ref, below_ref, above_ref, left_ref, right_ref, before_ref, after_ref,
    potential_ref, weight_ref, slope_ref, total_ref, own_out, near_ref, sems
):
    inner_x, inner_z = pl.ds(1, 2), pl.ds(1, 4)
    pairs = [
        (own_ref, slope_ref.at[1, inner_x, inner_z]),
        (left_ref, slope_ref.at[:, inner_x, pl.ds(0, 1)]),
        (right_ref, slope_ref.at[:, inner_x, pl.ds(5, 1)]),
        (before_ref, slope_ref.at[:, pl.ds(0, 1)]),
        (after_ref, slope_ref.at[:, pl.ds(3, 1)]),
        (below_ref, slope_ref.at[0, inner_x, inner_z]),
        (above_ref, slope_ref.at[2, inner_x, inner_z]),
        (stored_ref.at[pl.ds(0, 3)], weight_ref.at[pl.ds(0, 3)]),
        (stored_ref.at[pl.ds(3, 3)], weight_ref.at[pl.ds(3, 3)]),
    ]
    copies = [
        pltpu.make_async_copy(source, target, sems.at[i])
        for i, (source, target) in enumerate(pairs)
    ]
    for copy in copies:
        copy.start()
    for copy in copies[:7]:
        copy.wait()
    columns = jnp.transpose(potential_ref[...])
    for x in range(4):
        for z in range(6):
            near_ref[x, z] = scaled(columns, x * 6 + z, slope_ref[1, x, z])
    own_out[...] = near_ref[1:3, 1:5]
    total_ref[...] = jnp.zeros_like(total_ref)
    for copy in copies[7:]:
        copy.wait()

    def combination(t, carry):
        x, a = combination_of(t)
        for pair, (start, stop, first, width) in enumerate(SPANS):
            part = dot(
                weight_ref[t, start:stop, :, 512:768].reshape(width * 128, 256),
                near_ref[x, 2 * pair : 2 * pair + 2].reshape(256, 128),
            )
            total_ref[a, first : first + width] += part.reshape(width, 128, 128)
        return carry

    lax.fori_loop(0, 6, combination, 0)


def beside(weights, own, near, ends, potential):
    return pl.pallas_call(
        beside_kernel,
        in_specs=[ANY] * 8 + [VM],
        out_specs=[VM] * 4,
        out_shape=[
            jax.ShapeDtypeStruct((6, 8, 128, 768), bf16),
            jax.ShapeDtypeStruct((3, 4, 6, 128, 128), bf16),
            jax.ShapeDtypeStruct((2, 4, 128, 128), f32),
            jax.ShapeDtypeStruct((2, 4, 128, 128), bf16),
        ],
        scratch_shapes=[
            pltpu.VMEM((4, 6, 128, 128), bf16),
            pltpu.SemaphoreType.DMA((9,)),
        ],
        cost_estimate=pl.CostEstimate(
            flops=3000000000, bytes_accessed=12000000, transcendentals=0
        ),
        compiler_params=MIDDLE,
        name="beside",
    )(weights, own, *near, *ends, potential)


def backward_kernel(
    weight_ref, slope_ref, part_ref, own_ref, below_ref, above_ref, msg_ref, self_ref, out_ref,
    near_ref, total_ref, potential_ref
):
    potential_ref[0] = below_ref[...]
    potential_ref[1] = above_ref[...]

    def scale(side, carry):
        columns = jnp.transpose(potential_ref[side])
        for x in range(4):
            for z in range(6):
                near_ref[side, x, z] = scaled(columns, x * 6 + z, slope_ref[2 * side, x, z])
        return carry

    lax.fori_loop(0, 2, scale, 0)
    total_ref[...] = part_ref[...]

    def combination(t, carry):
        x, a = combination_of(t)
        for pair, (start, stop, first, width) in enumerate(SPANS):
            near = jnp.concatenate(
                [
                    near_ref[side, x, 2 * pair : 2 * pair + 2].reshape(256, 128)
                    for side in range(2)
                ],
                axis=0,
            )
            part = dot(weight_ref[t, start:stop, :, 0:512].reshape(width * 128, 512), near)
            total_ref[a, first : first + width] += part.reshape(width, 128, 128)
        return carry

    lax.fori_loop(0, 6, combination, 0)

    def finish(a, carry):
        back = total_ref[a].reshape(512, 128).astype(bf16)
        own = own_ref[a].reshape(512, 128)
        out_ref[a] = (dot_t(back, msg_ref[...]) + dot_t(own, self_ref[...])).reshape(4, 128, 128)
        return carry

    lax.fori_loop(0, 2, finish, 0)


def backward(weights, slope, part, own, below, above, msg_weight, self_weight):
    return pl.pallas_call(
        backward_kernel,
        in_specs=[VM] * 8,
        out_specs=VM,
        out_shape=jax.ShapeDtypeStruct((2, 4, 128, 128), f32),
        scratch_shapes=[
            pltpu.VMEM((2, 4, 6, 128, 128), bf16),
            pltpu.VMEM((2, 4, 128, 128), f32),
            pltpu.VMEM((2, 24, 128), f32),
        ],
        cost_estimate=pl.CostEstimate(
            flops=4000000000, bytes_accessed=12000000, transcendentals=0
        ),
        compiler_params=SMALL,
        name="backward",
    )(weights, slope, part, own, below, above, msg_weight, self_weight)


def wave_tables(size_x, size_y, size_z):
    i16 = np.arange(16)
    along_z = np.zeros((4, 2, 64, 2, size_z))
    for g in range(4):
        table = cas(g * 64 + np.arange(64), np.arange(size_z), size_z)
        for a in range(2):
            along_z[g, a, :, a, :] = table
    points_x = np.array([g * 32 + a * 16 + i for a in range(2) for g in range(4) for i in i16])
    along_x = cas(np.arange(size_x), points_x, size_x)
    points_y = np.array(
        [gy * 16 + gx * 4 + gz for gx in range(4) for gy in range(16) for gz in range(4)]
    )
    into_y = cas(np.arange(size_y), points_y, size_y)
    back_x = np.array(
        [((2 * g - 1 + a) % 8) * 16 + i for g in range(4) for a in range(4) for i in i16]
    )
    back_z = np.array(
        [((4 * g - 2 + c) % 16) * 16 + k for g in range(4) for c in range(8) for k in i16]
    )
    tables = (
        along_z.reshape(4, 128, 2 * size_z),
        along_x,
        into_y,
        into_y.T,
        cas(back_x, np.arange(size_x), size_x),
        cas(np.arange(size_z), back_z, size_z),
    )
    return [jnp.asarray(np.ascontiguousarray(t), dtype=bf16) for t in tables]


def influence_of(size_x, size_y, size_z):
    device = lax.axis_index(everyone)

    def wave(index, size):
        signed = jnp.where(2 * index >= size, index - size, index)
        return signed.astype(f32) * (PC / size)

    wave_x = wave(device % size_x, size_x)
    wave_y = wave(jnp.arange(size_y, dtype=jnp.int32), size_y)[:, None]
    wave_z = wave(
        device // size_x * 128 + jnp.arange(size_z // 2, dtype=jnp.int32), size_z
    )[None, :]
    squared = wave_x * wave_x + wave_y * wave_y + wave_z * wave_z
    safe = jnp.where(squared > 0, squared, 1.0)
    return jnp.where(squared > 0, jnp.exp(-((math.pi * spread_width) ** 2) * squared) / safe, 0.0)


def swapped(value, axis):
    return lax.all_to_all(value, axis, split_axis=0, concat_axis=0, tiled=True)


def body(features, msg_weight, self_weight, charge_weight, spline_corner, spline_fraction):
    cells_x, cells_y, cells_z, slots, width = features.shape
    size_x = cells_x * PC * lax.axis_size("gx")
    size_y = cells_y * PC * lax.axis_size("gy")
    size_z = cells_z * PC * lax.axis_size("gz")
    volume = size_x // PC * (size_y // PC) * (size_z // PC)
    natoms = volume * slots
    cells = cells_x * cells_z

    features_own = features.reshape(cells, slots, width)
    own = project(
        features_own,
        msg_weight,
        spline_corner.reshape(cells, 3, slots),
        spline_fraction.reshape(cells, 3, slots),
    ).reshape(cells_x, cells_z, slots + 16, width)
    near = halo_yz(own)
    ends = halo_x(own, near)
    weights, part, place = inner_pairs(own, near, features_own, self_weight)
    influence = influence_of(size_x, size_y, size_z)
    along_z, along_x, into_y, from_y, back_x, back_z = wave_tables(size_x, size_y, size_z)

    weights, slope, mesh, row_place = message_layer(
        ends, part, place, charge_weight[None, :], weights
    )
    slope_near = halo_yz(slope)
    slope_ends = halo_x(slope, slope_near)

    mesh = swapped(mesh, plane).reshape(4, 4, PC, 128)
    lines = swapped(forward_xz(mesh, along_z, along_x), everyone)
    lines = swapped(filter_y(lines, into_y, from_y, influence), everyone)
    field, energy = inverse_xz(lines, back_x, back_z, coupling / (2.0 * volume * natoms))
    field = swapped(field.reshape(16, 64, 128), plane)
    potential, atom_potential = interpolate(field, row_place.reshape(24, 8, slots), coupling / volume)
    below, above = moved(potential, "gy", 1), moved(potential, "gy", -1)
    weights, slopes, total, cotangent = beside(
        weights, slope, slope_near, slope_ends, potential
    )
    grad = backward(weights, slopes, total, cotangent, below, above, msg_weight, self_weight)
    return (
        grad.reshape(features.shape),
        atom_potential.reshape(cells_x, cells_y, cells_z, slots),
        energy[0, 0],
    )


def solution(mesh):
    in_specs = (
        P("gx", "gy", "gz", None, None),
        P(),
        P(),
        P(),
        P("gx", "gy", "gz", None, None),
        P("gx", "gy", "gz", None, None),
    )
    out_specs = (P("gx", "gy", "gz", None, None), P("gx", "gy", "gz", None), P())
    return jax.shard_map(body, mesh=mesh, in_specs=in_specs, out_specs=out_specs, check_vma=False)
```

profile of v0, /device:TPU:32, one launch (start us, length us, event | category | flops | bytes accessed | tf_op | source)
XLA Modules:
  0.0 170.4 jit_solution(1961254293170752592)
XLA Ops:
  0.6 0.7 copy.39
  1.4 0.7 copy.40
  2.1 0.9 copy-done.1
  3.0 0.8 copy-done.7
  3.8 0.2 project.1
  4.0 0.1 collective-permute-start
  4.1 8.0 %collective-permute-start.1 = (bf16[1152,128]{1,0:T(8,128)(2,1)S(1)}, bf16[1152,128]{1,0:T(8,128)(2,1)S(1)}, u32[]{:S(2)}, u32[]{:S(2)}) collective-permute-start(bf16[1152,128]{1,0:T(8,128)(2,1)S(1)} %bitcast.164), channel_id=1, source_target_pairs={{0,60},{4,0},{8,4},{12,8},{16,12},{20,16},{24,20},{28,24},{32,28},... | collective-permute-start | bytes 884744 | tf_op jit(solution)/shard_map/ppermute | solution.py:53
  12.2 0.1 fusion.influence_ref
  12.3 7.4 %collective-permute-done = bf16[1152,128]{1,0:T(8,128)(2,1)S(1)} collective-permute-done((bf16[1152,128]{1,0:T(8,128)(2,1)S(1)}, bf16[1152,128]{1,0:T(8,128)(2,1)S(1)}, u32[]{:S(2)}, u32[]{:S(2)}) %collective-permute-start) | collective-permute-done | bytes 294944 | tf_op jit(solution)/shard_map/ppermute | solution.py:53
  19.7 2.4 %collective-permute-done.1 = bf16[1152,128]{1,0:T(8,128)(2,1)S(1)} collective-permute-done((bf16[1152,128]{1,0:T(8,128)(2,1)S(1)}, bf16[1152,128]{1,0:T(8,128)(2,1)S(1)}, u32[]{:S(2)}, u32[]{:S(2)}) %collective-permute-start.1) | collective-permute-done | bytes 294944 | tf_op jit(solution)/shard_map/ppermute | solution.py:53
  22.2 2.5 %collective-permute-start.2 = (bf16[864,128]{1,0:T(8,128)(2,1)S(1)}, bf16[864,128]{1,0:T(8,128)(2,1)S(1)}, u32[]{:S(2)}, u32[]{:S(2)}) collective-permute-start(bf16[864,128]{1,0:T(8,128)(2,1)S(1)} %bitcast.208), channel_id=1, source_target_pairs={{0,1},{1,2},{2,3},{3,0},{4,5},{5,6},{6,7},{7,4},{8,9},{9,10},{10,1... | collective-permute-start | bytes 663560 | tf_op jit(solution)/shard_map/ppermute | solution.py:53
  24.7 0.1 collective-permute-start.3
  24.9 6.0 %collective-permute-done.2 = bf16[864,128]{1,0:T(8,128)(2,1)S(1)} collective-permute-done((bf16[864,128]{1,0:T(8,128)(2,1)S(1)}, bf16[864,128]{1,0:T(8,128)(2,1)S(1)}, u32[]{:S(2)}, u32[]{:S(2)}) %collective-permute-start.2) | collective-permute-done | bytes 221216 | tf_op jit(solution)/shard_map/ppermute | solution.py:53
  30.9 6.6 %collective-permute-done.3 = bf16[864,128]{1,0:T(8,128)(2,1)S(1)} collective-permute-done((bf16[864,128]{1,0:T(8,128)(2,1)S(1)}, bf16[864,128]{1,0:T(8,128)(2,1)S(1)}, u32[]{:S(2)}, u32[]{:S(2)}) %collective-permute-start.3) | collective-permute-done | bytes 221216 | tf_op jit(solution)/shard_map/ppermute | solution.py:53
  37.6 0.1 maximum_bitcast_fusion.2
  37.6 0.1 maximum_bitcast_fusion.4
  37.7 0.1 pad_maximum_fusion.1
  37.8 2.4 %collective-permute-start.5 = (bf16[2592,128]{1,0:T(8,128)(2,1)S(1)}, bf16[2592,128]{1,0:T(8,128)(2,1)S(1)}, u32[]{:S(2)}, u32[]{:S(2)}) collective-permute-start(bf16[2592,128]{1,0:T(8,128)(2,1)S(1)} %bitcast.198), channel_id=1, source_target_pairs={{0,192},{64,0},{128,64},{192,128},{1,193},{65,1},{129,65},{193,129... | collective-permute-start | bytes 1990664 | tf_op jit(solution)/shard_map/ppermute | solution.py:53
  40.2 0.1 maximum_bitcast_fusion
  40.3 0.1 pad_maximum_fusion
  40.3 0.0 copy-start.11
  40.4 0.1 collective-permute-start.4
  40.5 7.9 %inner_pairs.1 = (bf16[6,8,128,768]{3,2,1,0:T(8,128)(2,1)}, f32[2,4,128,128]{3,2,1,0:T(8,128)S(1)}, f32[3,2,6,8,128]{4,3,2,1,0:T(8,128)S(1)}) custom-call(bf16[2,4,144,128]{3,2,1,0:T(8,128)(2,1)S(1)} %bitcast.166, bf16[2,4,144,128]{3,2,1,0:T(8,128)(2,1)S(1)} %bitcast.179, bf16[2,4,144,128]{3,2,1,0:T(8,128)(2,1)S(1)} %bitcast.181, ...), custom_call_target="tpu_custom_call" | custom-call | flops 8999999488 | bytes 9000000 | tf_op jit(solution)/shard_map/inner_pairs/pallas_call | solution.py:208
  48.4 6.4 %collective-permute-done.5 = bf16[2592,128]{1,0:T(8,128)(2,1)S(1)} collective-permute-done((bf16[2592,128]{1,0:T(8,128)(2,1)S(1)}, bf16[2592,128]{1,0:T(8,128)(2,1)S(1)}, u32[]{:S(2)}, u32[]{:S(2)}) %collective-permute-start.5) | collective-permute-done | bytes 663584 | tf_op jit(solution)/shard_map/ppermute | solution.py:53
  54.8 3.5 %collective-permute-done.4 = bf16[2592,128]{1,0:T(8,128)(2,1)S(1)} collective-permute-done((bf16[2592,128]{1,0:T(8,128)(2,1)S(1)}, bf16[2592,128]{1,0:T(8,128)(2,1)S(1)}, u32[]{:S(2)}, u32[]{:S(2)}) %collective-permute-start.4) | collective-permute-done | bytes 663584 | tf_op jit(solution)/shard_map/ppermute | solution.py:53
  58.3 0.0 copy-start.5
  58.4 6.0 %message.1 = (bf16[6,8,128,768]{3,2,1,0:T(8,128)(2,1)}, bf16[2,4,128,128]{3,2,1,0:T(8,128)(2,1)S(1)}, bf16[16,16,128]{2,1,0:T(8,128)(2,1)}, f32[4,6,8,128]{3,2,1,0:T(8,128)S(1)}) custom-call(bf16[3,1,6,144,128]{4,3,2,1,0:T(8,128)(2,1)S(1)} %bitcast.195, bf16[3,1,6,144,128]{4,3,2,1,0:T(8,128)(2,1)S(1)} %bitcast.194, ...), custom_call_target="tpu_custom_call", output_to_operand_aliasing={{0}: (5, {})} | custom-call | flops 5000000000 | bytes 6000000 | tf_op jit(solution)/shard_map/message/pallas_call | solution.py:340
  64.3 0.0 copy-start.3
  64.3 0.0 copy-start.6
  64.3 0.1 collective-permute-start.6
  64.4 7.7 %collective-permute-start.7 = (bf16[1024,128]{1,0:T(8,128)(2,1)S(1)}, bf16[1024,128]{1,0:T(8,128)(2,1)S(1)}, u32[]{:S(2)}, u32[]{:S(2)}) collective-permute-start(bf16[1024,128]{1,0:T(8,128)(2,1)S(1)} %bitcast.168), channel_id=1, source_target_pairs={{0,60},{4,0},{8,4},{12,8},{16,12},{20,16},{24,20},{28,24},{32,28},... | collective-permute-start | bytes 786440 | tf_op jit(solution)/shard_map/ppermute | solution.py:53
  72.2 3.7 %all-to-all-start = ((bf16[16,16,128]{2,1,0:T(8,128)(2,1)}), bf16[16,16,128]{2,1,0:T(8,128)(2,1)S(1)}, u32[]{:S(2)}, u32[]{:S(2)}) async-start(bf16[16,16,128]{2,1,0:T(8,128)(2,1)} %get-tuple-element.23), calls=%async_computation | async-start | bytes 131072 | tf_op jit(solution)/shard_map/all_to_all | solution.py:671
  75.9 7.0 %all-to-all-done = bf16[16,16,128]{2,1,0:T(8,128)(2,1)S(1)} async-done(((bf16[16,16,128]{2,1,0:T(8,128)(2,1)}), bf16[16,16,128]{2,1,0:T(8,128)(2,1)S(1)}, u32[]{:S(2)}, u32[]{:S(2)}) %all-to-all-start) | async-done | bytes 65568 | tf_op jit(solution)/shard_map/all_to_all | solution.py:671
  82.9 1.0 forward_xz.1
  83.9 12.0 %all-to-all-start.1 = ((f32[256,1,128]{2,1,0:T(1,128)}), f32[256,1,128]{2,1,0:T(1,128)S(1)}, u32[]{:S(2)}, u32[]{:S(2)}) async-start(f32[256,1,128]{2,1,0:T(1,128)} %bitcast.87), calls=%async_computation.1 | async-start | bytes 262144 | tf_op jit(solution)/shard_map/all_to_all | solution.py:671
  95.9 0.0 collective-permute-done.6
  96.0 0.0 collective-permute-done.7
  96.0 0.7 pad_maximum_fusion.7
  96.7 2.0 %collective-permute-start.9 = (bf16[768,128]{1,0:T(8,128)(2,1)}, bf16[768,128]{1,0:T(8,128)(2,1)S(1)}, u32[]{:S(2)}, u32[]{:S(2)}) collective-permute-start(bf16[768,128]{1,0:T(8,128)(2,1)} %bitcast.57), channel_id=1, source_target_pairs={{0,3},{1,0},{2,1},{3,2},{4,7},{5,4},{6,5},{7,6},{8,11},{9,8},{10,9... | collective-permute-start | bytes 589832 | tf_op jit(solution)/shard_map/ppermute | solution.py:53
  98.7 0.7 pad_maximum_fusion.6
  99.4 0.0 collective-permute-start.8
  99.5 9.2 %all-to-all-done.1 = f32[256,1,128]{2,1,0:T(1,128)S(1)} async-done(((f32[256,1,128]{2,1,0:T(1,128)}), f32[256,1,128]{2,1,0:T(1,128)S(1)}, u32[]{:S(2)}, u32[]{:S(2)}) %all-to-all-start.1) | async-done | bytes 131104 | tf_op jit(solution)/shard_map/all_to_all | solution.py:671
  108.6 1.1 filter_y.1
  109.7 6.2 %all-to-all-start.2 = ((f32[256,2,128]{2,1,0:T(2,128)}), f32[256,2,128]{2,1,0:T(2,128)S(1)}, u32[]{:S(2)}, u32[]{:S(2)}) async-start(f32[256,2,128]{2,1,0:T(2,128)} %bitcast.89), calls=%async_computation.2 | async-start | bytes 524288 | tf_op jit(solution)/shard_map/all_to_all | solution.py:671
  115.9 0.0 collective-permute-done.9
  116.0 0.0 copy-start.8
  116.0 0.0 collective-permute-done.8
  116.1 0.9 pad_maximum_fusion.3
  117.0 2.9 %collective-permute-start.11 = (bf16[2304,128]{1,0:T(8,128)(2,1)}, bf16[2304,128]{1,0:T(8,128)(2,1)S(1)}, u32[]{:S(2)}, u32[]{:S(2)}) collective-permute-start(bf16[2304,128]{1,0:T(8,128)(2,1)} %bitcast.83), channel_id=1, source_target_pairs={{0,192},{64,0},{128,64},{192,128},{1,193},{65,1},{129,65},{193,129... | collective-permute-start | bytes 1769480 | tf_op jit(solution)/shard_map/ppermute | solution.py:53
  120.0 0.9 pad_maximum_fusion.2
  120.9 0.0 collective-permute-start.10
  120.9 10.3 %all-to-all-done.2 = f32[256,2,128]{2,1,0:T(2,128)S(1)} async-done(((f32[256,2,128]{2,1,0:T(2,128)}), f32[256,2,128]{2,1,0:T(2,128)S(1)}, u32[]{:S(2)}, u32[]{:S(2)}) %all-to-all-start.2) | async-done | bytes 262176 | tf_op jit(solution)/shard_map/all_to_all | solution.py:671
  131.2 1.0 inverse_xz.1
  132.3 4.4 %all-to-all-start.3 = ((bf16[16,64,128]{2,1,0:T(8,128)(2,1)}), bf16[16,64,128]{2,1,0:T(8,128)(2,1)S(1)}, u32[]{:S(2)}, u32[]{:S(2)}) async-start(bf16[16,64,128]{2,1,0:T(8,128)(2,1)} %bitcast.91), calls=%async_computation.3 | async-start | bytes 524288 | tf_op jit(solution)/shard_map/all_to_all | solution.py:671
  136.6 0.5 slice.235
  137.1 9.1 %all-to-all-done.3.field_ref = bf16[16,64,128]{2,1,0:T(8,128)(2,1)S(1)} async-done(((bf16[16,64,128]{2,1,0:T(8,128)(2,1)}), bf16[16,64,128]{2,1,0:T(8,128)(2,1)S(1)}, u32[]{:S(2)}, u32[]{:S(2)}) %all-to-all-start.3) | async-done | bytes 262176 | tf_op jit(solution)/shard_map/all_to_all | solution.py:671
  146.3 5.3 %interpolate.1 = (f32[24,128]{1,0:T(8,128)S(1)}, f32[8,128]{1,0:T(8,128)}) custom-call(bf16[16,64,128]{2,1,0:T(8,128)(2,1)S(1)} %all-to-all-done.3.field_ref, f32[24,8,128]{2,1,0:T(8,128)S(1)} %bitcast.197), custom_call_target="tpu_custom_call" | custom-call | flops 201326592 | bytes 400000 | tf_op jit(solution)/shard_map/interpolate/pallas_call | solution.py:469
  151.6 0.0 collective-permute-start.12
  151.6 7.8 %collective-permute-start.13 = (f32[24,128]{1,0:T(8,128)S(1)}, f32[24,128]{1,0:T(8,128)S(1)}, u32[]{:S(2)}, u32[]{:S(2)}) collective-permute-start(f32[24,128]{1,0:T(8,128)S(1)} %get-tuple-element.26.potential_ref), channel_id=1, source_target_pairs={{0,60},{4,0},{8,4},{12,8},{16,12},{20,16},{24,20},{28,24},{32,28},... | collective-permute-start | bytes 36872 | tf_op jit(solution)/shard_map/ppermute | solution.py:53
  159.4 0.0 collective-permute-done.11
  159.4 0.0 collective-permute-done.10
  159.4 5.9 %beside.1 = (bf16[6,8,128,768]{3,2,1,0:T(8,128)(2,1)S(1)}, bf16[3,4,6,128,128]{4,3,2,1,0:T(8,128)(2,1)S(1)}, f32[2,4,128,128]{3,2,1,0:T(8,128)S(1)}, bf16[2,4,128,128]{3,2,1,0:T(8,128)(2,1)S(1)}) custom-call(bf16[6,8,128,768]{3,2,1,0:T(8,128)(2,1)} %get-tuple-element.21.stored_ref, bf16[2,4,128,128]{3,2,1,0:T(8,128)(2,1)S(1)} %get-tuple-element.22.own_ref, ...), custom_call_target="tpu_custom_call" | custom-call | flops 3000000000 | bytes 12000000 | tf_op jit(solution)/shard_map/beside/pallas_call | solution.py:540
  165.2 0.0 collective-permute-done.12.below_ref
  165.3 5.2 %backward.1 = f32[2,4,128,128]{3,2,1,0:T(8,128)} custom-call(bf16[6,8,128,768]{3,2,1,0:T(8,128)(2,1)S(1)} %get-tuple-element.27.weight_ref, bf16[3,4,6,128,128]{4,3,2,1,0:T(8,128)(2,1)S(1)} %get-tuple-element.28.slope_ref, f32[2,4,128,128]{3,2,1,0:T(8,128)S(1)} %get-tuple-element.29.part_ref, bf16[2,4,128,128]{3,2,1,0:T(8,128)(2,1)S(1)} %get-tuple-element.30.own_ref, ...), custom_call_target="tpu_custom_call" | custom-call | flops 4000000000 | bytes 12000000 | tf_op jit(solution)/shard_map/backward/pallas_call | solution.py:605
  (44 shorter events, 0.5 us)
Async XLA Ops:
  0.6 39.8 %copy-start.10 = (bf16[128,128]{1,0:T(8,128)(2,1)S(1)}, bf16[128,128]{1,0:T(8,128)(2,1)}, u32[]{:S(2)}) copy-start(bf16[128,128]{1,0:T(8,128)(2,1)} %self_ref.3) | copy-start | bytes 98308
  2.1 0.9 copy-start.1
  3.0 0.8 copy-start.7
  3.8 36.7 %copy-start.2 = (bf16[2,1,4,128,128]{4,3,2,1,0:T(8,128)(2,1)S(1)}, bf16[2,1,4,128,128]{4,3,2,1,0:T(8,128)(2,1)}, u32[]{:S(2)}) copy-start(bf16[2,1,4,128,128]{4,3,2,1,0:T(8,128)(2,1)} %param.12) | copy-start | bytes 786436
  4.0 15.7 %collective-permute-start = (bf16[1152,128]{1,0:T(8,128)(2,1)S(1)}, bf16[1152,128]{1,0:T(8,128)(2,1)S(1)}, u32[]{:S(2)}, u32[]{:S(2)}) collective-permute-start(bf16[1152,128]{1,0:T(8,128)(2,1)S(1)} %bitcast.163), channel_id=1, source_target_pairs={{0,4},{4,8},{8,12},{12,16},{16,20},{20,24},{24,28},{28,32},{32,36}... | collective-permute-start | bytes 884744 | tf_op jit(solution)/shard_map/ppermute | solution.py:53
  4.1 18.0 %collective-permute-start.1 = (bf16[1152,128]{1,0:T(8,128)(2,1)S(1)}, bf16[1152,128]{1,0:T(8,128)(2,1)S(1)}, u32[]{:S(2)}, u32[]{:S(2)}) collective-permute-start(bf16[1152,128]{1,0:T(8,128)(2,1)S(1)} %bitcast.164), channel_id=1, source_target_pairs={{0,60},{4,0},{8,4},{12,8},{16,12},{20,16},{24,20},{28,24},{32,28},... | collective-permute-start | bytes 884744 | tf_op jit(solution)/shard_map/ppermute | solution.py:53
  22.2 8.8 %collective-permute-start.2 = (bf16[864,128]{1,0:T(8,128)(2,1)S(1)}, bf16[864,128]{1,0:T(8,128)(2,1)S(1)}, u32[]{:S(2)}, u32[]{:S(2)}) collective-permute-start(bf16[864,128]{1,0:T(8,128)(2,1)S(1)} %bitcast.208), channel_id=1, source_target_pairs={{0,1},{1,2},{2,3},{3,0},{4,5},{5,6},{6,7},{7,4},{8,9},{9,10},{10,1... | collective-permute-start | bytes 663560 | tf_op jit(solution)/shard_map/ppermute | solution.py:53
  24.7 12.8 %collective-permute-start.3 = (bf16[864,128]{1,0:T(8,128)(2,1)S(1)}, bf16[864,128]{1,0:T(8,128)(2,1)S(1)}, u32[]{:S(2)}, u32[]{:S(2)}) collective-permute-start(bf16[864,128]{1,0:T(8,128)(2,1)S(1)} %bitcast.209), channel_id=1, source_target_pairs={{0,3},{1,0},{2,1},{3,2},{4,7},{5,4},{6,5},{7,6},{8,11},{9,8},{10,9... | collective-permute-start | bytes 663560 | tf_op jit(solution)/shard_map/ppermute | solution.py:53
  37.8 17.0 %collective-permute-start.5 = (bf16[2592,128]{1,0:T(8,128)(2,1)S(1)}, bf16[2592,128]{1,0:T(8,128)(2,1)S(1)}, u32[]{:S(2)}, u32[]{:S(2)}) collective-permute-start(bf16[2592,128]{1,0:T(8,128)(2,1)S(1)} %bitcast.198), channel_id=1, source_target_pairs={{0,192},{64,0},{128,64},{192,128},{1,193},{65,1},{129,65},{193,129... | collective-permute-start | bytes 1990664 | tf_op jit(solution)/shard_map/ppermute | solution.py:53
  40.3 18.0 %copy-start.11 = (bf16[128]{0:T(256)(128)(2,1)S(1)}, bf16[128]{0:T(256)(128)(2,1)}, u32[]{:S(2)}) copy-start(bf16[128]{0:T(256)(128)(2,1)} %param.15) | copy-start | bytes 772
  40.4 18.0 %collective-permute-start.4 = (bf16[2592,128]{1,0:T(8,128)(2,1)S(1)}, bf16[2592,128]{1,0:T(8,128)(2,1)S(1)}, u32[]{:S(2)}, u32[]{:S(2)}) collective-permute-start(bf16[2592,128]{1,0:T(8,128)(2,1)S(1)} %bitcast.199), channel_id=1, source_target_pairs={{0,64},{64,128},{128,192},{192,0},{1,65},{65,129},{129,193},{193,1... | collective-permute-start | bytes 1990664 | tf_op jit(solution)/shard_map/ppermute | solution.py:53
  58.3 24.5 %copy-start = (bf16[4,128,512]{2,1,0:T(8,128)(2,1)S(1)}, bf16[4,128,512]{2,1,0:T(8,128)(2,1)}, u32[]{:S(2)}) copy-start(bf16[4,128,512]{2,1,0:T(8,128)(2,1)} %constant.80.clone.along_z_ref) | copy-start | bytes 1572868
  58.3 24.5 %copy-start.9 = (bf16[128,128]{1,0:T(8,128)(2,1)S(1)}, bf16[128,128]{1,0:T(8,128)(2,1)}, u32[]{:S(2)}) copy-start(bf16[128,128]{1,0:T(8,128)(2,1)} %constant.81.clone.along_x_ref) | copy-start | bytes 98308
  58.3 50.3 %copy-start.4 = (bf16[256,256]{1,0:T(8,128)(2,1)S(1)}, bf16[256,256]{1,0:T(8,128)(2,1)}, u32[]{:S(2)}) copy-start(bf16[256,256]{1,0:T(8,128)(2,1)} %constant.82.clone.into_ref) | copy-start | bytes 393220
  58.3 50.3 %copy-start.5 = (bf16[256,256]{1,0:T(8,128)(2,1)S(1)}, bf16[256,256]{1,0:T(8,128)(2,1)}, u32[]{:S(2)}) copy-start(bf16[256,256]{1,0:T(8,128)(2,1)} %constant.83.clone.back_ref) | copy-start | bytes 393220
  64.3 66.9 %copy-start.3 = (bf16[256,512]{1,0:T(8,128)(2,1)S(1)}, bf16[256,512]{1,0:T(8,128)(2,1)}, u32[]{:S(2)}) copy-start(bf16[256,512]{1,0:T(8,128)(2,1)} %constant.85.clone.along_z_ref) | copy-start | bytes 786436
  64.3 66.9 %copy-start.6 = (bf16[256,128]{1,0:T(8,128)(2,1)S(1)}, bf16[256,128]{1,0:T(8,128)(2,1)}, u32[]{:S(2)}) copy-start(bf16[256,128]{1,0:T(8,128)(2,1)} %constant.84.clone.along_x_ref) | copy-start | bytes 196612
  64.3 31.6 %collective-permute-start.6 = (bf16[1024,128]{1,0:T(8,128)(2,1)S(1)}, bf16[1024,128]{1,0:T(8,128)(2,1)S(1)}, u32[]{:S(2)}, u32[]{:S(2)}) collective-permute-start(bf16[1024,128]{1,0:T(8,128)(2,1)S(1)} %bitcast.167), channel_id=1, source_target_pairs={{0,4},{4,8},{8,12},{12,16},{16,20},{20,24},{24,28},{28,32},{32,36}... | collective-permute-start | bytes 786440 | tf_op jit(solution)/shard_map/ppermute | solution.py:53
  64.4 31.5 %collective-permute-start.7 = (bf16[1024,128]{1,0:T(8,128)(2,1)S(1)}, bf16[1024,128]{1,0:T(8,128)(2,1)S(1)}, u32[]{:S(2)}, u32[]{:S(2)}) collective-permute-start(bf16[1024,128]{1,0:T(8,128)(2,1)S(1)} %bitcast.168), channel_id=1, source_target_pairs={{0,60},{4,0},{8,4},{12,8},{16,12},{20,16},{24,20},{28,24},{32,28},... | collective-permute-start | bytes 786440 | tf_op jit(solution)/shard_map/ppermute | solution.py:53
  72.2 10.6 %all-to-all-start = ((bf16[16,16,128]{2,1,0:T(8,128)(2,1)}), bf16[16,16,128]{2,1,0:T(8,128)(2,1)S(1)}, u32[]{:S(2)}, u32[]{:S(2)}) async-start(bf16[16,16,128]{2,1,0:T(8,128)(2,1)} %get-tuple-element.23), calls=%async_computation | async-start | bytes 131072 | tf_op jit(solution)/shard_map/all_to_all | solution.py:671
  83.9 24.7 %all-to-all-start.1 = ((f32[256,1,128]{2,1,0:T(1,128)}), f32[256,1,128]{2,1,0:T(1,128)S(1)}, u32[]{:S(2)}, u32[]{:S(2)}) async-start(f32[256,1,128]{2,1,0:T(1,128)} %bitcast.87), calls=%async_computation.1 | async-start | bytes 262144 | tf_op jit(solution)/shard_map/all_to_all | solution.py:671
  96.7 19.2 %collective-permute-start.9 = (bf16[768,128]{1,0:T(8,128)(2,1)}, bf16[768,128]{1,0:T(8,128)(2,1)S(1)}, u32[]{:S(2)}, u32[]{:S(2)}) collective-permute-start(bf16[768,128]{1,0:T(8,128)(2,1)} %bitcast.57), channel_id=1, source_target_pairs={{0,3},{1,0},{2,1},{3,2},{4,7},{5,4},{6,5},{7,6},{8,11},{9,8},{10,9... | collective-permute-start | bytes 589832 | tf_op jit(solution)/shard_map/ppermute | solution.py:53
  99.4 16.6 %collective-permute-start.8 = (bf16[768,128]{1,0:T(8,128)(2,1)}, bf16[768,128]{1,0:T(8,128)(2,1)S(1)}, u32[]{:S(2)}, u32[]{:S(2)}) collective-permute-start(bf16[768,128]{1,0:T(8,128)(2,1)} %bitcast.52), channel_id=1, source_target_pairs={{0,1},{1,2},{2,3},{3,0},{4,5},{5,6},{6,7},{7,4},{8,9},{9,10},{10,1... | collective-permute-start | bytes 589832 | tf_op jit(solution)/shard_map/ppermute | solution.py:53
  109.7 21.5 %all-to-all-start.2 = ((f32[256,2,128]{2,1,0:T(2,128)}), f32[256,2,128]{2,1,0:T(2,128)S(1)}, u32[]{:S(2)}, u32[]{:S(2)}) async-start(f32[256,2,128]{2,1,0:T(2,128)} %bitcast.89), calls=%async_computation.2 | async-start | bytes 524288 | tf_op jit(solution)/shard_map/all_to_all | solution.py:671
  116.0 49.3 %copy-start.8 = (bf16[128,128]{1,0:T(8,128)(2,1)S(1)}, bf16[128,128]{1,0:T(8,128)(2,1)}, u32[]{:S(2)}) copy-start(bf16[128,128]{1,0:T(8,128)(2,1)} %msg_ref.1) | copy-start | bytes 98308
  117.0 42.4 %collective-permute-start.11 = (bf16[2304,128]{1,0:T(8,128)(2,1)}, bf16[2304,128]{1,0:T(8,128)(2,1)S(1)}, u32[]{:S(2)}, u32[]{:S(2)}) collective-permute-start(bf16[2304,128]{1,0:T(8,128)(2,1)} %bitcast.83), channel_id=1, source_target_pairs={{0,192},{64,0},{128,64},{192,128},{1,193},{65,1},{129,65},{193,129... | collective-permute-start | bytes 1769480 | tf_op jit(solution)/shard_map/ppermute | solution.py:53
  120.9 38.5 %collective-permute-start.10 = (bf16[2304,128]{1,0:T(8,128)(2,1)}, bf16[2304,128]{1,0:T(8,128)(2,1)S(1)}, u32[]{:S(2)}, u32[]{:S(2)}) collective-permute-start(bf16[2304,128]{1,0:T(8,128)(2,1)} %bitcast.70), channel_id=1, source_target_pairs={{0,64},{64,128},{128,192},{192,0},{1,65},{65,129},{129,193},{193,1... | collective-permute-start | bytes 1769480 | tf_op jit(solution)/shard_map/ppermute | solution.py:53
  132.3 14.0 %all-to-all-start.3 = ((bf16[16,64,128]{2,1,0:T(8,128)(2,1)}), bf16[16,64,128]{2,1,0:T(8,128)(2,1)S(1)}, u32[]{:S(2)}, u32[]{:S(2)}) async-start(bf16[16,64,128]{2,1,0:T(8,128)(2,1)} %bitcast.91), calls=%async_computation.3 | async-start | bytes 524288 | tf_op jit(solution)/shard_map/all_to_all | solution.py:671
  151.6 13.6 %collective-permute-start.12 = (f32[24,128]{1,0:T(8,128)S(1)}, f32[24,128]{1,0:T(8,128)S(1)}, u32[]{:S(2)}, u32[]{:S(2)}) collective-permute-start(f32[24,128]{1,0:T(8,128)S(1)} %get-tuple-element.26.potential_ref), channel_id=1, source_target_pairs={{0,4},{4,8},{8,12},{12,16},{16,20},{20,24},{24,28},{28,32},{32,36}... | collective-permute-start | bytes 36872 | tf_op jit(solution)/shard_map/ppermute | solution.py:53
  151.6 13.6 %collective-permute-start.13 = (f32[24,128]{1,0:T(8,128)S(1)}, f32[24,128]{1,0:T(8,128)S(1)}, u32[]{:S(2)}, u32[]{:S(2)}) collective-permute-start(f32[24,128]{1,0:T(8,128)S(1)} %get-tuple-element.26.potential_ref), channel_id=1, source_target_pairs={{0,60},{4,0},{8,4},{12,8},{16,12},{20,16},{24,20},{28,24},{32,28},... | collective-permute-start | bytes 36872 | tf_op jit(solution)/shard_map/ppermute | solution.py:53
where the time goes:
time: 171 us; the launch traced here: 170 us
  waiting for transfers between devices  68 us (40%)
  starting transfers between devices  59.9 us (35%)
  Pallas kernels  33.6 us (20%)
  local copies, waits for them, and re-layouts  3.95 us (2%)
  other arithmetic  3.89 us (2%)
    all_to_all x4, waiting for transfers between devices, swapped(): return lax.all_to_all(value, axis, split_axis=0, concat_axis=0, tiled=True)  35.6 us
    ppermute x14, starting transfers between devices, moved(): lax.ppermute(value.reshape(-1, 128), axis, pairs).reshape(value.shape)  33.7 us
    ppermute x14, waiting for transfers between devices, moved(): lax.ppermute(value.reshape(-1, 128), axis, pairs).reshape(value.shape)  32.4 us
    all_to_all x4, starting transfers between devices, swapped(): return lax.all_to_all(value, axis, split_axis=0, concat_axis=0, tiled=True)  26.2 us
    pallas_call x1, Pallas kernels, inner_pairs(): pl.pallas_call(inner_kernel, in_specs=[VM] * 7, out_specs=[ANY, VM, VM],...  7.89 us
    pallas_call x1, Pallas kernels, message_layer(): pl.pallas_call(message_kernel, in_specs=[VM] * 5 + [ANY], out_specs=[ANY,...  5.96 us
    pallas_call x1, Pallas kernels, beside(): pl.pallas_call(beside_kernel, in_specs=[ANY] * 8 + [VM], out_specs=[VM] *...  5.85 us
    pallas_call x1, Pallas kernels, interpolate(): pl.pallas_call(functools.partial(interpolate_kernel, field_scale), in_spe...  5.32 us
  transfers between devices with their start and end apart: 18, of which 10 were waited for; matrix products, arithmetic and copies ran while one was open for 3% of the time, Pallas kernels for 13%

commit v1 on v0

--- a/solution.py
+++ b/solution.py
@@ -53,39 +53,35 @@
     return lax.ppermute(value.reshape(-1, 128), axis, pairs).reshape(value.shape)
 
 
-def halo_yz(own):
-    last = own.shape[1] - 1
-    sides = [moved(own, "gy", 1), moved(own, "gy", -1)]
-    rows = [sides[0], own, sides[1]]
-    ends = [
-        moved(jnp.stack([row[:, last:] for row in rows]), "gz", 1),
-        moved(jnp.stack([row[:, :1] for row in rows]), "gz", -1),
+def late_halo(own):
+    last_x, last_z = own.shape[0] - 1, own.shape[1] - 1
+    left, right = moved(own[:, last_z:], "gz", 1), moved(own[:, :1], "gz", -1)
+    row = jnp.concatenate([left, own, right], axis=1)
+    rows = jnp.stack([moved(row, "gy", 1), row, moved(row, "gy", -1)])
+    return [rows, moved(rows[:, last_x:], "gx", 1), moved(rows[:, :1], "gx", -1)]
+
+
+def early_halo(own):
+    last_x, last_z = own.shape[0] - 1, own.shape[1] - 1
+    below, above = moved(own, "gy", 1), moved(own, "gy", -1)
+    beside = [moved(own[last_x:], "gx", 1), moved(own[:1], "gx", -1)]
+    sides = jnp.stack([below, above])
+    rows = [below, own, above]
+    left = moved(jnp.stack([row[:, last_z:] for row in rows]), "gz", 1)
+    right = moved(jnp.stack([row[:, :1] for row in rows]), "gz", -1)
+    aside = [moved(sides[:, last_x:], "gx", 1), moved(sides[:, :1], "gx", -1)]
+    corners = [
+        moved(jnp.concatenate([left[:, at : at + 1], right[:, at : at + 1]], axis=2), "gx", step)
+        for at, step in ((last_x, 1), (0, -1))
     ]
-    return sides + ends
-
-
-def halo_x(own, near):
-    below, above, left, right = near
-    last = own.shape[0] - 1
-    rows = (below, own, above)
-
-    def slab(at):
-        return jnp.stack(
-            [
-                jnp.concatenate(
-                    [left[i, at : at + 1], row[at : at + 1], right[i, at : at + 1]], axis=1
-                )
-                for i, row in enumerate(rows)
-            ]
-        )
-
-    return [moved(slab(last), "gx", 1), moved(slab(0), "gx", -1)]
+    return [below, above, left, right], beside + aside + corners
 
 
 def project_kernel(features_ref, weight_ref, corner_ref, fraction_ref, out_ref):
     value = dot(features_ref[...].reshape(1024, 128), weight_ref[...]).astype(bf16)
     out_ref[:, :128, :] = value.reshape(8, 128, 128)
-    place = corner_ref[...].astype(f32) + 1.0 + fraction_ref[...]
+    place = corner_ref[:, 0].astype(f32) + 1.0 + fraction_ref[:, 0]
+    place = place.reshape(8, 3, 128)
     high = place.astype(bf16).astype(f32)
     rest = place - high
     middle = rest.astype(bf16).astype(f32)
@@ -99,7 +95,8 @@
     return pl.pallas_call(
         project_kernel,
         grid=(1,),
-        in_specs=[whole((8, 128, 128)), whole((128, 128)), whole((8, 3, 128)), whole((8, 3, 128))],
+        in_specs=[whole((8, 128, 128)), whole((128, 128))]
+        + [whole((2, 1, 4, 3, 128))] * 2,
         out_specs=whole((8, 144, 128)),
         out_shape=jax.ShapeDtypeStruct((8, 144, 128), bf16),
         compiler_params=SMALL,
@@ -237,29 +234,30 @@
 
 
 def message_kernel(
-    before_ref, after_ref, part_ref, place_ref, read_ref, _,
-    weight_out, slope_ref, mesh_ref, row_place_ref,
-    weight_ref, position_ref, centre_ref, total_ref, high_ref, low_ref, charge_ref, left_ref,
+    before_own, after_own, before_side, after_side, before_end, after_end,
+    part_ref, place_ref, read_ref, _,
+    weight_out, total_ref, mesh_ref, row_place_ref,
+    weight_ref, position_ref, centre_ref, high_ref, low_ref, charge_ref, left_ref,
     right_ref, sems
 ):
-    refs = (before_ref, after_ref)
+    refs = ((before_own, before_side, before_end), (after_own, after_side, after_end))
+
+    def cell(side, dy, z):
+        own, beside, end = refs[side]
+        if z in (0, 5):
+            return end.at[dy, 0, z // 5]
+        return own.at[0, z - 1] if dy == 1 else beside.at[dy // 2, 0, z - 1]
 
     def position(place):
         return (place * (1.0 / PC)).astype(bf16).astype(f32)
 
-    def places(dy, carry):
-        for side in range(2):
+    for side in range(2):
+        for dy in range(3):
             for z in range(6):
-                place = place_of(refs[side][dy, 0, z, 128:144, :])
+                place = place_of(cell(side, dy, z)[128:144, :])
                 position_ref[side, dy, z] = position(place)
-
-                @pl.when(dy == 1)
-                def _():
+                if dy == 1:
                     row_place_ref[3 * side, z] = place
-
-        return carry
-
-    lax.fori_loop(0, 3, places, 0)
     for x in range(2):
         for z in range(6):
             place = place_ref[1, x, z]
@@ -290,7 +288,7 @@
         for pair, (start, stop, first, width) in enumerate(SPANS):
             near = jnp.concatenate(
                 [
-                    refs[t][dy, 0, 2 * pair + half, 0:128, :]
+                    cell(t, dy, 2 * pair + half)[0:128, :]
                     for dy in ORDER_Y
                     for half in range(2)
                 ],
@@ -298,20 +296,16 @@
             )
             part = dot(weight_ref[t, start:stop].reshape(width * 128, 768), near)
             total_ref[t, first : first + width] += part.reshape(width, 128, 128)
-    read = read_ref[...].astype(f32)
-
-    def finish(cell, carry):
-        a, c = cell // 4, cell % 4
-        preact = total_ref[a, c]
-        sigma = 0.5 + 0.5 * jnp.tanh(0.5 * preact)
-        slope_ref[a, c] = (read * (sigma * (1.0 + preact * (1.0 - sigma)))).astype(bf16)
-        silu = preact * sigma
+
+    def finish(index, carry):
+        preact = total_ref[index // 4, index % 4]
+        silu = preact * (0.5 + 0.5 * jnp.tanh(0.5 * preact))
         high = silu.astype(bf16)
-        high_ref[cell] = high
-        low_ref[cell] = (silu - high.astype(f32)).astype(bf16)
-        return carry
-
-    lax.fori_loop(0, 8, finish, 0)
+        high_ref[index] = high
+        low_ref[index] = (silu - high.astype(f32)).astype(bf16)
+        return carry
+
+    lax.fori_loop(0, 8, finish, 0, unroll=2)
     wide = jnp.broadcast_to(read_ref[...], (16, 128))
     charge_ref[...] = dot_t(wide, high_ref[...].reshape(1024, 128)) + dot_t(
         wide, low_ref[...].reshape(1024, 128)
@@ -339,12 +333,12 @@
 def message_layer(ends, part, place, read, weights):
     return pl.pallas_call(
         message_kernel,
-        in_specs=[VM] * 5 + [ANY],
+        in_specs=[VM] * 9 + [ANY],
         out_specs=[ANY, VM, VM, VM],
-        input_output_aliases={5: 0},
+        input_output_aliases={9: 0},
         out_shape=[
             jax.ShapeDtypeStruct((6, 8, 128, 768), bf16),
-            jax.ShapeDtypeStruct((2, 4, 128, 128), bf16),
+            jax.ShapeDtypeStruct((2, 4, 128, 128), f32),
             jax.ShapeDtypeStruct((PC, PC, 128), bf16),
             jax.ShapeDtypeStruct((4, 6, 8, 128), f32),
         ],
@@ -352,7 +346,6 @@
             pltpu.VMEM((2, 8, 128, 768), bf16),
             pltpu.VMEM((2, 3, 6, 8, 128), f32),
             pltpu.VMEM((2, 4, 8, 128), f32),
-            pltpu.VMEM((2, 4, 128, 128), f32),
             pltpu.VMEM((8, 128, 128), bf16),
             pltpu.VMEM((8, 128, 128), bf16),
             pltpu.VMEM((16, 1024), f32),
@@ -366,6 +359,33 @@
         compiler_params=LARGE,
         name="message",
     )(*ends, part, place, read, weights)
+
+
+def slope_kernel(total_ref, read_ref, out_ref):
+    read = read_ref[...].astype(f32)
+
+    def one(index, carry):
+        a, c = index // 4, index % 4
+        preact = total_ref[a, c]
+        sigma = 0.5 + 0.5 * jnp.tanh(0.5 * preact)
+        out_ref[a, c] = (read * (sigma * (1.0 + preact * (1.0 - sigma)))).astype(bf16)
+        return carry
+
+    lax.fori_loop(0, 8, one, 0, unroll=2)
+
+
+def slope_of(total, read):
+    return pl.pallas_call(
+        slope_kernel,
+        in_specs=[VM] * 2,
+        out_specs=VM,
+        out_shape=jax.ShapeDtypeStruct(total.shape, bf16),
+        cost_estimate=pl.CostEstimate(
+            flops=8 * 16384 * 8, bytes_accessed=900000, transcendentals=8 * 16384
+        ),
+        compiler_params=SMALL,
+        name="slope",
+    )(total, read)
 
 
 def forward_kernel(mesh_ref, along_z_ref, along_x_ref, out_ref):
@@ -447,20 +467,24 @@
 def interpolate_kernel(field_scale, field_ref, place_ref, out_ref, own_ref):
     block = lax.broadcasted_iota(jnp.int32, (128, 128), 0) // PC
 
-    def gather(cell, carry):
-        ax, cz = cell // 6, cell % 6
+    def gather(step, carry):
+        ax, half = step // 2, 3 * (step % 2)
         field = field_ref[:, pl.ds(pl.multiple_of(ax * PC, PC), PC), :].reshape(PC * PC, 128)
-        place = place_ref[cell]
-        row_x = spline_row(place[0:1])
-        row_y = spline_row(place[1:2])
-        row_z = spline_row(place[2:3])
-        right = jnp.where(block == cz + 1, jnp.tile(row_z, (8, 1)), 0.0).astype(bf16)
-        partial = dot(field, right)
-        left = (row_y[:, None, :] * row_x[None, :, :]).reshape(PC * PC, 128)
-        out_ref[pl.ds(cell, 1), :] = jnp.sum(partial * left, axis=0, keepdims=True) * field_scale
-        return carry
-
-    lax.fori_loop(0, 24, gather, 0)
+        for third in range(3):
+            cz = half + third
+            place = place_ref[ax * 6 + cz]
+            row_x = spline_row(place[0:1])
+            row_y = spline_row(place[1:2])
+            row_z = spline_row(place[2:3])
+            right = jnp.where(block == cz + 1, jnp.tile(row_z, (8, 1)), 0.0).astype(bf16)
+            partial = dot(field, right)
+            left = (row_y[:, None, :] * row_x[None, :, :]).reshape(PC * PC, 128)
+            out_ref[pl.ds(ax * 6 + cz, 1), :] = (
+                jnp.sum(partial * left, axis=0, keepdims=True) * field_scale
+            )
+        return carry
+
+    lax.fori_loop(0, 8, gather, 0)
     own_ref[0:4, :] = out_ref[7:11, :]
     own_ref[4:8, :] = out_ref[13:17, :]
 
@@ -491,18 +515,13 @@
 
 
 def beside_kernel(
-    stored_ref, own_ref, below_ref, above_ref, left_ref, right_ref, before_ref, after_ref,
-    potential_ref, weight_ref, slope_ref, total_ref, own_out, near_ref, sems
+    stored_ref, rows_ref, before_ref, after_ref, potential_ref,
+    weight_ref, slope_ref, total_ref, own_out, near_ref, sems
 ):
-    inner_x, inner_z = pl.ds(1, 2), pl.ds(1, 4)
     pairs = [
-        (own_ref, slope_ref.at[1, inner_x, inner_z]),
-        (left_ref, slope_ref.at[:, inner_x, pl.ds(0, 1)]),
-        (right_ref, slope_ref.at[:, inner_x, pl.ds(5, 1)]),
+        (rows_ref, slope_ref.at[:, pl.ds(1, 2)]),
         (before_ref, slope_ref.at[:, pl.ds(0, 1)]),
         (after_ref, slope_ref.at[:, pl.ds(3, 1)]),
-        (below_ref, slope_ref.at[0, inner_x, inner_z]),
-        (above_ref, slope_ref.at[2, inner_x, inner_z]),
         (stored_ref.at[pl.ds(0, 3)], weight_ref.at[pl.ds(0, 3)]),
         (stored_ref.at[pl.ds(3, 3)], weight_ref.at[pl.ds(3, 3)]),
     ]
@@ -512,7 +531,7 @@
     ]
     for copy in copies:
         copy.start()
-    for copy in copies[:7]:
+    for copy in copies[:3]:
         copy.wait()
     columns = jnp.transpose(potential_ref[...])
     for x in range(4):
@@ -520,7 +539,7 @@
             near_ref[x, z] = scaled(columns, x * 6 + z, slope_ref[1, x, z])
     own_out[...] = near_ref[1:3, 1:5]
     total_ref[...] = jnp.zeros_like(total_ref)
-    for copy in copies[7:]:
+    for copy in copies[3:]:
         copy.wait()
 
     def combination(t, carry):
@@ -536,10 +555,10 @@
     lax.fori_loop(0, 6, combination, 0)
 
 
-def beside(weights, own, near, ends, potential):
+def beside(weights, slopes, potential):
     return pl.pallas_call(
         beside_kernel,
-        in_specs=[ANY] * 8 + [VM],
+        in_specs=[ANY] * 4 + [VM],
         out_specs=[VM] * 4,
         out_shape=[
             jax.ShapeDtypeStruct((6, 8, 128, 768), bf16),
@@ -549,14 +568,14 @@
         ],
         scratch_shapes=[
             pltpu.VMEM((4, 6, 128, 128), bf16),
-            pltpu.SemaphoreType.DMA((9,)),
+            pltpu.SemaphoreType.DMA((5,)),
         ],
         cost_estimate=pl.CostEstimate(
             flops=3000000000, bytes_accessed=12000000, transcendentals=0
         ),
         compiler_params=MIDDLE,
         name="beside",
-    )(weights, own, *near, *ends, potential)
+    )(weights, *slopes, potential)
 
 
 def backward_kernel(
@@ -681,23 +700,17 @@
     cells = cells_x * cells_z
 
     features_own = features.reshape(cells, slots, width)
-    own = project(
-        features_own,
-        msg_weight,
-        spline_corner.reshape(cells, 3, slots),
-        spline_fraction.reshape(cells, 3, slots),
-    ).reshape(cells_x, cells_z, slots + 16, width)
-    near = halo_yz(own)
-    ends = halo_x(own, near)
+    own = project(features_own, msg_weight, spline_corner, spline_fraction)
+    own = own.reshape(cells_x, cells_z, slots + 16, width)
+    near, ends = early_halo(own)
     weights, part, place = inner_pairs(own, near, features_own, self_weight)
     influence = influence_of(size_x, size_y, size_z)
     along_z, along_x, into_y, from_y, back_x, back_z = wave_tables(size_x, size_y, size_z)
 
-    weights, slope, mesh, row_place = message_layer(
-        ends, part, place, charge_weight[None, :], weights
-    )
-    slope_near = halo_yz(slope)
-    slope_ends = halo_x(slope, slope_near)
+    read = charge_weight[None, :]
+    weights, preact, mesh, row_place = message_layer(ends, part, place, read, weights)
+    slope = slope_of(preact, read)
+    slope_near = late_halo(slope)
 
     mesh = swapped(mesh, plane).reshape(4, 4, PC, 128)
     lines = swapped(forward_xz(mesh, along_z, along_x), everyone)
@@ -707,7 +720,7 @@
     potential, atom_potential = interpolate(field, row_place.reshape(24, 8, slots), coupling / volume)
     below, above = moved(potential, "gy", 1), moved(potential, "gy", -1)
     weights, slopes, total, cotangent = beside(
-        weights, slope, slope_near, slope_ends, potential
+        weights, slope_near, potential
     )
     grad = backward(weights, slopes, total, cotangent, below, above, msg_weight, self_weight)
     return (

time: 171 us -> 160 us (0.936)
  waiting for transfers between devices: 68 us -> 47.1 us
  starting transfers between devices: 59.9 us -> 75.2 us
  other arithmetic: 3.89 us -> 0.49 us
  Pallas kernels: 33.6 us -> 30.4 us
    ppermute x14 -> x18, waiting for transfers between devices: 32.4 us -> 15.4 us  [moved(): lax.ppermute(value.reshape(-1, 128), axis, pairs).reshape(value.shape)]
    ppermute x14 -> x18, starting transfers between devices: 33.7 us -> 42.3 us  [moved(): lax.ppermute(value.reshape(-1, 128), axis, pairs).reshape(value.shape)]
    all_to_all x4, starting transfers between devices: 26.2 us -> 32.8 us  [swapped(): return lax.all_to_all(value, axis, split_axis=0, concat_axis=0, tiled=True)]
    all_to_all x4, waiting for transfers between devices: 35.6 us -> 31.7 us  [swapped(): return lax.all_to_all(value, axis, split_axis=0, concat_axis=0, tiled=True)]
    another operation x17 -> x5, other arithmetic: 3.75 us -> 0.3 us  [the longest x2 0.19 us: late_halo(): rows = jnp.stack([moved(row, 'gy', 1), row, moved(row, 'gy', -1)])]
    pallas_call x1, Pallas kernels: 5.32 us -> 2.4 us  [interpolate(): pl.pallas_call(functools.partial(interpolate_kernel, field_scale), in_spe...]
    pallas_call x2 -> x3, Pallas kernels: 11.8 us -> 11.6 us  [the longest x1 5.76 us: beside(): pl.pallas_call(beside_kernel, in_specs=[ANY] * 4 + [VM], out_specs=[VM] *...]
  transfers between devices with their start and end apart: 18 -> 22, of which waited for: 10 -> 8; matrix products, arithmetic and copies ran while one was open for 3% -> 1% of each run, Pallas kernels for 13% -> 12%
where the time goes in v1:
time: 160 us; the launch traced here: 159 us
  starting transfers between devices  75.2 us (47%)
  waiting for transfers between devices  47.1 us (29%)
  Pallas kernels  30.4 us (19%)
  local copies, waits for them, and re-layouts  4.89 us (3%)
    ppermute x18, starting transfers between devices, moved(): lax.ppermute(value.reshape(-1, 128), axis, pairs).reshape(value.shape)  42.3 us
    all_to_all x4, starting transfers between devices, swapped(): return lax.all_to_all(value, axis, split_axis=0, concat_axis=0, tiled=True)  32.8 us
    all_to_all x4, waiting for transfers between devices, swapped(): return lax.all_to_all(value, axis, split_axis=0, concat_axis=0, tiled=True)  31.7 us
    ppermute x18, waiting for transfers between devices, moved(): lax.ppermute(value.reshape(-1, 128), axis, pairs).reshape(value.shape)  15.4 us
    pallas_call x1, Pallas kernels, inner_pairs(): pl.pallas_call(inner_kernel, in_specs=[VM] * 7, out_specs=[ANY, VM, VM],...  7.89 us
    pallas_call x1, Pallas kernels, beside(): pl.pallas_call(beside_kernel, in_specs=[ANY] * 4 + [VM], out_specs=[VM] *...  5.76 us
    pallas_call x1, Pallas kernels, message_layer(): pl.pallas_call(message_kernel, in_specs=[VM] * 9 + [ANY], out_specs=[ANY,...  5.59 us
    pallas_call x1, Pallas kernels, backward(): pl.pallas_call(backward_kernel, in_specs=[VM] * 8, out_specs=VM, out_shap...  5.17 us
  transfers between devices with their start and end apart: 22, of which 8 were waited for; matrix products, arithmetic and copies ran while one was open for 1% of the time, Pallas kernels for 12%

profile of v1, /device:TPU:32, one launch (start us, length us, event | category | flops | bytes accessed | tf_op | source)
XLA Modules:
  0.0 159.1 jit_solution(15228769880912939792)
XLA Ops:
  0.6 0.7 copy.33.corner_ref
  1.3 0.7 copy.34.fraction_ref
  2.1 0.9 copy-done.1
  3.0 0.8 copy-done.7
  3.8 0.2 project.1
  4.0 0.1 collective-permute-start.2
  4.1 8.0 %collective-permute-start.3 = (bf16[1152,128]{1,0:T(8,128)(2,1)S(1)}, bf16[1152,128]{1,0:T(8,128)(2,1)S(1)}, u32[]{:S(2)}, u32[]{:S(2)}) collective-permute-start(bf16[1152,128]{1,0:T(8,128)(2,1)S(1)} %bitcast.74), channel_id=1, source_target_pairs={{0,60},{4,0},{8,4},{12,8},{16,12},{20,16},{24,20},{28,24},{32,28},... | collective-permute-start | bytes 884744 | tf_op jit(solution)/shard_map/ppermute | solution.py:53
  12.1 1.7 %collective-permute-start = (bf16[576,128]{1,0:T(8,128)(2,1)S(1)}, bf16[576,128]{1,0:T(8,128)(2,1)S(1)}, u32[]{:S(2)}, u32[]{:S(2)}) collective-permute-start(bf16[576,128]{1,0:T(8,128)(2,1)S(1)} %bitcast.114), channel_id=1, source_target_pairs={{0,64},{64,128},{128,192},{192,0},{1,65},{65,129},{129,193},{193,1... | collective-permute-start | bytes 442376 | tf_op jit(solution)/shard_map/ppermute | solution.py:53
  13.8 1.7 %collective-permute-start.1 = (bf16[576,128]{1,0:T(8,128)(2,1)S(1)}, bf16[576,128]{1,0:T(8,128)(2,1)S(1)}, u32[]{:S(2)}, u32[]{:S(2)}) collective-permute-start(bf16[576,128]{1,0:T(8,128)(2,1)S(1)} %bitcast.113), channel_id=1, source_target_pairs={{0,192},{64,0},{128,64},{192,128},{1,193},{65,1},{129,65},{193,129... | collective-permute-start | bytes 442376 | tf_op jit(solution)/shard_map/ppermute | solution.py:53
  15.4 4.3 %collective-permute-done.2 = bf16[1152,128]{1,0:T(8,128)(2,1)S(1)} collective-permute-done((bf16[1152,128]{1,0:T(8,128)(2,1)S(1)}, bf16[1152,128]{1,0:T(8,128)(2,1)S(1)}, u32[]{:S(2)}, u32[]{:S(2)}) %collective-permute-start.2) | collective-permute-done | bytes 294944 | tf_op jit(solution)/shard_map/ppermute | solution.py:53
  19.7 2.4 %collective-permute-done.3 = bf16[1152,128]{1,0:T(8,128)(2,1)S(1)} collective-permute-done((bf16[1152,128]{1,0:T(8,128)(2,1)S(1)}, bf16[1152,128]{1,0:T(8,128)(2,1)S(1)}, u32[]{:S(2)}, u32[]{:S(2)}) %collective-permute-start.3) | collective-permute-done | bytes 294944 | tf_op jit(solution)/shard_map/ppermute | solution.py:53
  22.1 2.6 %collective-permute-start.6 = (bf16[864,128]{1,0:T(8,128)(2,1)S(1)}, bf16[864,128]{1,0:T(8,128)(2,1)S(1)}, u32[]{:S(2)}, u32[]{:S(2)}) collective-permute-start(bf16[864,128]{1,0:T(8,128)(2,1)S(1)} %bitcast.112), channel_id=1, source_target_pairs={{0,1},{1,2},{2,3},{3,0},{4,5},{5,6},{6,7},{7,4},{8,9},{9,10},{10,1... | collective-permute-start | bytes 663560 | tf_op jit(solution)/shard_map/ppermute | solution.py:53
  24.7 0.1 collective-permute-start.7
  24.8 0.1 pad_maximum_fusion.2
  24.9 0.0 copy-start.2
  24.9 0.0 copy-start.11
  24.9 3.0 %collective-permute-start.5 = (bf16[1152,128]{1,0:T(8,128)(2,1)S(1)}, bf16[1152,128]{1,0:T(8,128)(2,1)S(1)}, u32[]{:S(2)}, u32[]{:S(2)}) collective-permute-start(bf16[1152,128]{1,0:T(8,128)(2,1)S(1)} %bitcast.108), channel_id=1, source_target_pairs={{0,192},{64,0},{128,64},{192,128},{1,193},{65,1},{129,65},{193,129... | collective-permute-start | bytes 884744 | tf_op jit(solution)/shard_map/ppermute | solution.py:53
  27.9 3.0 %collective-permute-done.6 = bf16[864,128]{1,0:T(8,128)(2,1)S(1)} collective-permute-done((bf16[864,128]{1,0:T(8,128)(2,1)S(1)}, bf16[864,128]{1,0:T(8,128)(2,1)S(1)}, u32[]{:S(2)}, u32[]{:S(2)}) %collective-permute-start.6) | collective-permute-done | bytes 221216 | tf_op jit(solution)/shard_map/ppermute | solution.py:53
  30.9 1.6 collective-permute-start.4
  32.5 5.0 %collective-permute-done.7 = bf16[864,128]{1,0:T(8,128)(2,1)S(1)} collective-permute-done((bf16[864,128]{1,0:T(8,128)(2,1)S(1)}, bf16[864,128]{1,0:T(8,128)(2,1)S(1)}, u32[]{:S(2)}, u32[]{:S(2)}) %collective-permute-start.7) | collective-permute-done | bytes 221216 | tf_op jit(solution)/shard_map/ppermute | solution.py:53
  37.6 2.5 %collective-permute-start.9 = (bf16[864,128]{1,0:T(8,128)(2,1)S(1)}, bf16[864,128]{1,0:T(8,128)(2,1)S(1)}, u32[]{:S(2)}, u32[]{:S(2)}) collective-permute-start(bf16[864,128]{1,0:T(8,128)(2,1)S(1)} %bitcast.109), channel_id=1, source_target_pairs={{0,192},{64,0},{128,64},{192,128},{1,193},{65,1},{129,65},{193,129... | collective-permute-start | bytes 663560 | tf_op jit(solution)/shard_map/ppermute | solution.py:53
  40.1 0.0 collective-permute-done
  40.1 0.0 copy-start.10
  40.2 0.3 collective-permute-start.8
  40.4 7.9 %inner_pairs.1 = (bf16[6,8,128,768]{3,2,1,0:T(8,128)(2,1)}, f32[2,4,128,128]{3,2,1,0:T(8,128)S(1)}, f32[3,2,6,8,128]{4,3,2,1,0:T(8,128)S(1)}) custom-call(bf16[2,4,144,128]{3,2,1,0:T(8,128)(2,1)S(1)} %bitcast.76, bf16[2,4,144,128]{3,2,1,0:T(8,128)(2,1)S(1)} %bitcast.80, bf16[2,4,144,128]{3,2,1,0:T(8,128)(2,1)S(1)} %bitcast.83, ...), custom_call_target="tpu_custom_call" | custom-call | flops 8999999488 | bytes 9000000 | tf_op jit(solution)/shard_map/inner_pairs/pallas_call | solution.py:205
  48.4 0.0 collective-permute-done.4
  48.4 0.0 collective-permute-done.9
  48.4 0.6 collective-permute-done.8
  49.0 5.6 %message.1 = (bf16[6,8,128,768]{3,2,1,0:T(8,128)(2,1)}, f32[2,4,128,128]{3,2,1,0:T(8,128)S(1)}, bf16[16,16,128]{2,1,0:T(8,128)(2,1)}, f32[4,6,8,128]{3,2,1,0:T(8,128)S(1)}) custom-call(bf16[1,4,144,128]{3,2,1,0:T(8,128)(2,1)S(1)} %bitcast.100, bf16[1,4,144,128]{3,2,1,0:T(8,128)(2,1)S(1)} %bitcast.101, ...), custom_call_target="tpu_custom_call", output_to_operand_aliasing={{0}: (9, {})} | custom-call | flops 5000000000 | bytes 6000000 | tf_op jit(solution)/shard_map/message/pallas_call | solution.py:334
  54.6 0.0 copy-start
  54.7 0.0 copy-start.9
  54.7 0.2 slope.1
  54.9 0.6 collective-permute-start.10
  55.6 1.5 collective-permute-start.11
  57.0 6.0 %all-to-all-start = ((bf16[16,16,128]{2,1,0:T(8,128)(2,1)}), bf16[16,16,128]{2,1,0:T(8,128)(2,1)S(1)}, u32[]{:S(2)}, u32[]{:S(2)}) async-start(bf16[16,16,128]{2,1,0:T(8,128)(2,1)} %get-tuple-element.23), calls=%async_computation | async-start | bytes 131072 | tf_op jit(solution)/shard_map/all_to_all | solution.py:690
  63.1 0.0 collective-permute-done.10
  63.1 0.0 copy-start.4
  63.1 0.0 copy-start.5
  63.1 0.1 fusion.8
  63.2 0.1 collective-permute-start.12
  63.3 7.7 %collective-permute-start.13 = (bf16[1536,128]{1,0:T(8,128)(2,1)S(1)}, bf16[1536,128]{1,0:T(8,128)(2,1)S(1)}, u32[]{:S(2)}, u32[]{:S(2)}) collective-permute-start(bf16[1536,128]{1,0:T(8,128)(2,1)S(1)} %bitcast.106), channel_id=1, source_target_pairs={{0,60},{4,0},{8,4},{12,8},{16,12},{20,16},{24,20},{28,24},{32,28},... | collective-permute-start | bytes 1179656 | tf_op jit(solution)/shard_map/ppermute | solution.py:53
  71.0 0.0 all-to-all-done
  71.1 1.0 forward_xz.1
  72.1 13.7 %all-to-all-start.1 = ((f32[256,1,128]{2,1,0:T(1,128)}), f32[256,1,128]{2,1,0:T(1,128)S(1)}, u32[]{:S(2)}, u32[]{:S(2)}) async-start(f32[256,1,128]{2,1,0:T(1,128)} %bitcast.44), calls=%async_computation.1 | async-start | bytes 262144 | tf_op jit(solution)/shard_map/all_to_all | solution.py:690
  85.8 0.1 fusion.1.influence_ref
  85.9 11.8 %all-to-all-done.1 = f32[256,1,128]{2,1,0:T(1,128)S(1)} async-done(((f32[256,1,128]{2,1,0:T(1,128)}), f32[256,1,128]{2,1,0:T(1,128)S(1)}, u32[]{:S(2)}, u32[]{:S(2)}) %all-to-all-start.1) | async-done | bytes 131104 | tf_op jit(solution)/shard_map/all_to_all | solution.py:690
  97.7 1.1 filter_y.1
  98.8 8.8 %all-to-all-start.2 = ((f32[256,2,128]{2,1,0:T(2,128)}), f32[256,2,128]{2,1,0:T(2,128)S(1)}, u32[]{:S(2)}, u32[]{:S(2)}) async-start(f32[256,2,128]{2,1,0:T(2,128)} %bitcast.46), calls=%async_computation.2 | async-start | bytes 524288 | tf_op jit(solution)/shard_map/all_to_all | solution.py:690
  107.6 0.0 collective-permute-done.12
  107.6 0.1 pad_maximum_fusion.rows_ref
  107.7 0.0 copy-start.3
  107.8 0.0 copy-start.6
  107.8 1.1 fusion.9
  108.9 1.5 collective-permute-start.14
  110.4 1.7 %collective-permute-start.15 = (bf16[2304,128]{1,0:T(8,128)(2,1)}, bf16[2304,128]{1,0:T(8,128)(2,1)S(1)}, u32[]{:S(2)}, u32[]{:S(2)}) collective-permute-start(bf16[2304,128]{1,0:T(8,128)(2,1)} %bitcast.40), channel_id=1, source_target_pairs={{0,192},{64,0},{128,64},{192,128},{1,193},{65,1},{129,65},{193,129... | collective-permute-start | bytes 1769480 | tf_op jit(solution)/shard_map/ppermute | solution.py:53
  112.1 10.8 %all-to-all-done.2 = f32[256,2,128]{2,1,0:T(2,128)S(1)} async-done(((f32[256,2,128]{2,1,0:T(2,128)}), f32[256,2,128]{2,1,0:T(2,128)S(1)}, u32[]{:S(2)}, u32[]{:S(2)}) %all-to-all-start.2) | async-done | bytes 262176 | tf_op jit(solution)/shard_map/all_to_all | solution.py:690
  122.9 1.0 inverse_xz.1
  123.9 4.3 %all-to-all-start.3 = ((bf16[16,64,128]{2,1,0:T(8,128)(2,1)}), bf16[16,64,128]{2,1,0:T(8,128)(2,1)S(1)}, u32[]{:S(2)}, u32[]{:S(2)}) async-start(bf16[16,64,128]{2,1,0:T(8,128)(2,1)} %bitcast.48), calls=%async_computation.3 | async-start | bytes 524288 | tf_op jit(solution)/shard_map/all_to_all | solution.py:690
  128.3 0.5 slice.77
  128.8 9.2 %all-to-all-done.3.field_ref = bf16[16,64,128]{2,1,0:T(8,128)(2,1)S(1)} async-done(((bf16[16,64,128]{2,1,0:T(8,128)(2,1)}), bf16[16,64,128]{2,1,0:T(8,128)(2,1)S(1)}, u32[]{:S(2)}, u32[]{:S(2)}) %all-to-all-start.3) | async-done | bytes 262176 | tf_op jit(solution)/shard_map/all_to_all | solution.py:690
  138.0 2.4 %interpolate.1 = (f32[24,128]{1,0:T(8,128)S(1)}, f32[8,128]{1,0:T(8,128)}) custom-call(bf16[16,64,128]{2,1,0:T(8,128)(2,1)S(1)} %all-to-all-done.3.field_ref, f32[24,8,128]{2,1,0:T(8,128)S(1)} %bitcast.102), custom_call_target="tpu_custom_call" | custom-call | flops 201326592 | bytes 400000 | tf_op jit(solution)/shard_map/interpolate/pallas_call | solution.py:493
  140.4 7.8 %collective-permute-start.17 = (f32[24,128]{1,0:T(8,128)S(1)}, f32[24,128]{1,0:T(8,128)S(1)}, u32[]{:S(2)}, u32[]{:S(2)}) collective-permute-start(f32[24,128]{1,0:T(8,128)S(1)} %get-tuple-element.26.potential_ref), channel_id=1, source_target_pairs={{0,60},{4,0},{8,4},{12,8},{16,12},{20,16},{24,20},{28,24},{32,28},... | collective-permute-start | bytes 36872 | tf_op jit(solution)/shard_map/ppermute | solution.py:53
  148.1 5.8 %beside.1 = (bf16[6,8,128,768]{3,2,1,0:T(8,128)(2,1)S(1)}, bf16[3,4,6,128,128]{4,3,2,1,0:T(8,128)(2,1)S(1)}, f32[2,4,128,128]{3,2,1,0:T(8,128)S(1)}, bf16[2,4,128,128]{3,2,1,0:T(8,128)(2,1)S(1)}) custom-call(bf16[6,8,128,768]{3,2,1,0:T(8,128)(2,1)} %get-tuple-element.21.stored_ref, bf16[3,2,6,128,128]{4,3,2,1,0:T(8,128)(2,1)S(1)} %pad_maximum_fusion.rows_ref, ...), custom_call_target="tpu_custom_call" | custom-call | flops 3000000000 | bytes 12000000 | tf_op jit(solution)/shard_map/beside/pallas_call | solution.py:559
  153.9 5.2 %backward.1 = f32[2,4,128,128]{3,2,1,0:T(8,128)} custom-call(bf16[6,8,128,768]{3,2,1,0:T(8,128)(2,1)S(1)} %get-tuple-element.27.weight_ref, bf16[3,4,6,128,128]{4,3,2,1,0:T(8,128)(2,1)S(1)} %get-tuple-element.28.slope_ref, f32[2,4,128,128]{3,2,1,0:T(8,128)S(1)} %get-tuple-element.29.part_ref, bf16[2,4,128,128]{3,2,1,0:T(8,128)(2,1)S(1)} %get-tuple-element.30.own_ref, ...), custom_call_target="tpu_custom_call" | custom-call | flops 4000000000 | bytes 12000000 | tf_op jit(solution)/shard_map/backward/pallas_call | solution.py:624
  (35 shorter events, 0.3 us)
Async XLA Ops:
  2.1 0.9 copy-start.1
  3.0 0.8 copy-start.7
  4.0 15.7 %collective-permute-start.2 = (bf16[1152,128]{1,0:T(8,128)(2,1)S(1)}, bf16[1152,128]{1,0:T(8,128)(2,1)S(1)}, u32[]{:S(2)}, u32[]{:S(2)}) collective-permute-start(bf16[1152,128]{1,0:T(8,128)(2,1)S(1)} %bitcast.73), channel_id=1, source_target_pairs={{0,4},{4,8},{8,12},{12,16},{16,20},{20,24},{24,28},{28,32},{32,36}... | collective-permute-start | bytes 884744 | tf_op jit(solution)/shard_map/ppermute | solution.py:53
  4.1 18.0 %collective-permute-start.3 = (bf16[1152,128]{1,0:T(8,128)(2,1)S(1)}, bf16[1152,128]{1,0:T(8,128)(2,1)S(1)}, u32[]{:S(2)}, u32[]{:S(2)}) collective-permute-start(bf16[1152,128]{1,0:T(8,128)(2,1)S(1)} %bitcast.74), channel_id=1, source_target_pairs={{0,60},{4,0},{8,4},{12,8},{16,12},{20,16},{24,20},{28,24},{32,28},... | collective-permute-start | bytes 884744 | tf_op jit(solution)/shard_map/ppermute | solution.py:53
  12.1 28.0 %collective-permute-start = (bf16[576,128]{1,0:T(8,128)(2,1)S(1)}, bf16[576,128]{1,0:T(8,128)(2,1)S(1)}, u32[]{:S(2)}, u32[]{:S(2)}) collective-permute-start(bf16[576,128]{1,0:T(8,128)(2,1)S(1)} %bitcast.114), channel_id=1, source_target_pairs={{0,64},{64,128},{128,192},{192,0},{1,65},{65,129},{129,193},{193,1... | collective-permute-start | bytes 442376 | tf_op jit(solution)/shard_map/ppermute | solution.py:53
  13.8 34.6 %collective-permute-start.1 = (bf16[576,128]{1,0:T(8,128)(2,1)S(1)}, bf16[576,128]{1,0:T(8,128)(2,1)S(1)}, u32[]{:S(2)}, u32[]{:S(2)}) collective-permute-start(bf16[576,128]{1,0:T(8,128)(2,1)S(1)} %bitcast.113), channel_id=1, source_target_pairs={{0,192},{64,0},{128,64},{192,128},{1,193},{65,1},{129,65},{193,129... | collective-permute-start | bytes 442376 | tf_op jit(solution)/shard_map/ppermute | solution.py:53
  22.1 8.8 %collective-permute-start.6 = (bf16[864,128]{1,0:T(8,128)(2,1)S(1)}, bf16[864,128]{1,0:T(8,128)(2,1)S(1)}, u32[]{:S(2)}, u32[]{:S(2)}) collective-permute-start(bf16[864,128]{1,0:T(8,128)(2,1)S(1)} %bitcast.112), channel_id=1, source_target_pairs={{0,1},{1,2},{2,3},{3,0},{4,5},{5,6},{6,7},{7,4},{8,9},{9,10},{10,1... | collective-permute-start | bytes 663560 | tf_op jit(solution)/shard_map/ppermute | solution.py:53
  24.7 12.8 %collective-permute-start.7 = (bf16[864,128]{1,0:T(8,128)(2,1)S(1)}, bf16[864,128]{1,0:T(8,128)(2,1)S(1)}, u32[]{:S(2)}, u32[]{:S(2)}) collective-permute-start(bf16[864,128]{1,0:T(8,128)(2,1)S(1)} %bitcast.111), channel_id=1, source_target_pairs={{0,3},{1,0},{2,1},{3,2},{4,7},{5,4},{6,5},{7,6},{8,11},{9,8},{10,9... | collective-permute-start | bytes 663560 | tf_op jit(solution)/shard_map/ppermute | solution.py:53
  24.9 15.6 %copy-start.2 = (bf16[2,1,4,128,128]{4,3,2,1,0:T(8,128)(2,1)S(1)}, bf16[2,1,4,128,128]{4,3,2,1,0:T(8,128)(2,1)}, u32[]{:S(2)}) copy-start(bf16[2,1,4,128,128]{4,3,2,1,0:T(8,128)(2,1)} %param.12) | copy-start | bytes 786436
  24.9 15.6 %copy-start.11 = (bf16[128,128]{1,0:T(8,128)(2,1)S(1)}, bf16[128,128]{1,0:T(8,128)(2,1)}, u32[]{:S(2)}) copy-start(bf16[128,128]{1,0:T(8,128)(2,1)} %self_ref.3) | copy-start | bytes 98308
  24.9 23.5 %collective-permute-start.5 = (bf16[1152,128]{1,0:T(8,128)(2,1)S(1)}, bf16[1152,128]{1,0:T(8,128)(2,1)S(1)}, u32[]{:S(2)}, u32[]{:S(2)}) collective-permute-start(bf16[1152,128]{1,0:T(8,128)(2,1)S(1)} %bitcast.108), channel_id=1, source_target_pairs={{0,192},{64,0},{128,64},{192,128},{1,193},{65,1},{129,65},{193,129... | collective-permute-start | bytes 884744 | tf_op jit(solution)/shard_map/ppermute | solution.py:53
  30.9 17.5 %collective-permute-start.4 = (bf16[1152,128]{1,0:T(8,128)(2,1)S(1)}, bf16[1152,128]{1,0:T(8,128)(2,1)S(1)}, u32[]{:S(2)}, u32[]{:S(2)}) collective-permute-start(bf16[1152,128]{1,0:T(8,128)(2,1)S(1)} %bitcast.107), channel_id=1, source_target_pairs={{0,64},{64,128},{128,192},{192,0},{1,65},{65,129},{129,193},{193,1... | collective-permute-start | bytes 884744 | tf_op jit(solution)/shard_map/ppermute | solution.py:53
  37.6 10.8 %collective-permute-start.9 = (bf16[864,128]{1,0:T(8,128)(2,1)S(1)}, bf16[864,128]{1,0:T(8,128)(2,1)S(1)}, u32[]{:S(2)}, u32[]{:S(2)}) collective-permute-start(bf16[864,128]{1,0:T(8,128)(2,1)S(1)} %bitcast.109), channel_id=1, source_target_pairs={{0,192},{64,0},{128,64},{192,128},{1,193},{65,1},{129,65},{193,129... | collective-permute-start | bytes 663560 | tf_op jit(solution)/shard_map/ppermute | solution.py:53
  40.1 8.9 %copy-start.10 = (bf16[128]{0:T(256)(128)(2,1)S(1)}, bf16[128]{0:T(256)(128)(2,1)}, u32[]{:S(2)}) copy-start(bf16[128]{0:T(256)(128)(2,1)} %param.15) | copy-start | bytes 772
  40.2 8.9 %collective-permute-start.8 = (bf16[864,128]{1,0:T(8,128)(2,1)S(1)}, bf16[864,128]{1,0:T(8,128)(2,1)S(1)}, u32[]{:S(2)}, u32[]{:S(2)}) collective-permute-start(bf16[864,128]{1,0:T(8,128)(2,1)S(1)} %bitcast.110), channel_id=1, source_target_pairs={{0,64},{64,128},{128,192},{192,0},{1,65},{65,129},{129,193},{193,1... | collective-permute-start | bytes 663560 | tf_op jit(solution)/shard_map/ppermute | solution.py:53
  54.6 16.4 %copy-start = (bf16[4,128,512]{2,1,0:T(8,128)(2,1)S(1)}, bf16[4,128,512]{2,1,0:T(8,128)(2,1)}, u32[]{:S(2)}) copy-start(bf16[4,128,512]{2,1,0:T(8,128)(2,1)} %constant.80.clone.along_z_ref) | copy-start | bytes 1572868
  54.7 16.4 %copy-start.9 = (bf16[128,128]{1,0:T(8,128)(2,1)S(1)}, bf16[128,128]{1,0:T(8,128)(2,1)}, u32[]{:S(2)}) copy-start(bf16[128,128]{1,0:T(8,128)(2,1)} %constant.81.clone.along_x_ref) | copy-start | bytes 98308
  54.9 8.1 %collective-permute-start.10 = (bf16[256,128]{1,0:T(8,128)(2,1)S(1)}, bf16[256,128]{1,0:T(8,128)(2,1)S(1)}, u32[]{:S(2)}, u32[]{:S(2)}) collective-permute-start(bf16[256,128]{1,0:T(8,128)(2,1)S(1)} %bitcast.118), channel_id=1, source_target_pairs={{0,1},{1,2},{2,3},{3,0},{4,5},{5,6},{6,7},{7,4},{8,9},{9,10},{10,1... | collective-permute-start | bytes 196616 | tf_op jit(solution)/shard_map/ppermute | solution.py:53
  55.6 7.5 %collective-permute-start.11 = (bf16[256,128]{1,0:T(8,128)(2,1)S(1)}, bf16[256,128]{1,0:T(8,128)(2,1)S(1)}, u32[]{:S(2)}, u32[]{:S(2)}) collective-permute-start(bf16[256,128]{1,0:T(8,128)(2,1)S(1)} %bitcast.117), channel_id=1, source_target_pairs={{0,3},{1,0},{2,1},{3,2},{4,7},{5,4},{6,5},{7,6},{8,11},{9,8},{10,9... | collective-permute-start | bytes 196616 | tf_op jit(solution)/shard_map/ppermute | solution.py:53
  57.0 14.0 %all-to-all-start = ((bf16[16,16,128]{2,1,0:T(8,128)(2,1)}), bf16[16,16,128]{2,1,0:T(8,128)(2,1)S(1)}, u32[]{:S(2)}, u32[]{:S(2)}) async-start(bf16[16,16,128]{2,1,0:T(8,128)(2,1)} %get-tuple-element.23), calls=%async_computation | async-start | bytes 131072 | tf_op jit(solution)/shard_map/all_to_all | solution.py:690
  63.1 34.6 %copy-start.4 = (bf16[256,256]{1,0:T(8,128)(2,1)S(1)}, bf16[256,256]{1,0:T(8,128)(2,1)}, u32[]{:S(2)}) copy-start(bf16[256,256]{1,0:T(8,128)(2,1)} %constant.82.clone.into_ref) | copy-start | bytes 393220
  63.1 34.6 %copy-start.5 = (bf16[256,256]{1,0:T(8,128)(2,1)S(1)}, bf16[256,256]{1,0:T(8,128)(2,1)}, u32[]{:S(2)}) copy-start(bf16[256,256]{1,0:T(8,128)(2,1)} %constant.83.clone.back_ref) | copy-start | bytes 393220
  63.2 44.4 %collective-permute-start.12 = (bf16[1536,128]{1,0:T(8,128)(2,1)S(1)}, bf16[1536,128]{1,0:T(8,128)(2,1)S(1)}, u32[]{:S(2)}, u32[]{:S(2)}) collective-permute-start(bf16[1536,128]{1,0:T(8,128)(2,1)S(1)} %bitcast.105), channel_id=1, source_target_pairs={{0,4},{4,8},{8,12},{12,16},{16,20},{20,24},{24,28},{28,32},{32,36}... | collective-permute-start | bytes 1179656 | tf_op jit(solution)/shard_map/ppermute | solution.py:53
  63.3 44.3 %collective-permute-start.13 = (bf16[1536,128]{1,0:T(8,128)(2,1)S(1)}, bf16[1536,128]{1,0:T(8,128)(2,1)S(1)}, u32[]{:S(2)}, u32[]{:S(2)}) collective-permute-start(bf16[1536,128]{1,0:T(8,128)(2,1)S(1)} %bitcast.106), channel_id=1, source_target_pairs={{0,60},{4,0},{8,4},{12,8},{16,12},{20,16},{24,20},{28,24},{32,28},... | collective-permute-start | bytes 1179656 | tf_op jit(solution)/shard_map/ppermute | solution.py:53
  72.1 25.6 %all-to-all-start.1 = ((f32[256,1,128]{2,1,0:T(1,128)}), f32[256,1,128]{2,1,0:T(1,128)S(1)}, u32[]{:S(2)}, u32[]{:S(2)}) async-start(f32[256,1,128]{2,1,0:T(1,128)} %bitcast.44), calls=%async_computation.1 | async-start | bytes 262144 | tf_op jit(solution)/shard_map/all_to_all | solution.py:690
  98.8 24.1 %all-to-all-start.2 = ((f32[256,2,128]{2,1,0:T(2,128)}), f32[256,2,128]{2,1,0:T(2,128)S(1)}, u32[]{:S(2)}, u32[]{:S(2)}) async-start(f32[256,2,128]{2,1,0:T(2,128)} %bitcast.46), calls=%async_computation.2 | async-start | bytes 524288 | tf_op jit(solution)/shard_map/all_to_all | solution.py:690
  107.7 15.2 %copy-start.3 = (bf16[256,512]{1,0:T(8,128)(2,1)S(1)}, bf16[256,512]{1,0:T(8,128)(2,1)}, u32[]{:S(2)}) copy-start(bf16[256,512]{1,0:T(8,128)(2,1)} %constant.85.clone.along_z_ref) | copy-start | bytes 786436
  107.8 15.1 %copy-start.6 = (bf16[256,128]{1,0:T(8,128)(2,1)S(1)}, bf16[256,128]{1,0:T(8,128)(2,1)}, u32[]{:S(2)}) copy-start(bf16[256,128]{1,0:T(8,128)(2,1)} %constant.84.clone.along_x_ref) | copy-start | bytes 196612
  108.9 39.3 %collective-permute-start.14 = (bf16[2304,128]{1,0:T(8,128)(2,1)}, bf16[2304,128]{1,0:T(8,128)(2,1)S(1)}, u32[]{:S(2)}, u32[]{:S(2)}) collective-permute-start(bf16[2304,128]{1,0:T(8,128)(2,1)} %bitcast.38), channel_id=1, source_target_pairs={{0,64},{64,128},{128,192},{192,0},{1,65},{65,129},{129,193},{193,1... | collective-permute-start | bytes 1769480 | tf_op jit(solution)/shard_map/ppermute | solution.py:53
  110.4 37.7 %collective-permute-start.15 = (bf16[2304,128]{1,0:T(8,128)(2,1)}, bf16[2304,128]{1,0:T(8,128)(2,1)S(1)}, u32[]{:S(2)}, u32[]{:S(2)}) collective-permute-start(bf16[2304,128]{1,0:T(8,128)(2,1)} %bitcast.40), channel_id=1, source_target_pairs={{0,192},{64,0},{128,64},{192,128},{1,193},{65,1},{129,65},{193,129... | collective-permute-start | bytes 1769480 | tf_op jit(solution)/shard_map/ppermute | solution.py:53
  123.9 14.0 %all-to-all-start.3 = ((bf16[16,64,128]{2,1,0:T(8,128)(2,1)}), bf16[16,64,128]{2,1,0:T(8,128)(2,1)S(1)}, u32[]{:S(2)}, u32[]{:S(2)}) async-start(bf16[16,64,128]{2,1,0:T(8,128)(2,1)} %bitcast.48), calls=%async_computation.3 | async-start | bytes 524288 | tf_op jit(solution)/shard_map/all_to_all | solution.py:690
  140.4 13.5 %collective-permute-start.16 = (f32[24,128]{1,0:T(8,128)S(1)}, f32[24,128]{1,0:T(8,128)S(1)}, u32[]{:S(2)}, u32[]{:S(2)}) collective-permute-start(f32[24,128]{1,0:T(8,128)S(1)} %get-tuple-element.26.potential_ref), channel_id=1, source_target_pairs={{0,4},{4,8},{8,12},{12,16},{16,20},{20,24},{24,28},{28,32},{32,36}... | collective-permute-start | bytes 36872 | tf_op jit(solution)/shard_map/ppermute | solution.py:53
  140.4 13.6 %collective-permute-start.17 = (f32[24,128]{1,0:T(8,128)S(1)}, f32[24,128]{1,0:T(8,128)S(1)}, u32[]{:S(2)}, u32[]{:S(2)}) collective-permute-start(f32[24,128]{1,0:T(8,128)S(1)} %get-tuple-element.26.potential_ref), channel_id=1, source_target_pairs={{0,60},{4,0},{8,4},{12,8},{16,12},{20,16},{24,20},{28,24},{32,28},... | collective-permute-start | bytes 36872 | tf_op jit(solution)/shard_map/ppermute | solution.py:53
  148.1 5.8 %copy-start.8 = (bf16[128,128]{1,0:T(8,128)(2,1)S(1)}, bf16[128,128]{1,0:T(8,128)(2,1)}, u32[]{:S(2)}) copy-start(bf16[128,128]{1,0:T(8,128)(2,1)} %msg_ref.1) | copy-start | bytes 98308

commit v2 on v1

--- a/solution.py
+++ b/solution.py
@@ -37,6 +37,7 @@
 VM = pl.BlockSpec(memory_space=pltpu.VMEM)
 ANY = pl.BlockSpec(memory_space=pl.ANY)
 SMALL = pltpu.CompilerParams(vmem_limit_bytes=20 << 20)
+FIRST = pltpu.CompilerParams(vmem_limit_bytes=60 << 20)
 LARGE = pltpu.CompilerParams(vmem_limit_bytes=50 << 20)
 MIDDLE = pltpu.CompilerParams(vmem_limit_bytes=36 << 20)
 
@@ -74,21 +75,23 @@
         moved(jnp.concatenate([left[:, at : at + 1], right[:, at : at + 1]], axis=2), "gx", step)
         for at, step in ((last_x, 1), (0, -1))
     ]
-    return [below, above, left, right], beside + aside + corners
+    return [below, above], [left, right], beside + aside, corners
 
 
 def project_kernel(features_ref, weight_ref, corner_ref, fraction_ref, out_ref):
     value = dot(features_ref[...].reshape(1024, 128), weight_ref[...]).astype(bf16)
     out_ref[:, :128, :] = value.reshape(8, 128, 128)
-    place = corner_ref[:, 0].astype(f32) + 1.0 + fraction_ref[:, 0]
-    place = place.reshape(8, 3, 128)
-    high = place.astype(bf16).astype(f32)
-    rest = place - high
-    middle = rest.astype(bf16).astype(f32)
-    low = rest - middle
-    two = jnp.zeros((8, 2, 128), f32)
-    five = jnp.zeros((8, 5, 128), f32)
-    out_ref[:, 128:, :] = jnp.concatenate([high, low, two, middle, five], axis=1).astype(bf16)
+    none = jnp.zeros((5, 128), f32)
+    for x in range(2):
+        place = corner_ref[x, 0].astype(f32) + 1.0 + fraction_ref[x, 0]
+        high = place.astype(bf16).astype(f32)
+        rest = place - high
+        middle = rest.astype(bf16).astype(f32)
+        low = rest - middle
+        for z in range(4):
+            rows = [part[d, z : z + 1] for part in (high, low) for d in range(3)]
+            rows += [none[:2]] + [middle[d, z : z + 1] for d in range(3)] + [none]
+            out_ref[x * 4 + z, 128:, :] = jnp.concatenate(rows, axis=0).astype(bf16)
 
 
 def project(features, weight, corner, fraction):
@@ -96,10 +99,10 @@
         project_kernel,
         grid=(1,),
         in_specs=[whole((8, 128, 128)), whole((128, 128))]
-        + [whole((2, 1, 4, 3, 128))] * 2,
+        + [whole((2, 1, 3, 4, 128))] * 2,
         out_specs=whole((8, 144, 128)),
         out_shape=jax.ShapeDtypeStruct((8, 144, 128), bf16),
-        compiler_params=SMALL,
+        compiler_params=FIRST,
         name="project",
     )(features, weight, corner, fraction)
 
@@ -114,14 +117,18 @@
 ORDER_Y = (0, 2, 1)
 
 
-def weigh(centres, a, shift, near, store):
+def position_of(rows):
+    return (place_of(rows) * (1.0 / PC)).astype(bf16).astype(f32)
+
+
+def weigh(centres, a, shift, near, store, pairs):
     for c in range(4):
         columns = jnp.transpose(centres[a, c])
         centre_x = jnp.broadcast_to(columns[:, 0:1], (128, 128))
         centre_y = jnp.broadcast_to(columns[:, 1:2], (128, 128))
         centre_z = jnp.broadcast_to(columns[:, 2:3], (128, 128))
         for block, (pair, owner) in enumerate(BLOCKS):
-            if owner != c:
+            if owner != c or pair not in pairs:
                 continue
             for at, dy in enumerate(ORDER_Y):
                 for half in range(2):
@@ -139,11 +146,109 @@
                     store(block, (at * 2 + half) * 128, tile)
 
 
-def inner_kernel(
-    own_ref, below_ref, above_ref, left_ref, right_ref, features_ref, self_ref,
-    weight_out, total_ref, place_ref, weight_ref, position_ref, sems
+def add_near(weight_ref, t, a, cell, total_ref, pairs):
+    for pair in pairs:
+        start, stop, first, width = SPANS[pair]
+        near = jnp.concatenate(
+            [cell(dy, 2 * pair + half)[0:128, :] for dy in ORDER_Y for half in range(2)], axis=0
+        )
+        part = dot(weight_ref[t, start:stop].reshape(width * 128, 768), near)
+        total_ref[a, first : first + width] += part.reshape(width, 128, 128)
+
+
+def columns_kernel(first, count, weight_ref, weight_out, sems, slot, spans):
+    return [
+        pltpu.make_async_copy(
+            weight_ref.at[pl.ds(first, count), pl.ds(start, size)],
+            weight_out.at[pl.ds(first, count), pl.ds(start, size)],
+            sems.at[slot + i],
+        )
+        for i, (start, size) in enumerate(spans)
+    ]
+
+
+INSIDE = (1,)
+ENDS = (0, 2)
+INSIDE_BLOCKS = ((2, 4),)
+END_BLOCKS = ((0, 2), (6, 2))
+
+
+def centres_of(own_ref, centre_ref):
+    def one(cell, carry):
+        x, z = cell // 4, cell % 4
+        centre_ref[x, z] = position_of(own_ref[x, z, 128:144, :])
+        return carry
+
+    lax.fori_loop(0, 8, one, 0)
+
+
+def inside_kernel(
+    own_ref, below_ref, above_ref, features_ref, self_ref,
+    weight_out, total_ref, weight_ref, position_ref, sems
 ):
     refs = (below_ref, own_ref, above_ref)
+
+    def positions(x, carry):
+        for dy in range(3):
+            for z in range(4):
+                position_ref[dy, x, z] = position_of(refs[dy][x, z, 128:144, :])
+        return carry
+
+    lax.fori_loop(0, 2, positions, 0)
+    total_ref[...] = dot(features_ref[...].reshape(1024, 128), self_ref[...]).reshape(
+        2, 4, 128, 128
+    )
+
+    def column(t, carry):
+        x, a = t // 2, t % 2
+
+        def store(block, lane, tile):
+            weight_ref[t, block, :, lane : lane + 128] = tile
+
+        def near(dy, z):
+            return position_ref[dy, x, z - 1]
+
+        weigh(position_ref.at[1], a, (x - a).astype(f32), near, store, INSIDE)
+        add_near(weight_ref, t, a, lambda dy, z: refs[dy].at[x, z - 1], total_ref, INSIDE)
+        return carry
+
+    lax.fori_loop(0, 4, column, 0)
+    copies = columns_kernel(0, 4, weight_ref, weight_out, sems, 0, INSIDE_BLOCKS)
+    for copy in copies:
+        copy.start()
+    for copy in copies:
+        copy.wait()
+
+
+def inside_pairs(own, sides, features, self_weight):
+    return pl.pallas_call(
+        inside_kernel,
+        in_specs=[VM] * 5,
+        out_specs=[ANY, VM],
+        out_shape=[
+            jax.ShapeDtypeStruct((6, 8, 128, 768), bf16),
+            jax.ShapeDtypeStruct((2, 4, 128, 128), f32),
+        ],
+        scratch_shapes=[
+            pltpu.VMEM((4, 8, 128, 768), bf16),
+            pltpu.VMEM((3, 2, 4, 8, 128), f32),
+            pltpu.SemaphoreType.DMA((1,)),
+        ],
+        cost_estimate=pl.CostEstimate(
+            flops=5000000000, bytes_accessed=9000000, transcendentals=0
+        ),
+        compiler_params=LARGE,
+        name="inside_pairs",
+    )(own, *sides, features, self_weight)
+
+
+def ends_kernel(
+    own_ref, below_ref, above_ref, left_ref, right_ref,
+    before_own, after_own, before_side, after_side, part_ref, _,
+    weight_out, total_ref, weight_ref, centre_ref, position_ref, outer_ref, sems
+):
+    refs = (below_ref, own_ref, above_ref)
+    outer = ((before_own, before_side), (after_own, after_side))
 
     def cell(dy, x, z):
         if z == 0:
@@ -152,76 +257,88 @@
             return right_ref.at[dy, x, 0]
         return refs[dy].at[x, z - 1]
 
-    def places(x, carry):
+    def outer_cell(side, dy, z):
+        own, beside = outer[side]
+        return own.at[0, z - 1] if dy == 1 else beside.at[dy // 2, 0, z - 1]
+
+    centres_of(own_ref, centre_ref)
+
+    def positions(x, carry):
         for dy in range(3):
-            for z in range(6):
-                place = place_of(cell(dy, x, z)[128:144, :])
-                place_ref[dy, x, z] = place
-                position_ref[dy, x, z] = (place * (1.0 / PC)).astype(bf16).astype(f32)
-        return carry
-
-    lax.fori_loop(0, 2, places, 0)
-
-    def copy_out(t):
-        return pltpu.make_async_copy(weight_ref.at[t], weight_out.at[t], sems.at[t])
-
-    total_ref[...] = dot(features_ref[...].reshape(1024, 128), self_ref[...]).reshape(
-        2, 4, 128, 128
-    )
-
-    def combination(t, carry):
+            for z in (0, 1, 4, 5):
+                position_ref[dy, x, z] = position_of(cell(dy, x, z)[128:144, :])
+        return carry
+
+    lax.fori_loop(0, 2, positions, 0)
+    for side in range(2):
+        for dy in range(3):
+            for z in (2, 3):
+                outer_ref[side, dy, z] = position_of(outer_cell(side, dy, z)[128:144, :])
+    total_ref[...] = part_ref[...]
+
+    def column(t, carry):
         x, a = t // 2, t % 2
 
         def store(block, lane, tile):
             weight_ref[t, block, :, lane : lane + 128] = tile
 
-        weigh(
-            position_ref.at[1, :, 1:5],
-            a,
-            (x - a).astype(f32),
-            lambda dy, z: position_ref[dy, x, z],
-            store,
+        def near(dy, z):
+            return position_ref[dy, x, z]
+
+        weigh(centre_ref, a, (x - a).astype(f32), near, store, ENDS)
+        add_near(weight_ref, t, a, lambda dy, z: cell(dy, x, z), total_ref, ENDS)
+        return carry
+
+    lax.fori_loop(0, 4, column, 0)
+    copies = columns_kernel(0, 4, weight_ref, weight_out, sems, 0, END_BLOCKS)
+    for copy in copies:
+        copy.start()
+
+    def outer_column(side, carry):
+        def store(block, lane, tile):
+            weight_ref[4 + side, block, :, lane : lane + 128] = tile
+
+        def near(dy, z):
+            return outer_ref[side, dy, z]
+
+        weigh(centre_ref, side, (2 * side - 1).astype(f32), near, store, INSIDE)
+        return carry
+
+    lax.fori_loop(0, 2, outer_column, 0)
+    last = columns_kernel(4, 2, weight_ref, weight_out, sems, 2, INSIDE_BLOCKS)
+    for copy in last:
+        copy.start()
+    for side in range(2):
+        add_near(
+            weight_ref, 4 + side, side, lambda dy, z: outer_cell(side, dy, z), total_ref, INSIDE
         )
-        copy_out(t).start()
-        for pair, (start, stop, first, width) in enumerate(SPANS):
-            near = jnp.concatenate(
-                [
-                    cell(dy, x, 2 * pair + half)[0:128, :]
-                    for dy in ORDER_Y
-                    for half in range(2)
-                ],
-                axis=0,
-            )
-            part = dot(weight_ref[t, start:stop].reshape(width * 128, 768), near)
-            total_ref[a, first : first + width] += part.reshape(width, 128, 128)
-        return carry
-
-    lax.fori_loop(0, 4, combination, 0)
-    for t in range(4):
-        copy_out(t).wait()
-
-
-def inner_pairs(own, near, features, self_weight):
-    return pl.pallas_call(
-        inner_kernel,
-        in_specs=[VM] * 7,
-        out_specs=[ANY, VM, VM],
+    for copy in copies + last:
+        copy.wait()
+
+
+def ends_pairs(own, sides, ends, outer, part, weights):
+    return pl.pallas_call(
+        ends_kernel,
+        in_specs=[VM] * 10 + [ANY],
+        out_specs=[ANY, VM],
+        input_output_aliases={10: 0},
         out_shape=[
             jax.ShapeDtypeStruct((6, 8, 128, 768), bf16),
             jax.ShapeDtypeStruct((2, 4, 128, 128), f32),
-            jax.ShapeDtypeStruct((3, 2, 6, 8, 128), f32),
         ],
         scratch_shapes=[
-            pltpu.VMEM((4, 8, 128, 768), bf16),
+            pltpu.VMEM((6, 8, 128, 768), bf16),
+            pltpu.VMEM((2, 4, 8, 128), f32),
             pltpu.VMEM((3, 2, 6, 8, 128), f32),
-            pltpu.SemaphoreType.DMA((4,)),
+            pltpu.VMEM((2, 3, 6, 8, 128), f32),
+            pltpu.SemaphoreType.DMA((3,)),
         ],
         cost_estimate=pl.CostEstimate(
             flops=9000000000, bytes_accessed=9000000, transcendentals=0
         ),
         compiler_params=LARGE,
-        name="inner_pairs",
-    )(own, *near, features, self_weight)
+        name="ends_pairs",
+    )(own, *sides, *ends, *outer, part, weights)
 
 
 def spline_row(place):
@@ -234,11 +351,10 @@
 
 
 def message_kernel(
-    before_own, after_own, before_side, after_side, before_end, after_end,
-    part_ref, place_ref, read_ref, _,
+    own_ref, left_ref, right_ref, before_own, after_own, before_side, after_side, before_end,
+    after_end, part_ref, read_ref, _,
     weight_out, total_ref, mesh_ref, row_place_ref,
-    weight_ref, position_ref, centre_ref, high_ref, low_ref, charge_ref, left_ref,
-    right_ref, sems
+    weight_ref, position_ref, centre_ref, high_ref, low_ref, charge_ref, left_rows, right_rows, sems
 ):
     refs = ((before_own, before_side, before_end), (after_own, after_side, after_end))
 
@@ -248,54 +364,47 @@
             return end.at[dy, 0, z // 5]
         return own.at[0, z - 1] if dy == 1 else beside.at[dy // 2, 0, z - 1]
 
-    def position(place):
-        return (place * (1.0 / PC)).astype(bf16).astype(f32)
-
+    centres_of(own_ref, centre_ref)
     for side in range(2):
         for dy in range(3):
-            for z in range(6):
-                place = place_of(cell(side, dy, z)[128:144, :])
-                position_ref[side, dy, z] = position(place)
-                if dy == 1:
-                    row_place_ref[3 * side, z] = place
-    for x in range(2):
+            for z in (0, 1, 4, 5):
+                position_ref[side, dy, z] = position_of(cell(side, dy, z)[128:144, :])
         for z in range(6):
-            place = place_ref[1, x, z]
-            row_place_ref[1 + x, z] = place
-            if 1 <= z <= 4:
-                centre_ref[x, z - 1] = position(place)
-
-    def copy_out(t):
-        return pltpu.make_async_copy(weight_ref.at[t], weight_out.at[4 + t], sems.at[t])
-
-    def combination(t, carry):
+            row_place_ref[3 * side, z] = place_of(cell(side, 1, z)[128:144, :])
+
+    def row_places(x, carry):
+        row_place_ref[1 + x, 0] = place_of(left_ref[1, x, 0, 128:144, :])
+        for z in range(4):
+            row_place_ref[1 + x, 1 + z] = place_of(own_ref[x, z, 128:144, :])
+        row_place_ref[1 + x, 5] = place_of(right_ref[1, x, 0, 128:144, :])
+        return carry
+
+    lax.fori_loop(0, 2, row_places, 0)
+
+    def column(side, carry):
         def store(block, lane, tile):
-            weight_ref[t, block, :, lane : lane + 128] = tile
-
-        weigh(
-            centre_ref,
-            t,
-            (2 * t - 1).astype(f32),
-            lambda dy, z: position_ref[t, dy, z],
-            store,
+            weight_ref[side, block, :, lane : lane + 128] = tile
+
+        def near(dy, z):
+            return position_ref[side, dy, z]
+
+        weigh(centre_ref, side, (2 * side - 1).astype(f32), near, store, ENDS)
+        return carry
+
+    lax.fori_loop(0, 2, column, 0)
+    copies = [
+        pltpu.make_async_copy(
+            weight_ref.at[:, pl.ds(start, size)],
+            weight_out.at[pl.ds(4, 2), pl.ds(start, size)],
+            sems.at[i],
         )
-        copy_out(t).start()
-        return carry
-
-    lax.fori_loop(0, 2, combination, 0)
+        for i, (start, size) in enumerate(END_BLOCKS)
+    ]
+    for copy in copies:
+        copy.start()
     total_ref[...] = part_ref[...]
-    for t in range(2):
-        for pair, (start, stop, first, width) in enumerate(SPANS):
-            near = jnp.concatenate(
-                [
-                    cell(t, dy, 2 * pair + half)[0:128, :]
-                    for dy in ORDER_Y
-                    for half in range(2)
-                ],
-                axis=0,
-            )
-            part = dot(weight_ref[t, start:stop].reshape(width * 128, 768), near)
-            total_ref[t, first : first + width] += part.reshape(width, 128, 128)
+    for side in range(2):
+        add_near(weight_ref, side, side, lambda dy, z: cell(side, dy, z), total_ref, ENDS)
 
     def finish(index, carry):
         preact = total_ref[index // 4, index % 4]
@@ -314,28 +423,28 @@
 
     def spread(cell, carry):
         lanes = pl.ds(pl.multiple_of(cell * 128, 128), 128)
-        place = place_ref[1, cell // 4, cell % 4 + 1]
+        place = row_place_ref[1 + cell // 4, 1 + cell % 4]
         row_x = spline_row(place[0:1])
         row_y = spline_row(place[1:2]) * charge_ref[0:1, lanes]
         row_z = spline_row(place[2:3])
-        left_ref[:, lanes] = (
+        left_rows[:, lanes] = (
             (row_y[:, None, :] * row_x[None, :, :]).reshape(PC * PC, 128).astype(bf16)
         )
-        right_ref[:, lanes] = jnp.where(block == cell, jnp.tile(row_z, (8, 1)), 0.0).astype(bf16)
+        right_rows[:, lanes] = jnp.where(block == cell, jnp.tile(row_z, (8, 1)), 0.0).astype(bf16)
         return carry
 
     lax.fori_loop(0, 8, spread, 0)
-    mesh_ref[...] = dot_t(left_ref[...], right_ref[...]).reshape(PC, PC, 128).astype(bf16)
-    for t in range(2):
-        copy_out(t).wait()
-
-
-def message_layer(ends, part, place, read, weights):
+    mesh_ref[...] = dot_t(left_rows[...], right_rows[...]).reshape(PC, PC, 128).astype(bf16)
+    for copy in copies:
+        copy.wait()
+
+
+def message_layer(own, ends, outer, corners, part, read, weights):
     return pl.pallas_call(
         message_kernel,
-        in_specs=[VM] * 9 + [ANY],
+        in_specs=[VM] * 11 + [ANY],
         out_specs=[ANY, VM, VM, VM],
-        input_output_aliases={9: 0},
+        input_output_aliases={11: 0},
         out_shape=[
             jax.ShapeDtypeStruct((6, 8, 128, 768), bf16),
             jax.ShapeDtypeStruct((2, 4, 128, 128), f32),
@@ -358,7 +467,7 @@
         ),
         compiler_params=LARGE,
         name="message",
-    )(*ends, part, place, read, weights)
+    )(own, *ends, *outer, *corners, part, read, weights)
 
 
 def slope_kernel(total_ref, read_ref, out_ref):
@@ -389,10 +498,17 @@
 
 
 def forward_kernel(mesh_ref, along_z_ref, along_x_ref, out_ref):
-    total = jnp.zeros((64, 512), f32)
+    lane = lax.broadcasted_iota(jnp.int32, (64, 128), 1)
+    total = jnp.zeros((128, 256), f32)
     for g in range(4):
-        total = total + dot(mesh_ref[:, g].reshape(64, 128), along_z_ref[g])
-    lines = jnp.concatenate([total[:, :256], total[:, 256:]], axis=0).astype(bf16)
+        mesh = mesh_ref[:, g].reshape(64, 128)
+        none = jnp.zeros_like(mesh)
+        halves = jnp.concatenate(
+            [jnp.where(lane < 64, mesh, none), jnp.where(lane < 64, none, mesh)], axis=0
+        )
+        table = along_z_ref[g * 64 : (g + 1) * 64, :]
+        total = total + dot(halves, jnp.concatenate([table, table], axis=0))
+    lines = total.astype(bf16)
     waves = dot(along_x_ref[...], lines)
     out_ref[0:128, :] = waves[:, :128]
     out_ref[128:256, :] = waves[:, 128:]
@@ -412,18 +528,23 @@
     )(mesh, along_z, along_x)
 
 
-def filter_kernel(lines_ref, into_ref, back_ref, influence_ref, out_ref):
+def filter_kernel(lines_ref, into_ref, influence_ref, out_ref):
     waves = dot(into_ref[...], lines_ref[...].astype(bf16))
     scaled = influence_ref[...] * waves
     power = jnp.sum(jnp.sum(scaled * waves, axis=0, keepdims=True), axis=1, keepdims=True)
-    out_ref[pl.ds(0, 256, stride=2), :] = dot(back_ref[...], scaled.astype(bf16))
+    out_ref[pl.ds(0, 256, stride=2), :] = lax.dot_general(
+        into_ref[...],
+        scaled.astype(bf16),
+        (((0,), (0,)), ((), ())),
+        preferred_element_type=f32,
+    )
     out_ref[pl.ds(1, 256, stride=2), :] = jnp.broadcast_to(power, (256, 128))
 
 
-def filter_y(lines, into, back, influence):
+def filter_y(lines, into, influence):
     return pl.pallas_call(
         filter_kernel,
-        in_specs=[VM] * 4,
+        in_specs=[VM] * 3,
         out_specs=VM,
         compiler_params=SMALL,
         out_shape=jax.ShapeDtypeStruct((512, 128), f32),
@@ -431,7 +552,7 @@
             flops=4 * 256 * 256 * 128, bytes_accessed=700000, transcendentals=0
         ),
         name="filter_y",
-    )(lines, into, back, influence)
+    )(lines, into, influence)
 
 
 def inverse_kernel(energy_scale, lines_ref, along_x_ref, along_z_ref, out_ref, energy_ref):
@@ -464,7 +585,23 @@
     )(lines, along_x, along_z)
 
 
-def interpolate_kernel(field_scale, field_ref, place_ref, out_ref, own_ref):
+def interpolate_kernel(
+    field_scale, field_ref, place_ref, stored_ref, rows_ref, before_ref, after_ref,
+    out_ref, own_ref, weight_ref, slope_ref, sems
+):
+    pairs = [
+        (rows_ref, slope_ref.at[:, pl.ds(1, 2)]),
+        (before_ref, slope_ref.at[:, pl.ds(0, 1)]),
+        (after_ref, slope_ref.at[:, pl.ds(3, 1)]),
+        (stored_ref.at[pl.ds(0, 3)], weight_ref.at[pl.ds(0, 3)]),
+        (stored_ref.at[pl.ds(3, 3)], weight_ref.at[pl.ds(3, 3)]),
+    ]
+    copies = [
+        pltpu.make_async_copy(source, target, sems.at[i])
+        for i, (source, target) in enumerate(pairs)
+    ]
+    for copy in copies:
+        copy.start()
     block = lax.broadcasted_iota(jnp.int32, (128, 128), 0) // PC
 
     def gather(step, carry):
@@ -487,23 +624,28 @@
     lax.fori_loop(0, 8, gather, 0)
     own_ref[0:4, :] = out_ref[7:11, :]
     own_ref[4:8, :] = out_ref[13:17, :]
-
-
-def interpolate(field, place, field_scale):
+    for copy in copies:
+        copy.wait()
+
+
+def interpolate(field, place, weights, slopes, field_scale):
     return pl.pallas_call(
         functools.partial(interpolate_kernel, field_scale),
-        in_specs=[VM] * 2,
-        out_specs=[VM, VM],
-        compiler_params=SMALL,
+        in_specs=[VM] * 2 + [ANY] * 4,
+        out_specs=[VM] * 4,
+        compiler_params=MIDDLE,
         out_shape=[
             jax.ShapeDtypeStruct((24, 128), f32),
             jax.ShapeDtypeStruct((8, 128), f32),
-        ],
+            jax.ShapeDtypeStruct((6, 8, 128, 768), bf16),
+            jax.ShapeDtypeStruct((3, 4, 6, 128, 128), bf16),
+        ],
+        scratch_shapes=[pltpu.SemaphoreType.DMA((5,))],
         cost_estimate=pl.CostEstimate(
             flops=24 * 2 * 256 * 128 * 128, bytes_accessed=400000, transcendentals=0
         ),
         name="interpolate",
-    )(field, place)
+    )(field, place, weights, *slopes)
 
 
 def combination_of(t):
@@ -515,32 +657,14 @@
 
 
 def beside_kernel(
-    stored_ref, rows_ref, before_ref, after_ref, potential_ref,
-    weight_ref, slope_ref, total_ref, own_out, near_ref, sems
+    weight_ref, slope_ref, potential_ref, total_ref, own_out, near_ref
 ):
-    pairs = [
-        (rows_ref, slope_ref.at[:, pl.ds(1, 2)]),
-        (before_ref, slope_ref.at[:, pl.ds(0, 1)]),
-        (after_ref, slope_ref.at[:, pl.ds(3, 1)]),
-        (stored_ref.at[pl.ds(0, 3)], weight_ref.at[pl.ds(0, 3)]),
-        (stored_ref.at[pl.ds(3, 3)], weight_ref.at[pl.ds(3, 3)]),
-    ]
-    copies = [
-        pltpu.make_async_copy(source, target, sems.at[i])
-        for i, (source, target) in enumerate(pairs)
-    ]
-    for copy in copies:
-        copy.start()
-    for copy in copies[:3]:
-        copy.wait()
     columns = jnp.transpose(potential_ref[...])
     for x in range(4):
         for z in range(6):
             near_ref[x, z] = scaled(columns, x * 6 + z, slope_ref[1, x, z])
     own_out[...] = near_ref[1:3, 1:5]
     total_ref[...] = jnp.zeros_like(total_ref)
-    for copy in copies[3:]:
-        copy.wait()
 
     def combination(t, carry):
         x, a = combination_of(t)
@@ -558,24 +682,21 @@
 def beside(weights, slopes, potential):
     return pl.pallas_call(
         beside_kernel,
-        in_specs=[ANY] * 4 + [VM],
-        out_specs=[VM] * 4,
+        in_specs=[VM] * 3,
+        out_specs=[VM] * 2,
         out_shape=[
-            jax.ShapeDtypeStruct((6, 8, 128, 768), bf16),
-            jax.ShapeDtypeStruct((3, 4, 6, 128, 128), bf16),
             jax.ShapeDtypeStruct((2, 4, 128, 128), f32),
             jax.ShapeDtypeStruct((2, 4, 128, 128), bf16),
         ],
         scratch_shapes=[
             pltpu.VMEM((4, 6, 128, 128), bf16),
-            pltpu.SemaphoreType.DMA((5,)),
         ],
         cost_estimate=pl.CostEstimate(
             flops=3000000000, bytes_accessed=12000000, transcendentals=0
         ),
-        compiler_params=MIDDLE,
+        compiler_params=SMALL,
         name="beside",
-    )(weights, *slopes, potential)
+    )(weights, slopes, potential)
 
 
 def backward_kernel(
@@ -641,11 +762,6 @@
 
 def wave_tables(size_x, size_y, size_z):
     i16 = np.arange(16)
-    along_z = np.zeros((4, 2, 64, 2, size_z))
-    for g in range(4):
-        table = cas(g * 64 + np.arange(64), np.arange(size_z), size_z)
-        for a in range(2):
-            along_z[g, a, :, a, :] = table
     points_x = np.array([g * 32 + a * 16 + i for a in range(2) for g in range(4) for i in i16])
     along_x = cas(np.arange(size_x), points_x, size_x)
     points_y = np.array(
@@ -659,10 +775,9 @@
         [((4 * g - 2 + c) % 16) * 16 + k for g in range(4) for c in range(8) for k in i16]
     )
     tables = (
-        along_z.reshape(4, 128, 2 * size_z),
+        cas(np.arange(size_z), np.arange(size_z), size_z),
         along_x,
         into_y,
-        into_y.T,
         cas(back_x, np.arange(size_x), size_x),
         cas(np.arange(size_z), back_z, size_z),
     )
@@ -700,28 +815,31 @@
     cells = cells_x * cells_z
 
     features_own = features.reshape(cells, slots, width)
-    own = project(features_own, msg_weight, spline_corner, spline_fraction)
+    own = project(
+        features_own, msg_weight, spline_corner.swapaxes(2, 3), spline_fraction.swapaxes(2, 3)
+    )
     own = own.reshape(cells_x, cells_z, slots + 16, width)
-    near, ends = early_halo(own)
-    weights, part, place = inner_pairs(own, near, features_own, self_weight)
+    sides, ends, outer, corners = early_halo(own)
+    weights, part = inside_pairs(own, sides, features_own, self_weight)
+    weights, part = ends_pairs(own, sides, ends, outer, part, weights)
     influence = influence_of(size_x, size_y, size_z)
-    along_z, along_x, into_y, from_y, back_x, back_z = wave_tables(size_x, size_y, size_z)
+    along_z, along_x, into_y, back_x, back_z = wave_tables(size_x, size_y, size_z)
 
     read = charge_weight[None, :]
-    weights, preact, mesh, row_place = message_layer(ends, part, place, read, weights)
-    slope = slope_of(preact, read)
-    slope_near = late_halo(slope)
-
+    weights, preact, mesh, row_place = message_layer(
+        own, ends, outer, corners, part, read, weights
+    )
     mesh = swapped(mesh, plane).reshape(4, 4, PC, 128)
+    slope_near = late_halo(slope_of(preact, read))
     lines = swapped(forward_xz(mesh, along_z, along_x), everyone)
-    lines = swapped(filter_y(lines, into_y, from_y, influence), everyone)
+    lines = swapped(filter_y(lines, into_y, influence), everyone)
     field, energy = inverse_xz(lines, back_x, back_z, coupling / (2.0 * volume * natoms))
     field = swapped(field.reshape(16, 64, 128), plane)
-    potential, atom_potential = interpolate(field, row_place.reshape(24, 8, slots), coupling / volume)
+    potential, atom_potential, weights, slopes = interpolate(
+        field, row_place.reshape(24, 8, slots), weights, slope_near, coupling / volume
+    )
     below, above = moved(potential, "gy", 1), moved(potential, "gy", -1)
-    weights, slopes, total, cotangent = beside(
-        weights, slope_near, potential
-    )
+    total, cotangent = beside(weights, slopes, potential)
     grad = backward(weights, slopes, total, cotangent, below, above, msg_weight, self_weight)
     return (
         grad.reshape(features.shape),

time: 160 us -> 160 us (level)
  starting transfers between devices: 75.2 us -> 64.9 us
  waiting for transfers between devices: 47.1 us -> 55.2 us
  Pallas kernels: 30.4 us -> 34.3 us
    ppermute x18, starting transfers between devices: 42.3 us -> 30 us  [moved(): lax.ppermute(value.reshape(-1, 128), axis, pairs).reshape(value.shape)]
    all_to_all x4, waiting for transfers between devices: 31.7 us -> 37.4 us  [swapped(): return lax.all_to_all(value, axis, split_axis=0, concat_axis=0, tiled=True)]
    unnamed x26 -> x20, local copies, waits for them, and re-layouts: 3.2 us -> 0.05 us
    ppermute x18, waiting for transfers between devices: 15.4 us -> 17.8 us  [moved(): lax.ppermute(value.reshape(-1, 128), axis, pairs).reshape(value.shape)]
    pallas_call x1, Pallas kernels: 2.4 us -> 4.57 us  [interpolate(): pl.pallas_call(functools.partial(interpolate_kernel, field_scale), in_spe...]
    all_to_all x4, starting transfers between devices: 32.8 us -> 34.9 us  [swapped(): return lax.all_to_all(value, axis, split_axis=0, concat_axis=0, tiled=True)]
    pallas_call x1, Pallas kernels: 0.21 us -> 1.91 us  [project(): pl.pallas_call(project_kernel, grid=(1,), in_specs=[whole((8, 128, 128)),...]
    pallas_call x4 -> x5, Pallas kernels: 20.3 us -> 20.3 us  [the longest x1 6.81 us: ends_pairs(): pl.pallas_call(ends_kernel, in_specs=[VM] * 10 + [ANY], out_specs=[ANY, V...]
  transfers between devices with their start and end apart: 22 -> 22, of which waited for: 8 -> 8; matrix products, arithmetic and copies ran while one was open for 1% -> 3% of each run, Pallas kernels for 12% -> 11%
where the time goes in v2:
time: 160 us; the launch traced here: 159 us
  starting transfers between devices  64.9 us (41%)
  waiting for transfers between devices  55.2 us (34%)
  Pallas kernels  34.3 us (21%)
  local copies, waits for them, and re-layouts  3.65 us (2%)
    all_to_all x4, waiting for transfers between devices, swapped(): return lax.all_to_all(value, axis, split_axis=0, concat_axis=0, tiled=True)  37.4 us
    all_to_all x4, starting transfers between devices, swapped(): return lax.all_to_all(value, axis, split_axis=0, concat_axis=0, tiled=True)  34.9 us
    ppermute x18, starting transfers between devices, moved(): lax.ppermute(value.reshape(-1, 128), axis, pairs).reshape(value.shape)  30 us
    ppermute x18, waiting for transfers between devices, moved(): lax.ppermute(value.reshape(-1, 128), axis, pairs).reshape(value.shape)  17.8 us
    pallas_call x1, Pallas kernels, ends_pairs(): pl.pallas_call(ends_kernel, in_specs=[VM] * 10 + [ANY], out_specs=[ANY, V...  6.81 us
    pallas_call x1, Pallas kernels, inside_pairs(): pl.pallas_call(inside_kernel, in_specs=[VM] * 5, out_specs=[ANY, VM], out...  5.71 us
    pallas_call x1, Pallas kernels, backward(): pl.pallas_call(backward_kernel, in_specs=[VM] * 8, out_specs=VM, out_shap...  5.17 us
    pallas_call x1, Pallas kernels, interpolate(): pl.pallas_call(functools.partial(interpolate_kernel, field_scale), in_spe...  4.57 us
  transfers between devices with their start and end apart: 22, of which 8 were waited for; matrix products, arithmetic and copies ran while one was open for 3% of the time, Pallas kernels for 11%

profile of v2, /device:TPU:32, one launch (start us, length us, event | category | flops | bytes accessed | tf_op | source)
XLA Modules:
  0.0 159.4 jit_solution(13604733139169819519)
XLA Ops:
  0.6 1.9 %project.1 = bf16[8,144,128]{2,1,0:T(8,128)(2,1)} custom-call(bf16[8,128,128]{2,1,0:T(8,128)(2,1)} %bitcast.93, bf16[128,128]{1,0:T(8,128)(2,1)} %msg_ref.1, s32[2,1,3,4,128]{4,3,2,1,0:T(4,128)} %bitcast.131, f32[2,1,3,4,128]{4,3,2,1,0:T(4,128)} %bitcast.132), custom_call_target="tpu_custom_call" | custom-call | tf_op jit(solution)/shard_map/project/pallas_call | solution.py:98
  2.5 7.9 %collective-permute-start.1 = (bf16[1152,128]{1,0:T(8,128)(2,1)}, bf16[1152,128]{1,0:T(8,128)(2,1)S(1)}, u32[]{:S(2)}, u32[]{:S(2)}) collective-permute-start(bf16[1152,128]{1,0:T(8,128)(2,1)} %bitcast.75), channel_id=1, source_target_pairs={{0,60},{4,0},{8,4},{12,8},{16,12},{20,16},{24,20},{28,24},{32,28},... | collective-permute-start | bytes 884744 | tf_op jit(solution)/shard_map/ppermute | solution.py:54
  10.5 0.0 collective-permute-start
  10.5 1.0 fusion.10
  11.5 1.7 %collective-permute-start.4 = (bf16[576,128]{1,0:T(8,128)(2,1)S(1)}, bf16[576,128]{1,0:T(8,128)(2,1)S(1)}, u32[]{:S(2)}, u32[]{:S(2)}) collective-permute-start(bf16[576,128]{1,0:T(8,128)(2,1)S(1)} %bitcast.126), channel_id=1, source_target_pairs={{0,64},{64,128},{128,192},{192,0},{1,65},{65,129},{129,193},{193,1... | collective-permute-start | bytes 442376 | tf_op jit(solution)/shard_map/ppermute | solution.py:54
  13.1 1.7 %collective-permute-start.5 = (bf16[576,128]{1,0:T(8,128)(2,1)S(1)}, bf16[576,128]{1,0:T(8,128)(2,1)S(1)}, u32[]{:S(2)}, u32[]{:S(2)}) collective-permute-start(bf16[576,128]{1,0:T(8,128)(2,1)S(1)} %bitcast.125), channel_id=1, source_target_pairs={{0,192},{64,0},{128,64},{192,128},{1,193},{65,1},{129,65},{193,129... | collective-permute-start | bytes 442376 | tf_op jit(solution)/shard_map/ppermute | solution.py:54
  14.8 0.9 slice_bitcast_fusion.1
  15.7 6.6 %collective-permute-done.1 = bf16[1152,128]{1,0:T(8,128)(2,1)S(1)} collective-permute-done((bf16[1152,128]{1,0:T(8,128)(2,1)}, bf16[1152,128]{1,0:T(8,128)(2,1)S(1)}, u32[]{:S(2)}, u32[]{:S(2)}) %collective-permute-start.1) | collective-permute-done | bytes 294944 | tf_op jit(solution)/shard_map/ppermute | solution.py:54
  22.3 3.5 %collective-permute-done = bf16[1152,128]{1,0:T(8,128)(2,1)S(1)} collective-permute-done((bf16[1152,128]{1,0:T(8,128)(2,1)}, bf16[1152,128]{1,0:T(8,128)(2,1)S(1)}, u32[]{:S(2)}, u32[]{:S(2)}) %collective-permute-start) | collective-permute-done | bytes 294944 | tf_op jit(solution)/shard_map/ppermute | solution.py:54
  25.9 0.1 collective-permute-start.2
  26.0 2.1 %collective-permute-start.3 = (bf16[864,128]{1,0:T(8,128)(2,1)S(1)}, bf16[864,128]{1,0:T(8,128)(2,1)S(1)}, u32[]{:S(2)}, u32[]{:S(2)}) collective-permute-start(bf16[864,128]{1,0:T(8,128)(2,1)S(1)} %bitcast.123), channel_id=1, source_target_pairs={{0,3},{1,0},{2,1},{3,2},{4,7},{5,4},{6,5},{7,6},{8,11},{9,8},{10,9... | collective-permute-start | bytes 663560 | tf_op jit(solution)/shard_map/ppermute | solution.py:54
  28.1 0.1 pad_maximum_fusion.2
  28.1 1.7 %collective-permute-start.6 = (bf16[1152,128]{1,0:T(8,128)(2,1)S(1)}, bf16[1152,128]{1,0:T(8,128)(2,1)S(1)}, u32[]{:S(2)}, u32[]{:S(2)}) collective-permute-start(bf16[1152,128]{1,0:T(8,128)(2,1)S(1)} %bitcast.120), channel_id=1, source_target_pairs={{0,64},{64,128},{128,192},{192,0},{1,65},{65,129},{129,193},{193,1... | collective-permute-start | bytes 884744 | tf_op jit(solution)/shard_map/ppermute | solution.py:54
  29.8 5.7 %inside_pairs.1 = (bf16[6,8,128,768]{3,2,1,0:T(8,128)(2,1)}, f32[2,4,128,128]{3,2,1,0:T(8,128)S(1)}) custom-call(bf16[2,4,144,128]{3,2,1,0:T(8,128)(2,1)S(1)} %bitcast.78, bf16[2,4,144,128]{3,2,1,0:T(8,128)(2,1)S(1)} %bitcast.88, bf16[2,4,144,128]{3,2,1,0:T(8,128)(2,1)S(1)} %bitcast.84, bf16[8,128,128]{2,1,0:T(8,128)(2,1)S(1)} %bitcast.94, ...), custom_call_target="tpu_custom_call" | custom-call | flops 5000000000 | bytes 9000000 | tf_op jit(solution)/shard_map/inside_pairs/pallas_call | solution.py:224
  35.6 0.0 collective-permute-done.2
  35.6 1.7 %collective-permute-start.7 = (bf16[1152,128]{1,0:T(8,128)(2,1)S(1)}, bf16[1152,128]{1,0:T(8,128)(2,1)S(1)}, u32[]{:S(2)}, u32[]{:S(2)}) collective-permute-start(bf16[1152,128]{1,0:T(8,128)(2,1)S(1)} %bitcast.119), channel_id=1, source_target_pairs={{0,192},{64,0},{128,64},{192,128},{1,193},{65,1},{129,65},{193,129... | collective-permute-start | bytes 884744 | tf_op jit(solution)/shard_map/ppermute | solution.py:54
  37.3 0.0 collective-permute-done.3
  37.4 0.5 collective-permute-start.8
  37.9 0.0 collective-permute-done.4
  37.9 3.1 %collective-permute-start.9 = (bf16[864,128]{1,0:T(8,128)(2,1)S(1)}, bf16[864,128]{1,0:T(8,128)(2,1)S(1)}, u32[]{:S(2)}, u32[]{:S(2)}) collective-permute-start(bf16[864,128]{1,0:T(8,128)(2,1)S(1)} %bitcast.122), channel_id=1, source_target_pairs={{0,192},{64,0},{128,64},{192,128},{1,193},{65,1},{129,65},{193,129... | collective-permute-start | bytes 663560 | tf_op jit(solution)/shard_map/ppermute | solution.py:54
  41.0 0.0 collective-permute-done.5
  41.0 0.0 collective-permute-done.6
  41.0 1.4 collective-permute-done.7
  42.4 6.8 %ends_pairs.1 = (bf16[6,8,128,768]{3,2,1,0:T(8,128)(2,1)}, f32[2,4,128,128]{3,2,1,0:T(8,128)S(1)}) custom-call(bf16[2,4,144,128]{3,2,1,0:T(8,128)(2,1)S(1)} %bitcast.79, bf16[2,4,144,128]{3,2,1,0:T(8,128)(2,1)S(1)} %bitcast.89, bf16[2,4,144,128]{3,2,1,0:T(8,128)(2,1)S(1)} %bitcast.85, ...), custom_call_target="tpu_custom_call", output_to_operand_aliasing={{0}: (10, {})} | custom-call | flops 8999999488 | bytes 9000000 | tf_op jit(solution)/shard_map/ends_pairs/pallas_call | solution.py:320
  49.2 0.0 collective-permute-done.8
  49.2 0.0 collective-permute-done.9
  49.2 4.2 %message.1 = (bf16[6,8,128,768]{3,2,1,0:T(8,128)(2,1)}, f32[2,4,128,128]{3,2,1,0:T(8,128)S(1)}, bf16[16,16,128]{2,1,0:T(8,128)(2,1)}, f32[4,6,8,128]{3,2,1,0:T(8,128)S(1)}) custom-call(bf16[2,4,144,128]{3,2,1,0:T(8,128)(2,1)S(1)} %bitcast.80, bf16[3,2,1,144,128]{4,3,2,1,0:T(8,128)(2,1)S(1)} %bitcast.98, ...), custom_call_target="tpu_custom_call", output_to_operand_aliasing={{0}: (11, {})} | custom-call | flops 5000000000 | bytes 6000000 | tf_op jit(solution)/shard_map/message/pallas_call | solution.py:443
  53.5 0.0 copy-start.4
  53.5 0.0 copy-start.7
  53.5 0.2 slope.1
  53.7 0.0 copy-start.3
  53.8 3.2 %collective-permute-start.11 = (bf16[256,128]{1,0:T(8,128)(2,1)S(1)}, bf16[256,128]{1,0:T(8,128)(2,1)S(1)}, u32[]{:S(2)}, u32[]{:S(2)}) collective-permute-start(bf16[256,128]{1,0:T(8,128)(2,1)S(1)} %bitcast.130), channel_id=1, source_target_pairs={{0,3},{1,0},{2,1},{3,2},{4,7},{5,4},{6,5},{7,6},{8,11},{9,8},{10,9... | collective-permute-start | bytes 196616 | tf_op jit(solution)/shard_map/ppermute | solution.py:54
  56.9 0.0 collective-permute-start.10
  56.9 7.5 %all-to-all-start = ((bf16[16,16,128]{2,1,0:T(8,128)(2,1)}), bf16[16,16,128]{2,1,0:T(8,128)(2,1)S(1)}, u32[]{:S(2)}, u32[]{:S(2)}) async-start(bf16[16,16,128]{2,1,0:T(8,128)(2,1)} %get-tuple-element.23), calls=%async_computation | async-start | bytes 131072 | tf_op jit(solution)/shard_map/all_to_all | solution.py:805
  64.5 0.0 collective-permute-done.11
  64.5 0.0 collective-permute-done.10
  64.5 0.1 fusion.8
  64.6 2.6 %collective-permute-start.13 = (bf16[1536,128]{1,0:T(8,128)(2,1)S(1)}, bf16[1536,128]{1,0:T(8,128)(2,1)S(1)}, u32[]{:S(2)}, u32[]{:S(2)}) collective-permute-start(bf16[1536,128]{1,0:T(8,128)(2,1)S(1)} %bitcast.117), channel_id=1, source_target_pairs={{0,60},{4,0},{8,4},{12,8},{16,12},{20,16},{24,20},{28,24},{32,28},... | collective-permute-start | bytes 1179656 | tf_op jit(solution)/shard_map/ppermute | solution.py:54
  67.2 0.0 collective-permute-start.12
  67.2 4.9 %all-to-all-done = bf16[16,16,128]{2,1,0:T(8,128)(2,1)S(1)} async-done(((bf16[16,16,128]{2,1,0:T(8,128)(2,1)}), bf16[16,16,128]{2,1,0:T(8,128)(2,1)S(1)}, u32[]{:S(2)}, u32[]{:S(2)}) %all-to-all-start) | async-done | bytes 65568 | tf_op jit(solution)/shard_map/all_to_all | solution.py:805
  72.1 1.0 forward_xz.1
  73.2 16.6 %all-to-all-start.1 = ((f32[256,1,128]{2,1,0:T(1,128)}), f32[256,1,128]{2,1,0:T(1,128)S(1)}, u32[]{:S(2)}, u32[]{:S(2)}) async-start(f32[256,1,128]{2,1,0:T(1,128)} %bitcast.34), calls=%async_computation.1 | async-start | bytes 262144 | tf_op jit(solution)/shard_map/all_to_all | solution.py:805
  89.8 0.1 fusion.1.influence_ref
  89.9 12.6 %all-to-all-done.1 = f32[256,1,128]{2,1,0:T(1,128)S(1)} async-done(((f32[256,1,128]{2,1,0:T(1,128)}), f32[256,1,128]{2,1,0:T(1,128)S(1)}, u32[]{:S(2)}, u32[]{:S(2)}) %all-to-all-start.1) | async-done | bytes 131104 | tf_op jit(solution)/shard_map/all_to_all | solution.py:805
  102.5 1.1 filter_y.1
  103.6 6.2 %all-to-all-start.2 = ((f32[256,2,128]{2,1,0:T(2,128)}), f32[256,2,128]{2,1,0:T(2,128)S(1)}, u32[]{:S(2)}, u32[]{:S(2)}) async-start(f32[256,2,128]{2,1,0:T(2,128)} %bitcast.36), calls=%async_computation.2 | async-start | bytes 524288 | tf_op jit(solution)/shard_map/all_to_all | solution.py:805
  109.8 0.0 collective-permute-done.12
  109.8 0.1 pad_maximum_fusion.rows_ref
  109.9 0.0 copy-start.2
  109.9 0.0 copy-start.5
  110.0 1.1 fusion.9
  111.0 1.5 collective-permute-start.14
  112.6 1.7 %collective-permute-start.15 = (bf16[2304,128]{1,0:T(8,128)(2,1)}, bf16[2304,128]{1,0:T(8,128)(2,1)S(1)}, u32[]{:S(2)}, u32[]{:S(2)}) collective-permute-start(bf16[2304,128]{1,0:T(8,128)(2,1)} %bitcast.50), channel_id=1, source_target_pairs={{0,192},{64,0},{128,64},{192,128},{1,193},{65,1},{129,65},{193,129... | collective-permute-start | bytes 1769480 | tf_op jit(solution)/shard_map/ppermute | solution.py:54
  114.3 10.8 %all-to-all-done.2 = f32[256,2,128]{2,1,0:T(2,128)S(1)} async-done(((f32[256,2,128]{2,1,0:T(2,128)}), f32[256,2,128]{2,1,0:T(2,128)S(1)}, u32[]{:S(2)}, u32[]{:S(2)}) %all-to-all-start.2) | async-done | bytes 262176 | tf_op jit(solution)/shard_map/all_to_all | solution.py:805
  125.1 1.0 inverse_xz.1
  126.1 4.6 %all-to-all-start.3 = ((bf16[16,64,128]{2,1,0:T(8,128)(2,1)}), bf16[16,64,128]{2,1,0:T(8,128)(2,1)S(1)}, u32[]{:S(2)}, u32[]{:S(2)}) async-start(bf16[16,64,128]{2,1,0:T(8,128)(2,1)} %bitcast.38), calls=%async_computation.3 | async-start | bytes 524288 | tf_op jit(solution)/shard_map/all_to_all | solution.py:805
  130.7 0.5 slice.77
  131.2 9.1 %all-to-all-done.3.field_ref = bf16[16,64,128]{2,1,0:T(8,128)(2,1)S(1)} async-done(((bf16[16,64,128]{2,1,0:T(8,128)(2,1)}), bf16[16,64,128]{2,1,0:T(8,128)(2,1)S(1)}, u32[]{:S(2)}, u32[]{:S(2)}) %all-to-all-start.3) | async-done | bytes 262176 | tf_op jit(solution)/shard_map/all_to_all | solution.py:805
  140.4 4.6 %interpolate.1 = (f32[24,128]{1,0:T(8,128)S(1)}, f32[8,128]{1,0:T(8,128)}, bf16[6,8,128,768]{3,2,1,0:T(8,128)(2,1)S(1)}, bf16[3,4,6,128,128]{4,3,2,1,0:T(8,128)(2,1)S(1)}) custom-call(bf16[16,64,128]{2,1,0:T(8,128)(2,1)S(1)} %all-to-all-done.3.field_ref, f32[24,8,128]{2,1,0:T(8,128)S(1)} %bitcast.102, bf16[6,8,128,768]{3,2,1,0:T(8,128)(2,1)} %get-tuple-element.26.stored_ref, ...), custom_call_target="tpu_custom_call" | custom-call | flops 201326592 | bytes 400000 | tf_op jit(solution)/shard_map/interpolate/pallas_call | solution.py:632
  144.9 0.1 collective-permute-start.17
  145.0 0.5 collective-permute-start.16
  145.5 2.5 %beside.1 = (f32[2,4,128,128]{3,2,1,0:T(8,128)S(1)}, bf16[2,4,128,128]{3,2,1,0:T(8,128)(2,1)S(1)}) custom-call(bf16[6,8,128,768]{3,2,1,0:T(8,128)(2,1)S(1)} %get-tuple-element.28.weight_ref, bf16[3,4,6,128,128]{4,3,2,1,0:T(8,128)(2,1)S(1)} %get-tuple-element.29.slope_ref, f32[24,128]{1,0:T(8,128)S(1)} %get-tuple-element.30.potential_ref), custom_call_target="tpu_custom_call" | custom-call | flops 3000000000 | bytes 12000000 | tf_op jit(solution)/shard_map/beside/pallas_call | solution.py:683
  148.0 6.2 %collective-permute-done.16.below_ref = f32[24,128]{1,0:T(8,128)S(1)} collective-permute-done((f32[24,128]{1,0:T(8,128)S(1)}, f32[24,128]{1,0:T(8,128)S(1)}, u32[]{:S(2)}, u32[]{:S(2)}) %collective-permute-start.16) | collective-permute-done | bytes 12320 | tf_op jit(solution)/shard_map/ppermute | solution.py:54
  154.2 5.2 %backward.1 = f32[2,4,128,128]{3,2,1,0:T(8,128)} custom-call(bf16[6,8,128,768]{3,2,1,0:T(8,128)(2,1)S(1)} %get-tuple-element.28.weight_ref, bf16[3,4,6,128,128]{4,3,2,1,0:T(8,128)(2,1)S(1)} %get-tuple-element.29.slope_ref, f32[2,4,128,128]{3,2,1,0:T(8,128)S(1)} %get-tuple-element.31.part_ref, bf16[2,4,128,128]{3,2,1,0:T(8,128)(2,1)S(1)} %get-tuple-element.32.own_ref, ...), custom_call_target="tpu_custom_call" | custom-call | flops 4000000000 | bytes 12000000 | tf_op jit(solution)/shard_map/backward/pallas_call | solution.py:745
  (30 shorter events, 0.2 us)
Async XLA Ops:
  2.5 19.8 %collective-permute-start.1 = (bf16[1152,128]{1,0:T(8,128)(2,1)}, bf16[1152,128]{1,0:T(8,128)(2,1)S(1)}, u32[]{:S(2)}, u32[]{:S(2)}) collective-permute-start(bf16[1152,128]{1,0:T(8,128)(2,1)} %bitcast.75), channel_id=1, source_target_pairs={{0,60},{4,0},{8,4},{12,8},{16,12},{20,16},{24,20},{28,24},{32,28},... | collective-permute-start | bytes 884744 | tf_op jit(solution)/shard_map/ppermute | solution.py:54
  10.5 15.4 %collective-permute-start = (bf16[1152,128]{1,0:T(8,128)(2,1)}, bf16[1152,128]{1,0:T(8,128)(2,1)S(1)}, u32[]{:S(2)}, u32[]{:S(2)}) collective-permute-start(bf16[1152,128]{1,0:T(8,128)(2,1)} %bitcast.76), channel_id=1, source_target_pairs={{0,4},{4,8},{8,12},{12,16},{16,20},{20,24},{24,28},{28,32},{32,36}... | collective-permute-start | bytes 884744 | tf_op jit(solution)/shard_map/ppermute | solution.py:54
  11.5 26.4 %collective-permute-start.4 = (bf16[576,128]{1,0:T(8,128)(2,1)S(1)}, bf16[576,128]{1,0:T(8,128)(2,1)S(1)}, u32[]{:S(2)}, u32[]{:S(2)}) collective-permute-start(bf16[576,128]{1,0:T(8,128)(2,1)S(1)} %bitcast.126), channel_id=1, source_target_pairs={{0,64},{64,128},{128,192},{192,0},{1,65},{65,129},{129,193},{193,1... | collective-permute-start | bytes 442376 | tf_op jit(solution)/shard_map/ppermute | solution.py:54
  13.1 27.8 %collective-permute-start.5 = (bf16[576,128]{1,0:T(8,128)(2,1)S(1)}, bf16[576,128]{1,0:T(8,128)(2,1)S(1)}, u32[]{:S(2)}, u32[]{:S(2)}) collective-permute-start(bf16[576,128]{1,0:T(8,128)(2,1)S(1)} %bitcast.125), channel_id=1, source_target_pairs={{0,192},{64,0},{128,64},{192,128},{1,193},{65,1},{129,65},{193,129... | collective-permute-start | bytes 442376 | tf_op jit(solution)/shard_map/ppermute | solution.py:54
  25.8 4.0 %copy-start = (bf16[8,144,128]{2,1,0:T(8,128)(2,1)S(1)}, bf16[8,144,128]{2,1,0:T(8,128)(2,1)}, u32[]{:S(2)}) copy-start(bf16[8,144,128]{2,1,0:T(8,128)(2,1)} %project.1) | copy-start | bytes 884740
  25.8 4.0 %copy-start.1 = (bf16[2,1,4,128,128]{4,3,2,1,0:T(8,128)(2,1)S(1)}, bf16[2,1,4,128,128]{4,3,2,1,0:T(8,128)(2,1)}, u32[]{:S(2)}) copy-start(bf16[2,1,4,128,128]{4,3,2,1,0:T(8,128)(2,1)} %param.11) | copy-start | bytes 786436
  25.8 4.0 %copy-start.9 = (bf16[128,128]{1,0:T(8,128)(2,1)S(1)}, bf16[128,128]{1,0:T(8,128)(2,1)}, u32[]{:S(2)}) copy-start(bf16[128,128]{1,0:T(8,128)(2,1)} %self_ref.3) | copy-start | bytes 98308
  25.9 9.7 %collective-permute-start.2 = (bf16[864,128]{1,0:T(8,128)(2,1)S(1)}, bf16[864,128]{1,0:T(8,128)(2,1)S(1)}, u32[]{:S(2)}, u32[]{:S(2)}) collective-permute-start(bf16[864,128]{1,0:T(8,128)(2,1)S(1)} %bitcast.124), channel_id=1, source_target_pairs={{0,1},{1,2},{2,3},{3,0},{4,5},{5,6},{6,7},{7,4},{8,9},{9,10},{10,1... | collective-permute-start | bytes 663560 | tf_op jit(solution)/shard_map/ppermute | solution.py:54
  26.0 11.3 %collective-permute-start.3 = (bf16[864,128]{1,0:T(8,128)(2,1)S(1)}, bf16[864,128]{1,0:T(8,128)(2,1)S(1)}, u32[]{:S(2)}, u32[]{:S(2)}) collective-permute-start(bf16[864,128]{1,0:T(8,128)(2,1)S(1)} %bitcast.123), channel_id=1, source_target_pairs={{0,3},{1,0},{2,1},{3,2},{4,7},{5,4},{6,5},{7,6},{8,11},{9,8},{10,9... | collective-permute-start | bytes 663560 | tf_op jit(solution)/shard_map/ppermute | solution.py:54
  28.1 12.8 %collective-permute-start.6 = (bf16[1152,128]{1,0:T(8,128)(2,1)S(1)}, bf16[1152,128]{1,0:T(8,128)(2,1)S(1)}, u32[]{:S(2)}, u32[]{:S(2)}) collective-permute-start(bf16[1152,128]{1,0:T(8,128)(2,1)S(1)} %bitcast.120), channel_id=1, source_target_pairs={{0,64},{64,128},{128,192},{192,0},{1,65},{65,129},{129,193},{193,1... | collective-permute-start | bytes 884744 | tf_op jit(solution)/shard_map/ppermute | solution.py:54
  35.6 6.8 %collective-permute-start.7 = (bf16[1152,128]{1,0:T(8,128)(2,1)S(1)}, bf16[1152,128]{1,0:T(8,128)(2,1)S(1)}, u32[]{:S(2)}, u32[]{:S(2)}) collective-permute-start(bf16[1152,128]{1,0:T(8,128)(2,1)S(1)} %bitcast.119), channel_id=1, source_target_pairs={{0,192},{64,0},{128,64},{192,128},{1,193},{65,1},{129,65},{193,129... | collective-permute-start | bytes 884744 | tf_op jit(solution)/shard_map/ppermute | solution.py:54
  37.4 11.8 %collective-permute-start.8 = (bf16[864,128]{1,0:T(8,128)(2,1)S(1)}, bf16[864,128]{1,0:T(8,128)(2,1)S(1)}, u32[]{:S(2)}, u32[]{:S(2)}) collective-permute-start(bf16[864,128]{1,0:T(8,128)(2,1)S(1)} %bitcast.121), channel_id=1, source_target_pairs={{0,64},{64,128},{128,192},{192,0},{1,65},{65,129},{129,193},{193,1... | collective-permute-start | bytes 663560 | tf_op jit(solution)/shard_map/ppermute | solution.py:54
  37.9 11.3 %collective-permute-start.9 = (bf16[864,128]{1,0:T(8,128)(2,1)S(1)}, bf16[864,128]{1,0:T(8,128)(2,1)S(1)}, u32[]{:S(2)}, u32[]{:S(2)}) collective-permute-start(bf16[864,128]{1,0:T(8,128)(2,1)S(1)} %bitcast.122), channel_id=1, source_target_pairs={{0,192},{64,0},{128,64},{192,128},{1,193},{65,1},{129,65},{193,129... | collective-permute-start | bytes 663560 | tf_op jit(solution)/shard_map/ppermute | solution.py:54
  42.4 6.8 %copy-start.8 = (bf16[128]{0:T(256)(128)(2,1)S(1)}, bf16[128]{0:T(256)(128)(2,1)}, u32[]{:S(2)}) copy-start(bf16[128]{0:T(256)(128)(2,1)} %param.14) | copy-start | bytes 772
  53.5 18.7 %copy-start.4 = (bf16[256,256]{1,0:T(8,128)(2,1)S(1)}, bf16[256,256]{1,0:T(8,128)(2,1)}, u32[]{:S(2)}) copy-start(bf16[256,256]{1,0:T(8,128)(2,1)} %constant.78.clone.along_z_ref) | copy-start | bytes 393220
  53.5 18.7 %copy-start.7 = (bf16[128,128]{1,0:T(8,128)(2,1)S(1)}, bf16[128,128]{1,0:T(8,128)(2,1)}, u32[]{:S(2)}) copy-start(bf16[128,128]{1,0:T(8,128)(2,1)} %constant.79.clone.along_x_ref) | copy-start | bytes 98308
  53.7 48.8 %copy-start.3 = (bf16[256,256]{1,0:T(8,128)(2,1)S(1)}, bf16[256,256]{1,0:T(8,128)(2,1)}, u32[]{:S(2)}) copy-start(bf16[256,256]{1,0:T(8,128)(2,1)} %constant.80.clone.into_ref) | copy-start | bytes 393220
  53.8 10.7 %collective-permute-start.11 = (bf16[256,128]{1,0:T(8,128)(2,1)S(1)}, bf16[256,128]{1,0:T(8,128)(2,1)S(1)}, u32[]{:S(2)}, u32[]{:S(2)}) collective-permute-start(bf16[256,128]{1,0:T(8,128)(2,1)S(1)} %bitcast.130), channel_id=1, source_target_pairs={{0,3},{1,0},{2,1},{3,2},{4,7},{5,4},{6,5},{7,6},{8,11},{9,8},{10,9... | collective-permute-start | bytes 196616 | tf_op jit(solution)/shard_map/ppermute | solution.py:54
  56.9 7.5 %collective-permute-start.10 = (bf16[256,128]{1,0:T(8,128)(2,1)S(1)}, bf16[256,128]{1,0:T(8,128)(2,1)S(1)}, u32[]{:S(2)}, u32[]{:S(2)}) collective-permute-start(bf16[256,128]{1,0:T(8,128)(2,1)S(1)} %bitcast.129), channel_id=1, source_target_pairs={{0,1},{1,2},{2,3},{3,0},{4,5},{5,6},{6,7},{7,4},{8,9},{9,10},{10,1... | collective-permute-start | bytes 196616 | tf_op jit(solution)/shard_map/ppermute | solution.py:54
  56.9 15.2 %all-to-all-start = ((bf16[16,16,128]{2,1,0:T(8,128)(2,1)}), bf16[16,16,128]{2,1,0:T(8,128)(2,1)S(1)}, u32[]{:S(2)}, u32[]{:S(2)}) async-start(bf16[16,16,128]{2,1,0:T(8,128)(2,1)} %get-tuple-element.23), calls=%async_computation | async-start | bytes 131072 | tf_op jit(solution)/shard_map/all_to_all | solution.py:805
  64.6 45.2 %collective-permute-start.13 = (bf16[1536,128]{1,0:T(8,128)(2,1)S(1)}, bf16[1536,128]{1,0:T(8,128)(2,1)S(1)}, u32[]{:S(2)}, u32[]{:S(2)}) collective-permute-start(bf16[1536,128]{1,0:T(8,128)(2,1)S(1)} %bitcast.117), channel_id=1, source_target_pairs={{0,60},{4,0},{8,4},{12,8},{16,12},{20,16},{24,20},{28,24},{32,28},... | collective-permute-start | bytes 1179656 | tf_op jit(solution)/shard_map/ppermute | solution.py:54
  67.2 42.6 %collective-permute-start.12 = (bf16[1536,128]{1,0:T(8,128)(2,1)S(1)}, bf16[1536,128]{1,0:T(8,128)(2,1)S(1)}, u32[]{:S(2)}, u32[]{:S(2)}) collective-permute-start(bf16[1536,128]{1,0:T(8,128)(2,1)S(1)} %bitcast.118), channel_id=1, source_target_pairs={{0,4},{4,8},{8,12},{12,16},{16,20},{20,24},{24,28},{28,32},{32,36}... | collective-permute-start | bytes 1179656 | tf_op jit(solution)/shard_map/ppermute | solution.py:54
  73.2 29.3 %all-to-all-start.1 = ((f32[256,1,128]{2,1,0:T(1,128)}), f32[256,1,128]{2,1,0:T(1,128)S(1)}, u32[]{:S(2)}, u32[]{:S(2)}) async-start(f32[256,1,128]{2,1,0:T(1,128)} %bitcast.34), calls=%async_computation.1 | async-start | bytes 262144 | tf_op jit(solution)/shard_map/all_to_all | solution.py:805
  103.6 21.5 %all-to-all-start.2 = ((f32[256,2,128]{2,1,0:T(2,128)}), f32[256,2,128]{2,1,0:T(2,128)S(1)}, u32[]{:S(2)}, u32[]{:S(2)}) async-start(f32[256,2,128]{2,1,0:T(2,128)} %bitcast.36), calls=%async_computation.2 | async-start | bytes 524288 | tf_op jit(solution)/shard_map/all_to_all | solution.py:805
  109.9 15.2 %copy-start.2 = (bf16[256,512]{1,0:T(8,128)(2,1)S(1)}, bf16[256,512]{1,0:T(8,128)(2,1)}, u32[]{:S(2)}) copy-start(bf16[256,512]{1,0:T(8,128)(2,1)} %constant.82.clone.along_z_ref) | copy-start | bytes 786436
  109.9 15.1 %copy-start.5 = (bf16[256,128]{1,0:T(8,128)(2,1)S(1)}, bf16[256,128]{1,0:T(8,128)(2,1)}, u32[]{:S(2)}) copy-start(bf16[256,128]{1,0:T(8,128)(2,1)} %constant.81.clone.along_x_ref) | copy-start | bytes 196612
  111.0 20.2 %collective-permute-start.14 = (bf16[2304,128]{1,0:T(8,128)(2,1)}, bf16[2304,128]{1,0:T(8,128)(2,1)S(1)}, u32[]{:S(2)}, u32[]{:S(2)}) collective-permute-start(bf16[2304,128]{1,0:T(8,128)(2,1)} %bitcast.48), channel_id=1, source_target_pairs={{0,64},{64,128},{128,192},{192,0},{1,65},{65,129},{129,193},{193,1... | collective-permute-start | bytes 1769480 | tf_op jit(solution)/shard_map/ppermute | solution.py:54
  112.6 18.6 %collective-permute-start.15 = (bf16[2304,128]{1,0:T(8,128)(2,1)}, bf16[2304,128]{1,0:T(8,128)(2,1)S(1)}, u32[]{:S(2)}, u32[]{:S(2)}) collective-permute-start(bf16[2304,128]{1,0:T(8,128)(2,1)} %bitcast.50), channel_id=1, source_target_pairs={{0,192},{64,0},{128,64},{192,128},{1,193},{65,1},{129,65},{193,129... | collective-permute-start | bytes 1769480 | tf_op jit(solution)/shard_map/ppermute | solution.py:54
  126.1 14.2 %all-to-all-start.3 = ((bf16[16,64,128]{2,1,0:T(8,128)(2,1)}), bf16[16,64,128]{2,1,0:T(8,128)(2,1)S(1)}, u32[]{:S(2)}, u32[]{:S(2)}) async-start(bf16[16,64,128]{2,1,0:T(8,128)(2,1)} %bitcast.38), calls=%async_computation.3 | async-start | bytes 524288 | tf_op jit(solution)/shard_map/all_to_all | solution.py:805
  144.9 3.1 %collective-permute-start.17 = (f32[24,128]{1,0:T(8,128)S(1)}, f32[24,128]{1,0:T(8,128)S(1)}, u32[]{:S(2)}, u32[]{:S(2)}) collective-permute-start(f32[24,128]{1,0:T(8,128)S(1)} %get-tuple-element.30.potential_ref), channel_id=1, source_target_pairs={{0,60},{4,0},{8,4},{12,8},{16,12},{20,16},{24,20},{28,24},{32,28},... | collective-permute-start | bytes 36872 | tf_op jit(solution)/shard_map/ppermute | solution.py:54
  145.0 9.2 %collective-permute-start.16 = (f32[24,128]{1,0:T(8,128)S(1)}, f32[24,128]{1,0:T(8,128)S(1)}, u32[]{:S(2)}, u32[]{:S(2)}) collective-permute-start(f32[24,128]{1,0:T(8,128)S(1)} %get-tuple-element.30.potential_ref), channel_id=1, source_target_pairs={{0,4},{4,8},{8,12},{12,16},{16,20},{20,24},{24,28},{28,32},{32,36}... | collective-permute-start | bytes 36872 | tf_op jit(solution)/shard_map/ppermute | solution.py:54
  145.5 8.7 %copy-start.6 = (bf16[128,128]{1,0:T(8,128)(2,1)S(1)}, bf16[128,128]{1,0:T(8,128)(2,1)}, u32[]{:S(2)}) copy-start(bf16[128,128]{1,0:T(8,128)(2,1)} %msg_ref.1) | copy-start | bytes 98308

commit v3 on v2

--- a/solution.py
+++ b/solution.py
@@ -39,7 +39,8 @@
 SMALL = pltpu.CompilerParams(vmem_limit_bytes=20 << 20)
 FIRST = pltpu.CompilerParams(vmem_limit_bytes=60 << 20)
 LARGE = pltpu.CompilerParams(vmem_limit_bytes=50 << 20)
-MIDDLE = pltpu.CompilerParams(vmem_limit_bytes=36 << 20)
+MIDDLE = pltpu.CompilerParams(vmem_limit_bytes=40 << 20)
+FIELD = pltpu.CompilerParams(vmem_limit_bytes=44 << 20)
 
 
 def cas(rows, columns, size):
@@ -52,14 +53,6 @@
     count = lax.axis_size(axis)
     pairs = [(i, (i + step) % count) for i in range(count)]
     return lax.ppermute(value.reshape(-1, 128), axis, pairs).reshape(value.shape)
-
-
-def late_halo(own):
-    last_x, last_z = own.shape[0] - 1, own.shape[1] - 1
-    left, right = moved(own[:, last_z:], "gz", 1), moved(own[:, :1], "gz", -1)
-    row = jnp.concatenate([left, own, right], axis=1)
-    rows = jnp.stack([moved(row, "gy", 1), row, moved(row, "gy", -1)])
-    return [rows, moved(rows[:, last_x:], "gx", 1), moved(rows[:, :1], "gx", -1)]
 
 
 def early_halo(own):
@@ -593,8 +586,7 @@
         (rows_ref, slope_ref.at[:, pl.ds(1, 2)]),
         (before_ref, slope_ref.at[:, pl.ds(0, 1)]),
         (after_ref, slope_ref.at[:, pl.ds(3, 1)]),
-        (stored_ref.at[pl.ds(0, 3)], weight_ref.at[pl.ds(0, 3)]),
-        (stored_ref.at[pl.ds(3, 3)], weight_ref.at[pl.ds(3, 3)]),
+        (stored_ref.at[:, :, :, pl.ds(512, 256)], weight_ref),
     ]
     copies = [
         pltpu.make_async_copy(source, target, sems.at[i])
@@ -633,14 +625,14 @@
         functools.partial(interpolate_kernel, field_scale),
         in_specs=[VM] * 2 + [ANY] * 4,
         out_specs=[VM] * 4,
-        compiler_params=MIDDLE,
+        compiler_params=FIELD,
         out_shape=[
             jax.ShapeDtypeStruct((24, 128), f32),
             jax.ShapeDtypeStruct((8, 128), f32),
-            jax.ShapeDtypeStruct((6, 8, 128, 768), bf16),
+            jax.ShapeDtypeStruct((6, 8, 128, 256), bf16),
             jax.ShapeDtypeStruct((3, 4, 6, 128, 128), bf16),
         ],
-        scratch_shapes=[pltpu.SemaphoreType.DMA((5,))],
+        scratch_shapes=[pltpu.SemaphoreType.DMA((4,))],
         cost_estimate=pl.CostEstimate(
             flops=24 * 2 * 256 * 128 * 128, bytes_accessed=400000, transcendentals=0
         ),
@@ -657,8 +649,16 @@
 
 
 def beside_kernel(
-    weight_ref, slope_ref, potential_ref, total_ref, own_out, near_ref
+    stored_ref, weight_ref, slope_ref, potential_ref, rest_ref, total_ref, own_out, near_ref, sems
 ):
+    copies = [
+        pltpu.make_async_copy(
+            stored_ref.at[pl.ds(i, 3), :, :, pl.ds(0, 512)], rest_ref.at[pl.ds(i, 3)], sems.at[i // 3]
+        )
+        for i in (0, 3)
+    ]
+    for copy in copies:
+        copy.start()
     columns = jnp.transpose(potential_ref[...])
     for x in range(4):
         for z in range(6):
@@ -670,33 +670,37 @@
         x, a = combination_of(t)
         for pair, (start, stop, first, width) in enumerate(SPANS):
             part = dot(
-                weight_ref[t, start:stop, :, 512:768].reshape(width * 128, 256),
+                weight_ref[t, start:stop].reshape(width * 128, 256),
                 near_ref[x, 2 * pair : 2 * pair + 2].reshape(256, 128),
             )
             total_ref[a, first : first + width] += part.reshape(width, 128, 128)
         return carry
 
     lax.fori_loop(0, 6, combination, 0)
-
-
-def beside(weights, slopes, potential):
+    for copy in copies:
+        copy.wait()
+
+
+def beside(stored, weights, slopes, potential):
     return pl.pallas_call(
         beside_kernel,
-        in_specs=[VM] * 3,
-        out_specs=[VM] * 2,
+        in_specs=[ANY] + [VM] * 3,
+        out_specs=[VM] * 3,
         out_shape=[
+            jax.ShapeDtypeStruct((6, 8, 128, 512), bf16),
             jax.ShapeDtypeStruct((2, 4, 128, 128), f32),
             jax.ShapeDtypeStruct((2, 4, 128, 128), bf16),
         ],
         scratch_shapes=[
             pltpu.VMEM((4, 6, 128, 128), bf16),
+            pltpu.SemaphoreType.DMA((2,)),
         ],
         cost_estimate=pl.CostEstimate(
             flops=3000000000, bytes_accessed=12000000, transcendentals=0
         ),
-        compiler_params=SMALL,
+        compiler_params=MIDDLE,
         name="beside",
-    )(weights, slopes, potential)
+    )(stored, weights, slopes, potential)
 
 
 def backward_kernel(
@@ -726,7 +730,7 @@
                 ],
                 axis=0,
             )
-            part = dot(weight_ref[t, start:stop, :, 0:512].reshape(width * 128, 512), near)
+            part = dot(weight_ref[t, start:stop].reshape(width * 128, 512), near)
             total_ref[a, first : first + width] += part.reshape(width, 128, 128)
         return carry
 
@@ -829,17 +833,26 @@
     weights, preact, mesh, row_place = message_layer(
         own, ends, outer, corners, part, read, weights
     )
-    mesh = swapped(mesh, plane).reshape(4, 4, PC, 128)
-    slope_near = late_halo(slope_of(preact, read))
-    lines = swapped(forward_xz(mesh, along_z, along_x), everyone)
+    slope = slope_of(preact, read)
+    left, right = moved(slope[:, cells_z - 1 :], "gz", 1), moved(slope[:, :1], "gz", -1)
+    mesh, left, right = lax.optimization_barrier((swapped(mesh, plane), left, right))
+    row = jnp.concatenate([left, slope, right], axis=1)
+    waves = forward_xz(mesh.reshape(4, 4, PC, 128), along_z, along_x)
+    waves, row = lax.optimization_barrier((waves, row))
+    below = [moved(part, "gy", 1) for part in (row[:1], row[1:])]
+    above = [moved(part, "gy", -1) for part in (row[:1], row[1:])]
+    lines, *parts = lax.optimization_barrier((swapped(waves, everyone), *below, *above))
+    below, above = jnp.concatenate(parts[:2]), jnp.concatenate(parts[2:])
+    rows = jnp.stack([below, row, above])
+    before, after = moved(rows[:, cells_x - 1 :], "gx", 1), moved(rows[:, :1], "gx", -1)
     lines = swapped(filter_y(lines, into_y, influence), everyone)
     field, energy = inverse_xz(lines, back_x, back_z, coupling / (2.0 * volume * natoms))
     field = swapped(field.reshape(16, 64, 128), plane)
-    potential, atom_potential, weights, slopes = interpolate(
-        field, row_place.reshape(24, 8, slots), weights, slope_near, coupling / volume
+    potential, atom_potential, own_weights, slopes = interpolate(
+        field, row_place.reshape(24, 8, slots), weights, (rows, before, after), coupling / volume
     )
     below, above = moved(potential, "gy", 1), moved(potential, "gy", -1)
-    total, cotangent = beside(weights, slopes, potential)
+    weights, total, cotangent = beside(weights, own_weights, slopes, potential)
     grad = backward(weights, slopes, total, cotangent, below, above, msg_weight, self_weight)
     return (
         grad.reshape(features.shape),

time: 160 us -> 173 us (1.081)
  starting transfers between devices: 64.9 us -> 88.5 us
  waiting for transfers between devices: 55.2 us -> 45.1 us
    ppermute x18 -> x20, starting transfers between devices: 30 us -> 49.6 us  [moved(): lax.ppermute(value.reshape(-1, 128), axis, pairs).reshape(value.shape)]
    all_to_all x4, waiting for transfers between devices: 37.4 us -> 19.9 us  [swapped(): return lax.all_to_all(value, axis, split_axis=0, concat_axis=0, tiled=True)]
    ppermute x18 -> x20, waiting for transfers between devices: 17.8 us -> 25.2 us  [moved(): lax.ppermute(value.reshape(-1, 128), axis, pairs).reshape(value.shape)]
    all_to_all x4, starting transfers between devices: 34.9 us -> 38.9 us  [swapped(): return lax.all_to_all(value, axis, split_axis=0, concat_axis=0, tiled=True)]
    pallas_call x1, Pallas kernels: 4.57 us -> 2.67 us  [interpolate(): pl.pallas_call(functools.partial(interpolate_kernel, field_scale), in_spe...]
  transfers between devices with their start and end apart: 22 -> 24, of which waited for: 8 -> 9; matrix products, arithmetic and copies ran while one was open for 3% -> 2% of each run, Pallas kernels for 11% -> 10%
where the time goes in v3:
time: 173 us; the launch traced here: 172 us
  starting transfers between devices  88.5 us (51%)
  waiting for transfers between devices  45.1 us (26%)
  Pallas kernels  33.2 us (19%)
  local copies, waits for them, and re-layouts  3.68 us (2%)
    ppermute x20, starting transfers between devices, moved(): lax.ppermute(value.reshape(-1, 128), axis, pairs).reshape(value.shape)  49.6 us
    all_to_all x4, starting transfers between devices, swapped(): return lax.all_to_all(value, axis, split_axis=0, concat_axis=0, tiled=True)  38.9 us
    ppermute x20, waiting for transfers between devices, moved(): lax.ppermute(value.reshape(-1, 128), axis, pairs).reshape(value.shape)  25.2 us
    all_to_all x4, waiting for transfers between devices, swapped(): return lax.all_to_all(value, axis, split_axis=0, concat_axis=0, tiled=True)  19.9 us
    pallas_call x1, Pallas kernels, ends_pairs(): pl.pallas_call(ends_kernel, in_specs=[VM] * 10 + [ANY], out_specs=[ANY, V...  6.79 us
    pallas_call x1, Pallas kernels, inside_pairs(): pl.pallas_call(inside_kernel, in_specs=[VM] * 5, out_specs=[ANY, VM], out...  5.71 us
    pallas_call x1, Pallas kernels, backward(): pl.pallas_call(backward_kernel, in_specs=[VM] * 8, out_specs=VM, out_shap...  5.12 us
    pallas_call x1, Pallas kernels, message_layer(): pl.pallas_call(message_kernel, in_specs=[VM] * 11 + [ANY], out_specs=[ANY...  4.21 us
  transfers between devices with their start and end apart: 24, of which 9 were waited for; matrix products, arithmetic and copies ran while one was open for 2% of the time, Pallas kernels for 10%

profile of v3, /device:TPU:32, one launch (start us, length us, event | category | flops | bytes accessed | tf_op | source)
XLA Modules:
  0.0 172.0 jit_solution(14241971913568925211)
XLA Ops:
  0.6 1.9 %project.1 = bf16[8,144,128]{2,1,0:T(8,128)(2,1)} custom-call(bf16[8,128,128]{2,1,0:T(8,128)(2,1)} %bitcast.99, bf16[128,128]{1,0:T(8,128)(2,1)} %msg_ref.1, s32[2,1,3,4,128]{4,3,2,1,0:T(4,128)} %bitcast.142, f32[2,1,3,4,128]{4,3,2,1,0:T(4,128)} %bitcast.143), custom_call_target="tpu_custom_call" | custom-call | tf_op jit(solution)/shard_map/project/pallas_call | solution.py:91
  2.5 0.1 collective-permute-start
  2.6 8.0 %collective-permute-start.1 = (bf16[1152,128]{1,0:T(8,128)(2,1)}, bf16[1152,128]{1,0:T(8,128)(2,1)S(1)}, u32[]{:S(2)}, u32[]{:S(2)}) collective-permute-start(bf16[1152,128]{1,0:T(8,128)(2,1)} %bitcast.82), channel_id=1, source_target_pairs={{0,60},{4,0},{8,4},{12,8},{16,12},{20,16},{24,20},{28,24},{32,28},... | collective-permute-start | bytes 884744 | tf_op jit(solution)/shard_map/ppermute | solution.py:55
  10.6 1.0 fusion.10
  11.6 1.7 collective-permute-start.4
  13.3 1.7 collective-permute-start.5
  15.0 0.9 slice_bitcast_fusion.1
  15.9 2.6 %collective-permute-done = bf16[1152,128]{1,0:T(8,128)(2,1)S(1)} collective-permute-done((bf16[1152,128]{1,0:T(8,128)(2,1)}, bf16[1152,128]{1,0:T(8,128)(2,1)S(1)}, u32[]{:S(2)}, u32[]{:S(2)}) %collective-permute-start) | collective-permute-done | bytes 294944 | tf_op jit(solution)/shard_map/ppermute | solution.py:55
  18.5 2.5 %collective-permute-done.1 = bf16[1152,128]{1,0:T(8,128)(2,1)S(1)} collective-permute-done((bf16[1152,128]{1,0:T(8,128)(2,1)}, bf16[1152,128]{1,0:T(8,128)(2,1)S(1)}, u32[]{:S(2)}, u32[]{:S(2)}) %collective-permute-start.1) | collective-permute-done | bytes 294944 | tf_op jit(solution)/shard_map/ppermute | solution.py:55
  21.0 2.5 %collective-permute-start.3 = (bf16[864,128]{1,0:T(8,128)(2,1)S(1)}, bf16[864,128]{1,0:T(8,128)(2,1)S(1)}, u32[]{:S(2)}, u32[]{:S(2)}) collective-permute-start(bf16[864,128]{1,0:T(8,128)(2,1)S(1)} %bitcast.127), channel_id=1, source_target_pairs={{0,3},{1,0},{2,1},{3,2},{4,7},{5,4},{6,5},{7,6},{8,11},{9,8},{10,9... | collective-permute-start | bytes 663560 | tf_op jit(solution)/shard_map/ppermute | solution.py:55
  23.5 0.1 collective-permute-start.2
  23.7 5.7 %inside_pairs.1 = (bf16[6,8,128,768]{3,2,1,0:T(8,128)(2,1)}, f32[2,4,128,128]{3,2,1,0:T(8,128)S(1)}) custom-call(bf16[2,4,144,128]{3,2,1,0:T(8,128)(2,1)S(1)} %bitcast.84, bf16[2,4,144,128]{3,2,1,0:T(8,128)(2,1)S(1)} %bitcast.89, bf16[2,4,144,128]{3,2,1,0:T(8,128)(2,1)S(1)} %bitcast.93, bf16[8,128,128]{2,1,0:T(8,128)(2,1)S(1)} %bitcast.100, ...), custom_call_target="tpu_custom_call" | custom-call | flops 5000000000 | bytes 9000000 | tf_op jit(solution)/shard_map/inside_pairs/pallas_call | solution.py:217
  29.4 0.1 pad_maximum_fusion.2
  29.4 1.6 collective-permute-start.6
  31.1 1.7 collective-permute-start.7
  32.8 1.1 collective-permute-done.2
  34.0 1.7 collective-permute-start.8
  35.7 1.9 %collective-permute-start.9 = (bf16[864,128]{1,0:T(8,128)(2,1)S(1)}, bf16[864,128]{1,0:T(8,128)(2,1)S(1)}, u32[]{:S(2)}, u32[]{:S(2)}) collective-permute-start(bf16[864,128]{1,0:T(8,128)(2,1)S(1)} %bitcast.125), channel_id=1, source_target_pairs={{0,192},{64,0},{128,64},{192,128},{1,193},{65,1},{129,65},{193,129... | collective-permute-start | bytes 663560 | tf_op jit(solution)/shard_map/ppermute | solution.py:55
  37.6 2.3 %collective-permute-done.6 = bf16[1152,128]{1,0:T(8,128)(2,1)S(1)} collective-permute-done((bf16[1152,128]{1,0:T(8,128)(2,1)S(1)}, bf16[1152,128]{1,0:T(8,128)(2,1)S(1)}, u32[]{:S(2)}, u32[]{:S(2)}) %collective-permute-start.6) | collective-permute-done | bytes 294944 | tf_op jit(solution)/shard_map/ppermute | solution.py:55
  39.9 6.8 %ends_pairs.1 = (bf16[6,8,128,768]{3,2,1,0:T(8,128)(2,1)}, f32[2,4,128,128]{3,2,1,0:T(8,128)S(1)}) custom-call(bf16[2,4,144,128]{3,2,1,0:T(8,128)(2,1)S(1)} %bitcast.85, bf16[2,4,144,128]{3,2,1,0:T(8,128)(2,1)S(1)} %bitcast.91, bf16[2,4,144,128]{3,2,1,0:T(8,128)(2,1)S(1)} %bitcast.95, ...), custom_call_target="tpu_custom_call", output_to_operand_aliasing={{0}: (10, {})} | custom-call | flops 8999999488 | bytes 9000000 | tf_op jit(solution)/shard_map/ends_pairs/pallas_call | solution.py:313
  46.7 0.0 collective-permute-done.8
  46.7 0.0 collective-permute-done.9
  46.7 4.2 %message.1 = (bf16[6,8,128,768]{3,2,1,0:T(8,128)(2,1)}, f32[2,4,128,128]{3,2,1,0:T(8,128)S(1)}, bf16[16,16,128]{2,1,0:T(8,128)(2,1)}, f32[4,6,8,128]{3,2,1,0:T(8,128)S(1)}) custom-call(bf16[2,4,144,128]{3,2,1,0:T(8,128)(2,1)S(1)} %bitcast.86, bf16[3,2,1,144,128]{4,3,2,1,0:T(8,128)(2,1)S(1)} %bitcast.107, ...), custom_call_target="tpu_custom_call", output_to_operand_aliasing={{0}: (11, {})} | custom-call | flops 5000000000 | bytes 6000000 | tf_op jit(solution)/shard_map/message/pallas_call | solution.py:436
  51.0 0.0 copy-start.4
  51.0 0.0 copy-start.7
  51.0 0.2 slope.1
  51.2 8.7 %all-to-all-start = ((bf16[16,16,128]{2,1,0:T(8,128)(2,1)}), bf16[16,16,128]{2,1,0:T(8,128)(2,1)S(1)}, u32[]{:S(2)}, u32[]{:S(2)}) async-start(bf16[16,16,128]{2,1,0:T(8,128)(2,1)} %get-tuple-element.35), calls=%async_computation | async-start | bytes 131072 | tf_op jit(solution)/shard_map/all_to_all | solution.py:809
  60.0 0.0 copy-start.3
  60.0 1.5 collective-permute-start.10
  61.5 0.6 collective-permute-start.11
  62.1 2.8 %collective-permute-done.10 = bf16[256,128]{1,0:T(8,128)(2,1)S(1)} collective-permute-done((bf16[256,128]{1,0:T(8,128)(2,1)S(1)}, bf16[256,128]{1,0:T(8,128)(2,1)S(1)}, u32[]{:S(2)}, u32[]{:S(2)}) %collective-permute-start.10) | collective-permute-done | bytes 65568 | tf_op jit(solution)/shard_map/ppermute | solution.py:55
  64.9 2.9 %collective-permute-done.11 = bf16[256,128]{1,0:T(8,128)(2,1)S(1)} collective-permute-done((bf16[256,128]{1,0:T(8,128)(2,1)S(1)}, bf16[256,128]{1,0:T(8,128)(2,1)S(1)}, u32[]{:S(2)}, u32[]{:S(2)}) %collective-permute-start.11) | collective-permute-done | bytes 65568 | tf_op jit(solution)/shard_map/ppermute | solution.py:55
  67.8 0.0 all-to-all-done
  67.9 1.0 forward_xz.1
  68.9 15.3 %all-to-all-start.1 = ((f32[256,1,128]{2,1,0:T(1,128)}), f32[256,1,128]{2,1,0:T(1,128)S(1)}, u32[]{:S(2)}, u32[]{:S(2)}) async-start(f32[256,1,128]{2,1,0:T(1,128)} %bitcast.38), calls=%async_computation.1 | async-start | bytes 262144 | tf_op jit(solution)/shard_map/all_to_all | solution.py:809
  84.3 0.2 collective-permute-start.12
  84.5 7.6 %collective-permute-start.14 = (bf16[768,128]{1,0:T(8,128)(2,1)S(1)}, bf16[768,128]{1,0:T(8,128)(2,1)S(1)}, u32[]{:S(2)}, u32[]{:S(2)}) collective-permute-start(bf16[768,128]{1,0:T(8,128)(2,1)S(1)} %bitcast.135), channel_id=1, source_target_pairs={{0,60},{4,0},{8,4},{12,8},{16,12},{20,16},{24,20},{28,24},{32,28},... | collective-permute-start | bytes 589832 | tf_op jit(solution)/shard_map/ppermute | solution.py:55
  92.1 7.8 %collective-permute-start.15 = (bf16[768,128]{1,0:T(8,128)(2,1)S(1)}, bf16[768,128]{1,0:T(8,128)(2,1)S(1)}, u32[]{:S(2)}, u32[]{:S(2)}) collective-permute-start(bf16[768,128]{1,0:T(8,128)(2,1)S(1)} %bitcast.133), channel_id=1, source_target_pairs={{0,60},{4,0},{8,4},{12,8},{16,12},{20,16},{24,20},{28,24},{32,28},... | collective-permute-start | bytes 589832 | tf_op jit(solution)/shard_map/ppermute | solution.py:55
  99.9 0.1 fusion.1.influence_ref
  100.0 0.0 collective-permute-done.12
  100.0 10.9 %collective-permute-done.13 = bf16[768,128]{1,0:T(8,128)(2,1)S(1)} collective-permute-done((bf16[768,128]{1,0:T(8,128)(2,1)S(1)}, bf16[768,128]{1,0:T(8,128)(2,1)S(1)}, u32[]{:S(2)}, u32[]{:S(2)}) %collective-permute-start.13) | collective-permute-done | bytes 196640 | tf_op jit(solution)/shard_map/ppermute | solution.py:55
  110.9 0.0 all-to-all-done.1
  110.9 1.1 filter_y.1
  112.0 10.5 %all-to-all-start.2 = ((f32[256,2,128]{2,1,0:T(2,128)}), f32[256,2,128]{2,1,0:T(2,128)S(1)}, u32[]{:S(2)}, u32[]{:S(2)}) async-start(f32[256,2,128]{2,1,0:T(2,128)} %bitcast.46), calls=%async_computation.2 | async-start | bytes 524288 | tf_op jit(solution)/shard_map/all_to_all | solution.py:809
  122.5 0.1 maximum_bitcast_fusion
  122.6 0.1 pad_maximum_fusion.rows_ref
  122.8 0.0 copy-start.2
  122.8 0.0 copy-start.5
  122.8 1.1 fusion.8
  123.9 1.5 collective-permute-start.16
  125.4 1.7 collective-permute-start.17
  127.1 10.7 %all-to-all-done.2 = f32[256,2,128]{2,1,0:T(2,128)S(1)} async-done(((f32[256,2,128]{2,1,0:T(2,128)}), f32[256,2,128]{2,1,0:T(2,128)S(1)}, u32[]{:S(2)}, u32[]{:S(2)}) %all-to-all-start.2) | async-done | bytes 262176 | tf_op jit(solution)/shard_map/all_to_all | solution.py:809
  137.9 1.0 inverse_xz.1
  138.9 4.3 %all-to-all-start.3 = ((bf16[16,64,128]{2,1,0:T(8,128)(2,1)}), bf16[16,64,128]{2,1,0:T(8,128)(2,1)S(1)}, u32[]{:S(2)}, u32[]{:S(2)}) async-start(bf16[16,64,128]{2,1,0:T(8,128)(2,1)} %bitcast.48), calls=%async_computation.3 | async-start | bytes 524288 | tf_op jit(solution)/shard_map/all_to_all | solution.py:809
  143.3 0.5 slice.87
  143.8 0.0 collective-permute-done.16
  143.8 0.0 collective-permute-done.17
  143.8 9.1 %all-to-all-done.3.field_ref = bf16[16,64,128]{2,1,0:T(8,128)(2,1)S(1)} async-done(((bf16[16,64,128]{2,1,0:T(8,128)(2,1)}), bf16[16,64,128]{2,1,0:T(8,128)(2,1)S(1)}, u32[]{:S(2)}, u32[]{:S(2)}) %all-to-all-start.3) | async-done | bytes 262176 | tf_op jit(solution)/shard_map/all_to_all | solution.py:809
  152.9 2.7 %interpolate.1 = (f32[24,128]{1,0:T(8,128)S(1)}, f32[8,128]{1,0:T(8,128)}, bf16[6,8,128,256]{3,2,1,0:T(8,128)(2,1)S(1)}, bf16[3,4,6,128,128]{4,3,2,1,0:T(8,128)(2,1)S(1)}) custom-call(bf16[16,64,128]{2,1,0:T(8,128)(2,1)S(1)} %all-to-all-done.3.field_ref, f32[24,8,128]{2,1,0:T(8,128)S(1)} %bitcast.108, bf16[6,8,128,768]{3,2,1,0:T(8,128)(2,1)} %get-tuple-element.34.stored_ref, ...), custom_call_target="tpu_custom_call" | custom-call | flops 201326592 | bytes 400000 | tf_op jit(solution)/shard_map/interpolate/pallas_call | solution.py:624
  155.6 0.1 collective-permute-start.18
  155.7 7.7 %collective-permute-start.19 = (f32[24,128]{1,0:T(8,128)S(1)}, f32[24,128]{1,0:T(8,128)S(1)}, u32[]{:S(2)}, u32[]{:S(2)}) collective-permute-start(f32[24,128]{1,0:T(8,128)S(1)} %get-tuple-element.51.potential_ref), channel_id=1, source_target_pairs={{0,60},{4,0},{8,4},{12,8},{16,12},{20,16},{24,20},{28,24},{32,28},... | collective-permute-start | bytes 36872 | tf_op jit(solution)/shard_map/ppermute | solution.py:55
  163.4 3.4 %beside.1 = (bf16[6,8,128,512]{3,2,1,0:T(8,128)(2,1)S(1)}, f32[2,4,128,128]{3,2,1,0:T(8,128)S(1)}, bf16[2,4,128,128]{3,2,1,0:T(8,128)(2,1)S(1)}) custom-call(bf16[6,8,128,768]{3,2,1,0:T(8,128)(2,1)} %get-tuple-element.34.stored_ref, bf16[6,8,128,256]{3,2,1,0:T(8,128)(2,1)S(1)} %get-tuple-element.49.weight_ref, ...), custom_call_target="tpu_custom_call" | custom-call | flops 3000000000 | bytes 12000000 | tf_op jit(solution)/shard_map/beside/pallas_call | solution.py:685
  166.9 0.0 collective-permute-done.19.above_ref
  166.9 5.1 %backward.1 = f32[2,4,128,128]{3,2,1,0:T(8,128)} custom-call(bf16[6,8,128,512]{3,2,1,0:T(8,128)(2,1)S(1)} %get-tuple-element.52.weight_ref, bf16[3,4,6,128,128]{4,3,2,1,0:T(8,128)(2,1)S(1)} %get-tuple-element.50.slope_ref, f32[2,4,128,128]{3,2,1,0:T(8,128)S(1)} %get-tuple-element.53.part_ref, bf16[2,4,128,128]{3,2,1,0:T(8,128)(2,1)S(1)} %get-tuple-element.54.own_ref, ...), custom_call_target="tpu_custom_call" | custom-call | flops 4000000000 | bytes 12000000 | tf_op jit(solution)/shard_map/backward/pallas_call | solution.py:749
  (36 shorter events, 0.3 us)
Async XLA Ops:
  2.5 21.1 %copy-start = (bf16[8,144,128]{2,1,0:T(8,128)(2,1)S(1)}, bf16[8,144,128]{2,1,0:T(8,128)(2,1)}, u32[]{:S(2)}) copy-start(bf16[8,144,128]{2,1,0:T(8,128)(2,1)} %project.1) | copy-start | bytes 884740
  2.5 21.1 %copy-start.1 = (bf16[2,1,4,128,128]{4,3,2,1,0:T(8,128)(2,1)S(1)}, bf16[2,1,4,128,128]{4,3,2,1,0:T(8,128)(2,1)}, u32[]{:S(2)}) copy-start(bf16[2,1,4,128,128]{4,3,2,1,0:T(8,128)(2,1)} %param.11) | copy-start | bytes 786436
  2.5 21.1 %copy-start.9 = (bf16[128,128]{1,0:T(8,128)(2,1)S(1)}, bf16[128,128]{1,0:T(8,128)(2,1)}, u32[]{:S(2)}) copy-start(bf16[128,128]{1,0:T(8,128)(2,1)} %self_ref.3) | copy-start | bytes 98308
  2.5 15.9 %collective-permute-start = (bf16[1152,128]{1,0:T(8,128)(2,1)}, bf16[1152,128]{1,0:T(8,128)(2,1)S(1)}, u32[]{:S(2)}, u32[]{:S(2)}) collective-permute-start(bf16[1152,128]{1,0:T(8,128)(2,1)} %bitcast.81), channel_id=1, source_target_pairs={{0,4},{4,8},{8,12},{12,16},{16,20},{20,24},{24,28},{28,32},{32,36}... | collective-permute-start | bytes 884744 | tf_op jit(solution)/shard_map/ppermute | solution.py:55
  2.6 18.3 %collective-permute-start.1 = (bf16[1152,128]{1,0:T(8,128)(2,1)}, bf16[1152,128]{1,0:T(8,128)(2,1)S(1)}, u32[]{:S(2)}, u32[]{:S(2)}) collective-permute-start(bf16[1152,128]{1,0:T(8,128)(2,1)} %bitcast.82), channel_id=1, source_target_pairs={{0,60},{4,0},{8,4},{12,8},{16,12},{20,16},{24,20},{28,24},{32,28},... | collective-permute-start | bytes 884744 | tf_op jit(solution)/shard_map/ppermute | solution.py:55
  11.6 24.0 %collective-permute-start.4 = (bf16[576,128]{1,0:T(8,128)(2,1)S(1)}, bf16[576,128]{1,0:T(8,128)(2,1)S(1)}, u32[]{:S(2)}, u32[]{:S(2)}) collective-permute-start(bf16[576,128]{1,0:T(8,128)(2,1)S(1)} %bitcast.137), channel_id=1, source_target_pairs={{0,64},{64,128},{128,192},{192,0},{1,65},{65,129},{129,193},{193,1... | collective-permute-start | bytes 442376 | tf_op jit(solution)/shard_map/ppermute | solution.py:55
  13.3 24.3 %collective-permute-start.5 = (bf16[576,128]{1,0:T(8,128)(2,1)S(1)}, bf16[576,128]{1,0:T(8,128)(2,1)S(1)}, u32[]{:S(2)}, u32[]{:S(2)}) collective-permute-start(bf16[576,128]{1,0:T(8,128)(2,1)S(1)} %bitcast.136), channel_id=1, source_target_pairs={{0,192},{64,0},{128,64},{192,128},{1,193},{65,1},{129,65},{193,129... | collective-permute-start | bytes 442376 | tf_op jit(solution)/shard_map/ppermute | solution.py:55
  21.0 10.1 %collective-permute-start.3 = (bf16[864,128]{1,0:T(8,128)(2,1)S(1)}, bf16[864,128]{1,0:T(8,128)(2,1)S(1)}, u32[]{:S(2)}, u32[]{:S(2)}) collective-permute-start(bf16[864,128]{1,0:T(8,128)(2,1)S(1)} %bitcast.127), channel_id=1, source_target_pairs={{0,3},{1,0},{2,1},{3,2},{4,7},{5,4},{6,5},{7,6},{8,11},{9,8},{10,9... | collective-permute-start | bytes 663560 | tf_op jit(solution)/shard_map/ppermute | solution.py:55
  23.5 10.4 %collective-permute-start.2 = (bf16[864,128]{1,0:T(8,128)(2,1)S(1)}, bf16[864,128]{1,0:T(8,128)(2,1)S(1)}, u32[]{:S(2)}, u32[]{:S(2)}) collective-permute-start(bf16[864,128]{1,0:T(8,128)(2,1)S(1)} %bitcast.126), channel_id=1, source_target_pairs={{0,1},{1,2},{2,3},{3,0},{4,5},{5,6},{6,7},{7,4},{8,9},{9,10},{10,1... | collective-permute-start | bytes 663560 | tf_op jit(solution)/shard_map/ppermute | solution.py:55
  29.4 10.5 %collective-permute-start.6 = (bf16[1152,128]{1,0:T(8,128)(2,1)S(1)}, bf16[1152,128]{1,0:T(8,128)(2,1)S(1)}, u32[]{:S(2)}, u32[]{:S(2)}) collective-permute-start(bf16[1152,128]{1,0:T(8,128)(2,1)S(1)} %bitcast.123), channel_id=1, source_target_pairs={{0,64},{64,128},{128,192},{192,0},{1,65},{65,129},{129,193},{193,1... | collective-permute-start | bytes 884744 | tf_op jit(solution)/shard_map/ppermute | solution.py:55
  31.1 8.8 %collective-permute-start.7 = (bf16[1152,128]{1,0:T(8,128)(2,1)S(1)}, bf16[1152,128]{1,0:T(8,128)(2,1)S(1)}, u32[]{:S(2)}, u32[]{:S(2)}) collective-permute-start(bf16[1152,128]{1,0:T(8,128)(2,1)S(1)} %bitcast.122), channel_id=1, source_target_pairs={{0,192},{64,0},{128,64},{192,128},{1,193},{65,1},{129,65},{193,129... | collective-permute-start | bytes 884744 | tf_op jit(solution)/shard_map/ppermute | solution.py:55
  34.0 12.7 %collective-permute-start.8 = (bf16[864,128]{1,0:T(8,128)(2,1)S(1)}, bf16[864,128]{1,0:T(8,128)(2,1)S(1)}, u32[]{:S(2)}, u32[]{:S(2)}) collective-permute-start(bf16[864,128]{1,0:T(8,128)(2,1)S(1)} %bitcast.124), channel_id=1, source_target_pairs={{0,64},{64,128},{128,192},{192,0},{1,65},{65,129},{129,193},{193,1... | collective-permute-start | bytes 663560 | tf_op jit(solution)/shard_map/ppermute | solution.py:55
  35.7 11.1 %collective-permute-start.9 = (bf16[864,128]{1,0:T(8,128)(2,1)S(1)}, bf16[864,128]{1,0:T(8,128)(2,1)S(1)}, u32[]{:S(2)}, u32[]{:S(2)}) collective-permute-start(bf16[864,128]{1,0:T(8,128)(2,1)S(1)} %bitcast.125), channel_id=1, source_target_pairs={{0,192},{64,0},{128,64},{192,128},{1,193},{65,1},{129,65},{193,129... | collective-permute-start | bytes 663560 | tf_op jit(solution)/shard_map/ppermute | solution.py:55
  39.9 6.8 %copy-start.8 = (bf16[128]{0:T(256)(128)(2,1)S(1)}, bf16[128]{0:T(256)(128)(2,1)}, u32[]{:S(2)}) copy-start(bf16[128]{0:T(256)(128)(2,1)} %param.14) | copy-start | bytes 772
  51.0 16.9 %copy-start.4 = (bf16[256,256]{1,0:T(8,128)(2,1)S(1)}, bf16[256,256]{1,0:T(8,128)(2,1)}, u32[]{:S(2)}) copy-start(bf16[256,256]{1,0:T(8,128)(2,1)} %constant.78.clone.along_z_ref) | copy-start | bytes 393220
  51.0 16.9 %copy-start.7 = (bf16[128,128]{1,0:T(8,128)(2,1)S(1)}, bf16[128,128]{1,0:T(8,128)(2,1)}, u32[]{:S(2)}) copy-start(bf16[128,128]{1,0:T(8,128)(2,1)} %constant.79.clone.along_x_ref) | copy-start | bytes 98308
  51.2 16.6 %all-to-all-start = ((bf16[16,16,128]{2,1,0:T(8,128)(2,1)}), bf16[16,16,128]{2,1,0:T(8,128)(2,1)S(1)}, u32[]{:S(2)}, u32[]{:S(2)}) async-start(bf16[16,16,128]{2,1,0:T(8,128)(2,1)} %get-tuple-element.35), calls=%async_computation | async-start | bytes 131072 | tf_op jit(solution)/shard_map/all_to_all | solution.py:809
  60.0 51.0 %copy-start.3 = (bf16[256,256]{1,0:T(8,128)(2,1)S(1)}, bf16[256,256]{1,0:T(8,128)(2,1)}, u32[]{:S(2)}) copy-start(bf16[256,256]{1,0:T(8,128)(2,1)} %constant.80.clone.into_ref) | copy-start | bytes 393220
  60.0 4.9 %collective-permute-start.10 = (bf16[256,128]{1,0:T(8,128)(2,1)S(1)}, bf16[256,128]{1,0:T(8,128)(2,1)S(1)}, u32[]{:S(2)}, u32[]{:S(2)}) collective-permute-start(bf16[256,128]{1,0:T(8,128)(2,1)S(1)} %bitcast.141), channel_id=1, source_target_pairs={{0,1},{1,2},{2,3},{3,0},{4,5},{5,6},{6,7},{7,4},{8,9},{9,10},{10,1... | collective-permute-start | bytes 196616 | tf_op jit(solution)/shard_map/ppermute | solution.py:55
  61.5 6.3 %collective-permute-start.11 = (bf16[256,128]{1,0:T(8,128)(2,1)S(1)}, bf16[256,128]{1,0:T(8,128)(2,1)S(1)}, u32[]{:S(2)}, u32[]{:S(2)}) collective-permute-start(bf16[256,128]{1,0:T(8,128)(2,1)S(1)} %bitcast.140), channel_id=1, source_target_pairs={{0,3},{1,0},{2,1},{3,2},{4,7},{5,4},{6,5},{7,6},{8,11},{9,8},{10,9... | collective-permute-start | bytes 196616 | tf_op jit(solution)/shard_map/ppermute | solution.py:55
  68.9 42.0 %all-to-all-start.1 = ((f32[256,1,128]{2,1,0:T(1,128)}), f32[256,1,128]{2,1,0:T(1,128)S(1)}, u32[]{:S(2)}, u32[]{:S(2)}) async-start(f32[256,1,128]{2,1,0:T(1,128)} %bitcast.38), calls=%async_computation.1 | async-start | bytes 262144 | tf_op jit(solution)/shard_map/all_to_all | solution.py:809
  84.3 15.7 %collective-permute-start.12 = (bf16[768,128]{1,0:T(8,128)(2,1)S(1)}, bf16[768,128]{1,0:T(8,128)(2,1)S(1)}, u32[]{:S(2)}, u32[]{:S(2)}) collective-permute-start(bf16[768,128]{1,0:T(8,128)(2,1)S(1)} %bitcast.134), channel_id=1, source_target_pairs={{0,4},{4,8},{8,12},{12,16},{16,20},{20,24},{24,28},{28,32},{32,36}... | collective-permute-start | bytes 589832 | tf_op jit(solution)/shard_map/ppermute | solution.py:55
  84.5 26.4 %collective-permute-start.14 = (bf16[768,128]{1,0:T(8,128)(2,1)S(1)}, bf16[768,128]{1,0:T(8,128)(2,1)S(1)}, u32[]{:S(2)}, u32[]{:S(2)}) collective-permute-start(bf16[768,128]{1,0:T(8,128)(2,1)S(1)} %bitcast.135), channel_id=1, source_target_pairs={{0,60},{4,0},{8,4},{12,8},{16,12},{20,16},{24,20},{28,24},{32,28},... | collective-permute-start | bytes 589832 | tf_op jit(solution)/shard_map/ppermute | solution.py:55
  92.1 18.8 %collective-permute-start.13 = (bf16[768,128]{1,0:T(8,128)(2,1)S(1)}, bf16[768,128]{1,0:T(8,128)(2,1)S(1)}, u32[]{:S(2)}, u32[]{:S(2)}) collective-permute-start(bf16[768,128]{1,0:T(8,128)(2,1)S(1)} %bitcast.132), channel_id=1, source_target_pairs={{0,4},{4,8},{8,12},{12,16},{16,20},{20,24},{24,28},{28,32},{32,36}... | collective-permute-start | bytes 589832 | tf_op jit(solution)/shard_map/ppermute | solution.py:55
  92.1 18.8 %collective-permute-start.15 = (bf16[768,128]{1,0:T(8,128)(2,1)S(1)}, bf16[768,128]{1,0:T(8,128)(2,1)S(1)}, u32[]{:S(2)}, u32[]{:S(2)}) collective-permute-start(bf16[768,128]{1,0:T(8,128)(2,1)S(1)} %bitcast.133), channel_id=1, source_target_pairs={{0,60},{4,0},{8,4},{12,8},{16,12},{20,16},{24,20},{28,24},{32,28},... | collective-permute-start | bytes 589832 | tf_op jit(solution)/shard_map/ppermute | solution.py:55
  112.0 25.8 %all-to-all-start.2 = ((f32[256,2,128]{2,1,0:T(2,128)}), f32[256,2,128]{2,1,0:T(2,128)S(1)}, u32[]{:S(2)}, u32[]{:S(2)}) async-start(f32[256,2,128]{2,1,0:T(2,128)} %bitcast.46), calls=%async_computation.2 | async-start | bytes 524288 | tf_op jit(solution)/shard_map/all_to_all | solution.py:809
  122.8 15.1 %copy-start.2 = (bf16[256,512]{1,0:T(8,128)(2,1)S(1)}, bf16[256,512]{1,0:T(8,128)(2,1)}, u32[]{:S(2)}) copy-start(bf16[256,512]{1,0:T(8,128)(2,1)} %constant.82.clone.along_z_ref) | copy-start | bytes 786436
  122.8 15.1 %copy-start.5 = (bf16[256,128]{1,0:T(8,128)(2,1)S(1)}, bf16[256,128]{1,0:T(8,128)(2,1)}, u32[]{:S(2)}) copy-start(bf16[256,128]{1,0:T(8,128)(2,1)} %constant.81.clone.along_x_ref) | copy-start | bytes 196612
  123.9 19.9 %collective-permute-start.16 = (bf16[2304,128]{1,0:T(8,128)(2,1)}, bf16[2304,128]{1,0:T(8,128)(2,1)S(1)}, u32[]{:S(2)}, u32[]{:S(2)}) collective-permute-start(bf16[2304,128]{1,0:T(8,128)(2,1)} %bitcast.53), channel_id=1, source_target_pairs={{0,64},{64,128},{128,192},{192,0},{1,65},{65,129},{129,193},{193,1... | collective-permute-start | bytes 1769480 | tf_op jit(solution)/shard_map/ppermute | solution.py:55
  125.4 18.3 %collective-permute-start.17 = (bf16[2304,128]{1,0:T(8,128)(2,1)}, bf16[2304,128]{1,0:T(8,128)(2,1)S(1)}, u32[]{:S(2)}, u32[]{:S(2)}) collective-permute-start(bf16[2304,128]{1,0:T(8,128)(2,1)} %bitcast.55), channel_id=1, source_target_pairs={{0,192},{64,0},{128,64},{192,128},{1,193},{65,1},{129,65},{193,129... | collective-permute-start | bytes 1769480 | tf_op jit(solution)/shard_map/ppermute | solution.py:55
  138.9 14.0 %all-to-all-start.3 = ((bf16[16,64,128]{2,1,0:T(8,128)(2,1)}), bf16[16,64,128]{2,1,0:T(8,128)(2,1)S(1)}, u32[]{:S(2)}, u32[]{:S(2)}) async-start(bf16[16,64,128]{2,1,0:T(8,128)(2,1)} %bitcast.48), calls=%async_computation.3 | async-start | bytes 524288 | tf_op jit(solution)/shard_map/all_to_all | solution.py:809
  155.6 11.3 %collective-permute-start.18 = (f32[24,128]{1,0:T(8,128)S(1)}, f32[24,128]{1,0:T(8,128)S(1)}, u32[]{:S(2)}, u32[]{:S(2)}) collective-permute-start(f32[24,128]{1,0:T(8,128)S(1)} %get-tuple-element.51.potential_ref), channel_id=1, source_target_pairs={{0,4},{4,8},{8,12},{12,16},{16,20},{20,24},{24,28},{28,32},{32,36}... | collective-permute-start | bytes 36872 | tf_op jit(solution)/shard_map/ppermute | solution.py:55
  155.7 11.2 %collective-permute-start.19 = (f32[24,128]{1,0:T(8,128)S(1)}, f32[24,128]{1,0:T(8,128)S(1)}, u32[]{:S(2)}, u32[]{:S(2)}) collective-permute-start(f32[24,128]{1,0:T(8,128)S(1)} %get-tuple-element.51.potential_ref), channel_id=1, source_target_pairs={{0,60},{4,0},{8,4},{12,8},{16,12},{20,16},{24,20},{28,24},{32,28},... | collective-permute-start | bytes 36872 | tf_op jit(solution)/shard_map/ppermute | solution.py:55
  163.4 3.4 %copy-start.6 = (bf16[128,128]{1,0:T(8,128)(2,1)S(1)}, bf16[128,128]{1,0:T(8,128)(2,1)}, u32[]{:S(2)}) copy-start(bf16[128,128]{1,0:T(8,128)(2,1)} %msg_ref.1) | copy-start | bytes 98308

commit v4 on v3

--- a/solution.py
+++ b/solution.py
@@ -53,6 +53,14 @@
     count = lax.axis_size(axis)
     pairs = [(i, (i + step) % count) for i in range(count)]
     return lax.ppermute(value.reshape(-1, 128), axis, pairs).reshape(value.shape)
+
+
+def late_halo(own):
+    last_x, last_z = own.shape[0] - 1, own.shape[1] - 1
+    left, right = moved(own[:, last_z:], "gz", 1), moved(own[:, :1], "gz", -1)
+    row = jnp.concatenate([left, own, right], axis=1)
+    rows = jnp.stack([moved(row, "gy", 1), row, moved(row, "gy", -1)])
+    return [rows, moved(rows[:, last_x:], "gx", 1), moved(rows[:, :1], "gx", -1)]
 
 
 def early_halo(own):
@@ -237,11 +245,9 @@
 
 def ends_kernel(
     own_ref, below_ref, above_ref, left_ref, right_ref,
-    before_own, after_own, before_side, after_side, part_ref, _,
-    weight_out, total_ref, weight_ref, centre_ref, position_ref, outer_ref, sems
+    part_ref, _, weight_out, total_ref, weight_ref, centre_ref, position_ref, sems
 ):
     refs = (below_ref, own_ref, above_ref)
-    outer = ((before_own, before_side), (after_own, after_side))
 
     def cell(dy, x, z):
         if z == 0:
@@ -250,10 +256,6 @@
             return right_ref.at[dy, x, 0]
         return refs[dy].at[x, z - 1]
 
-    def outer_cell(side, dy, z):
-        own, beside = outer[side]
-        return own.at[0, z - 1] if dy == 1 else beside.at[dy // 2, 0, z - 1]
-
     centres_of(own_ref, centre_ref)
 
     def positions(x, carry):
@@ -263,10 +265,6 @@
         return carry
 
     lax.fori_loop(0, 2, positions, 0)
-    for side in range(2):
-        for dy in range(3):
-            for z in (2, 3):
-                outer_ref[side, dy, z] = position_of(outer_cell(side, dy, z)[128:144, :])
     total_ref[...] = part_ref[...]
 
     def column(t, carry):
@@ -287,51 +285,32 @@
     for copy in copies:
         copy.start()
 
-    def outer_column(side, carry):
-        def store(block, lane, tile):
-            weight_ref[4 + side, block, :, lane : lane + 128] = tile
-
-        def near(dy, z):
-            return outer_ref[side, dy, z]
-
-        weigh(centre_ref, side, (2 * side - 1).astype(f32), near, store, INSIDE)
-        return carry
-
-    lax.fori_loop(0, 2, outer_column, 0)
-    last = columns_kernel(4, 2, weight_ref, weight_out, sems, 2, INSIDE_BLOCKS)
-    for copy in last:
-        copy.start()
-    for side in range(2):
-        add_near(
-            weight_ref, 4 + side, side, lambda dy, z: outer_cell(side, dy, z), total_ref, INSIDE
-        )
-    for copy in copies + last:
+    for copy in copies:
         copy.wait()
 
 
-def ends_pairs(own, sides, ends, outer, part, weights):
+def ends_pairs(own, sides, ends, part, weights):
     return pl.pallas_call(
         ends_kernel,
-        in_specs=[VM] * 10 + [ANY],
+        in_specs=[VM] * 6 + [ANY],
         out_specs=[ANY, VM],
-        input_output_aliases={10: 0},
+        input_output_aliases={6: 0},
         out_shape=[
             jax.ShapeDtypeStruct((6, 8, 128, 768), bf16),
             jax.ShapeDtypeStruct((2, 4, 128, 128), f32),
         ],
         scratch_shapes=[
-            pltpu.VMEM((6, 8, 128, 768), bf16),
+            pltpu.VMEM((4, 8, 128, 768), bf16),
             pltpu.VMEM((2, 4, 8, 128), f32),
             pltpu.VMEM((3, 2, 6, 8, 128), f32),
-            pltpu.VMEM((2, 3, 6, 8, 128), f32),
-            pltpu.SemaphoreType.DMA((3,)),
-        ],
-        cost_estimate=pl.CostEstimate(
-            flops=9000000000, bytes_accessed=9000000, transcendentals=0
+            pltpu.SemaphoreType.DMA((2,)),
+        ],
+        cost_estimate=pl.CostEstimate(
+            flops=6000000000, bytes_accessed=9000000, transcendentals=0
         ),
         compiler_params=LARGE,
         name="ends_pairs",
-    )(own, *sides, *ends, *outer, part, weights)
+    )(own, *sides, *ends, part, weights)
 
 
 def spline_row(place):
@@ -360,7 +339,7 @@
     centres_of(own_ref, centre_ref)
     for side in range(2):
         for dy in range(3):
-            for z in (0, 1, 4, 5):
+            for z in range(6):
                 position_ref[side, dy, z] = position_of(cell(side, dy, z)[128:144, :])
         for z in range(6):
             row_place_ref[3 * side, z] = place_of(cell(side, 1, z)[128:144, :])
@@ -381,23 +360,18 @@
         def near(dy, z):
             return position_ref[side, dy, z]
 
-        weigh(centre_ref, side, (2 * side - 1).astype(f32), near, store, ENDS)
+        weigh(centre_ref, side, (2 * side - 1).astype(f32), near, store, ENDS + INSIDE)
         return carry
 
     lax.fori_loop(0, 2, column, 0)
-    copies = [
-        pltpu.make_async_copy(
-            weight_ref.at[:, pl.ds(start, size)],
-            weight_out.at[pl.ds(4, 2), pl.ds(start, size)],
-            sems.at[i],
-        )
-        for i, (start, size) in enumerate(END_BLOCKS)
-    ]
+    copies = [pltpu.make_async_copy(weight_ref, weight_out.at[pl.ds(4, 2)], sems.at[0])]
     for copy in copies:
         copy.start()
     total_ref[...] = part_ref[...]
     for side in range(2):
-        add_near(weight_ref, side, side, lambda dy, z: cell(side, dy, z), total_ref, ENDS)
+        add_near(
+            weight_ref, side, side, lambda dy, z: cell(side, dy, z), total_ref, ENDS + INSIDE
+        )
 
     def finish(index, carry):
         preact = total_ref[index // 4, index % 4]
@@ -453,7 +427,7 @@
             pltpu.VMEM((16, 1024), f32),
             pltpu.VMEM((PC * PC, 1024), bf16),
             pltpu.VMEM((128, 1024), bf16),
-            pltpu.SemaphoreType.DMA((2,)),
+            pltpu.SemaphoreType.DMA((1,)),
         ],
         cost_estimate=pl.CostEstimate(
             flops=5000000000, bytes_accessed=6000000, transcendentals=8 * 16384
@@ -734,7 +708,7 @@
             total_ref[a, first : first + width] += part.reshape(width, 128, 128)
         return carry
 
-    lax.fori_loop(0, 6, combination, 0)
+    lax.fori_loop(0, 6, combination, 0, unroll=2)
 
     def finish(a, carry):
         back = total_ref[a].reshape(512, 128).astype(bf16)
@@ -825,7 +799,7 @@
     own = own.reshape(cells_x, cells_z, slots + 16, width)
     sides, ends, outer, corners = early_halo(own)
     weights, part = inside_pairs(own, sides, features_own, self_weight)
-    weights, part = ends_pairs(own, sides, ends, outer, part, weights)
+    weights, part = ends_pairs(own, sides, ends, part, weights)
     influence = influence_of(size_x, size_y, size_z)
     along_z, along_x, into_y, back_x, back_z = wave_tables(size_x, size_y, size_z)
 
@@ -833,23 +807,14 @@
     weights, preact, mesh, row_place = message_layer(
         own, ends, outer, corners, part, read, weights
     )
-    slope = slope_of(preact, read)
-    left, right = moved(slope[:, cells_z - 1 :], "gz", 1), moved(slope[:, :1], "gz", -1)
-    mesh, left, right = lax.optimization_barrier((swapped(mesh, plane), left, right))
-    row = jnp.concatenate([left, slope, right], axis=1)
-    waves = forward_xz(mesh.reshape(4, 4, PC, 128), along_z, along_x)
-    waves, row = lax.optimization_barrier((waves, row))
-    below = [moved(part, "gy", 1) for part in (row[:1], row[1:])]
-    above = [moved(part, "gy", -1) for part in (row[:1], row[1:])]
-    lines, *parts = lax.optimization_barrier((swapped(waves, everyone), *below, *above))
-    below, above = jnp.concatenate(parts[:2]), jnp.concatenate(parts[2:])
-    rows = jnp.stack([below, row, above])
-    before, after = moved(rows[:, cells_x - 1 :], "gx", 1), moved(rows[:, :1], "gx", -1)
+    mesh = swapped(mesh, plane).reshape(4, 4, PC, 128)
+    slope_near = late_halo(slope_of(preact, read))
+    lines = swapped(forward_xz(mesh, along_z, along_x), everyone)
     lines = swapped(filter_y(lines, into_y, influence), everyone)
     field, energy = inverse_xz(lines, back_x, back_z, coupling / (2.0 * volume * natoms))
     field = swapped(field.reshape(16, 64, 128), plane)
     potential, atom_potential, own_weights, slopes = interpolate(
-        field, row_place.reshape(24, 8, slots), weights, (rows, before, after), coupling / volume
+        field, row_place.reshape(24, 8, slots), weights, slope_near, coupling / volume
     )
     below, above = moved(potential, "gy", 1), moved(potential, "gy", -1)
     weights, total, cotangent = beside(weights, own_weights, slopes, potential)

time: 173 us -> 159 us (0.919)
  starting transfers between devices: 88.5 us -> 80 us
  waiting for transfers between devices: 45.1 us -> 40.1 us
    ppermute x20 -> x18, waiting for transfers between devices: 25.2 us -> 7.62 us  [moved(): lax.ppermute(value.reshape(-1, 128), axis, pairs).reshape(value.shape)]
    all_to_all x4, waiting for transfers between devices: 19.9 us -> 32.5 us  [swapped(): return lax.all_to_all(value, axis, split_axis=0, concat_axis=0, tiled=True)]
    ppermute x20 -> x18, starting transfers between devices: 49.6 us -> 42.9 us  [moved(): lax.ppermute(value.reshape(-1, 128), axis, pairs).reshape(value.shape)]
    all_to_all x4, starting transfers between devices: 38.9 us -> 37.1 us  [swapped(): return lax.all_to_all(value, axis, split_axis=0, concat_axis=0, tiled=True)]
  transfers between devices with their start and end apart: 24 -> 22, of which waited for: 9 -> 7; matrix products, arithmetic and copies ran while one was open for 2% -> 3% of each run, Pallas kernels for 10% -> 11%
where the time goes in v4:
time: 159 us; the launch traced here: 158 us
  starting transfers between devices  80 us (50%)
  waiting for transfers between devices  40.1 us (25%)
  Pallas kernels  33.1 us (21%)
  local copies, waits for them, and re-layouts  3.65 us (2%)
    ppermute x18, starting transfers between devices, moved(): lax.ppermute(value.reshape(-1, 128), axis, pairs).reshape(value.shape)  42.9 us
    all_to_all x4, starting transfers between devices, swapped(): return lax.all_to_all(value, axis, split_axis=0, concat_axis=0, tiled=True)  37.1 us
    all_to_all x4, waiting for transfers between devices, swapped(): return lax.all_to_all(value, axis, split_axis=0, concat_axis=0, tiled=True)  32.5 us
    ppermute x18, waiting for transfers between devices, moved(): lax.ppermute(value.reshape(-1, 128), axis, pairs).reshape(value.shape)  7.62 us
    pallas_call x1, Pallas kernels, message_layer(): pl.pallas_call(message_kernel, in_specs=[VM] * 11 + [ANY], out_specs=[ANY...  5.74 us
    pallas_call x1, Pallas kernels, inside_pairs(): pl.pallas_call(inside_kernel, in_specs=[VM] * 5, out_specs=[ANY, VM], out...  5.71 us
    pallas_call x1, Pallas kernels, ends_pairs(): pl.pallas_call(ends_kernel, in_specs=[VM] * 6 + [ANY], out_specs=[ANY, VM...  5.57 us
    pallas_call x1, Pallas kernels, backward(): pl.pallas_call(backward_kernel, in_specs=[VM] * 8, out_specs=VM, out_shap...  4.71 us
  transfers between devices with their start and end apart: 22, of which 7 were waited for; matrix products, arithmetic and copies ran while one was open for 3% of the time, Pallas kernels for 11%

profile of v4, /device:TPU:32, one launch (start us, length us, event | category | flops | bytes accessed | tf_op | source)
XLA Modules:
  0.0 158.4 jit_solution(1217232650458492839)
XLA Ops:
  0.6 1.9 %project.1 = bf16[8,144,128]{2,1,0:T(8,128)(2,1)} custom-call(bf16[8,128,128]{2,1,0:T(8,128)(2,1)} %bitcast.93, bf16[128,128]{1,0:T(8,128)(2,1)} %msg_ref.1, s32[2,1,3,4,128]{4,3,2,1,0:T(4,128)} %bitcast.127, f32[2,1,3,4,128]{4,3,2,1,0:T(4,128)} %bitcast.128), custom_call_target="tpu_custom_call" | custom-call | tf_op jit(solution)/shard_map/project/pallas_call | solution.py:99
  2.5 0.1 collective-permute-start
  2.6 8.0 %collective-permute-start.1 = (bf16[1152,128]{1,0:T(8,128)(2,1)}, bf16[1152,128]{1,0:T(8,128)(2,1)S(1)}, u32[]{:S(2)}, u32[]{:S(2)}) collective-permute-start(bf16[1152,128]{1,0:T(8,128)(2,1)} %bitcast.76), channel_id=1, source_target_pairs={{0,60},{4,0},{8,4},{12,8},{16,12},{20,16},{24,20},{28,24},{32,28},... | collective-permute-start | bytes 884744 | tf_op jit(solution)/shard_map/ppermute | solution.py:55
  10.6 1.0 fusion.10
  11.6 1.7 %collective-permute-start.4 = (bf16[576,128]{1,0:T(8,128)(2,1)S(1)}, bf16[576,128]{1,0:T(8,128)(2,1)S(1)}, u32[]{:S(2)}, u32[]{:S(2)}) collective-permute-start(bf16[576,128]{1,0:T(8,128)(2,1)S(1)} %bitcast.122), channel_id=1, source_target_pairs={{0,64},{64,128},{128,192},{192,0},{1,65},{65,129},{129,193},{193,1... | collective-permute-start | bytes 442376 | tf_op jit(solution)/shard_map/ppermute | solution.py:55
  13.3 1.7 %collective-permute-start.5 = (bf16[576,128]{1,0:T(8,128)(2,1)S(1)}, bf16[576,128]{1,0:T(8,128)(2,1)S(1)}, u32[]{:S(2)}, u32[]{:S(2)}) collective-permute-start(bf16[576,128]{1,0:T(8,128)(2,1)S(1)} %bitcast.121), channel_id=1, source_target_pairs={{0,192},{64,0},{128,64},{192,128},{1,193},{65,1},{129,65},{193,129... | collective-permute-start | bytes 442376 | tf_op jit(solution)/shard_map/ppermute | solution.py:55
  15.0 0.9 slice_bitcast_fusion.1
  15.9 2.6 %collective-permute-done = bf16[1152,128]{1,0:T(8,128)(2,1)S(1)} collective-permute-done((bf16[1152,128]{1,0:T(8,128)(2,1)}, bf16[1152,128]{1,0:T(8,128)(2,1)S(1)}, u32[]{:S(2)}, u32[]{:S(2)}) %collective-permute-start) | collective-permute-done | bytes 294944 | tf_op jit(solution)/shard_map/ppermute | solution.py:55
  18.5 2.5 %collective-permute-done.1 = bf16[1152,128]{1,0:T(8,128)(2,1)S(1)} collective-permute-done((bf16[1152,128]{1,0:T(8,128)(2,1)}, bf16[1152,128]{1,0:T(8,128)(2,1)S(1)}, u32[]{:S(2)}, u32[]{:S(2)}) %collective-permute-start.1) | collective-permute-done | bytes 294944 | tf_op jit(solution)/shard_map/ppermute | solution.py:55
  21.0 2.5 %collective-permute-start.3 = (bf16[864,128]{1,0:T(8,128)(2,1)S(1)}, bf16[864,128]{1,0:T(8,128)(2,1)S(1)}, u32[]{:S(2)}, u32[]{:S(2)}) collective-permute-start(bf16[864,128]{1,0:T(8,128)(2,1)S(1)} %bitcast.120), channel_id=1, source_target_pairs={{0,3},{1,0},{2,1},{3,2},{4,7},{5,4},{6,5},{7,6},{8,11},{9,8},{10,9... | collective-permute-start | bytes 663560 | tf_op jit(solution)/shard_map/ppermute | solution.py:55
  23.5 0.1 collective-permute-start.2
  23.7 5.7 %inside_pairs.1 = (bf16[6,8,128,768]{3,2,1,0:T(8,128)(2,1)}, f32[2,4,128,128]{3,2,1,0:T(8,128)S(1)}) custom-call(bf16[2,4,144,128]{3,2,1,0:T(8,128)(2,1)S(1)} %bitcast.78, bf16[2,4,144,128]{3,2,1,0:T(8,128)(2,1)S(1)} %bitcast.83, bf16[2,4,144,128]{3,2,1,0:T(8,128)(2,1)S(1)} %bitcast.87, bf16[8,128,128]{2,1,0:T(8,128)(2,1)S(1)} %bitcast.94, ...), custom_call_target="tpu_custom_call" | custom-call | flops 5000000000 | bytes 9000000 | tf_op jit(solution)/shard_map/inside_pairs/pallas_call | solution.py:225
  29.4 0.1 pad_maximum_fusion.2
  29.4 1.6 %collective-permute-start.6 = (bf16[1152,128]{1,0:T(8,128)(2,1)S(1)}, bf16[1152,128]{1,0:T(8,128)(2,1)S(1)}, u32[]{:S(2)}, u32[]{:S(2)}) collective-permute-start(bf16[1152,128]{1,0:T(8,128)(2,1)S(1)} %bitcast.116), channel_id=1, source_target_pairs={{0,64},{64,128},{128,192},{192,0},{1,65},{65,129},{129,193},{193,1... | collective-permute-start | bytes 884744 | tf_op jit(solution)/shard_map/ppermute | solution.py:55
  31.1 0.0 collective-permute-done.3
  31.1 1.7 %collective-permute-start.7 = (bf16[1152,128]{1,0:T(8,128)(2,1)S(1)}, bf16[1152,128]{1,0:T(8,128)(2,1)S(1)}, u32[]{:S(2)}, u32[]{:S(2)}) collective-permute-start(bf16[1152,128]{1,0:T(8,128)(2,1)S(1)} %bitcast.115), channel_id=1, source_target_pairs={{0,192},{64,0},{128,64},{192,128},{1,193},{65,1},{129,65},{193,129... | collective-permute-start | bytes 884744 | tf_op jit(solution)/shard_map/ppermute | solution.py:55
  32.8 1.1 collective-permute-done.2
  34.0 1.7 %collective-permute-start.8 = (bf16[864,128]{1,0:T(8,128)(2,1)S(1)}, bf16[864,128]{1,0:T(8,128)(2,1)S(1)}, u32[]{:S(2)}, u32[]{:S(2)}) collective-permute-start(bf16[864,128]{1,0:T(8,128)(2,1)S(1)} %bitcast.117), channel_id=1, source_target_pairs={{0,64},{64,128},{128,192},{192,0},{1,65},{65,129},{129,193},{193,1... | collective-permute-start | bytes 663560 | tf_op jit(solution)/shard_map/ppermute | solution.py:55
  35.7 0.0 collective-permute-done.4
  35.7 1.9 %collective-permute-start.9 = (bf16[864,128]{1,0:T(8,128)(2,1)S(1)}, bf16[864,128]{1,0:T(8,128)(2,1)S(1)}, u32[]{:S(2)}, u32[]{:S(2)}) collective-permute-start(bf16[864,128]{1,0:T(8,128)(2,1)S(1)} %bitcast.118), channel_id=1, source_target_pairs={{0,192},{64,0},{128,64},{192,128},{1,193},{65,1},{129,65},{193,129... | collective-permute-start | bytes 663560 | tf_op jit(solution)/shard_map/ppermute | solution.py:55
  37.6 5.6 %ends_pairs.1 = (bf16[6,8,128,768]{3,2,1,0:T(8,128)(2,1)}, f32[2,4,128,128]{3,2,1,0:T(8,128)S(1)}) custom-call(bf16[2,4,144,128]{3,2,1,0:T(8,128)(2,1)S(1)} %bitcast.79, bf16[2,4,144,128]{3,2,1,0:T(8,128)(2,1)S(1)} %bitcast.85, bf16[2,4,144,128]{3,2,1,0:T(8,128)(2,1)S(1)} %bitcast.89, ...), custom_call_target="tpu_custom_call", output_to_operand_aliasing={{0}: (6, {})} | custom-call | flops 6000000000 | bytes 9000000 | tf_op jit(solution)/shard_map/ends_pairs/pallas_call | solution.py:293
  43.2 0.0 collective-permute-done.5
  43.2 0.0 collective-permute-done.6
  43.2 0.0 collective-permute-done.7
  43.2 1.4 collective-permute-done.8
  44.6 0.0 collective-permute-done.9
  44.6 5.7 %message.1 = (bf16[6,8,128,768]{3,2,1,0:T(8,128)(2,1)}, f32[2,4,128,128]{3,2,1,0:T(8,128)S(1)}, bf16[16,16,128]{2,1,0:T(8,128)(2,1)}, f32[4,6,8,128]{3,2,1,0:T(8,128)S(1)}) custom-call(bf16[2,4,144,128]{3,2,1,0:T(8,128)(2,1)S(1)} %bitcast.80, bf16[3,2,1,144,128]{4,3,2,1,0:T(8,128)(2,1)S(1)} %bitcast.101, ...), custom_call_target="tpu_custom_call", output_to_operand_aliasing={{0}: (11, {})} | custom-call | flops 5000000000 | bytes 6000000 | tf_op jit(solution)/shard_map/message/pallas_call | solution.py:410
  50.3 0.0 copy-start.4
  50.3 0.0 copy-start.7
  50.4 0.2 slope.1
  50.6 0.0 copy-start.3
  50.6 2.4 %collective-permute-start.10 = (bf16[256,128]{1,0:T(8,128)(2,1)S(1)}, bf16[256,128]{1,0:T(8,128)(2,1)S(1)}, u32[]{:S(2)}, u32[]{:S(2)}) collective-permute-start(bf16[256,128]{1,0:T(8,128)(2,1)S(1)} %bitcast.126), channel_id=1, source_target_pairs={{0,1},{1,2},{2,3},{3,0},{4,5},{5,6},{6,7},{7,4},{8,9},{9,10},{10,1... | collective-permute-start | bytes 196616 | tf_op jit(solution)/shard_map/ppermute | solution.py:55
  53.0 0.8 collective-permute-start.11
  53.8 7.9 %all-to-all-start = ((bf16[16,16,128]{2,1,0:T(8,128)(2,1)}), bf16[16,16,128]{2,1,0:T(8,128)(2,1)S(1)}, u32[]{:S(2)}, u32[]{:S(2)}) async-start(bf16[16,16,128]{2,1,0:T(8,128)(2,1)} %get-tuple-element.25), calls=%async_computation | async-start | bytes 131072 | tf_op jit(solution)/shard_map/all_to_all | solution.py:783
  61.7 0.0 collective-permute-done.10
  61.7 0.0 collective-permute-done.11
  61.7 0.1 fusion.8
  61.8 0.1 collective-permute-start.12
  61.9 7.7 %collective-permute-start.13 = (bf16[1536,128]{1,0:T(8,128)(2,1)S(1)}, bf16[1536,128]{1,0:T(8,128)(2,1)S(1)}, u32[]{:S(2)}, u32[]{:S(2)}) collective-permute-start(bf16[1536,128]{1,0:T(8,128)(2,1)S(1)} %bitcast.114), channel_id=1, source_target_pairs={{0,60},{4,0},{8,4},{12,8},{16,12},{20,16},{24,20},{28,24},{32,28},... | collective-permute-start | bytes 1179656 | tf_op jit(solution)/shard_map/ppermute | solution.py:55
  69.7 0.0 all-to-all-done
  69.7 1.0 forward_xz.1
  70.7 18.4 %all-to-all-start.1 = ((f32[256,1,128]{2,1,0:T(1,128)}), f32[256,1,128]{2,1,0:T(1,128)S(1)}, u32[]{:S(2)}, u32[]{:S(2)}) async-start(f32[256,1,128]{2,1,0:T(1,128)} %bitcast.34), calls=%async_computation.1 | async-start | bytes 262144 | tf_op jit(solution)/shard_map/all_to_all | solution.py:783
  89.2 0.1 fusion.1.influence_ref
  89.3 12.6 %all-to-all-done.1 = f32[256,1,128]{2,1,0:T(1,128)S(1)} async-done(((f32[256,1,128]{2,1,0:T(1,128)}), f32[256,1,128]{2,1,0:T(1,128)S(1)}, u32[]{:S(2)}, u32[]{:S(2)}) %all-to-all-start.1) | async-done | bytes 131104 | tf_op jit(solution)/shard_map/all_to_all | solution.py:783
  101.8 1.1 filter_y.1
  102.9 6.2 %all-to-all-start.2 = ((f32[256,2,128]{2,1,0:T(2,128)}), f32[256,2,128]{2,1,0:T(2,128)S(1)}, u32[]{:S(2)}, u32[]{:S(2)}) async-start(f32[256,2,128]{2,1,0:T(2,128)} %bitcast.36), calls=%async_computation.2 | async-start | bytes 524288 | tf_op jit(solution)/shard_map/all_to_all | solution.py:783
  109.1 0.0 collective-permute-done.12
  109.1 0.0 collective-permute-done.13
  109.1 0.1 pad_maximum_fusion.rows_ref
  109.3 0.0 copy-start.2
  109.3 0.0 copy-start.5
  109.3 1.1 fusion.9
  110.4 1.5 collective-permute-start.14
  111.9 1.7 %collective-permute-start.15 = (bf16[2304,128]{1,0:T(8,128)(2,1)}, bf16[2304,128]{1,0:T(8,128)(2,1)S(1)}, u32[]{:S(2)}, u32[]{:S(2)}) collective-permute-start(bf16[2304,128]{1,0:T(8,128)(2,1)} %bitcast.50), channel_id=1, source_target_pairs={{0,192},{64,0},{128,64},{192,128},{1,193},{65,1},{129,65},{193,129... | collective-permute-start | bytes 1769480 | tf_op jit(solution)/shard_map/ppermute | solution.py:55
  113.6 10.8 %all-to-all-done.2 = f32[256,2,128]{2,1,0:T(2,128)S(1)} async-done(((f32[256,2,128]{2,1,0:T(2,128)}), f32[256,2,128]{2,1,0:T(2,128)S(1)}, u32[]{:S(2)}, u32[]{:S(2)}) %all-to-all-start.2) | async-done | bytes 262176 | tf_op jit(solution)/shard_map/all_to_all | solution.py:783
  124.4 1.0 inverse_xz.1
  125.5 4.6 %all-to-all-start.3 = ((bf16[16,64,128]{2,1,0:T(8,128)(2,1)}), bf16[16,64,128]{2,1,0:T(8,128)(2,1)S(1)}, u32[]{:S(2)}, u32[]{:S(2)}) async-start(bf16[16,64,128]{2,1,0:T(8,128)(2,1)} %bitcast.38), calls=%async_computation.3 | async-start | bytes 524288 | tf_op jit(solution)/shard_map/all_to_all | solution.py:783
  130.1 0.5 slice.77
  130.6 9.1 %all-to-all-done.3.field_ref = bf16[16,64,128]{2,1,0:T(8,128)(2,1)S(1)} async-done(((bf16[16,64,128]{2,1,0:T(8,128)(2,1)}), bf16[16,64,128]{2,1,0:T(8,128)(2,1)S(1)}, u32[]{:S(2)}, u32[]{:S(2)}) %all-to-all-start.3) | async-done | bytes 262176 | tf_op jit(solution)/shard_map/all_to_all | solution.py:783
  139.7 2.7 %interpolate.1 = (f32[24,128]{1,0:T(8,128)S(1)}, f32[8,128]{1,0:T(8,128)}, bf16[6,8,128,256]{3,2,1,0:T(8,128)(2,1)S(1)}, bf16[3,4,6,128,128]{4,3,2,1,0:T(8,128)(2,1)S(1)}) custom-call(bf16[16,64,128]{2,1,0:T(8,128)(2,1)S(1)} %all-to-all-done.3.field_ref, f32[24,8,128]{2,1,0:T(8,128)S(1)} %bitcast.102, bf16[6,8,128,768]{3,2,1,0:T(8,128)(2,1)} %get-tuple-element.24.stored_ref, ...), custom_call_target="tpu_custom_call" | custom-call | flops 201326592 | bytes 400000 | tf_op jit(solution)/shard_map/interpolate/pallas_call | solution.py:598
  142.4 0.1 collective-permute-start.16
  142.5 7.7 %collective-permute-start.17 = (f32[24,128]{1,0:T(8,128)S(1)}, f32[24,128]{1,0:T(8,128)S(1)}, u32[]{:S(2)}, u32[]{:S(2)}) collective-permute-start(f32[24,128]{1,0:T(8,128)S(1)} %get-tuple-element.31.potential_ref), channel_id=1, source_target_pairs={{0,60},{4,0},{8,4},{12,8},{16,12},{20,16},{24,20},{28,24},{32,28},... | collective-permute-start | bytes 36872 | tf_op jit(solution)/shard_map/ppermute | solution.py:55
  150.2 3.4 %beside.1 = (bf16[6,8,128,512]{3,2,1,0:T(8,128)(2,1)S(1)}, f32[2,4,128,128]{3,2,1,0:T(8,128)S(1)}, bf16[2,4,128,128]{3,2,1,0:T(8,128)(2,1)S(1)}) custom-call(bf16[6,8,128,768]{3,2,1,0:T(8,128)(2,1)} %get-tuple-element.24.stored_ref, bf16[6,8,128,256]{3,2,1,0:T(8,128)(2,1)S(1)} %get-tuple-element.29.weight_ref, ...), custom_call_target="tpu_custom_call" | custom-call | flops 3000000000 | bytes 12000000 | tf_op jit(solution)/shard_map/beside/pallas_call | solution.py:659
  153.7 4.7 %backward.1 = f32[2,4,128,128]{3,2,1,0:T(8,128)} custom-call(bf16[6,8,128,512]{3,2,1,0:T(8,128)(2,1)S(1)} %get-tuple-element.32.weight_ref, bf16[3,4,6,128,128]{4,3,2,1,0:T(8,128)(2,1)S(1)} %get-tuple-element.30.slope_ref, f32[2,4,128,128]{3,2,1,0:T(8,128)S(1)} %get-tuple-element.33.part_ref, bf16[2,4,128,128]{3,2,1,0:T(8,128)(2,1)S(1)} %get-tuple-element.34.own_ref, ...), custom_call_target="tpu_custom_call" | custom-call | flops 4000000000 | bytes 12000000 | tf_op jit(solution)/shard_map/backward/pallas_call | solution.py:723
  (30 shorter events, 0.2 us)
Async XLA Ops:
  2.5 21.1 %copy-start = (bf16[8,144,128]{2,1,0:T(8,128)(2,1)S(1)}, bf16[8,144,128]{2,1,0:T(8,128)(2,1)}, u32[]{:S(2)}) copy-start(bf16[8,144,128]{2,1,0:T(8,128)(2,1)} %project.1) | copy-start | bytes 884740
  2.5 21.1 %copy-start.1 = (bf16[2,1,4,128,128]{4,3,2,1,0:T(8,128)(2,1)S(1)}, bf16[2,1,4,128,128]{4,3,2,1,0:T(8,128)(2,1)}, u32[]{:S(2)}) copy-start(bf16[2,1,4,128,128]{4,3,2,1,0:T(8,128)(2,1)} %param.11) | copy-start | bytes 786436
  2.5 21.1 %copy-start.9 = (bf16[128,128]{1,0:T(8,128)(2,1)S(1)}, bf16[128,128]{1,0:T(8,128)(2,1)}, u32[]{:S(2)}) copy-start(bf16[128,128]{1,0:T(8,128)(2,1)} %self_ref.3) | copy-start | bytes 98308
  2.5 15.9 %collective-permute-start = (bf16[1152,128]{1,0:T(8,128)(2,1)}, bf16[1152,128]{1,0:T(8,128)(2,1)S(1)}, u32[]{:S(2)}, u32[]{:S(2)}) collective-permute-start(bf16[1152,128]{1,0:T(8,128)(2,1)} %bitcast.75), channel_id=1, source_target_pairs={{0,4},{4,8},{8,12},{12,16},{16,20},{20,24},{24,28},{28,32},{32,36}... | collective-permute-start | bytes 884744 | tf_op jit(solution)/shard_map/ppermute | solution.py:55
  2.6 18.3 %collective-permute-start.1 = (bf16[1152,128]{1,0:T(8,128)(2,1)}, bf16[1152,128]{1,0:T(8,128)(2,1)S(1)}, u32[]{:S(2)}, u32[]{:S(2)}) collective-permute-start(bf16[1152,128]{1,0:T(8,128)(2,1)} %bitcast.76), channel_id=1, source_target_pairs={{0,60},{4,0},{8,4},{12,8},{16,12},{20,16},{24,20},{28,24},{32,28},... | collective-permute-start | bytes 884744 | tf_op jit(solution)/shard_map/ppermute | solution.py:55
  11.6 24.0 %collective-permute-start.4 = (bf16[576,128]{1,0:T(8,128)(2,1)S(1)}, bf16[576,128]{1,0:T(8,128)(2,1)S(1)}, u32[]{:S(2)}, u32[]{:S(2)}) collective-permute-start(bf16[576,128]{1,0:T(8,128)(2,1)S(1)} %bitcast.122), channel_id=1, source_target_pairs={{0,64},{64,128},{128,192},{192,0},{1,65},{65,129},{129,193},{193,1... | collective-permute-start | bytes 442376 | tf_op jit(solution)/shard_map/ppermute | solution.py:55
  13.3 29.9 %collective-permute-start.5 = (bf16[576,128]{1,0:T(8,128)(2,1)S(1)}, bf16[576,128]{1,0:T(8,128)(2,1)S(1)}, u32[]{:S(2)}, u32[]{:S(2)}) collective-permute-start(bf16[576,128]{1,0:T(8,128)(2,1)S(1)} %bitcast.121), channel_id=1, source_target_pairs={{0,192},{64,0},{128,64},{192,128},{1,193},{65,1},{129,65},{193,129... | collective-permute-start | bytes 442376 | tf_op jit(solution)/shard_map/ppermute | solution.py:55
  21.0 10.1 %collective-permute-start.3 = (bf16[864,128]{1,0:T(8,128)(2,1)S(1)}, bf16[864,128]{1,0:T(8,128)(2,1)S(1)}, u32[]{:S(2)}, u32[]{:S(2)}) collective-permute-start(bf16[864,128]{1,0:T(8,128)(2,1)S(1)} %bitcast.120), channel_id=1, source_target_pairs={{0,3},{1,0},{2,1},{3,2},{4,7},{5,4},{6,5},{7,6},{8,11},{9,8},{10,9... | collective-permute-start | bytes 663560 | tf_op jit(solution)/shard_map/ppermute | solution.py:55
  23.5 10.4 %collective-permute-start.2 = (bf16[864,128]{1,0:T(8,128)(2,1)S(1)}, bf16[864,128]{1,0:T(8,128)(2,1)S(1)}, u32[]{:S(2)}, u32[]{:S(2)}) collective-permute-start(bf16[864,128]{1,0:T(8,128)(2,1)S(1)} %bitcast.119), channel_id=1, source_target_pairs={{0,1},{1,2},{2,3},{3,0},{4,5},{5,6},{6,7},{7,4},{8,9},{9,10},{10,1... | collective-permute-start | bytes 663560 | tf_op jit(solution)/shard_map/ppermute | solution.py:55
  29.4 13.7 %collective-permute-start.6 = (bf16[1152,128]{1,0:T(8,128)(2,1)S(1)}, bf16[1152,128]{1,0:T(8,128)(2,1)S(1)}, u32[]{:S(2)}, u32[]{:S(2)}) collective-permute-start(bf16[1152,128]{1,0:T(8,128)(2,1)S(1)} %bitcast.116), channel_id=1, source_target_pairs={{0,64},{64,128},{128,192},{192,0},{1,65},{65,129},{129,193},{193,1... | collective-permute-start | bytes 884744 | tf_op jit(solution)/shard_map/ppermute | solution.py:55
  31.1 12.1 %collective-permute-start.7 = (bf16[1152,128]{1,0:T(8,128)(2,1)S(1)}, bf16[1152,128]{1,0:T(8,128)(2,1)S(1)}, u32[]{:S(2)}, u32[]{:S(2)}) collective-permute-start(bf16[1152,128]{1,0:T(8,128)(2,1)S(1)} %bitcast.115), channel_id=1, source_target_pairs={{0,192},{64,0},{128,64},{192,128},{1,193},{65,1},{129,65},{193,129... | collective-permute-start | bytes 884744 | tf_op jit(solution)/shard_map/ppermute | solution.py:55
  34.0 10.6 %collective-permute-start.8 = (bf16[864,128]{1,0:T(8,128)(2,1)S(1)}, bf16[864,128]{1,0:T(8,128)(2,1)S(1)}, u32[]{:S(2)}, u32[]{:S(2)}) collective-permute-start(bf16[864,128]{1,0:T(8,128)(2,1)S(1)} %bitcast.117), channel_id=1, source_target_pairs={{0,64},{64,128},{128,192},{192,0},{1,65},{65,129},{129,193},{193,1... | collective-permute-start | bytes 663560 | tf_op jit(solution)/shard_map/ppermute | solution.py:55
  35.7 8.9 %collective-permute-start.9 = (bf16[864,128]{1,0:T(8,128)(2,1)S(1)}, bf16[864,128]{1,0:T(8,128)(2,1)S(1)}, u32[]{:S(2)}, u32[]{:S(2)}) collective-permute-start(bf16[864,128]{1,0:T(8,128)(2,1)S(1)} %bitcast.118), channel_id=1, source_target_pairs={{0,192},{64,0},{128,64},{192,128},{1,193},{65,1},{129,65},{193,129... | collective-permute-start | bytes 663560 | tf_op jit(solution)/shard_map/ppermute | solution.py:55
  37.6 7.0 %copy-start.8 = (bf16[128]{0:T(256)(128)(2,1)S(1)}, bf16[128]{0:T(256)(128)(2,1)}, u32[]{:S(2)}) copy-start(bf16[128]{0:T(256)(128)(2,1)} %param.14) | copy-start | bytes 772
  50.3 19.3 %copy-start.4 = (bf16[256,256]{1,0:T(8,128)(2,1)S(1)}, bf16[256,256]{1,0:T(8,128)(2,1)}, u32[]{:S(2)}) copy-start(bf16[256,256]{1,0:T(8,128)(2,1)} %constant.78.clone.along_z_ref) | copy-start | bytes 393220
  50.3 19.3 %copy-start.7 = (bf16[128,128]{1,0:T(8,128)(2,1)S(1)}, bf16[128,128]{1,0:T(8,128)(2,1)}, u32[]{:S(2)}) copy-start(bf16[128,128]{1,0:T(8,128)(2,1)} %constant.79.clone.along_x_ref) | copy-start | bytes 98308
  50.6 51.2 %copy-start.3 = (bf16[256,256]{1,0:T(8,128)(2,1)S(1)}, bf16[256,256]{1,0:T(8,128)(2,1)}, u32[]{:S(2)}) copy-start(bf16[256,256]{1,0:T(8,128)(2,1)} %constant.80.clone.into_ref) | copy-start | bytes 393220
  50.6 11.1 %collective-permute-start.10 = (bf16[256,128]{1,0:T(8,128)(2,1)S(1)}, bf16[256,128]{1,0:T(8,128)(2,1)S(1)}, u32[]{:S(2)}, u32[]{:S(2)}) collective-permute-start(bf16[256,128]{1,0:T(8,128)(2,1)S(1)} %bitcast.126), channel_id=1, source_target_pairs={{0,1},{1,2},{2,3},{3,0},{4,5},{5,6},{6,7},{7,4},{8,9},{9,10},{10,1... | collective-permute-start | bytes 196616 | tf_op jit(solution)/shard_map/ppermute | solution.py:55
  53.0 8.7 %collective-permute-start.11 = (bf16[256,128]{1,0:T(8,128)(2,1)S(1)}, bf16[256,128]{1,0:T(8,128)(2,1)S(1)}, u32[]{:S(2)}, u32[]{:S(2)}) collective-permute-start(bf16[256,128]{1,0:T(8,128)(2,1)S(1)} %bitcast.125), channel_id=1, source_target_pairs={{0,3},{1,0},{2,1},{3,2},{4,7},{5,4},{6,5},{7,6},{8,11},{9,8},{10,9... | collective-permute-start | bytes 196616 | tf_op jit(solution)/shard_map/ppermute | solution.py:55
  53.8 15.9 %all-to-all-start = ((bf16[16,16,128]{2,1,0:T(8,128)(2,1)}), bf16[16,16,128]{2,1,0:T(8,128)(2,1)S(1)}, u32[]{:S(2)}, u32[]{:S(2)}) async-start(bf16[16,16,128]{2,1,0:T(8,128)(2,1)} %get-tuple-element.25), calls=%async_computation | async-start | bytes 131072 | tf_op jit(solution)/shard_map/all_to_all | solution.py:783
  61.8 47.3 %collective-permute-start.12 = (bf16[1536,128]{1,0:T(8,128)(2,1)S(1)}, bf16[1536,128]{1,0:T(8,128)(2,1)S(1)}, u32[]{:S(2)}, u32[]{:S(2)}) collective-permute-start(bf16[1536,128]{1,0:T(8,128)(2,1)S(1)} %bitcast.113), channel_id=1, source_target_pairs={{0,4},{4,8},{8,12},{12,16},{16,20},{20,24},{24,28},{28,32},{32,36}... | collective-permute-start | bytes 1179656 | tf_op jit(solution)/shard_map/ppermute | solution.py:55
  61.9 47.2 %collective-permute-start.13 = (bf16[1536,128]{1,0:T(8,128)(2,1)S(1)}, bf16[1536,128]{1,0:T(8,128)(2,1)S(1)}, u32[]{:S(2)}, u32[]{:S(2)}) collective-permute-start(bf16[1536,128]{1,0:T(8,128)(2,1)S(1)} %bitcast.114), channel_id=1, source_target_pairs={{0,60},{4,0},{8,4},{12,8},{16,12},{20,16},{24,20},{28,24},{32,28},... | collective-permute-start | bytes 1179656 | tf_op jit(solution)/shard_map/ppermute | solution.py:55
  70.7 31.1 %all-to-all-start.1 = ((f32[256,1,128]{2,1,0:T(1,128)}), f32[256,1,128]{2,1,0:T(1,128)S(1)}, u32[]{:S(2)}, u32[]{:S(2)}) async-start(f32[256,1,128]{2,1,0:T(1,128)} %bitcast.34), calls=%async_computation.1 | async-start | bytes 262144 | tf_op jit(solution)/shard_map/all_to_all | solution.py:783
  102.9 21.5 %all-to-all-start.2 = ((f32[256,2,128]{2,1,0:T(2,128)}), f32[256,2,128]{2,1,0:T(2,128)S(1)}, u32[]{:S(2)}, u32[]{:S(2)}) async-start(f32[256,2,128]{2,1,0:T(2,128)} %bitcast.36), calls=%async_computation.2 | async-start | bytes 524288 | tf_op jit(solution)/shard_map/all_to_all | solution.py:783
  109.3 15.2 %copy-start.2 = (bf16[256,512]{1,0:T(8,128)(2,1)S(1)}, bf16[256,512]{1,0:T(8,128)(2,1)}, u32[]{:S(2)}) copy-start(bf16[256,512]{1,0:T(8,128)(2,1)} %constant.82.clone.along_z_ref) | copy-start | bytes 786436
  109.3 15.1 %copy-start.5 = (bf16[256,128]{1,0:T(8,128)(2,1)S(1)}, bf16[256,128]{1,0:T(8,128)(2,1)}, u32[]{:S(2)}) copy-start(bf16[256,128]{1,0:T(8,128)(2,1)} %constant.81.clone.along_x_ref) | copy-start | bytes 196612
  110.4 20.2 %collective-permute-start.14 = (bf16[2304,128]{1,0:T(8,128)(2,1)}, bf16[2304,128]{1,0:T(8,128)(2,1)S(1)}, u32[]{:S(2)}, u32[]{:S(2)}) collective-permute-start(bf16[2304,128]{1,0:T(8,128)(2,1)} %bitcast.48), channel_id=1, source_target_pairs={{0,64},{64,128},{128,192},{192,0},{1,65},{65,129},{129,193},{193,1... | collective-permute-start | bytes 1769480 | tf_op jit(solution)/shard_map/ppermute | solution.py:55
  111.9 18.6 %collective-permute-start.15 = (bf16[2304,128]{1,0:T(8,128)(2,1)}, bf16[2304,128]{1,0:T(8,128)(2,1)S(1)}, u32[]{:S(2)}, u32[]{:S(2)}) collective-permute-start(bf16[2304,128]{1,0:T(8,128)(2,1)} %bitcast.50), channel_id=1, source_target_pairs={{0,192},{64,0},{128,64},{192,128},{1,193},{65,1},{129,65},{193,129... | collective-permute-start | bytes 1769480 | tf_op jit(solution)/shard_map/ppermute | solution.py:55
  125.5 14.2 %all-to-all-start.3 = ((bf16[16,64,128]{2,1,0:T(8,128)(2,1)}), bf16[16,64,128]{2,1,0:T(8,128)(2,1)S(1)}, u32[]{:S(2)}, u32[]{:S(2)}) async-start(bf16[16,64,128]{2,1,0:T(8,128)(2,1)} %bitcast.38), calls=%async_computation.3 | async-start | bytes 524288 | tf_op jit(solution)/shard_map/all_to_all | solution.py:783
  142.4 11.3 %collective-permute-start.16 = (f32[24,128]{1,0:T(8,128)S(1)}, f32[24,128]{1,0:T(8,128)S(1)}, u32[]{:S(2)}, u32[]{:S(2)}) collective-permute-start(f32[24,128]{1,0:T(8,128)S(1)} %get-tuple-element.31.potential_ref), channel_id=1, source_target_pairs={{0,4},{4,8},{8,12},{12,16},{16,20},{20,24},{24,28},{28,32},{32,36}... | collective-permute-start | bytes 36872 | tf_op jit(solution)/shard_map/ppermute | solution.py:55
  142.5 11.2 %collective-permute-start.17 = (f32[24,128]{1,0:T(8,128)S(1)}, f32[24,128]{1,0:T(8,128)S(1)}, u32[]{:S(2)}, u32[]{:S(2)}) collective-permute-start(f32[24,128]{1,0:T(8,128)S(1)} %get-tuple-element.31.potential_ref), channel_id=1, source_target_pairs={{0,60},{4,0},{8,4},{12,8},{16,12},{20,16},{24,20},{28,24},{32,28},... | collective-permute-start | bytes 36872 | tf_op jit(solution)/shard_map/ppermute | solution.py:55
  150.2 3.4 %copy-start.6 = (bf16[128,128]{1,0:T(8,128)(2,1)S(1)}, bf16[128,128]{1,0:T(8,128)(2,1)}, u32[]{:S(2)}) copy-start(bf16[128,128]{1,0:T(8,128)(2,1)} %msg_ref.1) | copy-start | bytes 98308

commit v5 on v4

--- a/solution.py
+++ b/solution.py
@@ -55,17 +55,26 @@
     return lax.ppermute(value.reshape(-1, 128), axis, pairs).reshape(value.shape)
 
 
+def partners(value):
+    count = lax.axis_size("gy")
+    across = [(i, (i + 1 if i % 2 else i - 1) % count) for i in range(count)]
+    within = [(i, i ^ 1) for i in range(count)]
+    flat = value.reshape(-1, 128)
+    return [lax.ppermute(flat, "gy", pairs).reshape(value.shape) for pairs in (across, within)]
+
+
 def late_halo(own):
     last_x, last_z = own.shape[0] - 1, own.shape[1] - 1
     left, right = moved(own[:, last_z:], "gz", 1), moved(own[:, :1], "gz", -1)
     row = jnp.concatenate([left, own, right], axis=1)
-    rows = jnp.stack([moved(row, "gy", 1), row, moved(row, "gy", -1)])
+    across, within = partners(row)
+    rows = jnp.stack([across, row, within])
     return [rows, moved(rows[:, last_x:], "gx", 1), moved(rows[:, :1], "gx", -1)]
 
 
 def early_halo(own):
     last_x, last_z = own.shape[0] - 1, own.shape[1] - 1
-    below, above = moved(own, "gy", 1), moved(own, "gy", -1)
+    below, above = partners(own)
     beside = [moved(own[last_x:], "gx", 1), moved(own[:1], "gx", -1)]
     sides = jnp.stack([below, above])
     rows = [below, own, above]
@@ -122,7 +131,7 @@
     return (place_of(rows) * (1.0 / PC)).astype(bf16).astype(f32)
 
 
-def weigh(centres, a, shift, near, store, pairs):
+def weigh(centres, a, shift, side, near, store, pairs):
     for c in range(4):
         columns = jnp.transpose(centres[a, c])
         centre_x = jnp.broadcast_to(columns[:, 0:1], (128, 128))
@@ -139,7 +148,7 @@
                     else:
                         row = near(dy, 2 * pair + half)
                         gap_x = (row[0:1] + shift) - centre_x
-                        gap_y = (row[1:2] + (dy - 1.0)) - centre_y
+                        gap_y = (row[1:2] + (dy - 1.0) * side) - centre_y
                         gap_z = (row[2:3] + float(dz)) - centre_z
                         squared = gap_x * gap_x + gap_y * gap_y + gap_z * gap_z
                         inside = jnp.maximum(1.0 - squared, 0.0)
@@ -184,7 +193,7 @@
 
 
 def inside_kernel(
-    own_ref, below_ref, above_ref, features_ref, self_ref,
+    side_ref, own_ref, below_ref, above_ref, features_ref, self_ref,
     weight_out, total_ref, weight_ref, position_ref, sems
 ):
     refs = (below_ref, own_ref, above_ref)
@@ -209,7 +218,7 @@
         def near(dy, z):
             return position_ref[dy, x, z - 1]
 
-        weigh(position_ref.at[1], a, (x - a).astype(f32), near, store, INSIDE)
+        weigh(position_ref.at[1], a, (x - a).astype(f32), side_ref[...], near, store, INSIDE)
         add_near(weight_ref, t, a, lambda dy, z: refs[dy].at[x, z - 1], total_ref, INSIDE)
         return carry
 
@@ -221,10 +230,10 @@
         copy.wait()
 
 
-def inside_pairs(own, sides, features, self_weight):
+def inside_pairs(side, own, sides, features, self_weight):
     return pl.pallas_call(
         inside_kernel,
-        in_specs=[VM] * 5,
+        in_specs=[VM] * 6,
         out_specs=[ANY, VM],
         out_shape=[
             jax.ShapeDtypeStruct((6, 8, 128, 768), bf16),
@@ -240,11 +249,11 @@
         ),
         compiler_params=LARGE,
         name="inside_pairs",
-    )(own, *sides, features, self_weight)
+    )(side, own, *sides, features, self_weight)
 
 
 def ends_kernel(
-    own_ref, below_ref, above_ref, left_ref, right_ref,
+    side_ref, own_ref, below_ref, above_ref, left_ref, right_ref,
     part_ref, _, weight_out, total_ref, weight_ref, centre_ref, position_ref, sems
 ):
     refs = (below_ref, own_ref, above_ref)
@@ -276,7 +285,7 @@
         def near(dy, z):
             return position_ref[dy, x, z]
 
-        weigh(centre_ref, a, (x - a).astype(f32), near, store, ENDS)
+        weigh(centre_ref, a, (x - a).astype(f32), side_ref[...], near, store, ENDS)
         add_near(weight_ref, t, a, lambda dy, z: cell(dy, x, z), total_ref, ENDS)
         return carry
 
@@ -289,12 +298,12 @@
         copy.wait()
 
 
-def ends_pairs(own, sides, ends, part, weights):
+def ends_pairs(side, own, sides, ends, part, weights):
     return pl.pallas_call(
         ends_kernel,
-        in_specs=[VM] * 6 + [ANY],
+        in_specs=[VM] * 7 + [ANY],
         out_specs=[ANY, VM],
-        input_output_aliases={6: 0},
+        input_output_aliases={7: 0},
         out_shape=[
             jax.ShapeDtypeStruct((6, 8, 128, 768), bf16),
             jax.ShapeDtypeStruct((2, 4, 128, 128), f32),
@@ -310,7 +319,7 @@
         ),
         compiler_params=LARGE,
         name="ends_pairs",
-    )(own, *sides, *ends, part, weights)
+    )(side, own, *sides, *ends, part, weights)
 
 
 def spline_row(place):
@@ -323,7 +332,7 @@
 
 
 def message_kernel(
-    own_ref, left_ref, right_ref, before_own, after_own, before_side, after_side, before_end,
+    side_ref, own_ref, left_ref, right_ref, before_own, after_own, before_side, after_side, before_end,
     after_end, part_ref, read_ref, _,
     weight_out, total_ref, mesh_ref, row_place_ref,
     weight_ref, position_ref, centre_ref, high_ref, low_ref, charge_ref, left_rows, right_rows, sems
@@ -360,7 +369,7 @@
         def near(dy, z):
             return position_ref[side, dy, z]
 
-        weigh(centre_ref, side, (2 * side - 1).astype(f32), near, store, ENDS + INSIDE)
+        weigh(centre_ref, side, (2 * side - 1).astype(f32), side_ref[...], near, store, ENDS + INSIDE)
         return carry
 
     lax.fori_loop(0, 2, column, 0)
@@ -406,12 +415,12 @@
         copy.wait()
 
 
-def message_layer(own, ends, outer, corners, part, read, weights):
+def message_layer(side, own, ends, outer, corners, part, read, weights):
     return pl.pallas_call(
         message_kernel,
-        in_specs=[VM] * 11 + [ANY],
+        in_specs=[VM] * 12 + [ANY],
         out_specs=[ANY, VM, VM, VM],
-        input_output_aliases={11: 0},
+        input_output_aliases={12: 0},
         out_shape=[
             jax.ShapeDtypeStruct((6, 8, 128, 768), bf16),
             jax.ShapeDtypeStruct((2, 4, 128, 128), f32),
@@ -434,7 +443,7 @@
         ),
         compiler_params=LARGE,
         name="message",
-    )(own, *ends, *outer, *corners, part, read, weights)
+    )(side, own, *ends, *outer, *corners, part, read, weights)
 
 
 def slope_kernel(total_ref, read_ref, out_ref):
@@ -798,14 +807,15 @@
     )
     own = own.reshape(cells_x, cells_z, slots + 16, width)
     sides, ends, outer, corners = early_halo(own)
-    weights, part = inside_pairs(own, sides, features_own, self_weight)
-    weights, part = ends_pairs(own, sides, ends, part, weights)
+    side = jnp.full((1, slots), 1 - 2 * (lax.axis_index("gy") % 2), f32)
+    weights, part = inside_pairs(side, own, sides, features_own, self_weight)
+    weights, part = ends_pairs(side, own, sides, ends, part, weights)
     influence = influence_of(size_x, size_y, size_z)
     along_z, along_x, into_y, back_x, back_z = wave_tables(size_x, size_y, size_z)
 
     read = charge_weight[None, :]
     weights, preact, mesh, row_place = message_layer(
-        own, ends, outer, corners, part, read, weights
+        side, own, ends, outer, corners, part, read, weights
     )
     mesh = swapped(mesh, plane).reshape(4, 4, PC, 128)
     slope_near = late_halo(slope_of(preact, read))
@@ -816,7 +826,7 @@
     potential, atom_potential, own_weights, slopes = interpolate(
         field, row_place.reshape(24, 8, slots), weights, slope_near, coupling / volume
     )
-    below, above = moved(potential, "gy", 1), moved(potential, "gy", -1)
+    below, above = partners(potential)
     weights, total, cotangent = beside(weights, own_weights, slopes, potential)
     grad = backward(weights, slopes, total, cotangent, below, above, msg_weight, self_weight)
     return (

time: 159 us -> 165 us (1.038)
  waiting for transfers between devices: 40.1 us -> 46.8 us
    ppermute x18 -> x12, starting transfers between devices: 42.9 us -> 17.5 us  [moved(): lax.ppermute(value.reshape(-1, 128), axis, pairs).reshape(value.shape)]
    ppermute x0 -> x6, starting transfers between devices: none -> 16.1 us  [partners(): lax.ppermute(flat, 'gy', pairs).reshape(value.shape)]
    ppermute x0 -> x6, waiting for transfers between devices: none -> 12.1 us  [partners(): lax.ppermute(flat, 'gy', pairs).reshape(value.shape)]
    all_to_all x4, starting transfers between devices: 37.1 us -> 45.6 us  [swapped(): return lax.all_to_all(value, axis, split_axis=0, concat_axis=0, tiled=True)]
    ppermute x18 -> x12, waiting for transfers between devices: 7.62 us -> 1.62 us  [moved(): lax.ppermute(value.reshape(-1, 128), axis, pairs).reshape(value.shape)]
  transfers between devices with their start and end apart: 22 -> 22, of which waited for: 7 -> 7; matrix products, arithmetic and copies ran while one was open for 3% -> 2% of each run, Pallas kernels for 11% -> 11%
where the time goes in v5:
time: 165 us; the launch traced here: 164 us
  starting transfers between devices  79.2 us (48%)
  waiting for transfers between devices  46.8 us (28%)
  Pallas kernels  33.2 us (20%)
  local copies, waits for them, and re-layouts  3.66 us (2%)
    all_to_all x4, starting transfers between devices, swapped(): return lax.all_to_all(value, axis, split_axis=0, concat_axis=0, tiled=True)  45.6 us
    all_to_all x4, waiting for transfers between devices, swapped(): return lax.all_to_all(value, axis, split_axis=0, concat_axis=0, tiled=True)  33.1 us
    ppermute x12, starting transfers between devices, moved(): lax.ppermute(value.reshape(-1, 128), axis, pairs).reshape(value.shape)  17.5 us
    ppermute x6, starting transfers between devices, partners(): lax.ppermute(flat, 'gy', pairs).reshape(value.shape)  16.1 us
    ppermute x6, waiting for transfers between devices, partners(): lax.ppermute(flat, 'gy', pairs).reshape(value.shape)  12.1 us
    pallas_call x1, Pallas kernels, message_layer(): pl.pallas_call(message_kernel, in_specs=[VM] * 12 + [ANY], out_specs=[ANY...  5.76 us
    pallas_call x1, Pallas kernels, inside_pairs(): pl.pallas_call(inside_kernel, in_specs=[VM] * 6, out_specs=[ANY, VM], out...  5.72 us
    pallas_call x1, Pallas kernels, ends_pairs(): pl.pallas_call(ends_kernel, in_specs=[VM] * 7 + [ANY], out_specs=[ANY, VM...  5.65 us
  transfers between devices with their start and end apart: 22, of which 7 were waited for; matrix products, arithmetic and copies ran while one was open for 2% of the time, Pallas kernels for 11%

profile of v5, /device:TPU:32, one launch (start us, length us, event | category | flops | bytes accessed | tf_op | source)
XLA Modules:
  0.0 164.4 jit_solution(16258553408719416204)
XLA Ops:
  0.6 1.9 %project.1 = bf16[8,144,128]{2,1,0:T(8,128)(2,1)} custom-call(bf16[8,128,128]{2,1,0:T(8,128)(2,1)} %bitcast.93, bf16[128,128]{1,0:T(8,128)(2,1)} %msg_ref.1, s32[2,1,3,4,128]{4,3,2,1,0:T(4,128)} %bitcast.127, f32[2,1,3,4,128]{4,3,2,1,0:T(4,128)} %bitcast.128), custom_call_target="tpu_custom_call" | custom-call | tf_op jit(solution)/shard_map/project/pallas_call | solution.py:108
  2.5 7.9 %collective-permute-start = (bf16[1152,128]{1,0:T(8,128)(2,1)}, bf16[1152,128]{1,0:T(8,128)(2,1)S(1)}, u32[]{:S(2)}, u32[]{:S(2)}) collective-permute-start(bf16[1152,128]{1,0:T(8,128)(2,1)} %bitcast.75), channel_id=1, source_target_pairs={{0,60},{4,8},{8,4},{12,16},{16,12},{20,24},{24,20},{28,32},{32,28}... | collective-permute-start | bytes 884744 | tf_op jit(solution)/shard_map/ppermute | solution.py:63
  10.5 0.0 collective-permute-start.1
  10.5 1.0 fusion.10
  11.5 1.7 %collective-permute-start.4 = (bf16[576,128]{1,0:T(8,128)(2,1)S(1)}, bf16[576,128]{1,0:T(8,128)(2,1)S(1)}, u32[]{:S(2)}, u32[]{:S(2)}) collective-permute-start(bf16[576,128]{1,0:T(8,128)(2,1)S(1)} %bitcast.122), channel_id=1, source_target_pairs={{0,64},{64,128},{128,192},{192,0},{1,65},{65,129},{129,193},{193,1... | collective-permute-start | bytes 442376 | tf_op jit(solution)/shard_map/ppermute | solution.py:55
  13.1 1.7 %collective-permute-start.5 = (bf16[576,128]{1,0:T(8,128)(2,1)S(1)}, bf16[576,128]{1,0:T(8,128)(2,1)S(1)}, u32[]{:S(2)}, u32[]{:S(2)}) collective-permute-start(bf16[576,128]{1,0:T(8,128)(2,1)S(1)} %bitcast.121), channel_id=1, source_target_pairs={{0,192},{64,0},{128,64},{192,128},{1,193},{65,1},{129,65},{193,129... | collective-permute-start | bytes 442376 | tf_op jit(solution)/shard_map/ppermute | solution.py:55
  14.8 0.9 slice_bitcast_fusion.1
  15.7 8.1 %collective-permute-done = bf16[1152,128]{1,0:T(8,128)(2,1)S(1)} collective-permute-done((bf16[1152,128]{1,0:T(8,128)(2,1)}, bf16[1152,128]{1,0:T(8,128)(2,1)S(1)}, u32[]{:S(2)}, u32[]{:S(2)}) %collective-permute-start) | collective-permute-done | bytes 294944 | tf_op jit(solution)/shard_map/ppermute | solution.py:63
  23.8 0.0 collective-permute-done.1
  23.8 0.0 copy-start
  23.9 0.0 copy-start.1
  23.9 0.0 copy-start.9
  23.9 0.1 collective-permute-start.3
  24.1 2.6 %collective-permute-start.2 = (bf16[864,128]{1,0:T(8,128)(2,1)S(1)}, bf16[864,128]{1,0:T(8,128)(2,1)S(1)}, u32[]{:S(2)}, u32[]{:S(2)}) collective-permute-start(bf16[864,128]{1,0:T(8,128)(2,1)S(1)} %bitcast.119), channel_id=1, source_target_pairs={{0,1},{1,2},{2,3},{3,0},{4,5},{5,6},{6,7},{7,4},{8,9},{9,10},{10,1... | collective-permute-start | bytes 663560 | tf_op jit(solution)/shard_map/ppermute | solution.py:55
  26.6 0.1 pad_maximum_fusion.2
  26.7 1.7 %collective-permute-start.6 = (bf16[1152,128]{1,0:T(8,128)(2,1)S(1)}, bf16[1152,128]{1,0:T(8,128)(2,1)S(1)}, u32[]{:S(2)}, u32[]{:S(2)}) collective-permute-start(bf16[1152,128]{1,0:T(8,128)(2,1)S(1)} %bitcast.116), channel_id=1, source_target_pairs={{0,64},{64,128},{128,192},{192,0},{1,65},{65,129},{129,193},{193,1... | collective-permute-start | bytes 884744 | tf_op jit(solution)/shard_map/ppermute | solution.py:55
  28.4 5.7 %inside_pairs.1 = (bf16[6,8,128,768]{3,2,1,0:T(8,128)(2,1)}, f32[2,4,128,128]{3,2,1,0:T(8,128)S(1)}) custom-call(f32[1,128]{1,0:T(1,128)S(1)} %broadcast_in_dim.13.side_ref, bf16[2,4,144,128]{3,2,1,0:T(8,128)(2,1)S(1)} %bitcast.78, bf16[2,4,144,128]{3,2,1,0:T(8,128)(2,1)S(1)} %bitcast.84, bf16[2,4,144,128]{3,2,1,0:T(8,128)(2,1)S(1)} %bitcast.88, ...), custom_call_target="tpu_custom_call" | custom-call | flops 5000000000 | bytes 9000000 | tf_op jit(solution)/shard_map/inside_pairs/pallas_call | solution.py:234
  34.2 2.1 %collective-permute-start.7 = (bf16[1152,128]{1,0:T(8,128)(2,1)S(1)}, bf16[1152,128]{1,0:T(8,128)(2,1)S(1)}, u32[]{:S(2)}, u32[]{:S(2)}) collective-permute-start(bf16[1152,128]{1,0:T(8,128)(2,1)S(1)} %bitcast.115), channel_id=1, source_target_pairs={{0,192},{64,0},{128,64},{192,128},{1,193},{65,1},{129,65},{193,129... | collective-permute-start | bytes 884744 | tf_op jit(solution)/shard_map/ppermute | solution.py:55
  36.2 0.0 collective-permute-done.2
  36.3 1.6 collective-permute-start.9
  37.9 0.8 collective-permute-start.8
  38.7 5.7 %ends_pairs.1 = (bf16[6,8,128,768]{3,2,1,0:T(8,128)(2,1)}, f32[2,4,128,128]{3,2,1,0:T(8,128)S(1)}) custom-call(f32[1,128]{1,0:T(1,128)S(1)} %broadcast_in_dim.13.side_ref, bf16[2,4,144,128]{3,2,1,0:T(8,128)(2,1)S(1)} %bitcast.79, bf16[2,4,144,128]{3,2,1,0:T(8,128)(2,1)S(1)} %bitcast.85, ...), custom_call_target="tpu_custom_call", output_to_operand_aliasing={{0}: (7, {})} | custom-call | flops 6000000000 | bytes 9000000 | tf_op jit(solution)/shard_map/ends_pairs/pallas_call | solution.py:302
  44.4 0.0 collective-permute-done.6
  44.4 1.6 collective-permute-done.9
  46.0 0.0 collective-permute-done.8
  46.0 5.8 %message.1 = (bf16[6,8,128,768]{3,2,1,0:T(8,128)(2,1)}, f32[2,4,128,128]{3,2,1,0:T(8,128)S(1)}, bf16[16,16,128]{2,1,0:T(8,128)(2,1)}, f32[4,6,8,128]{3,2,1,0:T(8,128)S(1)}) custom-call(f32[1,128]{1,0:T(1,128)S(1)} %broadcast_in_dim.13.side_ref, bf16[2,4,144,128]{3,2,1,0:T(8,128)(2,1)S(1)} %bitcast.80, ...), custom_call_target="tpu_custom_call", output_to_operand_aliasing={{0}: (12, {})} | custom-call | flops 5000000000 | bytes 6000000 | tf_op jit(solution)/shard_map/message/pallas_call | solution.py:419
  51.8 0.0 copy-start.4
  51.8 0.0 copy-start.7
  51.8 0.2 slope.1
  52.0 0.0 copy-start.3
  52.1 1.4 collective-permute-start.10
  53.5 0.8 collective-permute-start.11
  54.2 7.0 %all-to-all-start = ((bf16[16,16,128]{2,1,0:T(8,128)(2,1)}), bf16[16,16,128]{2,1,0:T(8,128)(2,1)S(1)}, u32[]{:S(2)}, u32[]{:S(2)}) async-start(bf16[16,16,128]{2,1,0:T(8,128)(2,1)} %get-tuple-element.25), calls=%async_computation | async-start | bytes 131072 | tf_op jit(solution)/shard_map/all_to_all | solution.py:792
  61.3 0.0 collective-permute-done.10
  61.3 0.1 fusion.8
  61.4 6.1 %collective-permute-start.12 = (bf16[1536,128]{1,0:T(8,128)(2,1)S(1)}, bf16[1536,128]{1,0:T(8,128)(2,1)S(1)}, u32[]{:S(2)}, u32[]{:S(2)}) collective-permute-start(bf16[1536,128]{1,0:T(8,128)(2,1)S(1)} %bitcast.113), channel_id=1, source_target_pairs={{0,60},{4,8},{8,4},{12,16},{16,12},{20,24},{24,20},{28,32},{32,28}... | collective-permute-start | bytes 1179656 | tf_op jit(solution)/shard_map/ppermute | solution.py:63
  67.5 0.0 collective-permute-start.13
  67.5 0.6 all-to-all-done
  68.1 1.0 forward_xz.1
  69.1 28.1 %all-to-all-start.1 = ((f32[256,1,128]{2,1,0:T(1,128)}), f32[256,1,128]{2,1,0:T(1,128)S(1)}, u32[]{:S(2)}, u32[]{:S(2)}) async-start(f32[256,1,128]{2,1,0:T(1,128)} %bitcast.34), calls=%async_computation.1 | async-start | bytes 262144 | tf_op jit(solution)/shard_map/all_to_all | solution.py:792
  97.2 0.1 fusion.1.influence_ref
  97.3 12.6 %all-to-all-done.1 = f32[256,1,128]{2,1,0:T(1,128)S(1)} async-done(((f32[256,1,128]{2,1,0:T(1,128)}), f32[256,1,128]{2,1,0:T(1,128)S(1)}, u32[]{:S(2)}, u32[]{:S(2)}) %all-to-all-start.1) | async-done | bytes 131104 | tf_op jit(solution)/shard_map/all_to_all | solution.py:792
  109.9 1.1 filter_y.1
  111.0 6.2 %all-to-all-start.2 = ((f32[256,2,128]{2,1,0:T(2,128)}), f32[256,2,128]{2,1,0:T(2,128)S(1)}, u32[]{:S(2)}, u32[]{:S(2)}) async-start(f32[256,2,128]{2,1,0:T(2,128)} %bitcast.36), calls=%async_computation.2 | async-start | bytes 524288 | tf_op jit(solution)/shard_map/all_to_all | solution.py:792
  117.2 0.0 collective-permute-done.12
  117.2 0.1 pad_maximum_fusion.rows_ref
  117.4 0.0 copy-start.2
  117.4 0.0 copy-start.5
  117.4 1.1 fusion.9
  118.5 1.5 collective-permute-start.14
  120.0 1.7 %collective-permute-start.15 = (bf16[2304,128]{1,0:T(8,128)(2,1)}, bf16[2304,128]{1,0:T(8,128)(2,1)S(1)}, u32[]{:S(2)}, u32[]{:S(2)}) collective-permute-start(bf16[2304,128]{1,0:T(8,128)(2,1)} %bitcast.50), channel_id=1, source_target_pairs={{0,192},{64,0},{128,64},{192,128},{1,193},{65,1},{129,65},{193,129... | collective-permute-start | bytes 1769480 | tf_op jit(solution)/shard_map/ppermute | solution.py:55
  121.7 10.8 %all-to-all-done.2 = f32[256,2,128]{2,1,0:T(2,128)S(1)} async-done(((f32[256,2,128]{2,1,0:T(2,128)}), f32[256,2,128]{2,1,0:T(2,128)S(1)}, u32[]{:S(2)}, u32[]{:S(2)}) %all-to-all-start.2) | async-done | bytes 262176 | tf_op jit(solution)/shard_map/all_to_all | solution.py:792
  132.5 1.0 inverse_xz.1
  133.6 4.3 %all-to-all-start.3 = ((bf16[16,64,128]{2,1,0:T(8,128)(2,1)}), bf16[16,64,128]{2,1,0:T(8,128)(2,1)S(1)}, u32[]{:S(2)}, u32[]{:S(2)}) async-start(bf16[16,64,128]{2,1,0:T(8,128)(2,1)} %bitcast.38), calls=%async_computation.3 | async-start | bytes 524288 | tf_op jit(solution)/shard_map/all_to_all | solution.py:792
  137.9 0.5 slice.77
  138.4 0.0 collective-permute-done.14
  138.4 0.0 collective-permute-done.15
  138.4 9.1 %all-to-all-done.3.field_ref = bf16[16,64,128]{2,1,0:T(8,128)(2,1)S(1)} async-done(((bf16[16,64,128]{2,1,0:T(8,128)(2,1)}), bf16[16,64,128]{2,1,0:T(8,128)(2,1)S(1)}, u32[]{:S(2)}, u32[]{:S(2)}) %all-to-all-start.3) | async-done | bytes 262176 | tf_op jit(solution)/shard_map/all_to_all | solution.py:792
  147.6 2.7 %interpolate.1 = (f32[24,128]{1,0:T(8,128)S(1)}, f32[8,128]{1,0:T(8,128)}, bf16[6,8,128,256]{3,2,1,0:T(8,128)(2,1)S(1)}, bf16[3,4,6,128,128]{4,3,2,1,0:T(8,128)(2,1)S(1)}) custom-call(bf16[16,64,128]{2,1,0:T(8,128)(2,1)S(1)} %all-to-all-done.3.field_ref, f32[24,8,128]{2,1,0:T(8,128)S(1)} %bitcast.102, bf16[6,8,128,768]{3,2,1,0:T(8,128)(2,1)} %get-tuple-element.24.stored_ref, ...), custom_call_target="tpu_custom_call" | custom-call | flops 201326592 | bytes 400000 | tf_op jit(solution)/shard_map/interpolate/pallas_call | solution.py:607
  150.2 0.3 collective-permute-start.16
  150.6 1.7 %collective-permute-start.17 = (f32[24,128]{1,0:T(8,128)S(1)}, f32[24,128]{1,0:T(8,128)S(1)}, u32[]{:S(2)}, u32[]{:S(2)}) collective-permute-start(f32[24,128]{1,0:T(8,128)S(1)} %get-tuple-element.31.potential_ref), channel_id=1, source_target_pairs={{0,4},{4,0},{8,12},{12,8},{16,20},{20,16},{24,28},{28,24},{32,36},... | collective-permute-start | bytes 36872 | tf_op jit(solution)/shard_map/ppermute | solution.py:63
  152.3 3.4 %beside.1 = (bf16[6,8,128,512]{3,2,1,0:T(8,128)(2,1)S(1)}, f32[2,4,128,128]{3,2,1,0:T(8,128)S(1)}, bf16[2,4,128,128]{3,2,1,0:T(8,128)(2,1)S(1)}) custom-call(bf16[6,8,128,768]{3,2,1,0:T(8,128)(2,1)} %get-tuple-element.24.stored_ref, bf16[6,8,128,256]{3,2,1,0:T(8,128)(2,1)S(1)} %get-tuple-element.29.weight_ref, ...), custom_call_target="tpu_custom_call" | custom-call | flops 3000000000 | bytes 12000000 | tf_op jit(solution)/shard_map/beside/pallas_call | solution.py:668
  155.7 4.0 %collective-permute-done.16.below_ref = f32[24,128]{1,0:T(8,128)S(1)} collective-permute-done((f32[24,128]{1,0:T(8,128)S(1)}, f32[24,128]{1,0:T(8,128)S(1)}, u32[]{:S(2)}, u32[]{:S(2)}) %collective-permute-start.16) | collective-permute-done | bytes 12320 | tf_op jit(solution)/shard_map/ppermute | solution.py:63
  159.7 4.7 %backward.1 = f32[2,4,128,128]{3,2,1,0:T(8,128)} custom-call(bf16[6,8,128,512]{3,2,1,0:T(8,128)(2,1)S(1)} %get-tuple-element.32.weight_ref, bf16[3,4,6,128,128]{4,3,2,1,0:T(8,128)(2,1)S(1)} %get-tuple-element.30.slope_ref, f32[2,4,128,128]{3,2,1,0:T(8,128)S(1)} %get-tuple-element.33.part_ref, bf16[2,4,128,128]{3,2,1,0:T(8,128)(2,1)S(1)} %get-tuple-element.34.own_ref, ...), custom_call_target="tpu_custom_call" | custom-call | flops 4000000000 | bytes 12000000 | tf_op jit(solution)/shard_map/backward/pallas_call | solution.py:732
  (31 shorter events, 0.2 us)
Async XLA Ops:
  2.5 21.3 %collective-permute-start = (bf16[1152,128]{1,0:T(8,128)(2,1)}, bf16[1152,128]{1,0:T(8,128)(2,1)S(1)}, u32[]{:S(2)}, u32[]{:S(2)}) collective-permute-start(bf16[1152,128]{1,0:T(8,128)(2,1)} %bitcast.75), channel_id=1, source_target_pairs={{0,60},{4,8},{8,4},{12,16},{16,12},{20,24},{24,20},{28,32},{32,28}... | collective-permute-start | bytes 884744 | tf_op jit(solution)/shard_map/ppermute | solution.py:63
  10.5 13.4 %collective-permute-start.1 = (bf16[1152,128]{1,0:T(8,128)(2,1)}, bf16[1152,128]{1,0:T(8,128)(2,1)S(1)}, u32[]{:S(2)}, u32[]{:S(2)}) collective-permute-start(bf16[1152,128]{1,0:T(8,128)(2,1)} %bitcast.76), channel_id=1, source_target_pairs={{0,4},{4,0},{8,12},{12,8},{16,20},{20,16},{24,28},{28,24},{32,36},... | collective-permute-start | bytes 884744 | tf_op jit(solution)/shard_map/ppermute | solution.py:63
  11.5 26.4 %collective-permute-start.4 = (bf16[576,128]{1,0:T(8,128)(2,1)S(1)}, bf16[576,128]{1,0:T(8,128)(2,1)S(1)}, u32[]{:S(2)}, u32[]{:S(2)}) collective-permute-start(bf16[576,128]{1,0:T(8,128)(2,1)S(1)} %bitcast.122), channel_id=1, source_target_pairs={{0,64},{64,128},{128,192},{192,0},{1,65},{65,129},{129,193},{193,1... | collective-permute-start | bytes 442376 | tf_op jit(solution)/shard_map/ppermute | solution.py:55
  13.1 31.2 %collective-permute-start.5 = (bf16[576,128]{1,0:T(8,128)(2,1)S(1)}, bf16[576,128]{1,0:T(8,128)(2,1)S(1)}, u32[]{:S(2)}, u32[]{:S(2)}) collective-permute-start(bf16[576,128]{1,0:T(8,128)(2,1)S(1)} %bitcast.121), channel_id=1, source_target_pairs={{0,192},{64,0},{128,64},{192,128},{1,193},{65,1},{129,65},{193,129... | collective-permute-start | bytes 442376 | tf_op jit(solution)/shard_map/ppermute | solution.py:55
  23.8 4.6 %copy-start = (bf16[8,144,128]{2,1,0:T(8,128)(2,1)S(1)}, bf16[8,144,128]{2,1,0:T(8,128)(2,1)}, u32[]{:S(2)}) copy-start(bf16[8,144,128]{2,1,0:T(8,128)(2,1)} %project.1) | copy-start | bytes 884740
  23.9 4.6 %copy-start.1 = (bf16[2,1,4,128,128]{4,3,2,1,0:T(8,128)(2,1)S(1)}, bf16[2,1,4,128,128]{4,3,2,1,0:T(8,128)(2,1)}, u32[]{:S(2)}) copy-start(bf16[2,1,4,128,128]{4,3,2,1,0:T(8,128)(2,1)} %param.11) | copy-start | bytes 786436
  23.9 4.6 %copy-start.9 = (bf16[128,128]{1,0:T(8,128)(2,1)S(1)}, bf16[128,128]{1,0:T(8,128)(2,1)}, u32[]{:S(2)}) copy-start(bf16[128,128]{1,0:T(8,128)(2,1)} %self_ref.3) | copy-start | bytes 98308
  23.9 10.2 %collective-permute-start.3 = (bf16[864,128]{1,0:T(8,128)(2,1)S(1)}, bf16[864,128]{1,0:T(8,128)(2,1)S(1)}, u32[]{:S(2)}, u32[]{:S(2)}) collective-permute-start(bf16[864,128]{1,0:T(8,128)(2,1)S(1)} %bitcast.120), channel_id=1, source_target_pairs={{0,3},{1,0},{2,1},{3,2},{4,7},{5,4},{6,5},{7,6},{8,11},{9,8},{10,9... | collective-permute-start | bytes 663560 | tf_op jit(solution)/shard_map/ppermute | solution.py:55
  24.1 12.2 %collective-permute-start.2 = (bf16[864,128]{1,0:T(8,128)(2,1)S(1)}, bf16[864,128]{1,0:T(8,128)(2,1)S(1)}, u32[]{:S(2)}, u32[]{:S(2)}) collective-permute-start(bf16[864,128]{1,0:T(8,128)(2,1)S(1)} %bitcast.119), channel_id=1, source_target_pairs={{0,1},{1,2},{2,3},{3,0},{4,5},{5,6},{6,7},{7,4},{8,9},{9,10},{10,1... | collective-permute-start | bytes 663560 | tf_op jit(solution)/shard_map/ppermute | solution.py:55
  26.7 17.7 %collective-permute-start.6 = (bf16[1152,128]{1,0:T(8,128)(2,1)S(1)}, bf16[1152,128]{1,0:T(8,128)(2,1)S(1)}, u32[]{:S(2)}, u32[]{:S(2)}) collective-permute-start(bf16[1152,128]{1,0:T(8,128)(2,1)S(1)} %bitcast.116), channel_id=1, source_target_pairs={{0,64},{64,128},{128,192},{192,0},{1,65},{65,129},{129,193},{193,1... | collective-permute-start | bytes 884744 | tf_op jit(solution)/shard_map/ppermute | solution.py:55
  34.2 10.2 %collective-permute-start.7 = (bf16[1152,128]{1,0:T(8,128)(2,1)S(1)}, bf16[1152,128]{1,0:T(8,128)(2,1)S(1)}, u32[]{:S(2)}, u32[]{:S(2)}) collective-permute-start(bf16[1152,128]{1,0:T(8,128)(2,1)S(1)} %bitcast.115), channel_id=1, source_target_pairs={{0,192},{64,0},{128,64},{192,128},{1,193},{65,1},{129,65},{193,129... | collective-permute-start | bytes 884744 | tf_op jit(solution)/shard_map/ppermute | solution.py:55
  36.3 9.7 %collective-permute-start.9 = (bf16[864,128]{1,0:T(8,128)(2,1)S(1)}, bf16[864,128]{1,0:T(8,128)(2,1)S(1)}, u32[]{:S(2)}, u32[]{:S(2)}) collective-permute-start(bf16[864,128]{1,0:T(8,128)(2,1)S(1)} %bitcast.117), channel_id=1, source_target_pairs={{0,192},{64,0},{128,64},{192,128},{1,193},{65,1},{129,65},{193,129... | collective-permute-start | bytes 663560 | tf_op jit(solution)/shard_map/ppermute | solution.py:55
  37.9 8.1 %collective-permute-start.8 = (bf16[864,128]{1,0:T(8,128)(2,1)S(1)}, bf16[864,128]{1,0:T(8,128)(2,1)S(1)}, u32[]{:S(2)}, u32[]{:S(2)}) collective-permute-start(bf16[864,128]{1,0:T(8,128)(2,1)S(1)} %bitcast.118), channel_id=1, source_target_pairs={{0,64},{64,128},{128,192},{192,0},{1,65},{65,129},{129,193},{193,1... | collective-permute-start | bytes 663560 | tf_op jit(solution)/shard_map/ppermute | solution.py:55
  38.7 7.3 %copy-start.8 = (bf16[128]{0:T(256)(128)(2,1)S(1)}, bf16[128]{0:T(256)(128)(2,1)}, u32[]{:S(2)}) copy-start(bf16[128]{0:T(256)(128)(2,1)} %param.14) | copy-start | bytes 772
  51.8 16.3 %copy-start.4 = (bf16[256,256]{1,0:T(8,128)(2,1)S(1)}, bf16[256,256]{1,0:T(8,128)(2,1)}, u32[]{:S(2)}) copy-start(bf16[256,256]{1,0:T(8,128)(2,1)} %constant.86.clone.along_z_ref) | copy-start | bytes 393220
  51.8 16.3 %copy-start.7 = (bf16[128,128]{1,0:T(8,128)(2,1)S(1)}, bf16[128,128]{1,0:T(8,128)(2,1)}, u32[]{:S(2)}) copy-start(bf16[128,128]{1,0:T(8,128)(2,1)} %constant.87.clone.along_x_ref) | copy-start | bytes 98308
  52.0 57.9 %copy-start.3 = (bf16[256,256]{1,0:T(8,128)(2,1)S(1)}, bf16[256,256]{1,0:T(8,128)(2,1)}, u32[]{:S(2)}) copy-start(bf16[256,256]{1,0:T(8,128)(2,1)} %constant.88.clone.into_ref) | copy-start | bytes 393220
  52.1 9.2 %collective-permute-start.10 = (bf16[256,128]{1,0:T(8,128)(2,1)S(1)}, bf16[256,128]{1,0:T(8,128)(2,1)S(1)}, u32[]{:S(2)}, u32[]{:S(2)}) collective-permute-start(bf16[256,128]{1,0:T(8,128)(2,1)S(1)} %bitcast.126), channel_id=1, source_target_pairs={{0,1},{1,2},{2,3},{3,0},{4,5},{5,6},{6,7},{7,4},{8,9},{9,10},{10,1... | collective-permute-start | bytes 196616 | tf_op jit(solution)/shard_map/ppermute | solution.py:55
  53.5 7.8 %collective-permute-start.11 = (bf16[256,128]{1,0:T(8,128)(2,1)S(1)}, bf16[256,128]{1,0:T(8,128)(2,1)S(1)}, u32[]{:S(2)}, u32[]{:S(2)}) collective-permute-start(bf16[256,128]{1,0:T(8,128)(2,1)S(1)} %bitcast.125), channel_id=1, source_target_pairs={{0,3},{1,0},{2,1},{3,2},{4,7},{5,4},{6,5},{7,6},{8,11},{9,8},{10,9... | collective-permute-start | bytes 196616 | tf_op jit(solution)/shard_map/ppermute | solution.py:55
  54.2 13.9 %all-to-all-start = ((bf16[16,16,128]{2,1,0:T(8,128)(2,1)}), bf16[16,16,128]{2,1,0:T(8,128)(2,1)S(1)}, u32[]{:S(2)}, u32[]{:S(2)}) async-start(bf16[16,16,128]{2,1,0:T(8,128)(2,1)} %get-tuple-element.25), calls=%async_computation | async-start | bytes 131072 | tf_op jit(solution)/shard_map/all_to_all | solution.py:792
  61.4 55.8 %collective-permute-start.12 = (bf16[1536,128]{1,0:T(8,128)(2,1)S(1)}, bf16[1536,128]{1,0:T(8,128)(2,1)S(1)}, u32[]{:S(2)}, u32[]{:S(2)}) collective-permute-start(bf16[1536,128]{1,0:T(8,128)(2,1)S(1)} %bitcast.113), channel_id=1, source_target_pairs={{0,60},{4,8},{8,4},{12,16},{16,12},{20,24},{24,20},{28,32},{32,28}... | collective-permute-start | bytes 1179656 | tf_op jit(solution)/shard_map/ppermute | solution.py:63
  67.5 49.7 %collective-permute-start.13 = (bf16[1536,128]{1,0:T(8,128)(2,1)S(1)}, bf16[1536,128]{1,0:T(8,128)(2,1)S(1)}, u32[]{:S(2)}, u32[]{:S(2)}) collective-permute-start(bf16[1536,128]{1,0:T(8,128)(2,1)S(1)} %bitcast.114), channel_id=1, source_target_pairs={{0,4},{4,0},{8,12},{12,8},{16,20},{20,16},{24,28},{28,24},{32,36},... | collective-permute-start | bytes 1179656 | tf_op jit(solution)/shard_map/ppermute | solution.py:63
  69.1 40.8 %all-to-all-start.1 = ((f32[256,1,128]{2,1,0:T(1,128)}), f32[256,1,128]{2,1,0:T(1,128)S(1)}, u32[]{:S(2)}, u32[]{:S(2)}) async-start(f32[256,1,128]{2,1,0:T(1,128)} %bitcast.34), calls=%async_computation.1 | async-start | bytes 262144 | tf_op jit(solution)/shard_map/all_to_all | solution.py:792
  111.0 21.5 %all-to-all-start.2 = ((f32[256,2,128]{2,1,0:T(2,128)}), f32[256,2,128]{2,1,0:T(2,128)S(1)}, u32[]{:S(2)}, u32[]{:S(2)}) async-start(f32[256,2,128]{2,1,0:T(2,128)} %bitcast.36), calls=%async_computation.2 | async-start | bytes 524288 | tf_op jit(solution)/shard_map/all_to_all | solution.py:792
  117.4 15.2 %copy-start.2 = (bf16[256,512]{1,0:T(8,128)(2,1)S(1)}, bf16[256,512]{1,0:T(8,128)(2,1)}, u32[]{:S(2)}) copy-start(bf16[256,512]{1,0:T(8,128)(2,1)} %constant.90.clone.along_z_ref) | copy-start | bytes 786436
  117.4 15.1 %copy-start.5 = (bf16[256,128]{1,0:T(8,128)(2,1)S(1)}, bf16[256,128]{1,0:T(8,128)(2,1)}, u32[]{:S(2)}) copy-start(bf16[256,128]{1,0:T(8,128)(2,1)} %constant.89.clone.along_x_ref) | copy-start | bytes 196612
  118.5 19.9 %collective-permute-start.14 = (bf16[2304,128]{1,0:T(8,128)(2,1)}, bf16[2304,128]{1,0:T(8,128)(2,1)S(1)}, u32[]{:S(2)}, u32[]{:S(2)}) collective-permute-start(bf16[2304,128]{1,0:T(8,128)(2,1)} %bitcast.48), channel_id=1, source_target_pairs={{0,64},{64,128},{128,192},{192,0},{1,65},{65,129},{129,193},{193,1... | collective-permute-start | bytes 1769480 | tf_op jit(solution)/shard_map/ppermute | solution.py:55
  120.0 18.4 %collective-permute-start.15 = (bf16[2304,128]{1,0:T(8,128)(2,1)}, bf16[2304,128]{1,0:T(8,128)(2,1)S(1)}, u32[]{:S(2)}, u32[]{:S(2)}) collective-permute-start(bf16[2304,128]{1,0:T(8,128)(2,1)} %bitcast.50), channel_id=1, source_target_pairs={{0,192},{64,0},{128,64},{192,128},{1,193},{65,1},{129,65},{193,129... | collective-permute-start | bytes 1769480 | tf_op jit(solution)/shard_map/ppermute | solution.py:55
  133.6 14.0 %all-to-all-start.3 = ((bf16[16,64,128]{2,1,0:T(8,128)(2,1)}), bf16[16,64,128]{2,1,0:T(8,128)(2,1)S(1)}, u32[]{:S(2)}, u32[]{:S(2)}) async-start(bf16[16,64,128]{2,1,0:T(8,128)(2,1)} %bitcast.38), calls=%async_computation.3 | async-start | bytes 524288 | tf_op jit(solution)/shard_map/all_to_all | solution.py:792
  150.2 9.4 %collective-permute-start.16 = (f32[24,128]{1,0:T(8,128)S(1)}, f32[24,128]{1,0:T(8,128)S(1)}, u32[]{:S(2)}, u32[]{:S(2)}) collective-permute-start(f32[24,128]{1,0:T(8,128)S(1)} %get-tuple-element.31.potential_ref), channel_id=1, source_target_pairs={{0,60},{4,8},{8,4},{12,16},{16,12},{20,24},{24,20},{28,32},{32,28}... | collective-permute-start | bytes 36872 | tf_op jit(solution)/shard_map/ppermute | solution.py:63
  150.6 9.1 %collective-permute-start.17 = (f32[24,128]{1,0:T(8,128)S(1)}, f32[24,128]{1,0:T(8,128)S(1)}, u32[]{:S(2)}, u32[]{:S(2)}) collective-permute-start(f32[24,128]{1,0:T(8,128)S(1)} %get-tuple-element.31.potential_ref), channel_id=1, source_target_pairs={{0,4},{4,0},{8,12},{12,8},{16,20},{20,16},{24,28},{28,24},{32,36},... | collective-permute-start | bytes 36872 | tf_op jit(solution)/shard_map/ppermute | solution.py:63
  152.3 7.4 %copy-start.6 = (bf16[128,128]{1,0:T(8,128)(2,1)S(1)}, bf16[128,128]{1,0:T(8,128)(2,1)}, u32[]{:S(2)}) copy-start(bf16[128,128]{1,0:T(8,128)(2,1)} %msg_ref.1) | copy-start | bytes 98308

commit v6 on v5

--- a/solution.py
+++ b/solution.py
@@ -67,7 +67,9 @@
     last_x, last_z = own.shape[0] - 1, own.shape[1] - 1
     left, right = moved(own[:, last_z:], "gz", 1), moved(own[:, :1], "gz", -1)
     row = jnp.concatenate([left, own, right], axis=1)
-    across, within = partners(row)
+    below, above = moved(row, "gy", 1), moved(row, "gy", -1)
+    even = lax.axis_index("gy") % 2 == 0
+    across, within = jnp.where(even, below, above), jnp.where(even, above, below)
     rows = jnp.stack([across, row, within])
     return [rows, moved(rows[:, last_x:], "gx", 1), moved(rows[:, :1], "gx", -1)]
 

time: 165 us -> 161 us (0.976)
  starting transfers between devices: 79.2 us -> 75.2 us
    ppermute x12 -> x14, starting transfers between devices: 17.5 us -> 25.3 us  [moved(): lax.ppermute(value.reshape(-1, 128), axis, pairs).reshape(value.shape)]
    ppermute x6 -> x4, starting transfers between devices: 16.1 us -> 9.5 us  [partners(): lax.ppermute(flat, 'gy', pairs).reshape(value.shape)]
    all_to_all x4, starting transfers between devices: 45.6 us -> 40.4 us  [swapped(): return lax.all_to_all(value, axis, split_axis=0, concat_axis=0, tiled=True)]
    ppermute x6 -> x4, waiting for transfers between devices: 12.1 us -> 12.2 us  [partners(): lax.ppermute(flat, 'gy', pairs).reshape(value.shape)]
  transfers between devices with their start and end apart: 22 -> 22, of which waited for: 7 -> 6; matrix products, arithmetic and copies ran while one was open for 2% -> 3% of each run, Pallas kernels for 11% -> 11%
where the time goes in v6:
time: 161 us; the launch traced here: 160 us
  starting transfers between devices  75.2 us (47%)
  waiting for transfers between devices  45.3 us (28%)
  Pallas kernels  33.4 us (21%)
  local copies, waits for them, and re-layouts  3.65 us (2%)
    all_to_all x4, starting transfers between devices, swapped(): return lax.all_to_all(value, axis, split_axis=0, concat_axis=0, tiled=True)  40.4 us
    all_to_all x4, waiting for transfers between devices, swapped(): return lax.all_to_all(value, axis, split_axis=0, concat_axis=0, tiled=True)  31.4 us
    ppermute x14, starting transfers between devices, moved(): lax.ppermute(value.reshape(-1, 128), axis, pairs).reshape(value.shape)  25.3 us
    ppermute x4, waiting for transfers between devices, partners(): lax.ppermute(flat, 'gy', pairs).reshape(value.shape)  12.2 us
    ppermute x4, starting transfers between devices, partners(): lax.ppermute(flat, 'gy', pairs).reshape(value.shape)  9.5 us
    pallas_call x1, Pallas kernels, message_layer(): pl.pallas_call(message_kernel, in_specs=[VM] * 12 + [ANY], out_specs=[ANY...  5.75 us
    pallas_call x1, Pallas kernels, inside_pairs(): pl.pallas_call(inside_kernel, in_specs=[VM] * 6, out_specs=[ANY, VM], out...  5.74 us
    pallas_call x1, Pallas kernels, ends_pairs(): pl.pallas_call(ends_kernel, in_specs=[VM] * 7 + [ANY], out_specs=[ANY, VM...  5.66 us
  transfers between devices with their start and end apart: 22, of which 6 were waited for; matrix products, arithmetic and copies ran while one was open for 3% of the time, Pallas kernels for 11%

profile of v6, /device:TPU:32, one launch (start us, length us, event | category | flops | bytes accessed | tf_op | source)
XLA Modules:
  0.0 160.1 jit_solution(16877431494623972926)
XLA Ops:
  0.6 1.9 %project.1 = bf16[8,144,128]{2,1,0:T(8,128)(2,1)} custom-call(bf16[8,128,128]{2,1,0:T(8,128)(2,1)} %bitcast.93, bf16[128,128]{1,0:T(8,128)(2,1)} %msg_ref.1, s32[2,1,3,4,128]{4,3,2,1,0:T(4,128)} %bitcast.127, f32[2,1,3,4,128]{4,3,2,1,0:T(4,128)} %bitcast.128), custom_call_target="tpu_custom_call" | custom-call | tf_op jit(solution)/shard_map/project/pallas_call | solution.py:110
  2.5 7.9 %collective-permute-start = (bf16[1152,128]{1,0:T(8,128)(2,1)}, bf16[1152,128]{1,0:T(8,128)(2,1)S(1)}, u32[]{:S(2)}, u32[]{:S(2)}) collective-permute-start(bf16[1152,128]{1,0:T(8,128)(2,1)} %bitcast.75), channel_id=1, source_target_pairs={{0,60},{4,8},{8,4},{12,16},{16,12},{20,24},{24,20},{28,32},{32,28}... | collective-permute-start | bytes 884744 | tf_op jit(solution)/shard_map/ppermute | solution.py:63
  10.5 0.0 collective-permute-start.1
  10.5 1.0 fusion.10
  11.5 1.7 %collective-permute-start.4 = (bf16[576,128]{1,0:T(8,128)(2,1)S(1)}, bf16[576,128]{1,0:T(8,128)(2,1)S(1)}, u32[]{:S(2)}, u32[]{:S(2)}) collective-permute-start(bf16[576,128]{1,0:T(8,128)(2,1)S(1)} %bitcast.122), channel_id=1, source_target_pairs={{0,64},{64,128},{128,192},{192,0},{1,65},{65,129},{129,193},{193,1... | collective-permute-start | bytes 442376 | tf_op jit(solution)/shard_map/ppermute | solution.py:55
  13.1 1.7 %collective-permute-start.5 = (bf16[576,128]{1,0:T(8,128)(2,1)S(1)}, bf16[576,128]{1,0:T(8,128)(2,1)S(1)}, u32[]{:S(2)}, u32[]{:S(2)}) collective-permute-start(bf16[576,128]{1,0:T(8,128)(2,1)S(1)} %bitcast.121), channel_id=1, source_target_pairs={{0,192},{64,0},{128,64},{192,128},{1,193},{65,1},{129,65},{193,129... | collective-permute-start | bytes 442376 | tf_op jit(solution)/shard_map/ppermute | solution.py:55
  14.8 0.9 slice_bitcast_fusion.1
  15.7 8.1 %collective-permute-done = bf16[1152,128]{1,0:T(8,128)(2,1)S(1)} collective-permute-done((bf16[1152,128]{1,0:T(8,128)(2,1)}, bf16[1152,128]{1,0:T(8,128)(2,1)S(1)}, u32[]{:S(2)}, u32[]{:S(2)}) %collective-permute-start) | collective-permute-done | bytes 294944 | tf_op jit(solution)/shard_map/ppermute | solution.py:63
  23.8 0.0 collective-permute-done.1
  23.8 0.0 copy-start
  23.9 0.0 copy-start.1
  23.9 0.0 copy-start.9
  23.9 0.1 collective-permute-start.3
  24.1 2.6 %collective-permute-start.2 = (bf16[864,128]{1,0:T(8,128)(2,1)S(1)}, bf16[864,128]{1,0:T(8,128)(2,1)S(1)}, u32[]{:S(2)}, u32[]{:S(2)}) collective-permute-start(bf16[864,128]{1,0:T(8,128)(2,1)S(1)} %bitcast.119), channel_id=1, source_target_pairs={{0,1},{1,2},{2,3},{3,0},{4,5},{5,6},{6,7},{7,4},{8,9},{9,10},{10,1... | collective-permute-start | bytes 663560 | tf_op jit(solution)/shard_map/ppermute | solution.py:55
  26.6 0.1 pad_maximum_fusion.2
  26.7 1.7 %collective-permute-start.6 = (bf16[1152,128]{1,0:T(8,128)(2,1)S(1)}, bf16[1152,128]{1,0:T(8,128)(2,1)S(1)}, u32[]{:S(2)}, u32[]{:S(2)}) collective-permute-start(bf16[1152,128]{1,0:T(8,128)(2,1)S(1)} %bitcast.116), channel_id=1, source_target_pairs={{0,64},{64,128},{128,192},{192,0},{1,65},{65,129},{129,193},{193,1... | collective-permute-start | bytes 884744 | tf_op jit(solution)/shard_map/ppermute | solution.py:55
  28.4 5.7 %inside_pairs.1 = (bf16[6,8,128,768]{3,2,1,0:T(8,128)(2,1)}, f32[2,4,128,128]{3,2,1,0:T(8,128)S(1)}) custom-call(f32[1,128]{1,0:T(1,128)S(1)} %broadcast_in_dim.13.side_ref, bf16[2,4,144,128]{3,2,1,0:T(8,128)(2,1)S(1)} %bitcast.78, bf16[2,4,144,128]{3,2,1,0:T(8,128)(2,1)S(1)} %bitcast.84, bf16[2,4,144,128]{3,2,1,0:T(8,128)(2,1)S(1)} %bitcast.88, ...), custom_call_target="tpu_custom_call" | custom-call | flops 5000000000 | bytes 9000000 | tf_op jit(solution)/shard_map/inside_pairs/pallas_call | solution.py:236
  34.2 0.0 collective-permute-done.3
  34.2 2.0 %collective-permute-start.7 = (bf16[1152,128]{1,0:T(8,128)(2,1)S(1)}, bf16[1152,128]{1,0:T(8,128)(2,1)S(1)}, u32[]{:S(2)}, u32[]{:S(2)}) collective-permute-start(bf16[1152,128]{1,0:T(8,128)(2,1)S(1)} %bitcast.115), channel_id=1, source_target_pairs={{0,192},{64,0},{128,64},{192,128},{1,193},{65,1},{129,65},{193,129... | collective-permute-start | bytes 884744 | tf_op jit(solution)/shard_map/ppermute | solution.py:55
  36.3 1.6 collective-permute-start.9
  37.9 0.0 collective-permute-done.4
  37.9 0.8 collective-permute-start.8
  38.7 5.7 %ends_pairs.1 = (bf16[6,8,128,768]{3,2,1,0:T(8,128)(2,1)}, f32[2,4,128,128]{3,2,1,0:T(8,128)S(1)}) custom-call(f32[1,128]{1,0:T(1,128)S(1)} %broadcast_in_dim.13.side_ref, bf16[2,4,144,128]{3,2,1,0:T(8,128)(2,1)S(1)} %bitcast.79, bf16[2,4,144,128]{3,2,1,0:T(8,128)(2,1)S(1)} %bitcast.85, ...), custom_call_target="tpu_custom_call", output_to_operand_aliasing={{0}: (7, {})} | custom-call | flops 6000000000 | bytes 9000000 | tf_op jit(solution)/shard_map/ends_pairs/pallas_call | solution.py:304
  44.4 0.0 collective-permute-done.5
  44.4 0.0 collective-permute-done.7
  44.4 1.6 collective-permute-done.9
  46.0 0.0 collective-permute-done.8
  46.0 5.8 %message.1 = (bf16[6,8,128,768]{3,2,1,0:T(8,128)(2,1)}, f32[2,4,128,128]{3,2,1,0:T(8,128)S(1)}, bf16[16,16,128]{2,1,0:T(8,128)(2,1)}, f32[4,6,8,128]{3,2,1,0:T(8,128)S(1)}) custom-call(f32[1,128]{1,0:T(1,128)S(1)} %broadcast_in_dim.13.side_ref, bf16[2,4,144,128]{3,2,1,0:T(8,128)(2,1)S(1)} %bitcast.80, ...), custom_call_target="tpu_custom_call", output_to_operand_aliasing={{0}: (12, {})} | custom-call | flops 5000000000 | bytes 6000000 | tf_op jit(solution)/shard_map/message/pallas_call | solution.py:421
  51.8 0.0 copy-start.4
  51.8 0.0 copy-start.7
  51.8 0.2 slope.1
  52.0 0.0 copy-start.3
  52.1 1.4 collective-permute-start.10
  53.5 0.8 collective-permute-start.11
  54.2 7.0 %all-to-all-start = ((bf16[16,16,128]{2,1,0:T(8,128)(2,1)}), bf16[16,16,128]{2,1,0:T(8,128)(2,1)S(1)}, u32[]{:S(2)}, u32[]{:S(2)}) async-start(bf16[16,16,128]{2,1,0:T(8,128)(2,1)} %get-tuple-element.25), calls=%async_computation | async-start | bytes 131072 | tf_op jit(solution)/shard_map/all_to_all | solution.py:794
  61.3 0.0 collective-permute-done.10
  61.3 0.1 fusion.8
  61.3 0.1 collective-permute-start.12
  61.4 7.7 %collective-permute-start.13 = (bf16[1536,128]{1,0:T(8,128)(2,1)S(1)}, bf16[1536,128]{1,0:T(8,128)(2,1)}, u32[]{:S(2)}, u32[]{:S(2)}) collective-permute-start(bf16[1536,128]{1,0:T(8,128)(2,1)S(1)} %bitcast.114), channel_id=1, source_target_pairs={{0,60},{4,0},{8,4},{12,8},{16,12},{20,16},{24,20},{28,24},{32,28},... | collective-permute-start | bytes 1179656 | tf_op jit(solution)/shard_map/ppermute | solution.py:55
  69.2 0.0 all-to-all-done
  69.2 1.0 forward_xz.1
  70.3 22.6 %all-to-all-start.1 = ((f32[256,1,128]{2,1,0:T(1,128)}), f32[256,1,128]{2,1,0:T(1,128)S(1)}, u32[]{:S(2)}, u32[]{:S(2)}) async-start(f32[256,1,128]{2,1,0:T(1,128)} %bitcast.34), calls=%async_computation.1 | async-start | bytes 262144 | tf_op jit(solution)/shard_map/all_to_all | solution.py:794
  92.9 0.1 fusion.1.influence_ref
  93.0 12.6 %all-to-all-done.1 = f32[256,1,128]{2,1,0:T(1,128)S(1)} async-done(((f32[256,1,128]{2,1,0:T(1,128)}), f32[256,1,128]{2,1,0:T(1,128)S(1)}, u32[]{:S(2)}, u32[]{:S(2)}) %all-to-all-start.1) | async-done | bytes 131104 | tf_op jit(solution)/shard_map/all_to_all | solution.py:794
  105.6 1.1 filter_y.1
  106.7 6.2 %all-to-all-start.2 = ((f32[256,2,128]{2,1,0:T(2,128)}), f32[256,2,128]{2,1,0:T(2,128)S(1)}, u32[]{:S(2)}, u32[]{:S(2)}) async-start(f32[256,2,128]{2,1,0:T(2,128)} %bitcast.36), calls=%async_computation.2 | async-start | bytes 524288 | tf_op jit(solution)/shard_map/all_to_all | solution.py:794
  112.9 1.1 broadcast_select_fusion.1
  113.9 0.1 pad_maximum_fusion.rows_ref
  114.1 0.0 copy-start.2
  114.1 0.0 copy-start.5
  114.1 1.1 fusion.9
  115.2 1.5 collective-permute-start.14
  116.7 1.7 %collective-permute-start.15 = (bf16[2304,128]{1,0:T(8,128)(2,1)}, bf16[2304,128]{1,0:T(8,128)(2,1)S(1)}, u32[]{:S(2)}, u32[]{:S(2)}) collective-permute-start(bf16[2304,128]{1,0:T(8,128)(2,1)} %bitcast.50), channel_id=1, source_target_pairs={{0,192},{64,0},{128,64},{192,128},{1,193},{65,1},{129,65},{193,129... | collective-permute-start | bytes 1769480 | tf_op jit(solution)/shard_map/ppermute | solution.py:55
  118.4 9.7 %all-to-all-done.2 = f32[256,2,128]{2,1,0:T(2,128)S(1)} async-done(((f32[256,2,128]{2,1,0:T(2,128)}), f32[256,2,128]{2,1,0:T(2,128)S(1)}, u32[]{:S(2)}, u32[]{:S(2)}) %all-to-all-start.2) | async-done | bytes 262176 | tf_op jit(solution)/shard_map/all_to_all | solution.py:794
  128.2 1.0 inverse_xz.1
  129.2 4.6 %all-to-all-start.3 = ((bf16[16,64,128]{2,1,0:T(8,128)(2,1)}), bf16[16,64,128]{2,1,0:T(8,128)(2,1)S(1)}, u32[]{:S(2)}, u32[]{:S(2)}) async-start(bf16[16,64,128]{2,1,0:T(8,128)(2,1)} %bitcast.38), calls=%async_computation.3 | async-start | bytes 524288 | tf_op jit(solution)/shard_map/all_to_all | solution.py:794
  133.8 0.5 slice.77
  134.3 9.1 %all-to-all-done.3.field_ref = bf16[16,64,128]{2,1,0:T(8,128)(2,1)S(1)} async-done(((bf16[16,64,128]{2,1,0:T(8,128)(2,1)}), bf16[16,64,128]{2,1,0:T(8,128)(2,1)S(1)}, u32[]{:S(2)}, u32[]{:S(2)}) %all-to-all-start.3) | async-done | bytes 262176 | tf_op jit(solution)/shard_map/all_to_all | solution.py:794
  143.5 2.7 %interpolate.1 = (f32[24,128]{1,0:T(8,128)S(1)}, f32[8,128]{1,0:T(8,128)}, bf16[6,8,128,256]{3,2,1,0:T(8,128)(2,1)S(1)}, bf16[3,4,6,128,128]{4,3,2,1,0:T(8,128)(2,1)S(1)}) custom-call(bf16[16,64,128]{2,1,0:T(8,128)(2,1)S(1)} %all-to-all-done.3.field_ref, f32[24,8,128]{2,1,0:T(8,128)S(1)} %bitcast.102, bf16[6,8,128,768]{3,2,1,0:T(8,128)(2,1)} %get-tuple-element.24.stored_ref, ...), custom_call_target="tpu_custom_call" | custom-call | flops 201326592 | bytes 400000 | tf_op jit(solution)/shard_map/interpolate/pallas_call | solution.py:609
  146.1 0.1 collective-permute-start.16
  146.2 1.5 collective-permute-start.17
  147.7 3.5 %beside.1 = (bf16[6,8,128,512]{3,2,1,0:T(8,128)(2,1)S(1)}, f32[2,4,128,128]{3,2,1,0:T(8,128)S(1)}, bf16[2,4,128,128]{3,2,1,0:T(8,128)(2,1)S(1)}) custom-call(bf16[6,8,128,768]{3,2,1,0:T(8,128)(2,1)} %get-tuple-element.24.stored_ref, bf16[6,8,128,256]{3,2,1,0:T(8,128)(2,1)S(1)} %get-tuple-element.29.weight_ref, ...), custom_call_target="tpu_custom_call" | custom-call | flops 3000000000 | bytes 12000000 | tf_op jit(solution)/shard_map/beside/pallas_call | solution.py:670
  151.2 4.1 %collective-permute-done.16.below_ref = f32[24,128]{1,0:T(8,128)S(1)} collective-permute-done((f32[24,128]{1,0:T(8,128)S(1)}, f32[24,128]{1,0:T(8,128)S(1)}, u32[]{:S(2)}, u32[]{:S(2)}) %collective-permute-start.16) | collective-permute-done | bytes 12320 | tf_op jit(solution)/shard_map/ppermute | solution.py:63
  155.4 4.7 %backward.1 = f32[2,4,128,128]{3,2,1,0:T(8,128)} custom-call(bf16[6,8,128,512]{3,2,1,0:T(8,128)(2,1)S(1)} %get-tuple-element.32.weight_ref, bf16[3,4,6,128,128]{4,3,2,1,0:T(8,128)(2,1)S(1)} %get-tuple-element.30.slope_ref, f32[2,4,128,128]{3,2,1,0:T(8,128)S(1)} %get-tuple-element.33.part_ref, bf16[2,4,128,128]{3,2,1,0:T(8,128)(2,1)S(1)} %get-tuple-element.34.own_ref, ...), custom_call_target="tpu_custom_call" | custom-call | flops 4000000000 | bytes 12000000 | tf_op jit(solution)/shard_map/backward/pallas_call | solution.py:734
  (32 shorter events, 0.2 us)
Async XLA Ops:
  2.5 21.3 %collective-permute-start = (bf16[1152,128]{1,0:T(8,128)(2,1)}, bf16[1152,128]{1,0:T(8,128)(2,1)S(1)}, u32[]{:S(2)}, u32[]{:S(2)}) collective-permute-start(bf16[1152,128]{1,0:T(8,128)(2,1)} %bitcast.75), channel_id=1, source_target_pairs={{0,60},{4,8},{8,4},{12,16},{16,12},{20,24},{24,20},{28,32},{32,28}... | collective-permute-start | bytes 884744 | tf_op jit(solution)/shard_map/ppermute | solution.py:63
  10.5 13.4 %collective-permute-start.1 = (bf16[1152,128]{1,0:T(8,128)(2,1)}, bf16[1152,128]{1,0:T(8,128)(2,1)S(1)}, u32[]{:S(2)}, u32[]{:S(2)}) collective-permute-start(bf16[1152,128]{1,0:T(8,128)(2,1)} %bitcast.76), channel_id=1, source_target_pairs={{0,4},{4,0},{8,12},{12,8},{16,20},{20,16},{24,28},{28,24},{32,36},... | collective-permute-start | bytes 884744 | tf_op jit(solution)/shard_map/ppermute | solution.py:63
  11.5 26.4 %collective-permute-start.4 = (bf16[576,128]{1,0:T(8,128)(2,1)S(1)}, bf16[576,128]{1,0:T(8,128)(2,1)S(1)}, u32[]{:S(2)}, u32[]{:S(2)}) collective-permute-start(bf16[576,128]{1,0:T(8,128)(2,1)S(1)} %bitcast.122), channel_id=1, source_target_pairs={{0,64},{64,128},{128,192},{192,0},{1,65},{65,129},{129,193},{193,1... | collective-permute-start | bytes 442376 | tf_op jit(solution)/shard_map/ppermute | solution.py:55
  13.1 31.3 %collective-permute-start.5 = (bf16[576,128]{1,0:T(8,128)(2,1)S(1)}, bf16[576,128]{1,0:T(8,128)(2,1)S(1)}, u32[]{:S(2)}, u32[]{:S(2)}) collective-permute-start(bf16[576,128]{1,0:T(8,128)(2,1)S(1)} %bitcast.121), channel_id=1, source_target_pairs={{0,192},{64,0},{128,64},{192,128},{1,193},{65,1},{129,65},{193,129... | collective-permute-start | bytes 442376 | tf_op jit(solution)/shard_map/ppermute | solution.py:55
  23.8 4.6 %copy-start = (bf16[8,144,128]{2,1,0:T(8,128)(2,1)S(1)}, bf16[8,144,128]{2,1,0:T(8,128)(2,1)}, u32[]{:S(2)}) copy-start(bf16[8,144,128]{2,1,0:T(8,128)(2,1)} %project.1) | copy-start | bytes 884740
  23.9 4.6 %copy-start.1 = (bf16[2,1,4,128,128]{4,3,2,1,0:T(8,128)(2,1)S(1)}, bf16[2,1,4,128,128]{4,3,2,1,0:T(8,128)(2,1)}, u32[]{:S(2)}) copy-start(bf16[2,1,4,128,128]{4,3,2,1,0:T(8,128)(2,1)} %param.11) | copy-start | bytes 786436
  23.9 4.6 %copy-start.9 = (bf16[128,128]{1,0:T(8,128)(2,1)S(1)}, bf16[128,128]{1,0:T(8,128)(2,1)}, u32[]{:S(2)}) copy-start(bf16[128,128]{1,0:T(8,128)(2,1)} %self_ref.3) | copy-start | bytes 98308
  23.9 10.2 %collective-permute-start.3 = (bf16[864,128]{1,0:T(8,128)(2,1)S(1)}, bf16[864,128]{1,0:T(8,128)(2,1)S(1)}, u32[]{:S(2)}, u32[]{:S(2)}) collective-permute-start(bf16[864,128]{1,0:T(8,128)(2,1)S(1)} %bitcast.120), channel_id=1, source_target_pairs={{0,3},{1,0},{2,1},{3,2},{4,7},{5,4},{6,5},{7,6},{8,11},{9,8},{10,9... | collective-permute-start | bytes 663560 | tf_op jit(solution)/shard_map/ppermute | solution.py:55
  24.1 12.2 %collective-permute-start.2 = (bf16[864,128]{1,0:T(8,128)(2,1)S(1)}, bf16[864,128]{1,0:T(8,128)(2,1)S(1)}, u32[]{:S(2)}, u32[]{:S(2)}) collective-permute-start(bf16[864,128]{1,0:T(8,128)(2,1)S(1)} %bitcast.119), channel_id=1, source_target_pairs={{0,1},{1,2},{2,3},{3,0},{4,5},{5,6},{6,7},{7,4},{8,9},{9,10},{10,1... | collective-permute-start | bytes 663560 | tf_op jit(solution)/shard_map/ppermute | solution.py:55
  26.7 17.7 %collective-permute-start.6 = (bf16[1152,128]{1,0:T(8,128)(2,1)S(1)}, bf16[1152,128]{1,0:T(8,128)(2,1)S(1)}, u32[]{:S(2)}, u32[]{:S(2)}) collective-permute-start(bf16[1152,128]{1,0:T(8,128)(2,1)S(1)} %bitcast.116), channel_id=1, source_target_pairs={{0,64},{64,128},{128,192},{192,0},{1,65},{65,129},{129,193},{193,1... | collective-permute-start | bytes 884744 | tf_op jit(solution)/shard_map/ppermute | solution.py:55
  34.2 10.2 %collective-permute-start.7 = (bf16[1152,128]{1,0:T(8,128)(2,1)S(1)}, bf16[1152,128]{1,0:T(8,128)(2,1)S(1)}, u32[]{:S(2)}, u32[]{:S(2)}) collective-permute-start(bf16[1152,128]{1,0:T(8,128)(2,1)S(1)} %bitcast.115), channel_id=1, source_target_pairs={{0,192},{64,0},{128,64},{192,128},{1,193},{65,1},{129,65},{193,129... | collective-permute-start | bytes 884744 | tf_op jit(solution)/shard_map/ppermute | solution.py:55
  36.3 9.7 %collective-permute-start.9 = (bf16[864,128]{1,0:T(8,128)(2,1)S(1)}, bf16[864,128]{1,0:T(8,128)(2,1)S(1)}, u32[]{:S(2)}, u32[]{:S(2)}) collective-permute-start(bf16[864,128]{1,0:T(8,128)(2,1)S(1)} %bitcast.117), channel_id=1, source_target_pairs={{0,192},{64,0},{128,64},{192,128},{1,193},{65,1},{129,65},{193,129... | collective-permute-start | bytes 663560 | tf_op jit(solution)/shard_map/ppermute | solution.py:55
  37.9 8.1 %collective-permute-start.8 = (bf16[864,128]{1,0:T(8,128)(2,1)S(1)}, bf16[864,128]{1,0:T(8,128)(2,1)S(1)}, u32[]{:S(2)}, u32[]{:S(2)}) collective-permute-start(bf16[864,128]{1,0:T(8,128)(2,1)S(1)} %bitcast.118), channel_id=1, source_target_pairs={{0,64},{64,128},{128,192},{192,0},{1,65},{65,129},{129,193},{193,1... | collective-permute-start | bytes 663560 | tf_op jit(solution)/shard_map/ppermute | solution.py:55
  38.7 7.3 %copy-start.8 = (bf16[128]{0:T(256)(128)(2,1)S(1)}, bf16[128]{0:T(256)(128)(2,1)}, u32[]{:S(2)}) copy-start(bf16[128]{0:T(256)(128)(2,1)} %param.14) | copy-start | bytes 772
  51.8 17.4 %copy-start.4 = (bf16[256,256]{1,0:T(8,128)(2,1)S(1)}, bf16[256,256]{1,0:T(8,128)(2,1)}, u32[]{:S(2)}) copy-start(bf16[256,256]{1,0:T(8,128)(2,1)} %constant.89.clone.along_z_ref) | copy-start | bytes 393220
  51.8 17.4 %copy-start.7 = (bf16[128,128]{1,0:T(8,128)(2,1)S(1)}, bf16[128,128]{1,0:T(8,128)(2,1)}, u32[]{:S(2)}) copy-start(bf16[128,128]{1,0:T(8,128)(2,1)} %constant.90.clone.along_x_ref) | copy-start | bytes 98308
  52.0 53.6 %copy-start.3 = (bf16[256,256]{1,0:T(8,128)(2,1)S(1)}, bf16[256,256]{1,0:T(8,128)(2,1)}, u32[]{:S(2)}) copy-start(bf16[256,256]{1,0:T(8,128)(2,1)} %constant.91.clone.into_ref) | copy-start | bytes 393220
  52.1 9.2 %collective-permute-start.10 = (bf16[256,128]{1,0:T(8,128)(2,1)S(1)}, bf16[256,128]{1,0:T(8,128)(2,1)S(1)}, u32[]{:S(2)}, u32[]{:S(2)}) collective-permute-start(bf16[256,128]{1,0:T(8,128)(2,1)S(1)} %bitcast.126), channel_id=1, source_target_pairs={{0,1},{1,2},{2,3},{3,0},{4,5},{5,6},{6,7},{7,4},{8,9},{9,10},{10,1... | collective-permute-start | bytes 196616 | tf_op jit(solution)/shard_map/ppermute | solution.py:55
  53.5 7.8 %collective-permute-start.11 = (bf16[256,128]{1,0:T(8,128)(2,1)S(1)}, bf16[256,128]{1,0:T(8,128)(2,1)S(1)}, u32[]{:S(2)}, u32[]{:S(2)}) collective-permute-start(bf16[256,128]{1,0:T(8,128)(2,1)S(1)} %bitcast.125), channel_id=1, source_target_pairs={{0,3},{1,0},{2,1},{3,2},{4,7},{5,4},{6,5},{7,6},{8,11},{9,8},{10,9... | collective-permute-start | bytes 196616 | tf_op jit(solution)/shard_map/ppermute | solution.py:55
  54.2 15.0 %all-to-all-start = ((bf16[16,16,128]{2,1,0:T(8,128)(2,1)}), bf16[16,16,128]{2,1,0:T(8,128)(2,1)S(1)}, u32[]{:S(2)}, u32[]{:S(2)}) async-start(bf16[16,16,128]{2,1,0:T(8,128)(2,1)} %get-tuple-element.25), calls=%async_computation | async-start | bytes 131072 | tf_op jit(solution)/shard_map/all_to_all | solution.py:794
  61.3 51.5 %collective-permute-start.12 = (bf16[1536,128]{1,0:T(8,128)(2,1)S(1)}, bf16[1536,128]{1,0:T(8,128)(2,1)S(1)}, u32[]{:S(2)}, u32[]{:S(2)}) collective-permute-start(bf16[1536,128]{1,0:T(8,128)(2,1)S(1)} %bitcast.113), channel_id=1, source_target_pairs={{0,4},{4,8},{8,12},{12,16},{16,20},{20,24},{24,28},{28,32},{32,36}... | collective-permute-start | bytes 1179656 | tf_op jit(solution)/shard_map/ppermute | solution.py:55
  61.4 51.4 %collective-permute-start.13 = (bf16[1536,128]{1,0:T(8,128)(2,1)S(1)}, bf16[1536,128]{1,0:T(8,128)(2,1)}, u32[]{:S(2)}, u32[]{:S(2)}) collective-permute-start(bf16[1536,128]{1,0:T(8,128)(2,1)S(1)} %bitcast.114), channel_id=1, source_target_pairs={{0,60},{4,0},{8,4},{12,8},{16,12},{20,16},{24,20},{28,24},{32,28},... | collective-permute-start | bytes 1179656 | tf_op jit(solution)/shard_map/ppermute | solution.py:55
  70.3 35.3 %all-to-all-start.1 = ((f32[256,1,128]{2,1,0:T(1,128)}), f32[256,1,128]{2,1,0:T(1,128)S(1)}, u32[]{:S(2)}, u32[]{:S(2)}) async-start(f32[256,1,128]{2,1,0:T(1,128)} %bitcast.34), calls=%async_computation.1 | async-start | bytes 262144 | tf_op jit(solution)/shard_map/all_to_all | solution.py:794
  106.7 21.5 %all-to-all-start.2 = ((f32[256,2,128]{2,1,0:T(2,128)}), f32[256,2,128]{2,1,0:T(2,128)S(1)}, u32[]{:S(2)}, u32[]{:S(2)}) async-start(f32[256,2,128]{2,1,0:T(2,128)} %bitcast.36), calls=%async_computation.2 | async-start | bytes 524288 | tf_op jit(solution)/shard_map/all_to_all | solution.py:794
  114.1 14.1 %copy-start.2 = (bf16[256,512]{1,0:T(8,128)(2,1)S(1)}, bf16[256,512]{1,0:T(8,128)(2,1)}, u32[]{:S(2)}) copy-start(bf16[256,512]{1,0:T(8,128)(2,1)} %constant.93.clone.along_z_ref) | copy-start | bytes 786436
  114.1 14.1 %copy-start.5 = (bf16[256,128]{1,0:T(8,128)(2,1)S(1)}, bf16[256,128]{1,0:T(8,128)(2,1)}, u32[]{:S(2)}) copy-start(bf16[256,128]{1,0:T(8,128)(2,1)} %constant.92.clone.along_x_ref) | copy-start | bytes 196612
  115.2 19.1 %collective-permute-start.14 = (bf16[2304,128]{1,0:T(8,128)(2,1)}, bf16[2304,128]{1,0:T(8,128)(2,1)S(1)}, u32[]{:S(2)}, u32[]{:S(2)}) collective-permute-start(bf16[2304,128]{1,0:T(8,128)(2,1)} %bitcast.48), channel_id=1, source_target_pairs={{0,64},{64,128},{128,192},{192,0},{1,65},{65,129},{129,193},{193,1... | collective-permute-start | bytes 1769480 | tf_op jit(solution)/shard_map/ppermute | solution.py:55
  116.7 17.6 %collective-permute-start.15 = (bf16[2304,128]{1,0:T(8,128)(2,1)}, bf16[2304,128]{1,0:T(8,128)(2,1)S(1)}, u32[]{:S(2)}, u32[]{:S(2)}) collective-permute-start(bf16[2304,128]{1,0:T(8,128)(2,1)} %bitcast.50), channel_id=1, source_target_pairs={{0,192},{64,0},{128,64},{192,128},{1,193},{65,1},{129,65},{193,129... | collective-permute-start | bytes 1769480 | tf_op jit(solution)/shard_map/ppermute | solution.py:55
  129.2 14.2 %all-to-all-start.3 = ((bf16[16,64,128]{2,1,0:T(8,128)(2,1)}), bf16[16,64,128]{2,1,0:T(8,128)(2,1)S(1)}, u32[]{:S(2)}, u32[]{:S(2)}) async-start(bf16[16,64,128]{2,1,0:T(8,128)(2,1)} %bitcast.38), calls=%async_computation.3 | async-start | bytes 524288 | tf_op jit(solution)/shard_map/all_to_all | solution.py:794
  146.1 9.2 %collective-permute-start.16 = (f32[24,128]{1,0:T(8,128)S(1)}, f32[24,128]{1,0:T(8,128)S(1)}, u32[]{:S(2)}, u32[]{:S(2)}) collective-permute-start(f32[24,128]{1,0:T(8,128)S(1)} %get-tuple-element.31.potential_ref), channel_id=1, source_target_pairs={{0,60},{4,8},{8,4},{12,16},{16,12},{20,24},{24,20},{28,32},{32,28}... | collective-permute-start | bytes 36872 | tf_op jit(solution)/shard_map/ppermute | solution.py:63
  146.2 9.1 %collective-permute-start.17 = (f32[24,128]{1,0:T(8,128)S(1)}, f32[24,128]{1,0:T(8,128)S(1)}, u32[]{:S(2)}, u32[]{:S(2)}) collective-permute-start(f32[24,128]{1,0:T(8,128)S(1)} %get-tuple-element.31.potential_ref), channel_id=1, source_target_pairs={{0,4},{4,0},{8,12},{12,8},{16,20},{20,16},{24,28},{28,24},{32,36},... | collective-permute-start | bytes 36872 | tf_op jit(solution)/shard_map/ppermute | solution.py:63
  147.7 7.6 %copy-start.6 = (bf16[128,128]{1,0:T(8,128)(2,1)S(1)}, bf16[128,128]{1,0:T(8,128)(2,1)}, u32[]{:S(2)}) copy-start(bf16[128,128]{1,0:T(8,128)(2,1)} %msg_ref.1) | copy-start | bytes 98308

commit v7 on v4

--- a/solution.py
+++ b/solution.py
@@ -53,6 +53,13 @@
     count = lax.axis_size(axis)
     pairs = [(i, (i + step) % count) for i in range(count)]
     return lax.ppermute(value.reshape(-1, 128), axis, pairs).reshape(value.shape)
+
+
+def partners(value):
+    count = lax.axis_size("gy")
+    across = [(i, (i + 1 if i % 2 else i - 1) % count) for i in range(count)]
+    within = [(i, i ^ 1) for i in range(count)]
+    return [lax.ppermute(value, "gy", pairs) for pairs in (across, within)]
 
 
 def late_halo(own):
@@ -678,11 +685,12 @@
 
 
 def backward_kernel(
-    weight_ref, slope_ref, part_ref, own_ref, below_ref, above_ref, msg_ref, self_ref, out_ref,
-    near_ref, total_ref, potential_ref
+    weight_ref, slope_ref, part_ref, own_ref, across_ref, within_ref, side_ref, msg_ref, self_ref,
+    out_ref, near_ref, total_ref, potential_ref
 ):
-    potential_ref[0] = below_ref[...]
-    potential_ref[1] = above_ref[...]
+    even = jnp.broadcast_to(side_ref[...], (24, 128)) > 0.0
+    potential_ref[0] = jnp.where(even, across_ref[...], within_ref[...])
+    potential_ref[1] = jnp.where(even, within_ref[...], across_ref[...])
 
     def scale(side, carry):
         columns = jnp.transpose(potential_ref[side])
@@ -719,10 +727,10 @@
     lax.fori_loop(0, 2, finish, 0)
 
 
-def backward(weights, slope, part, own, below, above, msg_weight, self_weight):
+def backward(weights, slope, part, own, across, within, side, msg_weight, self_weight):
     return pl.pallas_call(
         backward_kernel,
-        in_specs=[VM] * 8,
+        in_specs=[VM] * 9,
         out_specs=VM,
         out_shape=jax.ShapeDtypeStruct((2, 4, 128, 128), f32),
         scratch_shapes=[
@@ -735,7 +743,7 @@
         ),
         compiler_params=SMALL,
         name="backward",
-    )(weights, slope, part, own, below, above, msg_weight, self_weight)
+    )(weights, slope, part, own, across, within, side, msg_weight, self_weight)
 
 
 def wave_tables(size_x, size_y, size_z):
@@ -816,9 +824,12 @@
     potential, atom_potential, own_weights, slopes = interpolate(
         field, row_place.reshape(24, 8, slots), weights, slope_near, coupling / volume
     )
-    below, above = moved(potential, "gy", 1), moved(potential, "gy", -1)
+    across, within = partners(potential)
+    side = jnp.full((1, slots), 1 - 2 * (lax.axis_index("gy") % 2), f32)
     weights, total, cotangent = beside(weights, own_weights, slopes, potential)
-    grad = backward(weights, slopes, total, cotangent, below, above, msg_weight, self_weight)
+    grad = backward(
+        weights, slopes, total, cotangent, across, within, side, msg_weight, self_weight
+    )
     return (
         grad.reshape(features.shape),
         atom_potential.reshape(cells_x, cells_y, cells_z, slots),

time: 159 us -> 157 us (0.987)
  starting transfers between devices: 80 us -> 73.8 us
  waiting for transfers between devices: 40.1 us -> 44.3 us
    ppermute x18 -> x16, starting transfers between devices: 42.9 us -> 35.1 us  [moved(): lax.ppermute(value.reshape(-1, 128), axis, pairs).reshape(value.shape)]
    ppermute x0 -> x2, waiting for transfers between devices: none -> 4.22 us  [partners(): return [lax.ppermute(value, 'gy', pairs) for pairs in (across, within)]]
    ppermute x18 -> x16, waiting for transfers between devices: 7.62 us -> 7.62 us  [moved(): lax.ppermute(value.reshape(-1, 128), axis, pairs).reshape(value.shape)]
  transfers between devices with their start and end apart: 22 -> 22, of which waited for: 7 -> 8; matrix products, arithmetic and copies ran while one was open for 3% -> 3% of each run, Pallas kernels for 11% -> 11%
where the time goes in v7:
time: 157 us; the launch traced here: 156 us
  starting transfers between devices  73.8 us (47%)
  waiting for transfers between devices  44.3 us (28%)
  Pallas kernels  33.1 us (21%)
  local copies, waits for them, and re-layouts  3.65 us (2%)
    all_to_all x4, starting transfers between devices, swapped(): return lax.all_to_all(value, axis, split_axis=0, concat_axis=0, tiled=True)  37.1 us
    ppermute x16, starting transfers between devices, moved(): lax.ppermute(value.reshape(-1, 128), axis, pairs).reshape(value.shape)  35.1 us
    all_to_all x4, waiting for transfers between devices, swapped(): return lax.all_to_all(value, axis, split_axis=0, concat_axis=0, tiled=True)  32.5 us
    ppermute x16, waiting for transfers between devices, moved(): lax.ppermute(value.reshape(-1, 128), axis, pairs).reshape(value.shape)  7.62 us
    pallas_call x1, Pallas kernels, message_layer(): pl.pallas_call(message_kernel, in_specs=[VM] * 11 + [ANY], out_specs=[ANY...  5.74 us
    pallas_call x1, Pallas kernels, inside_pairs(): pl.pallas_call(inside_kernel, in_specs=[VM] * 5, out_specs=[ANY, VM], out...  5.71 us
    pallas_call x1, Pallas kernels, ends_pairs(): pl.pallas_call(ends_kernel, in_specs=[VM] * 6 + [ANY], out_specs=[ANY, VM...  5.57 us
    pallas_call x1, Pallas kernels, backward(): pl.pallas_call(backward_kernel, in_specs=[VM] * 9, out_specs=VM, out_shap...  4.72 us
  transfers between devices with their start and end apart: 22, of which 8 were waited for; matrix products, arithmetic and copies ran while one was open for 3% of the time, Pallas kernels for 11%

profile of v7, /device:TPU:32, one launch (start us, length us, event | category | flops | bytes accessed | tf_op | source)
XLA Modules:
  0.0 156.3 jit_solution(719158719796443530)
XLA Ops:
  0.6 1.9 %project.1 = bf16[8,144,128]{2,1,0:T(8,128)(2,1)} custom-call(bf16[8,128,128]{2,1,0:T(8,128)(2,1)} %bitcast.93, bf16[128,128]{1,0:T(8,128)(2,1)} %msg_ref.1, s32[2,1,3,4,128]{4,3,2,1,0:T(4,128)} %bitcast.127, f32[2,1,3,4,128]{4,3,2,1,0:T(4,128)} %bitcast.128), custom_call_target="tpu_custom_call" | custom-call | tf_op jit(solution)/shard_map/project/pallas_call | solution.py:106
  2.5 0.1 collective-permute-start
  2.6 8.0 %collective-permute-start.1 = (bf16[1152,128]{1,0:T(8,128)(2,1)}, bf16[1152,128]{1,0:T(8,128)(2,1)S(1)}, u32[]{:S(2)}, u32[]{:S(2)}) collective-permute-start(bf16[1152,128]{1,0:T(8,128)(2,1)} %bitcast.76), channel_id=1, source_target_pairs={{0,60},{4,0},{8,4},{12,8},{16,12},{20,16},{24,20},{28,24},{32,28},... | collective-permute-start | bytes 884744 | tf_op jit(solution)/shard_map/ppermute | solution.py:55
  10.6 1.0 fusion.10
  11.6 1.7 %collective-permute-start.4 = (bf16[576,128]{1,0:T(8,128)(2,1)S(1)}, bf16[576,128]{1,0:T(8,128)(2,1)S(1)}, u32[]{:S(2)}, u32[]{:S(2)}) collective-permute-start(bf16[576,128]{1,0:T(8,128)(2,1)S(1)} %bitcast.122), channel_id=1, source_target_pairs={{0,64},{64,128},{128,192},{192,0},{1,65},{65,129},{129,193},{193,1... | collective-permute-start | bytes 442376 | tf_op jit(solution)/shard_map/ppermute | solution.py:55
  13.3 1.7 %collective-permute-start.5 = (bf16[576,128]{1,0:T(8,128)(2,1)S(1)}, bf16[576,128]{1,0:T(8,128)(2,1)S(1)}, u32[]{:S(2)}, u32[]{:S(2)}) collective-permute-start(bf16[576,128]{1,0:T(8,128)(2,1)S(1)} %bitcast.121), channel_id=1, source_target_pairs={{0,192},{64,0},{128,64},{192,128},{1,193},{65,1},{129,65},{193,129... | collective-permute-start | bytes 442376 | tf_op jit(solution)/shard_map/ppermute | solution.py:55
  15.0 0.9 slice_bitcast_fusion.1
  15.9 2.6 %collective-permute-done = bf16[1152,128]{1,0:T(8,128)(2,1)S(1)} collective-permute-done((bf16[1152,128]{1,0:T(8,128)(2,1)}, bf16[1152,128]{1,0:T(8,128)(2,1)S(1)}, u32[]{:S(2)}, u32[]{:S(2)}) %collective-permute-start) | collective-permute-done | bytes 294944 | tf_op jit(solution)/shard_map/ppermute | solution.py:55
  18.5 2.5 %collective-permute-done.1 = bf16[1152,128]{1,0:T(8,128)(2,1)S(1)} collective-permute-done((bf16[1152,128]{1,0:T(8,128)(2,1)}, bf16[1152,128]{1,0:T(8,128)(2,1)S(1)}, u32[]{:S(2)}, u32[]{:S(2)}) %collective-permute-start.1) | collective-permute-done | bytes 294944 | tf_op jit(solution)/shard_map/ppermute | solution.py:55
  21.0 2.5 %collective-permute-start.3 = (bf16[864,128]{1,0:T(8,128)(2,1)S(1)}, bf16[864,128]{1,0:T(8,128)(2,1)S(1)}, u32[]{:S(2)}, u32[]{:S(2)}) collective-permute-start(bf16[864,128]{1,0:T(8,128)(2,1)S(1)} %bitcast.120), channel_id=1, source_target_pairs={{0,3},{1,0},{2,1},{3,2},{4,7},{5,4},{6,5},{7,6},{8,11},{9,8},{10,9... | collective-permute-start | bytes 663560 | tf_op jit(solution)/shard_map/ppermute | solution.py:55
  23.5 0.1 collective-permute-start.2
  23.7 5.7 %inside_pairs.1 = (bf16[6,8,128,768]{3,2,1,0:T(8,128)(2,1)}, f32[2,4,128,128]{3,2,1,0:T(8,128)S(1)}) custom-call(bf16[2,4,144,128]{3,2,1,0:T(8,128)(2,1)S(1)} %bitcast.78, bf16[2,4,144,128]{3,2,1,0:T(8,128)(2,1)S(1)} %bitcast.83, bf16[2,4,144,128]{3,2,1,0:T(8,128)(2,1)S(1)} %bitcast.87, bf16[8,128,128]{2,1,0:T(8,128)(2,1)S(1)} %bitcast.94, ...), custom_call_target="tpu_custom_call" | custom-call | flops 5000000000 | bytes 9000000 | tf_op jit(solution)/shard_map/inside_pairs/pallas_call | solution.py:232
  29.4 0.1 pad_maximum_fusion.2
  29.4 1.6 %collective-permute-start.6 = (bf16[1152,128]{1,0:T(8,128)(2,1)S(1)}, bf16[1152,128]{1,0:T(8,128)(2,1)S(1)}, u32[]{:S(2)}, u32[]{:S(2)}) collective-permute-start(bf16[1152,128]{1,0:T(8,128)(2,1)S(1)} %bitcast.116), channel_id=1, source_target_pairs={{0,64},{64,128},{128,192},{192,0},{1,65},{65,129},{129,193},{193,1... | collective-permute-start | bytes 884744 | tf_op jit(solution)/shard_map/ppermute | solution.py:55
  31.1 0.0 collective-permute-done.3
  31.1 1.7 %collective-permute-start.7 = (bf16[1152,128]{1,0:T(8,128)(2,1)S(1)}, bf16[1152,128]{1,0:T(8,128)(2,1)S(1)}, u32[]{:S(2)}, u32[]{:S(2)}) collective-permute-start(bf16[1152,128]{1,0:T(8,128)(2,1)S(1)} %bitcast.115), channel_id=1, source_target_pairs={{0,192},{64,0},{128,64},{192,128},{1,193},{65,1},{129,65},{193,129... | collective-permute-start | bytes 884744 | tf_op jit(solution)/shard_map/ppermute | solution.py:55
  32.8 1.1 collective-permute-done.2
  34.0 1.7 %collective-permute-start.8 = (bf16[864,128]{1,0:T(8,128)(2,1)S(1)}, bf16[864,128]{1,0:T(8,128)(2,1)S(1)}, u32[]{:S(2)}, u32[]{:S(2)}) collective-permute-start(bf16[864,128]{1,0:T(8,128)(2,1)S(1)} %bitcast.117), channel_id=1, source_target_pairs={{0,64},{64,128},{128,192},{192,0},{1,65},{65,129},{129,193},{193,1... | collective-permute-start | bytes 663560 | tf_op jit(solution)/shard_map/ppermute | solution.py:55
  35.7 0.0 collective-permute-done.4
  35.7 1.9 %collective-permute-start.9 = (bf16[864,128]{1,0:T(8,128)(2,1)S(1)}, bf16[864,128]{1,0:T(8,128)(2,1)S(1)}, u32[]{:S(2)}, u32[]{:S(2)}) collective-permute-start(bf16[864,128]{1,0:T(8,128)(2,1)S(1)} %bitcast.118), channel_id=1, source_target_pairs={{0,192},{64,0},{128,64},{192,128},{1,193},{65,1},{129,65},{193,129... | collective-permute-start | bytes 663560 | tf_op jit(solution)/shard_map/ppermute | solution.py:55
  37.6 5.6 %ends_pairs.1 = (bf16[6,8,128,768]{3,2,1,0:T(8,128)(2,1)}, f32[2,4,128,128]{3,2,1,0:T(8,128)S(1)}) custom-call(bf16[2,4,144,128]{3,2,1,0:T(8,128)(2,1)S(1)} %bitcast.79, bf16[2,4,144,128]{3,2,1,0:T(8,128)(2,1)S(1)} %bitcast.85, bf16[2,4,144,128]{3,2,1,0:T(8,128)(2,1)S(1)} %bitcast.89, ...), custom_call_target="tpu_custom_call", output_to_operand_aliasing={{0}: (6, {})} | custom-call | flops 6000000000 | bytes 9000000 | tf_op jit(solution)/shard_map/ends_pairs/pallas_call | solution.py:300
  43.2 0.0 collective-permute-done.5
  43.2 0.0 collective-permute-done.6
  43.2 0.0 collective-permute-done.7
  43.2 1.4 collective-permute-done.8
  44.6 0.0 collective-permute-done.9
  44.6 5.7 %message.1 = (bf16[6,8,128,768]{3,2,1,0:T(8,128)(2,1)}, f32[2,4,128,128]{3,2,1,0:T(8,128)S(1)}, bf16[16,16,128]{2,1,0:T(8,128)(2,1)}, f32[4,6,8,128]{3,2,1,0:T(8,128)S(1)}) custom-call(bf16[2,4,144,128]{3,2,1,0:T(8,128)(2,1)S(1)} %bitcast.80, bf16[3,2,1,144,128]{4,3,2,1,0:T(8,128)(2,1)S(1)} %bitcast.101, ...), custom_call_target="tpu_custom_call", output_to_operand_aliasing={{0}: (11, {})} | custom-call | flops 5000000000 | bytes 6000000 | tf_op jit(solution)/shard_map/message/pallas_call | solution.py:417
  50.3 0.0 copy-start.4
  50.3 0.0 copy-start.7
  50.4 0.2 slope.1
  50.6 0.0 copy-start.3
  50.6 2.4 %collective-permute-start.10 = (bf16[256,128]{1,0:T(8,128)(2,1)S(1)}, bf16[256,128]{1,0:T(8,128)(2,1)S(1)}, u32[]{:S(2)}, u32[]{:S(2)}) collective-permute-start(bf16[256,128]{1,0:T(8,128)(2,1)S(1)} %bitcast.126), channel_id=1, source_target_pairs={{0,1},{1,2},{2,3},{3,0},{4,5},{5,6},{6,7},{7,4},{8,9},{9,10},{10,1... | collective-permute-start | bytes 196616 | tf_op jit(solution)/shard_map/ppermute | solution.py:55
  53.0 0.8 collective-permute-start.11
  53.8 7.9 %all-to-all-start = ((bf16[16,16,128]{2,1,0:T(8,128)(2,1)}), bf16[16,16,128]{2,1,0:T(8,128)(2,1)S(1)}, u32[]{:S(2)}, u32[]{:S(2)}) async-start(bf16[16,16,128]{2,1,0:T(8,128)(2,1)} %get-tuple-element.25), calls=%async_computation | async-start | bytes 131072 | tf_op jit(solution)/shard_map/all_to_all | solution.py:791
  61.7 0.0 collective-permute-done.11
  61.7 0.1 fusion.8
  61.8 0.1 collective-permute-start.12
  61.9 7.7 %collective-permute-start.13 = (bf16[1536,128]{1,0:T(8,128)(2,1)S(1)}, bf16[1536,128]{1,0:T(8,128)(2,1)S(1)}, u32[]{:S(2)}, u32[]{:S(2)}) collective-permute-start(bf16[1536,128]{1,0:T(8,128)(2,1)S(1)} %bitcast.114), channel_id=1, source_target_pairs={{0,60},{4,0},{8,4},{12,8},{16,12},{20,16},{24,20},{28,24},{32,28},... | collective-permute-start | bytes 1179656 | tf_op jit(solution)/shard_map/ppermute | solution.py:55
  69.7 0.0 all-to-all-done
  69.7 1.0 forward_xz.1
  70.7 18.4 %all-to-all-start.1 = ((f32[256,1,128]{2,1,0:T(1,128)}), f32[256,1,128]{2,1,0:T(1,128)S(1)}, u32[]{:S(2)}, u32[]{:S(2)}) async-start(f32[256,1,128]{2,1,0:T(1,128)} %bitcast.34), calls=%async_computation.1 | async-start | bytes 262144 | tf_op jit(solution)/shard_map/all_to_all | solution.py:791
  89.2 0.1 fusion.1.influence_ref
  89.3 12.6 %all-to-all-done.1 = f32[256,1,128]{2,1,0:T(1,128)S(1)} async-done(((f32[256,1,128]{2,1,0:T(1,128)}), f32[256,1,128]{2,1,0:T(1,128)S(1)}, u32[]{:S(2)}, u32[]{:S(2)}) %all-to-all-start.1) | async-done | bytes 131104 | tf_op jit(solution)/shard_map/all_to_all | solution.py:791
  101.8 1.1 filter_y.1
  102.9 6.2 %all-to-all-start.2 = ((f32[256,2,128]{2,1,0:T(2,128)}), f32[256,2,128]{2,1,0:T(2,128)S(1)}, u32[]{:S(2)}, u32[]{:S(2)}) async-start(f32[256,2,128]{2,1,0:T(2,128)} %bitcast.36), calls=%async_computation.2 | async-start | bytes 524288 | tf_op jit(solution)/shard_map/all_to_all | solution.py:791
  109.1 0.0 collective-permute-done.12
  109.1 0.0 collective-permute-done.13
  109.1 0.1 pad_maximum_fusion.rows_ref
  109.3 0.0 copy-start.2
  109.3 0.0 copy-start.5
  109.3 1.1 fusion.9
  110.4 1.5 collective-permute-start.14
  111.9 1.7 %collective-permute-start.15 = (bf16[2304,128]{1,0:T(8,128)(2,1)}, bf16[2304,128]{1,0:T(8,128)(2,1)S(1)}, u32[]{:S(2)}, u32[]{:S(2)}) collective-permute-start(bf16[2304,128]{1,0:T(8,128)(2,1)} %bitcast.50), channel_id=1, source_target_pairs={{0,192},{64,0},{128,64},{192,128},{1,193},{65,1},{129,65},{193,129... | collective-permute-start | bytes 1769480 | tf_op jit(solution)/shard_map/ppermute | solution.py:55
  113.6 10.8 %all-to-all-done.2 = f32[256,2,128]{2,1,0:T(2,128)S(1)} async-done(((f32[256,2,128]{2,1,0:T(2,128)}), f32[256,2,128]{2,1,0:T(2,128)S(1)}, u32[]{:S(2)}, u32[]{:S(2)}) %all-to-all-start.2) | async-done | bytes 262176 | tf_op jit(solution)/shard_map/all_to_all | solution.py:791
  124.4 1.0 inverse_xz.1
  125.5 4.6 %all-to-all-start.3 = ((bf16[16,64,128]{2,1,0:T(8,128)(2,1)}), bf16[16,64,128]{2,1,0:T(8,128)(2,1)S(1)}, u32[]{:S(2)}, u32[]{:S(2)}) async-start(bf16[16,64,128]{2,1,0:T(8,128)(2,1)} %bitcast.38), calls=%async_computation.3 | async-start | bytes 524288 | tf_op jit(solution)/shard_map/all_to_all | solution.py:791
  130.1 0.5 slice.77
  130.6 9.1 %all-to-all-done.3.field_ref = bf16[16,64,128]{2,1,0:T(8,128)(2,1)S(1)} async-done(((bf16[16,64,128]{2,1,0:T(8,128)(2,1)}), bf16[16,64,128]{2,1,0:T(8,128)(2,1)S(1)}, u32[]{:S(2)}, u32[]{:S(2)}) %all-to-all-start.3) | async-done | bytes 262176 | tf_op jit(solution)/shard_map/all_to_all | solution.py:791
  139.7 2.7 %interpolate.1 = (f32[24,128]{1,0:T(8,128)S(1)}, f32[8,128]{1,0:T(8,128)}, bf16[6,8,128,256]{3,2,1,0:T(8,128)(2,1)S(1)}, bf16[3,4,6,128,128]{4,3,2,1,0:T(8,128)(2,1)S(1)}) custom-call(bf16[16,64,128]{2,1,0:T(8,128)(2,1)S(1)} %all-to-all-done.3.field_ref, f32[24,8,128]{2,1,0:T(8,128)S(1)} %bitcast.102, bf16[6,8,128,768]{3,2,1,0:T(8,128)(2,1)} %get-tuple-element.24.stored_ref, ...), custom_call_target="tpu_custom_call" | custom-call | flops 201326592 | bytes 400000 | tf_op jit(solution)/shard_map/interpolate/pallas_call | solution.py:605
  142.4 0.1 collective-permute-start.16
  142.5 1.5 collective-permute-start.17
  144.0 3.4 %beside.1 = (bf16[6,8,128,512]{3,2,1,0:T(8,128)(2,1)S(1)}, f32[2,4,128,128]{3,2,1,0:T(8,128)S(1)}, bf16[2,4,128,128]{3,2,1,0:T(8,128)(2,1)S(1)}) custom-call(bf16[6,8,128,768]{3,2,1,0:T(8,128)(2,1)} %get-tuple-element.24.stored_ref, bf16[6,8,128,256]{3,2,1,0:T(8,128)(2,1)S(1)} %get-tuple-element.29.weight_ref, ...), custom_call_target="tpu_custom_call" | custom-call | flops 3000000000 | bytes 12000000 | tf_op jit(solution)/shard_map/beside/pallas_call | solution.py:666
  147.4 4.2 %collective-permute-done.16.across_ref = f32[24,128]{1,0:T(8,128)S(1)} collective-permute-done((f32[24,128]{1,0:T(8,128)S(1)}, f32[24,128]{1,0:T(8,128)S(1)}, u32[]{:S(2)}, u32[]{:S(2)}) %collective-permute-start.16) | collective-permute-done | bytes 12320 | tf_op jit(solution)/shard_map/ppermute | solution.py:62
  151.6 4.7 %backward.1 = f32[2,4,128,128]{3,2,1,0:T(8,128)} custom-call(bf16[6,8,128,512]{3,2,1,0:T(8,128)(2,1)S(1)} %get-tuple-element.32.weight_ref, bf16[3,4,6,128,128]{4,3,2,1,0:T(8,128)(2,1)S(1)} %get-tuple-element.30.slope_ref, f32[2,4,128,128]{3,2,1,0:T(8,128)S(1)} %get-tuple-element.33.part_ref, bf16[2,4,128,128]{3,2,1,0:T(8,128)(2,1)S(1)} %get-tuple-element.34.own_ref, ...), custom_call_target="tpu_custom_call" | custom-call | flops 4000000000 | bytes 12000000 | tf_op jit(solution)/shard_map/backward/pallas_call | solution.py:731
  (31 shorter events, 0.2 us)
Async XLA Ops:
  2.5 21.1 %copy-start = (bf16[8,144,128]{2,1,0:T(8,128)(2,1)S(1)}, bf16[8,144,128]{2,1,0:T(8,128)(2,1)}, u32[]{:S(2)}) copy-start(bf16[8,144,128]{2,1,0:T(8,128)(2,1)} %project.1) | copy-start | bytes 884740
  2.5 21.1 %copy-start.1 = (bf16[2,1,4,128,128]{4,3,2,1,0:T(8,128)(2,1)S(1)}, bf16[2,1,4,128,128]{4,3,2,1,0:T(8,128)(2,1)}, u32[]{:S(2)}) copy-start(bf16[2,1,4,128,128]{4,3,2,1,0:T(8,128)(2,1)} %param.11) | copy-start | bytes 786436
  2.5 21.1 %copy-start.9 = (bf16[128,128]{1,0:T(8,128)(2,1)S(1)}, bf16[128,128]{1,0:T(8,128)(2,1)}, u32[]{:S(2)}) copy-start(bf16[128,128]{1,0:T(8,128)(2,1)} %self_ref.3) | copy-start | bytes 98308
  2.5 15.9 %collective-permute-start = (bf16[1152,128]{1,0:T(8,128)(2,1)}, bf16[1152,128]{1,0:T(8,128)(2,1)S(1)}, u32[]{:S(2)}, u32[]{:S(2)}) collective-permute-start(bf16[1152,128]{1,0:T(8,128)(2,1)} %bitcast.75), channel_id=1, source_target_pairs={{0,4},{4,8},{8,12},{12,16},{16,20},{20,24},{24,28},{28,32},{32,36}... | collective-permute-start | bytes 884744 | tf_op jit(solution)/shard_map/ppermute | solution.py:55
  2.6 18.3 %collective-permute-start.1 = (bf16[1152,128]{1,0:T(8,128)(2,1)}, bf16[1152,128]{1,0:T(8,128)(2,1)S(1)}, u32[]{:S(2)}, u32[]{:S(2)}) collective-permute-start(bf16[1152,128]{1,0:T(8,128)(2,1)} %bitcast.76), channel_id=1, source_target_pairs={{0,60},{4,0},{8,4},{12,8},{16,12},{20,16},{24,20},{28,24},{32,28},... | collective-permute-start | bytes 884744 | tf_op jit(solution)/shard_map/ppermute | solution.py:55
  11.6 24.0 %collective-permute-start.4 = (bf16[576,128]{1,0:T(8,128)(2,1)S(1)}, bf16[576,128]{1,0:T(8,128)(2,1)S(1)}, u32[]{:S(2)}, u32[]{:S(2)}) collective-permute-start(bf16[576,128]{1,0:T(8,128)(2,1)S(1)} %bitcast.122), channel_id=1, source_target_pairs={{0,64},{64,128},{128,192},{192,0},{1,65},{65,129},{129,193},{193,1... | collective-permute-start | bytes 442376 | tf_op jit(solution)/shard_map/ppermute | solution.py:55
  13.3 29.9 %collective-permute-start.5 = (bf16[576,128]{1,0:T(8,128)(2,1)S(1)}, bf16[576,128]{1,0:T(8,128)(2,1)S(1)}, u32[]{:S(2)}, u32[]{:S(2)}) collective-permute-start(bf16[576,128]{1,0:T(8,128)(2,1)S(1)} %bitcast.121), channel_id=1, source_target_pairs={{0,192},{64,0},{128,64},{192,128},{1,193},{65,1},{129,65},{193,129... | collective-permute-start | bytes 442376 | tf_op jit(solution)/shard_map/ppermute | solution.py:55
  21.0 10.1 %collective-permute-start.3 = (bf16[864,128]{1,0:T(8,128)(2,1)S(1)}, bf16[864,128]{1,0:T(8,128)(2,1)S(1)}, u32[]{:S(2)}, u32[]{:S(2)}) collective-permute-start(bf16[864,128]{1,0:T(8,128)(2,1)S(1)} %bitcast.120), channel_id=1, source_target_pairs={{0,3},{1,0},{2,1},{3,2},{4,7},{5,4},{6,5},{7,6},{8,11},{9,8},{10,9... | collective-permute-start | bytes 663560 | tf_op jit(solution)/shard_map/ppermute | solution.py:55
  23.5 10.4 %collective-permute-start.2 = (bf16[864,128]{1,0:T(8,128)(2,1)S(1)}, bf16[864,128]{1,0:T(8,128)(2,1)S(1)}, u32[]{:S(2)}, u32[]{:S(2)}) collective-permute-start(bf16[864,128]{1,0:T(8,128)(2,1)S(1)} %bitcast.119), channel_id=1, source_target_pairs={{0,1},{1,2},{2,3},{3,0},{4,5},{5,6},{6,7},{7,4},{8,9},{9,10},{10,1... | collective-permute-start | bytes 663560 | tf_op jit(solution)/shard_map/ppermute | solution.py:55
  29.4 13.7 %collective-permute-start.6 = (bf16[1152,128]{1,0:T(8,128)(2,1)S(1)}, bf16[1152,128]{1,0:T(8,128)(2,1)S(1)}, u32[]{:S(2)}, u32[]{:S(2)}) collective-permute-start(bf16[1152,128]{1,0:T(8,128)(2,1)S(1)} %bitcast.116), channel_id=1, source_target_pairs={{0,64},{64,128},{128,192},{192,0},{1,65},{65,129},{129,193},{193,1... | collective-permute-start | bytes 884744 | tf_op jit(solution)/shard_map/ppermute | solution.py:55
  31.1 12.1 %collective-permute-start.7 = (bf16[1152,128]{1,0:T(8,128)(2,1)S(1)}, bf16[1152,128]{1,0:T(8,128)(2,1)S(1)}, u32[]{:S(2)}, u32[]{:S(2)}) collective-permute-start(bf16[1152,128]{1,0:T(8,128)(2,1)S(1)} %bitcast.115), channel_id=1, source_target_pairs={{0,192},{64,0},{128,64},{192,128},{1,193},{65,1},{129,65},{193,129... | collective-permute-start | bytes 884744 | tf_op jit(solution)/shard_map/ppermute | solution.py:55
  34.0 10.6 %collective-permute-start.8 = (bf16[864,128]{1,0:T(8,128)(2,1)S(1)}, bf16[864,128]{1,0:T(8,128)(2,1)S(1)}, u32[]{:S(2)}, u32[]{:S(2)}) collective-permute-start(bf16[864,128]{1,0:T(8,128)(2,1)S(1)} %bitcast.117), channel_id=1, source_target_pairs={{0,64},{64,128},{128,192},{192,0},{1,65},{65,129},{129,193},{193,1... | collective-permute-start | bytes 663560 | tf_op jit(solution)/shard_map/ppermute | solution.py:55
  35.7 8.9 %collective-permute-start.9 = (bf16[864,128]{1,0:T(8,128)(2,1)S(1)}, bf16[864,128]{1,0:T(8,128)(2,1)S(1)}, u32[]{:S(2)}, u32[]{:S(2)}) collective-permute-start(bf16[864,128]{1,0:T(8,128)(2,1)S(1)} %bitcast.118), channel_id=1, source_target_pairs={{0,192},{64,0},{128,64},{192,128},{1,193},{65,1},{129,65},{193,129... | collective-permute-start | bytes 663560 | tf_op jit(solution)/shard_map/ppermute | solution.py:55
  37.6 7.0 %copy-start.8 = (bf16[128]{0:T(256)(128)(2,1)S(1)}, bf16[128]{0:T(256)(128)(2,1)}, u32[]{:S(2)}) copy-start(bf16[128]{0:T(256)(128)(2,1)} %param.14) | copy-start | bytes 772
  50.3 19.3 %copy-start.4 = (bf16[256,256]{1,0:T(8,128)(2,1)S(1)}, bf16[256,256]{1,0:T(8,128)(2,1)}, u32[]{:S(2)}) copy-start(bf16[256,256]{1,0:T(8,128)(2,1)} %constant.86.clone.along_z_ref) | copy-start | bytes 393220
  50.3 19.3 %copy-start.7 = (bf16[128,128]{1,0:T(8,128)(2,1)S(1)}, bf16[128,128]{1,0:T(8,128)(2,1)}, u32[]{:S(2)}) copy-start(bf16[128,128]{1,0:T(8,128)(2,1)} %constant.87.clone.along_x_ref) | copy-start | bytes 98308
  50.6 51.2 %copy-start.3 = (bf16[256,256]{1,0:T(8,128)(2,1)S(1)}, bf16[256,256]{1,0:T(8,128)(2,1)}, u32[]{:S(2)}) copy-start(bf16[256,256]{1,0:T(8,128)(2,1)} %constant.88.clone.into_ref) | copy-start | bytes 393220
  50.6 11.1 %collective-permute-start.10 = (bf16[256,128]{1,0:T(8,128)(2,1)S(1)}, bf16[256,128]{1,0:T(8,128)(2,1)S(1)}, u32[]{:S(2)}, u32[]{:S(2)}) collective-permute-start(bf16[256,128]{1,0:T(8,128)(2,1)S(1)} %bitcast.126), channel_id=1, source_target_pairs={{0,1},{1,2},{2,3},{3,0},{4,5},{5,6},{6,7},{7,4},{8,9},{9,10},{10,1... | collective-permute-start | bytes 196616 | tf_op jit(solution)/shard_map/ppermute | solution.py:55
  53.0 8.7 %collective-permute-start.11 = (bf16[256,128]{1,0:T(8,128)(2,1)S(1)}, bf16[256,128]{1,0:T(8,128)(2,1)S(1)}, u32[]{:S(2)}, u32[]{:S(2)}) collective-permute-start(bf16[256,128]{1,0:T(8,128)(2,1)S(1)} %bitcast.125), channel_id=1, source_target_pairs={{0,3},{1,0},{2,1},{3,2},{4,7},{5,4},{6,5},{7,6},{8,11},{9,8},{10,9... | collective-permute-start | bytes 196616 | tf_op jit(solution)/shard_map/ppermute | solution.py:55
  53.8 15.9 %all-to-all-start = ((bf16[16,16,128]{2,1,0:T(8,128)(2,1)}), bf16[16,16,128]{2,1,0:T(8,128)(2,1)S(1)}, u32[]{:S(2)}, u32[]{:S(2)}) async-start(bf16[16,16,128]{2,1,0:T(8,128)(2,1)} %get-tuple-element.25), calls=%async_computation | async-start | bytes 131072 | tf_op jit(solution)/shard_map/all_to_all | solution.py:791
  61.8 47.3 %collective-permute-start.12 = (bf16[1536,128]{1,0:T(8,128)(2,1)S(1)}, bf16[1536,128]{1,0:T(8,128)(2,1)S(1)}, u32[]{:S(2)}, u32[]{:S(2)}) collective-permute-start(bf16[1536,128]{1,0:T(8,128)(2,1)S(1)} %bitcast.113), channel_id=1, source_target_pairs={{0,4},{4,8},{8,12},{12,16},{16,20},{20,24},{24,28},{28,32},{32,36}... | collective-permute-start | bytes 1179656 | tf_op jit(solution)/shard_map/ppermute | solution.py:55
  61.9 47.2 %collective-permute-start.13 = (bf16[1536,128]{1,0:T(8,128)(2,1)S(1)}, bf16[1536,128]{1,0:T(8,128)(2,1)S(1)}, u32[]{:S(2)}, u32[]{:S(2)}) collective-permute-start(bf16[1536,128]{1,0:T(8,128)(2,1)S(1)} %bitcast.114), channel_id=1, source_target_pairs={{0,60},{4,0},{8,4},{12,8},{16,12},{20,16},{24,20},{28,24},{32,28},... | collective-permute-start | bytes 1179656 | tf_op jit(solution)/shard_map/ppermute | solution.py:55
  70.7 31.1 %all-to-all-start.1 = ((f32[256,1,128]{2,1,0:T(1,128)}), f32[256,1,128]{2,1,0:T(1,128)S(1)}, u32[]{:S(2)}, u32[]{:S(2)}) async-start(f32[256,1,128]{2,1,0:T(1,128)} %bitcast.34), calls=%async_computation.1 | async-start | bytes 262144 | tf_op jit(solution)/shard_map/all_to_all | solution.py:791
  102.9 21.5 %all-to-all-start.2 = ((f32[256,2,128]{2,1,0:T(2,128)}), f32[256,2,128]{2,1,0:T(2,128)S(1)}, u32[]{:S(2)}, u32[]{:S(2)}) async-start(f32[256,2,128]{2,1,0:T(2,128)} %bitcast.36), calls=%async_computation.2 | async-start | bytes 524288 | tf_op jit(solution)/shard_map/all_to_all | solution.py:791
  109.3 15.2 %copy-start.2 = (bf16[256,512]{1,0:T(8,128)(2,1)S(1)}, bf16[256,512]{1,0:T(8,128)(2,1)}, u32[]{:S(2)}) copy-start(bf16[256,512]{1,0:T(8,128)(2,1)} %constant.90.clone.along_z_ref) | copy-start | bytes 786436
  109.3 15.1 %copy-start.5 = (bf16[256,128]{1,0:T(8,128)(2,1)S(1)}, bf16[256,128]{1,0:T(8,128)(2,1)}, u32[]{:S(2)}) copy-start(bf16[256,128]{1,0:T(8,128)(2,1)} %constant.89.clone.along_x_ref) | copy-start | bytes 196612
  110.4 20.2 %collective-permute-start.14 = (bf16[2304,128]{1,0:T(8,128)(2,1)}, bf16[2304,128]{1,0:T(8,128)(2,1)S(1)}, u32[]{:S(2)}, u32[]{:S(2)}) collective-permute-start(bf16[2304,128]{1,0:T(8,128)(2,1)} %bitcast.48), channel_id=1, source_target_pairs={{0,64},{64,128},{128,192},{192,0},{1,65},{65,129},{129,193},{193,1... | collective-permute-start | bytes 1769480 | tf_op jit(solution)/shard_map/ppermute | solution.py:55
  111.9 18.6 %collective-permute-start.15 = (bf16[2304,128]{1,0:T(8,128)(2,1)}, bf16[2304,128]{1,0:T(8,128)(2,1)S(1)}, u32[]{:S(2)}, u32[]{:S(2)}) collective-permute-start(bf16[2304,128]{1,0:T(8,128)(2,1)} %bitcast.50), channel_id=1, source_target_pairs={{0,192},{64,0},{128,64},{192,128},{1,193},{65,1},{129,65},{193,129... | collective-permute-start | bytes 1769480 | tf_op jit(solution)/shard_map/ppermute | solution.py:55
  125.5 14.2 %all-to-all-start.3 = ((bf16[16,64,128]{2,1,0:T(8,128)(2,1)}), bf16[16,64,128]{2,1,0:T(8,128)(2,1)S(1)}, u32[]{:S(2)}, u32[]{:S(2)}) async-start(bf16[16,64,128]{2,1,0:T(8,128)(2,1)} %bitcast.38), calls=%async_computation.3 | async-start | bytes 524288 | tf_op jit(solution)/shard_map/all_to_all | solution.py:791
  142.4 9.2 %collective-permute-start.16 = (f32[24,128]{1,0:T(8,128)S(1)}, f32[24,128]{1,0:T(8,128)S(1)}, u32[]{:S(2)}, u32[]{:S(2)}) collective-permute-start(f32[24,128]{1,0:T(8,128)S(1)} %get-tuple-element.31.potential_ref), channel_id=1, source_target_pairs={{0,60},{4,8},{8,4},{12,16},{16,12},{20,24},{24,20},{28,32},{32,28}... | collective-permute-start | bytes 36872 | tf_op jit(solution)/shard_map/ppermute | solution.py:62
  142.5 9.1 %collective-permute-start.17 = (f32[24,128]{1,0:T(8,128)S(1)}, f32[24,128]{1,0:T(8,128)S(1)}, u32[]{:S(2)}, u32[]{:S(2)}) collective-permute-start(f32[24,128]{1,0:T(8,128)S(1)} %get-tuple-element.31.potential_ref), channel_id=1, source_target_pairs={{0,4},{4,0},{8,12},{12,8},{16,20},{20,16},{24,28},{28,24},{32,36},... | collective-permute-start | bytes 36872 | tf_op jit(solution)/shard_map/ppermute | solution.py:62
  144.0 7.7 %copy-start.6 = (bf16[128,128]{1,0:T(8,128)(2,1)S(1)}, bf16[128,128]{1,0:T(8,128)(2,1)}, u32[]{:S(2)}) copy-start(bf16[128,128]{1,0:T(8,128)(2,1)} %msg_ref.1) | copy-start | bytes 98308

commit v8 on v7

--- a/solution.py
+++ b/solution.py
@@ -287,7 +287,7 @@
         add_near(weight_ref, t, a, lambda dy, z: cell(dy, x, z), total_ref, ENDS)
         return carry
 
-    lax.fori_loop(0, 4, column, 0)
+    lax.fori_loop(0, 4, column, 0, unroll=2)
     copies = columns_kernel(0, 4, weight_ref, weight_out, sems, 0, END_BLOCKS)
     for copy in copies:
         copy.start()
@@ -388,7 +388,7 @@
         low_ref[index] = (silu - high.astype(f32)).astype(bf16)
         return carry
 
-    lax.fori_loop(0, 8, finish, 0, unroll=2)
+    lax.fori_loop(0, 8, finish, 0, unroll=4)
     wide = jnp.broadcast_to(read_ref[...], (16, 128))
     charge_ref[...] = dot_t(wide, high_ref[...].reshape(1024, 128)) + dot_t(
         wide, low_ref[...].reshape(1024, 128)
@@ -407,7 +407,7 @@
         right_rows[:, lanes] = jnp.where(block == cell, jnp.tile(row_z, (8, 1)), 0.0).astype(bf16)
         return carry
 
-    lax.fori_loop(0, 8, spread, 0)
+    lax.fori_loop(0, 8, spread, 0, unroll=4)
     mesh_ref[...] = dot_t(left_rows[...], right_rows[...]).reshape(PC, PC, 128).astype(bf16)
     for copy in copies:
         copy.wait()
@@ -594,7 +594,7 @@
             )
         return carry
 
-    lax.fori_loop(0, 8, gather, 0)
+    lax.fori_loop(0, 8, gather, 0, unroll=2)
     own_ref[0:4, :] = out_ref[7:11, :]
     own_ref[4:8, :] = out_ref[13:17, :]
     for copy in copies:
@@ -657,7 +657,7 @@
             total_ref[a, first : first + width] += part.reshape(width, 128, 128)
         return carry
 
-    lax.fori_loop(0, 6, combination, 0)
+    lax.fori_loop(0, 6, combination, 0, unroll=3)
     for copy in copies:
         copy.wait()
 
@@ -716,7 +716,7 @@
             total_ref[a, first : first + width] += part.reshape(width, 128, 128)
         return carry
 
-    lax.fori_loop(0, 6, combination, 0, unroll=2)
+    lax.fori_loop(0, 6, combination, 0, unroll=3)
 
     def finish(a, carry):
         back = total_ref[a].reshape(512, 128).astype(bf16)
@@ -724,7 +724,7 @@
         out_ref[a] = (dot_t(back, msg_ref[...]) + dot_t(own, self_ref[...])).reshape(4, 128, 128)
         return carry
 
-    lax.fori_loop(0, 2, finish, 0)
+    lax.fori_loop(0, 2, finish, 0, unroll=2)
 
 
 def backward(weights, slope, part, own, across, within, side, msg_weight, self_weight):

time: 157 us -> 156 us (level)
  no operation moved by 1% of the time
where the time goes in v8:
time: 156 us
  starting transfers between devices  73.8 us (47%)
  waiting for transfers between devices  44.5 us (29%)
  Pallas kernels  32.4 us (21%)
  local copies, waits for them, and re-layouts  3.65 us (2%)
    all_to_all x4, starting transfers between devices, swapped(): return lax.all_to_all(value, axis, split_axis=0, concat_axis=0, tiled=True)  36.9 us
    ppermute x16, starting transfers between devices, moved(): lax.ppermute(value.reshape(-1, 128), axis, pairs).reshape(value.shape)  35.1 us
    all_to_all x4, waiting for transfers between devices, swapped(): return lax.all_to_all(value, axis, split_axis=0, concat_axis=0, tiled=True)  32.5 us
    ppermute x16, waiting for transfers between devices, moved(): lax.ppermute(value.reshape(-1, 128), axis, pairs).reshape(value.shape)  8 us
    pallas_call x1, Pallas kernels, message_layer(): pl.pallas_call(message_kernel, in_specs=[VM] * 11 + [ANY], out_specs=[ANY...  5.74 us
    pallas_call x1, Pallas kernels, inside_pairs(): pl.pallas_call(inside_kernel, in_specs=[VM] * 5, out_specs=[ANY, VM], out...  5.71 us
    pallas_call x1, Pallas kernels, ends_pairs(): pl.pallas_call(ends_kernel, in_specs=[VM] * 6 + [ANY], out_specs=[ANY, VM...  5.19 us
    pallas_call x1, Pallas kernels, backward(): pl.pallas_call(backward_kernel, in_specs=[VM] * 9, out_specs=VM, out_shap...  4.4 us
  transfers between devices with their start and end apart: 22, of which 8 were waited for; matrix products, arithmetic and copies ran while one was open for 3% of the time, Pallas kernels for 11%

profile of v8, /device:TPU:32, one launch (start us, length us, event | category | flops | bytes accessed | tf_op | source)
XLA Modules:
  0.0 155.8 jit_solution(6750856824875075581)
XLA Ops:
  0.6 1.9 %project.1 = bf16[8,144,128]{2,1,0:T(8,128)(2,1)} custom-call(bf16[8,128,128]{2,1,0:T(8,128)(2,1)} %bitcast.93, bf16[128,128]{1,0:T(8,128)(2,1)} %msg_ref.1, s32[2,1,3,4,128]{4,3,2,1,0:T(4,128)} %bitcast.127, f32[2,1,3,4,128]{4,3,2,1,0:T(4,128)} %bitcast.128), custom_call_target="tpu_custom_call" | custom-call | tf_op jit(solution)/shard_map/project/pallas_call | solution.py:106
  2.5 0.1 collective-permute-start
  2.6 8.0 %collective-permute-start.1 = (bf16[1152,128]{1,0:T(8,128)(2,1)}, bf16[1152,128]{1,0:T(8,128)(2,1)S(1)}, u32[]{:S(2)}, u32[]{:S(2)}) collective-permute-start(bf16[1152,128]{1,0:T(8,128)(2,1)} %bitcast.76), channel_id=1, source_target_pairs={{0,60},{4,0},{8,4},{12,8},{16,12},{20,16},{24,20},{28,24},{32,28},... | collective-permute-start | bytes 884744 | tf_op jit(solution)/shard_map/ppermute | solution.py:55
  10.6 1.0 fusion.10
  11.6 1.7 %collective-permute-start.4 = (bf16[576,128]{1,0:T(8,128)(2,1)S(1)}, bf16[576,128]{1,0:T(8,128)(2,1)S(1)}, u32[]{:S(2)}, u32[]{:S(2)}) collective-permute-start(bf16[576,128]{1,0:T(8,128)(2,1)S(1)} %bitcast.122), channel_id=1, source_target_pairs={{0,64},{64,128},{128,192},{192,0},{1,65},{65,129},{129,193},{193,1... | collective-permute-start | bytes 442376 | tf_op jit(solution)/shard_map/ppermute | solution.py:55
  13.3 1.7 %collective-permute-start.5 = (bf16[576,128]{1,0:T(8,128)(2,1)S(1)}, bf16[576,128]{1,0:T(8,128)(2,1)S(1)}, u32[]{:S(2)}, u32[]{:S(2)}) collective-permute-start(bf16[576,128]{1,0:T(8,128)(2,1)S(1)} %bitcast.121), channel_id=1, source_target_pairs={{0,192},{64,0},{128,64},{192,128},{1,193},{65,1},{129,65},{193,129... | collective-permute-start | bytes 442376 | tf_op jit(solution)/shard_map/ppermute | solution.py:55
  15.0 0.9 slice_bitcast_fusion.1
  15.9 2.6 %collective-permute-done = bf16[1152,128]{1,0:T(8,128)(2,1)S(1)} collective-permute-done((bf16[1152,128]{1,0:T(8,128)(2,1)}, bf16[1152,128]{1,0:T(8,128)(2,1)S(1)}, u32[]{:S(2)}, u32[]{:S(2)}) %collective-permute-start) | collective-permute-done | bytes 294944 | tf_op jit(solution)/shard_map/ppermute | solution.py:55
  18.5 2.5 %collective-permute-done.1 = bf16[1152,128]{1,0:T(8,128)(2,1)S(1)} collective-permute-done((bf16[1152,128]{1,0:T(8,128)(2,1)}, bf16[1152,128]{1,0:T(8,128)(2,1)S(1)}, u32[]{:S(2)}, u32[]{:S(2)}) %collective-permute-start.1) | collective-permute-done | bytes 294944 | tf_op jit(solution)/shard_map/ppermute | solution.py:55
  21.0 2.5 %collective-permute-start.3 = (bf16[864,128]{1,0:T(8,128)(2,1)S(1)}, bf16[864,128]{1,0:T(8,128)(2,1)S(1)}, u32[]{:S(2)}, u32[]{:S(2)}) collective-permute-start(bf16[864,128]{1,0:T(8,128)(2,1)S(1)} %bitcast.120), channel_id=1, source_target_pairs={{0,3},{1,0},{2,1},{3,2},{4,7},{5,4},{6,5},{7,6},{8,11},{9,8},{10,9... | collective-permute-start | bytes 663560 | tf_op jit(solution)/shard_map/ppermute | solution.py:55
  23.5 0.1 collective-permute-start.2
  23.7 5.7 %inside_pairs.1 = (bf16[6,8,128,768]{3,2,1,0:T(8,128)(2,1)}, f32[2,4,128,128]{3,2,1,0:T(8,128)S(1)}) custom-call(bf16[2,4,144,128]{3,2,1,0:T(8,128)(2,1)S(1)} %bitcast.78, bf16[2,4,144,128]{3,2,1,0:T(8,128)(2,1)S(1)} %bitcast.83, bf16[2,4,144,128]{3,2,1,0:T(8,128)(2,1)S(1)} %bitcast.87, bf16[8,128,128]{2,1,0:T(8,128)(2,1)S(1)} %bitcast.94, ...), custom_call_target="tpu_custom_call" | custom-call | flops 5000000000 | bytes 9000000 | tf_op jit(solution)/shard_map/inside_pairs/pallas_call | solution.py:232
  29.4 0.1 pad_maximum_fusion.2
  29.4 1.6 %collective-permute-start.6 = (bf16[1152,128]{1,0:T(8,128)(2,1)S(1)}, bf16[1152,128]{1,0:T(8,128)(2,1)S(1)}, u32[]{:S(2)}, u32[]{:S(2)}) collective-permute-start(bf16[1152,128]{1,0:T(8,128)(2,1)S(1)} %bitcast.116), channel_id=1, source_target_pairs={{0,64},{64,128},{128,192},{192,0},{1,65},{65,129},{129,193},{193,1... | collective-permute-start | bytes 884744 | tf_op jit(solution)/shard_map/ppermute | solution.py:55
  31.1 0.0 collective-permute-done.3
  31.1 1.7 %collective-permute-start.7 = (bf16[1152,128]{1,0:T(8,128)(2,1)S(1)}, bf16[1152,128]{1,0:T(8,128)(2,1)S(1)}, u32[]{:S(2)}, u32[]{:S(2)}) collective-permute-start(bf16[1152,128]{1,0:T(8,128)(2,1)S(1)} %bitcast.115), channel_id=1, source_target_pairs={{0,192},{64,0},{128,64},{192,128},{1,193},{65,1},{129,65},{193,129... | collective-permute-start | bytes 884744 | tf_op jit(solution)/shard_map/ppermute | solution.py:55
  32.8 1.1 collective-permute-done.2
  34.0 1.7 %collective-permute-start.8 = (bf16[864,128]{1,0:T(8,128)(2,1)S(1)}, bf16[864,128]{1,0:T(8,128)(2,1)S(1)}, u32[]{:S(2)}, u32[]{:S(2)}) collective-permute-start(bf16[864,128]{1,0:T(8,128)(2,1)S(1)} %bitcast.117), channel_id=1, source_target_pairs={{0,64},{64,128},{128,192},{192,0},{1,65},{65,129},{129,193},{193,1... | collective-permute-start | bytes 663560 | tf_op jit(solution)/shard_map/ppermute | solution.py:55
  35.7 0.0 collective-permute-done.4
  35.7 1.9 %collective-permute-start.9 = (bf16[864,128]{1,0:T(8,128)(2,1)S(1)}, bf16[864,128]{1,0:T(8,128)(2,1)S(1)}, u32[]{:S(2)}, u32[]{:S(2)}) collective-permute-start(bf16[864,128]{1,0:T(8,128)(2,1)S(1)} %bitcast.118), channel_id=1, source_target_pairs={{0,192},{64,0},{128,64},{192,128},{1,193},{65,1},{129,65},{193,129... | collective-permute-start | bytes 663560 | tf_op jit(solution)/shard_map/ppermute | solution.py:55
  37.6 5.2 %ends_pairs.1 = (bf16[6,8,128,768]{3,2,1,0:T(8,128)(2,1)}, f32[2,4,128,128]{3,2,1,0:T(8,128)S(1)}) custom-call(bf16[2,4,144,128]{3,2,1,0:T(8,128)(2,1)S(1)} %bitcast.79, bf16[2,4,144,128]{3,2,1,0:T(8,128)(2,1)S(1)} %bitcast.85, bf16[2,4,144,128]{3,2,1,0:T(8,128)(2,1)S(1)} %bitcast.89, ...), custom_call_target="tpu_custom_call", output_to_operand_aliasing={{0}: (6, {})} | custom-call | flops 6000000000 | bytes 9000000 | tf_op jit(solution)/shard_map/ends_pairs/pallas_call | solution.py:300
  42.8 0.0 collective-permute-done.5
  42.8 0.0 collective-permute-done.6
  42.8 0.0 collective-permute-done.7
  42.8 1.8 %collective-permute-done.8 = bf16[864,128]{1,0:T(8,128)(2,1)S(1)} collective-permute-done((bf16[864,128]{1,0:T(8,128)(2,1)S(1)}, bf16[864,128]{1,0:T(8,128)(2,1)S(1)}, u32[]{:S(2)}, u32[]{:S(2)}) %collective-permute-start.8) | collective-permute-done | bytes 221216 | tf_op jit(solution)/shard_map/ppermute | solution.py:55
  44.6 0.0 collective-permute-done.9
  44.6 5.7 %message.1 = (bf16[6,8,128,768]{3,2,1,0:T(8,128)(2,1)}, f32[2,4,128,128]{3,2,1,0:T(8,128)S(1)}, bf16[16,16,128]{2,1,0:T(8,128)(2,1)}, f32[4,6,8,128]{3,2,1,0:T(8,128)S(1)}) custom-call(bf16[2,4,144,128]{3,2,1,0:T(8,128)(2,1)S(1)} %bitcast.80, bf16[3,2,1,144,128]{4,3,2,1,0:T(8,128)(2,1)S(1)} %bitcast.101, ...), custom_call_target="tpu_custom_call", output_to_operand_aliasing={{0}: (11, {})} | custom-call | flops 5000000000 | bytes 6000000 | tf_op jit(solution)/shard_map/message/pallas_call | solution.py:417
  50.3 0.0 copy-start.4
  50.3 0.0 copy-start.7
  50.4 0.2 slope.1
  50.6 0.0 copy-start.3
  50.6 2.4 %collective-permute-start.10 = (bf16[256,128]{1,0:T(8,128)(2,1)S(1)}, bf16[256,128]{1,0:T(8,128)(2,1)S(1)}, u32[]{:S(2)}, u32[]{:S(2)}) collective-permute-start(bf16[256,128]{1,0:T(8,128)(2,1)S(1)} %bitcast.126), channel_id=1, source_target_pairs={{0,1},{1,2},{2,3},{3,0},{4,5},{5,6},{6,7},{7,4},{8,9},{9,10},{10,1... | collective-permute-start | bytes 196616 | tf_op jit(solution)/shard_map/ppermute | solution.py:55
  53.0 0.8 collective-permute-start.11
  53.8 7.9 %all-to-all-start = ((bf16[16,16,128]{2,1,0:T(8,128)(2,1)}), bf16[16,16,128]{2,1,0:T(8,128)(2,1)S(1)}, u32[]{:S(2)}, u32[]{:S(2)}) async-start(bf16[16,16,128]{2,1,0:T(8,128)(2,1)} %get-tuple-element.25), calls=%async_computation | async-start | bytes 131072 | tf_op jit(solution)/shard_map/all_to_all | solution.py:791
  61.7 0.0 collective-permute-done.10
  61.7 0.0 collective-permute-done.11
  61.7 0.1 fusion.8
  61.8 0.1 collective-permute-start.12
  61.9 7.7 %collective-permute-start.13 = (bf16[1536,128]{1,0:T(8,128)(2,1)S(1)}, bf16[1536,128]{1,0:T(8,128)(2,1)S(1)}, u32[]{:S(2)}, u32[]{:S(2)}) collective-permute-start(bf16[1536,128]{1,0:T(8,128)(2,1)S(1)} %bitcast.114), channel_id=1, source_target_pairs={{0,60},{4,0},{8,4},{12,8},{16,12},{20,16},{24,20},{28,24},{32,28},... | collective-permute-start | bytes 1179656 | tf_op jit(solution)/shard_map/ppermute | solution.py:55
  69.7 0.0 all-to-all-done
  69.7 1.0 forward_xz.1
  70.7 18.4 %all-to-all-start.1 = ((f32[256,1,128]{2,1,0:T(1,128)}), f32[256,1,128]{2,1,0:T(1,128)S(1)}, u32[]{:S(2)}, u32[]{:S(2)}) async-start(f32[256,1,128]{2,1,0:T(1,128)} %bitcast.34), calls=%async_computation.1 | async-start | bytes 262144 | tf_op jit(solution)/shard_map/all_to_all | solution.py:791
  89.2 0.1 fusion.1.influence_ref
  89.3 12.6 %all-to-all-done.1 = f32[256,1,128]{2,1,0:T(1,128)S(1)} async-done(((f32[256,1,128]{2,1,0:T(1,128)}), f32[256,1,128]{2,1,0:T(1,128)S(1)}, u32[]{:S(2)}, u32[]{:S(2)}) %all-to-all-start.1) | async-done | bytes 131104 | tf_op jit(solution)/shard_map/all_to_all | solution.py:791
  101.8 1.1 filter_y.1
  102.9 6.2 %all-to-all-start.2 = ((f32[256,2,128]{2,1,0:T(2,128)}), f32[256,2,128]{2,1,0:T(2,128)S(1)}, u32[]{:S(2)}, u32[]{:S(2)}) async-start(f32[256,2,128]{2,1,0:T(2,128)} %bitcast.36), calls=%async_computation.2 | async-start | bytes 524288 | tf_op jit(solution)/shard_map/all_to_all | solution.py:791
  109.1 0.0 collective-permute-done.12
  109.1 0.1 pad_maximum_fusion.rows_ref
  109.3 0.0 copy-start.2
  109.3 0.0 copy-start.5
  109.3 1.1 fusion.9
  110.4 1.5 collective-permute-start.14
  111.9 1.7 %collective-permute-start.15 = (bf16[2304,128]{1,0:T(8,128)(2,1)}, bf16[2304,128]{1,0:T(8,128)(2,1)S(1)}, u32[]{:S(2)}, u32[]{:S(2)}) collective-permute-start(bf16[2304,128]{1,0:T(8,128)(2,1)} %bitcast.50), channel_id=1, source_target_pairs={{0,192},{64,0},{128,64},{192,128},{1,193},{65,1},{129,65},{193,129... | collective-permute-start | bytes 1769480 | tf_op jit(solution)/shard_map/ppermute | solution.py:55
  113.6 10.8 %all-to-all-done.2 = f32[256,2,128]{2,1,0:T(2,128)S(1)} async-done(((f32[256,2,128]{2,1,0:T(2,128)}), f32[256,2,128]{2,1,0:T(2,128)S(1)}, u32[]{:S(2)}, u32[]{:S(2)}) %all-to-all-start.2) | async-done | bytes 262176 | tf_op jit(solution)/shard_map/all_to_all | solution.py:791
  124.4 1.0 inverse_xz.1
  125.5 4.4 %all-to-all-start.3 = ((bf16[16,64,128]{2,1,0:T(8,128)(2,1)}), bf16[16,64,128]{2,1,0:T(8,128)(2,1)S(1)}, u32[]{:S(2)}, u32[]{:S(2)}) async-start(bf16[16,64,128]{2,1,0:T(8,128)(2,1)} %bitcast.38), calls=%async_computation.3 | async-start | bytes 524288 | tf_op jit(solution)/shard_map/all_to_all | solution.py:791
  129.8 0.5 slice.77
  130.4 9.1 %all-to-all-done.3.field_ref = bf16[16,64,128]{2,1,0:T(8,128)(2,1)S(1)} async-done(((bf16[16,64,128]{2,1,0:T(8,128)(2,1)}), bf16[16,64,128]{2,1,0:T(8,128)(2,1)S(1)}, u32[]{:S(2)}, u32[]{:S(2)}) %all-to-all-start.3) | async-done | bytes 262176 | tf_op jit(solution)/shard_map/all_to_all | solution.py:791
  139.5 2.7 %interpolate.1 = (f32[24,128]{1,0:T(8,128)S(1)}, f32[8,128]{1,0:T(8,128)}, bf16[6,8,128,256]{3,2,1,0:T(8,128)(2,1)S(1)}, bf16[3,4,6,128,128]{4,3,2,1,0:T(8,128)(2,1)S(1)}) custom-call(bf16[16,64,128]{2,1,0:T(8,128)(2,1)S(1)} %all-to-all-done.3.field_ref, f32[24,8,128]{2,1,0:T(8,128)S(1)} %bitcast.102, bf16[6,8,128,768]{3,2,1,0:T(8,128)(2,1)} %get-tuple-element.24.stored_ref, ...), custom_call_target="tpu_custom_call" | custom-call | flops 201326592 | bytes 400000 | tf_op jit(solution)/shard_map/interpolate/pallas_call | solution.py:605
  142.2 0.1 collective-permute-start.16
  142.3 1.7 %collective-permute-start.17 = (f32[24,128]{1,0:T(8,128)S(1)}, f32[24,128]{1,0:T(8,128)S(1)}, u32[]{:S(2)}, u32[]{:S(2)}) collective-permute-start(f32[24,128]{1,0:T(8,128)S(1)} %get-tuple-element.31.potential_ref), channel_id=1, source_target_pairs={{0,4},{4,0},{8,12},{12,8},{16,20},{20,16},{24,28},{28,24},{32,36},... | collective-permute-start | bytes 36872 | tf_op jit(solution)/shard_map/ppermute | solution.py:62
  144.0 3.4 %beside.1 = (bf16[6,8,128,512]{3,2,1,0:T(8,128)(2,1)S(1)}, f32[2,4,128,128]{3,2,1,0:T(8,128)S(1)}, bf16[2,4,128,128]{3,2,1,0:T(8,128)(2,1)S(1)}) custom-call(bf16[6,8,128,768]{3,2,1,0:T(8,128)(2,1)} %get-tuple-element.24.stored_ref, bf16[6,8,128,256]{3,2,1,0:T(8,128)(2,1)S(1)} %get-tuple-element.29.weight_ref, ...), custom_call_target="tpu_custom_call" | custom-call | flops 3000000000 | bytes 12000000 | tf_op jit(solution)/shard_map/beside/pallas_call | solution.py:666
  147.4 4.0 %collective-permute-done.16.across_ref = f32[24,128]{1,0:T(8,128)S(1)} collective-permute-done((f32[24,128]{1,0:T(8,128)S(1)}, f32[24,128]{1,0:T(8,128)S(1)}, u32[]{:S(2)}, u32[]{:S(2)}) %collective-permute-start.16) | collective-permute-done | bytes 12320 | tf_op jit(solution)/shard_map/ppermute | solution.py:62
  151.4 4.4 %backward.1 = f32[2,4,128,128]{3,2,1,0:T(8,128)} custom-call(bf16[6,8,128,512]{3,2,1,0:T(8,128)(2,1)S(1)} %get-tuple-element.32.weight_ref, bf16[3,4,6,128,128]{4,3,2,1,0:T(8,128)(2,1)S(1)} %get-tuple-element.30.slope_ref, f32[2,4,128,128]{3,2,1,0:T(8,128)S(1)} %get-tuple-element.33.part_ref, bf16[2,4,128,128]{3,2,1,0:T(8,128)(2,1)S(1)} %get-tuple-element.34.own_ref, ...), custom_call_target="tpu_custom_call" | custom-call | flops 4000000000 | bytes 12000000 | tf_op jit(solution)/shard_map/backward/pallas_call | solution.py:731
  (31 shorter events, 0.2 us)
Async XLA Ops:
  2.5 21.1 %copy-start = (bf16[8,144,128]{2,1,0:T(8,128)(2,1)S(1)}, bf16[8,144,128]{2,1,0:T(8,128)(2,1)}, u32[]{:S(2)}) copy-start(bf16[8,144,128]{2,1,0:T(8,128)(2,1)} %project.1) | copy-start | bytes 884740
  2.5 21.1 %copy-start.1 = (bf16[2,1,4,128,128]{4,3,2,1,0:T(8,128)(2,1)S(1)}, bf16[2,1,4,128,128]{4,3,2,1,0:T(8,128)(2,1)}, u32[]{:S(2)}) copy-start(bf16[2,1,4,128,128]{4,3,2,1,0:T(8,128)(2,1)} %param.11) | copy-start | bytes 786436
  2.5 21.1 %copy-start.9 = (bf16[128,128]{1,0:T(8,128)(2,1)S(1)}, bf16[128,128]{1,0:T(8,128)(2,1)}, u32[]{:S(2)}) copy-start(bf16[128,128]{1,0:T(8,128)(2,1)} %self_ref.3) | copy-start | bytes 98308
  2.5 15.9 %collective-permute-start = (bf16[1152,128]{1,0:T(8,128)(2,1)}, bf16[1152,128]{1,0:T(8,128)(2,1)S(1)}, u32[]{:S(2)}, u32[]{:S(2)}) collective-permute-start(bf16[1152,128]{1,0:T(8,128)(2,1)} %bitcast.75), channel_id=1, source_target_pairs={{0,4},{4,8},{8,12},{12,16},{16,20},{20,24},{24,28},{28,32},{32,36}... | collective-permute-start | bytes 884744 | tf_op jit(solution)/shard_map/ppermute | solution.py:55
  2.6 18.3 %collective-permute-start.1 = (bf16[1152,128]{1,0:T(8,128)(2,1)}, bf16[1152,128]{1,0:T(8,128)(2,1)S(1)}, u32[]{:S(2)}, u32[]{:S(2)}) collective-permute-start(bf16[1152,128]{1,0:T(8,128)(2,1)} %bitcast.76), channel_id=1, source_target_pairs={{0,60},{4,0},{8,4},{12,8},{16,12},{20,16},{24,20},{28,24},{32,28},... | collective-permute-start | bytes 884744 | tf_op jit(solution)/shard_map/ppermute | solution.py:55
  11.6 24.0 %collective-permute-start.4 = (bf16[576,128]{1,0:T(8,128)(2,1)S(1)}, bf16[576,128]{1,0:T(8,128)(2,1)S(1)}, u32[]{:S(2)}, u32[]{:S(2)}) collective-permute-start(bf16[576,128]{1,0:T(8,128)(2,1)S(1)} %bitcast.122), channel_id=1, source_target_pairs={{0,64},{64,128},{128,192},{192,0},{1,65},{65,129},{129,193},{193,1... | collective-permute-start | bytes 442376 | tf_op jit(solution)/shard_map/ppermute | solution.py:55
  13.3 29.5 %collective-permute-start.5 = (bf16[576,128]{1,0:T(8,128)(2,1)S(1)}, bf16[576,128]{1,0:T(8,128)(2,1)S(1)}, u32[]{:S(2)}, u32[]{:S(2)}) collective-permute-start(bf16[576,128]{1,0:T(8,128)(2,1)S(1)} %bitcast.121), channel_id=1, source_target_pairs={{0,192},{64,0},{128,64},{192,128},{1,193},{65,1},{129,65},{193,129... | collective-permute-start | bytes 442376 | tf_op jit(solution)/shard_map/ppermute | solution.py:55
  21.0 10.1 %collective-permute-start.3 = (bf16[864,128]{1,0:T(8,128)(2,1)S(1)}, bf16[864,128]{1,0:T(8,128)(2,1)S(1)}, u32[]{:S(2)}, u32[]{:S(2)}) collective-permute-start(bf16[864,128]{1,0:T(8,128)(2,1)S(1)} %bitcast.120), channel_id=1, source_target_pairs={{0,3},{1,0},{2,1},{3,2},{4,7},{5,4},{6,5},{7,6},{8,11},{9,8},{10,9... | collective-permute-start | bytes 663560 | tf_op jit(solution)/shard_map/ppermute | solution.py:55
  23.5 10.4 %collective-permute-start.2 = (bf16[864,128]{1,0:T(8,128)(2,1)S(1)}, bf16[864,128]{1,0:T(8,128)(2,1)S(1)}, u32[]{:S(2)}, u32[]{:S(2)}) collective-permute-start(bf16[864,128]{1,0:T(8,128)(2,1)S(1)} %bitcast.119), channel_id=1, source_target_pairs={{0,1},{1,2},{2,3},{3,0},{4,5},{5,6},{6,7},{7,4},{8,9},{9,10},{10,1... | collective-permute-start | bytes 663560 | tf_op jit(solution)/shard_map/ppermute | solution.py:55
  29.4 13.3 %collective-permute-start.6 = (bf16[1152,128]{1,0:T(8,128)(2,1)S(1)}, bf16[1152,128]{1,0:T(8,128)(2,1)S(1)}, u32[]{:S(2)}, u32[]{:S(2)}) collective-permute-start(bf16[1152,128]{1,0:T(8,128)(2,1)S(1)} %bitcast.116), channel_id=1, source_target_pairs={{0,64},{64,128},{128,192},{192,0},{1,65},{65,129},{129,193},{193,1... | collective-permute-start | bytes 884744 | tf_op jit(solution)/shard_map/ppermute | solution.py:55
  31.1 11.7 %collective-permute-start.7 = (bf16[1152,128]{1,0:T(8,128)(2,1)S(1)}, bf16[1152,128]{1,0:T(8,128)(2,1)S(1)}, u32[]{:S(2)}, u32[]{:S(2)}) collective-permute-start(bf16[1152,128]{1,0:T(8,128)(2,1)S(1)} %bitcast.115), channel_id=1, source_target_pairs={{0,192},{64,0},{128,64},{192,128},{1,193},{65,1},{129,65},{193,129... | collective-permute-start | bytes 884744 | tf_op jit(solution)/shard_map/ppermute | solution.py:55
  34.0 10.6 %collective-permute-start.8 = (bf16[864,128]{1,0:T(8,128)(2,1)S(1)}, bf16[864,128]{1,0:T(8,128)(2,1)S(1)}, u32[]{:S(2)}, u32[]{:S(2)}) collective-permute-start(bf16[864,128]{1,0:T(8,128)(2,1)S(1)} %bitcast.117), channel_id=1, source_target_pairs={{0,64},{64,128},{128,192},{192,0},{1,65},{65,129},{129,193},{193,1... | collective-permute-start | bytes 663560 | tf_op jit(solution)/shard_map/ppermute | solution.py:55
  35.7 8.9 %collective-permute-start.9 = (bf16[864,128]{1,0:T(8,128)(2,1)S(1)}, bf16[864,128]{1,0:T(8,128)(2,1)S(1)}, u32[]{:S(2)}, u32[]{:S(2)}) collective-permute-start(bf16[864,128]{1,0:T(8,128)(2,1)S(1)} %bitcast.118), channel_id=1, source_target_pairs={{0,192},{64,0},{128,64},{192,128},{1,193},{65,1},{129,65},{193,129... | collective-permute-start | bytes 663560 | tf_op jit(solution)/shard_map/ppermute | solution.py:55
  37.6 7.0 %copy-start.8 = (bf16[128]{0:T(256)(128)(2,1)S(1)}, bf16[128]{0:T(256)(128)(2,1)}, u32[]{:S(2)}) copy-start(bf16[128]{0:T(256)(128)(2,1)} %param.14) | copy-start | bytes 772
  50.3 19.3 %copy-start.4 = (bf16[256,256]{1,0:T(8,128)(2,1)S(1)}, bf16[256,256]{1,0:T(8,128)(2,1)}, u32[]{:S(2)}) copy-start(bf16[256,256]{1,0:T(8,128)(2,1)} %constant.86.clone.along_z_ref) | copy-start | bytes 393220
  50.3 19.3 %copy-start.7 = (bf16[128,128]{1,0:T(8,128)(2,1)S(1)}, bf16[128,128]{1,0:T(8,128)(2,1)}, u32[]{:S(2)}) copy-start(bf16[128,128]{1,0:T(8,128)(2,1)} %constant.87.clone.along_x_ref) | copy-start | bytes 98308
  50.6 51.2 %copy-start.3 = (bf16[256,256]{1,0:T(8,128)(2,1)S(1)}, bf16[256,256]{1,0:T(8,128)(2,1)}, u32[]{:S(2)}) copy-start(bf16[256,256]{1,0:T(8,128)(2,1)} %constant.88.clone.into_ref) | copy-start | bytes 393220
  50.6 11.1 %collective-permute-start.10 = (bf16[256,128]{1,0:T(8,128)(2,1)S(1)}, bf16[256,128]{1,0:T(8,128)(2,1)S(1)}, u32[]{:S(2)}, u32[]{:S(2)}) collective-permute-start(bf16[256,128]{1,0:T(8,128)(2,1)S(1)} %bitcast.126), channel_id=1, source_target_pairs={{0,1},{1,2},{2,3},{3,0},{4,5},{5,6},{6,7},{7,4},{8,9},{9,10},{10,1... | collective-permute-start | bytes 196616 | tf_op jit(solution)/shard_map/ppermute | solution.py:55
  53.0 8.7 %collective-permute-start.11 = (bf16[256,128]{1,0:T(8,128)(2,1)S(1)}, bf16[256,128]{1,0:T(8,128)(2,1)S(1)}, u32[]{:S(2)}, u32[]{:S(2)}) collective-permute-start(bf16[256,128]{1,0:T(8,128)(2,1)S(1)} %bitcast.125), channel_id=1, source_target_pairs={{0,3},{1,0},{2,1},{3,2},{4,7},{5,4},{6,5},{7,6},{8,11},{9,8},{10,9... | collective-permute-start | bytes 196616 | tf_op jit(solution)/shard_map/ppermute | solution.py:55
  53.8 15.9 %all-to-all-start = ((bf16[16,16,128]{2,1,0:T(8,128)(2,1)}), bf16[16,16,128]{2,1,0:T(8,128)(2,1)S(1)}, u32[]{:S(2)}, u32[]{:S(2)}) async-start(bf16[16,16,128]{2,1,0:T(8,128)(2,1)} %get-tuple-element.25), calls=%async_computation | async-start | bytes 131072 | tf_op jit(solution)/shard_map/all_to_all | solution.py:791
  61.8 47.3 %collective-permute-start.12 = (bf16[1536,128]{1,0:T(8,128)(2,1)S(1)}, bf16[1536,128]{1,0:T(8,128)(2,1)S(1)}, u32[]{:S(2)}, u32[]{:S(2)}) collective-permute-start(bf16[1536,128]{1,0:T(8,128)(2,1)S(1)} %bitcast.113), channel_id=1, source_target_pairs={{0,4},{4,8},{8,12},{12,16},{16,20},{20,24},{24,28},{28,32},{32,36}... | collective-permute-start | bytes 1179656 | tf_op jit(solution)/shard_map/ppermute | solution.py:55
  61.9 47.2 %collective-permute-start.13 = (bf16[1536,128]{1,0:T(8,128)(2,1)S(1)}, bf16[1536,128]{1,0:T(8,128)(2,1)S(1)}, u32[]{:S(2)}, u32[]{:S(2)}) collective-permute-start(bf16[1536,128]{1,0:T(8,128)(2,1)S(1)} %bitcast.114), channel_id=1, source_target_pairs={{0,60},{4,0},{8,4},{12,8},{16,12},{20,16},{24,20},{28,24},{32,28},... | collective-permute-start | bytes 1179656 | tf_op jit(solution)/shard_map/ppermute | solution.py:55
  70.7 31.1 %all-to-all-start.1 = ((f32[256,1,128]{2,1,0:T(1,128)}), f32[256,1,128]{2,1,0:T(1,128)S(1)}, u32[]{:S(2)}, u32[]{:S(2)}) async-start(f32[256,1,128]{2,1,0:T(1,128)} %bitcast.34), calls=%async_computation.1 | async-start | bytes 262144 | tf_op jit(solution)/shard_map/all_to_all | solution.py:791
  102.9 21.5 %all-to-all-start.2 = ((f32[256,2,128]{2,1,0:T(2,128)}), f32[256,2,128]{2,1,0:T(2,128)S(1)}, u32[]{:S(2)}, u32[]{:S(2)}) async-start(f32[256,2,128]{2,1,0:T(2,128)} %bitcast.36), calls=%async_computation.2 | async-start | bytes 524288 | tf_op jit(solution)/shard_map/all_to_all | solution.py:791
  109.3 15.2 %copy-start.2 = (bf16[256,512]{1,0:T(8,128)(2,1)S(1)}, bf16[256,512]{1,0:T(8,128)(2,1)}, u32[]{:S(2)}) copy-start(bf16[256,512]{1,0:T(8,128)(2,1)} %constant.90.clone.along_z_ref) | copy-start | bytes 786436
  109.3 15.1 %copy-start.5 = (bf16[256,128]{1,0:T(8,128)(2,1)S(1)}, bf16[256,128]{1,0:T(8,128)(2,1)}, u32[]{:S(2)}) copy-start(bf16[256,128]{1,0:T(8,128)(2,1)} %constant.89.clone.along_x_ref) | copy-start | bytes 196612
  110.4 20.0 %collective-permute-start.14 = (bf16[2304,128]{1,0:T(8,128)(2,1)}, bf16[2304,128]{1,0:T(8,128)(2,1)S(1)}, u32[]{:S(2)}, u32[]{:S(2)}) collective-permute-start(bf16[2304,128]{1,0:T(8,128)(2,1)} %bitcast.48), channel_id=1, source_target_pairs={{0,64},{64,128},{128,192},{192,0},{1,65},{65,129},{129,193},{193,1... | collective-permute-start | bytes 1769480 | tf_op jit(solution)/shard_map/ppermute | solution.py:55
  111.9 18.4 %collective-permute-start.15 = (bf16[2304,128]{1,0:T(8,128)(2,1)}, bf16[2304,128]{1,0:T(8,128)(2,1)S(1)}, u32[]{:S(2)}, u32[]{:S(2)}) collective-permute-start(bf16[2304,128]{1,0:T(8,128)(2,1)} %bitcast.50), channel_id=1, source_target_pairs={{0,192},{64,0},{128,64},{192,128},{1,193},{65,1},{129,65},{193,129... | collective-permute-start | bytes 1769480 | tf_op jit(solution)/shard_map/ppermute | solution.py:55
  125.5 14.0 %all-to-all-start.3 = ((bf16[16,64,128]{2,1,0:T(8,128)(2,1)}), bf16[16,64,128]{2,1,0:T(8,128)(2,1)S(1)}, u32[]{:S(2)}, u32[]{:S(2)}) async-start(bf16[16,64,128]{2,1,0:T(8,128)(2,1)} %bitcast.38), calls=%async_computation.3 | async-start | bytes 524288 | tf_op jit(solution)/shard_map/all_to_all | solution.py:791
  142.2 9.2 %collective-permute-start.16 = (f32[24,128]{1,0:T(8,128)S(1)}, f32[24,128]{1,0:T(8,128)S(1)}, u32[]{:S(2)}, u32[]{:S(2)}) collective-permute-start(f32[24,128]{1,0:T(8,128)S(1)} %get-tuple-element.31.potential_ref), channel_id=1, source_target_pairs={{0,60},{4,8},{8,4},{12,16},{16,12},{20,24},{24,20},{28,32},{32,28}... | collective-permute-start | bytes 36872 | tf_op jit(solution)/shard_map/ppermute | solution.py:62
  142.3 9.1 %collective-permute-start.17 = (f32[24,128]{1,0:T(8,128)S(1)}, f32[24,128]{1,0:T(8,128)S(1)}, u32[]{:S(2)}, u32[]{:S(2)}) collective-permute-start(f32[24,128]{1,0:T(8,128)S(1)} %get-tuple-element.31.potential_ref), channel_id=1, source_target_pairs={{0,4},{4,0},{8,12},{12,8},{16,20},{20,16},{24,28},{28,24},{32,36},... | collective-permute-start | bytes 36872 | tf_op jit(solution)/shard_map/ppermute | solution.py:62
  144.0 7.4 %copy-start.6 = (bf16[128,128]{1,0:T(8,128)(2,1)S(1)}, bf16[128,128]{1,0:T(8,128)(2,1)}, u32[]{:S(2)}) copy-start(bf16[128,128]{1,0:T(8,128)(2,1)} %msg_ref.1) | copy-start | bytes 98308

commit v9 on v8

--- a/solution.py
+++ b/solution.py
@@ -39,7 +39,7 @@
 SMALL = pltpu.CompilerParams(vmem_limit_bytes=20 << 20)
 FIRST = pltpu.CompilerParams(vmem_limit_bytes=60 << 20)
 LARGE = pltpu.CompilerParams(vmem_limit_bytes=50 << 20)
-MIDDLE = pltpu.CompilerParams(vmem_limit_bytes=40 << 20)
+MIDDLE = pltpu.CompilerParams(vmem_limit_bytes=37 << 20)
 FIELD = pltpu.CompilerParams(vmem_limit_bytes=44 << 20)
 
 
@@ -564,9 +564,9 @@
     out_ref, own_ref, weight_ref, slope_ref, sems
 ):
     pairs = [
-        (rows_ref, slope_ref.at[:, pl.ds(1, 2)]),
-        (before_ref, slope_ref.at[:, pl.ds(0, 1)]),
-        (after_ref, slope_ref.at[:, pl.ds(3, 1)]),
+        (rows_ref.at[1], slope_ref.at[pl.ds(1, 2)]),
+        (before_ref.at[1], slope_ref.at[pl.ds(0, 1)]),
+        (after_ref.at[1], slope_ref.at[pl.ds(3, 1)]),
         (stored_ref.at[:, :, :, pl.ds(512, 256)], weight_ref),
     ]
     copies = [
@@ -611,7 +611,7 @@
             jax.ShapeDtypeStruct((24, 128), f32),
             jax.ShapeDtypeStruct((8, 128), f32),
             jax.ShapeDtypeStruct((6, 8, 128, 256), bf16),
-            jax.ShapeDtypeStruct((3, 4, 6, 128, 128), bf16),
+            jax.ShapeDtypeStruct((4, 6, 128, 128), bf16),
         ],
         scratch_shapes=[pltpu.SemaphoreType.DMA((4,))],
         cost_estimate=pl.CostEstimate(
@@ -630,7 +630,8 @@
 
 
 def beside_kernel(
-    stored_ref, weight_ref, slope_ref, potential_ref, rest_ref, total_ref, own_out, near_ref, sems
+    stored_ref, rows_ref, before_ref, after_ref, weight_ref, slope_ref, potential_ref,
+    rest_ref, sides_ref, total_ref, own_out, near_ref, sems
 ):
     copies = [
         pltpu.make_async_copy(
@@ -638,12 +639,20 @@
         )
         for i in (0, 3)
     ]
+    pieces = ((rows_ref, 1, 2), (before_ref, 0, 1), (after_ref, 3, 1))
+    copies += [
+        pltpu.make_async_copy(
+            ref.at[2 * side], sides_ref.at[side, pl.ds(first, size)], sems.at[2 + 3 * side + i]
+        )
+        for side in range(2)
+        for i, (ref, first, size) in enumerate(pieces)
+    ]
     for copy in copies:
         copy.start()
     columns = jnp.transpose(potential_ref[...])
     for x in range(4):
         for z in range(6):
-            near_ref[x, z] = scaled(columns, x * 6 + z, slope_ref[1, x, z])
+            near_ref[x, z] = scaled(columns, x * 6 + z, slope_ref[x, z])
     own_out[...] = near_ref[1:3, 1:5]
     total_ref[...] = jnp.zeros_like(total_ref)
 
@@ -662,26 +671,27 @@
         copy.wait()
 
 
-def beside(stored, weights, slopes, potential):
+def beside(stored, parts, weights, slopes, potential):
     return pl.pallas_call(
         beside_kernel,
-        in_specs=[ANY] + [VM] * 3,
-        out_specs=[VM] * 3,
+        in_specs=[ANY] * 4 + [VM] * 3,
+        out_specs=[VM] * 4,
         out_shape=[
             jax.ShapeDtypeStruct((6, 8, 128, 512), bf16),
+            jax.ShapeDtypeStruct((2, 4, 6, 128, 128), bf16),
             jax.ShapeDtypeStruct((2, 4, 128, 128), f32),
             jax.ShapeDtypeStruct((2, 4, 128, 128), bf16),
         ],
         scratch_shapes=[
             pltpu.VMEM((4, 6, 128, 128), bf16),
-            pltpu.SemaphoreType.DMA((2,)),
+            pltpu.SemaphoreType.DMA((8,)),
         ],
         cost_estimate=pl.CostEstimate(
             flops=3000000000, bytes_accessed=12000000, transcendentals=0
         ),
         compiler_params=MIDDLE,
         name="beside",
-    )(stored, weights, slopes, potential)
+    )(stored, *parts, weights, slopes, potential)
 
 
 def backward_kernel(
@@ -696,7 +706,7 @@
         columns = jnp.transpose(potential_ref[side])
         for x in range(4):
             for z in range(6):
-                near_ref[side, x, z] = scaled(columns, x * 6 + z, slope_ref[2 * side, x, z])
+                near_ref[side, x, z] = scaled(columns, x * 6 + z, slope_ref[side, x, z])
         return carry
 
     lax.fori_loop(0, 2, scale, 0)
@@ -826,7 +836,9 @@
     )
     across, within = partners(potential)
     side = jnp.full((1, slots), 1 - 2 * (lax.axis_index("gy") % 2), f32)
-    weights, total, cotangent = beside(weights, own_weights, slopes, potential)
+    weights, slopes, total, cotangent = beside(
+        weights, slope_near, own_weights, slopes, potential
+    )
     grad = backward(
         weights, slopes, total, cotangent, across, within, side, msg_weight, self_weight
     )

time: 156 us -> 157 us (level)
  starting transfers between devices: 73.8 us -> 69.2 us
  waiting for transfers between devices: 44.5 us -> 48.3 us
    ppermute x16, starting transfers between devices: 35.1 us -> 31.5 us  [moved(): lax.ppermute(value.reshape(-1, 128), axis, pairs).reshape(value.shape)]
    ppermute x16, waiting for transfers between devices: 8 us -> 10.1 us  [moved(): lax.ppermute(value.reshape(-1, 128), axis, pairs).reshape(value.shape)]
    all_to_all x4, waiting for transfers between devices: 32.5 us -> 34.5 us  [swapped(): return lax.all_to_all(value, axis, split_axis=0, concat_axis=0, tiled=True)]
  transfers between devices with their start and end apart: 22 -> 22, of which waited for: 8 -> 7; matrix products, arithmetic and copies ran while one was open for 3% -> 3% of each run, Pallas kernels for 11% -> 11%
where the time goes in v9:
time: 157 us; the launch traced here: 156 us
  starting transfers between devices  69.2 us (44%)
  waiting for transfers between devices  48.3 us (31%)
  Pallas kernels  32.8 us (21%)
  local copies, waits for them, and re-layouts  3.65 us (2%)
    all_to_all x4, starting transfers between devices, swapped(): return lax.all_to_all(value, axis, split_axis=0, concat_axis=0, tiled=True)  35.6 us
    all_to_all x4, waiting for transfers between devices, swapped(): return lax.all_to_all(value, axis, split_axis=0, concat_axis=0, tiled=True)  34.5 us
    ppermute x16, starting transfers between devices, moved(): lax.ppermute(value.reshape(-1, 128), axis, pairs).reshape(value.shape)  31.5 us
    ppermute x16, waiting for transfers between devices, moved(): lax.ppermute(value.reshape(-1, 128), axis, pairs).reshape(value.shape)  10.1 us
    pallas_call x1, Pallas kernels, message_layer(): pl.pallas_call(message_kernel, in_specs=[VM] * 11 + [ANY], out_specs=[ANY...  5.77 us
    pallas_call x1, Pallas kernels, inside_pairs(): pl.pallas_call(inside_kernel, in_specs=[VM] * 5, out_specs=[ANY, VM], out...  5.7 us
    pallas_call x1, Pallas kernels, ends_pairs(): pl.pallas_call(ends_kernel, in_specs=[VM] * 6 + [ANY], out_specs=[ANY, VM...  5.19 us
    pallas_call x1, Pallas kernels, backward(): pl.pallas_call(backward_kernel, in_specs=[VM] * 9, out_specs=VM, out_shap...  4.29 us
  transfers between devices with their start and end apart: 22, of which 7 were waited for; matrix products, arithmetic and copies ran while one was open for 3% of the time, Pallas kernels for 11%

profile of v9, /device:TPU:32, one launch (start us, length us, event | category | flops | bytes accessed | tf_op | source)
XLA Modules:
  0.0 155.5 jit_solution(4491189503232177743)
XLA Ops:
  0.6 1.9 %project.1 = bf16[8,144,128]{2,1,0:T(8,128)(2,1)} custom-call(bf16[8,128,128]{2,1,0:T(8,128)(2,1)} %bitcast.95, bf16[128,128]{1,0:T(8,128)(2,1)} %msg_ref.1, s32[2,1,3,4,128]{4,3,2,1,0:T(4,128)} %bitcast.129, f32[2,1,3,4,128]{4,3,2,1,0:T(4,128)} %bitcast.130), custom_call_target="tpu_custom_call" | custom-call | tf_op jit(solution)/shard_map/project/pallas_call | solution.py:106
  2.5 7.9 %collective-permute-start.1 = (bf16[1152,128]{1,0:T(8,128)(2,1)}, bf16[1152,128]{1,0:T(8,128)(2,1)S(1)}, u32[]{:S(2)}, u32[]{:S(2)}) collective-permute-start(bf16[1152,128]{1,0:T(8,128)(2,1)} %bitcast.79), channel_id=1, source_target_pairs={{0,60},{4,0},{8,4},{12,8},{16,12},{20,16},{24,20},{28,24},{32,28},... | collective-permute-start | bytes 884744 | tf_op jit(solution)/shard_map/ppermute | solution.py:55
  10.5 0.0 collective-permute-start
  10.5 1.0 fusion.10
  11.5 1.7 %collective-permute-start.4 = (bf16[576,128]{1,0:T(8,128)(2,1)S(1)}, bf16[576,128]{1,0:T(8,128)(2,1)S(1)}, u32[]{:S(2)}, u32[]{:S(2)}) collective-permute-start(bf16[576,128]{1,0:T(8,128)(2,1)S(1)} %bitcast.124), channel_id=1, source_target_pairs={{0,64},{64,128},{128,192},{192,0},{1,65},{65,129},{129,193},{193,1... | collective-permute-start | bytes 442376 | tf_op jit(solution)/shard_map/ppermute | solution.py:55
  13.1 1.7 %collective-permute-start.5 = (bf16[576,128]{1,0:T(8,128)(2,1)S(1)}, bf16[576,128]{1,0:T(8,128)(2,1)S(1)}, u32[]{:S(2)}, u32[]{:S(2)}) collective-permute-start(bf16[576,128]{1,0:T(8,128)(2,1)S(1)} %bitcast.123), channel_id=1, source_target_pairs={{0,192},{64,0},{128,64},{192,128},{1,193},{65,1},{129,65},{193,129... | collective-permute-start | bytes 442376 | tf_op jit(solution)/shard_map/ppermute | solution.py:55
  14.8 0.9 slice_bitcast_fusion.1
  15.7 6.6 %collective-permute-done.1 = bf16[1152,128]{1,0:T(8,128)(2,1)S(1)} collective-permute-done((bf16[1152,128]{1,0:T(8,128)(2,1)}, bf16[1152,128]{1,0:T(8,128)(2,1)S(1)}, u32[]{:S(2)}, u32[]{:S(2)}) %collective-permute-start.1) | collective-permute-done | bytes 294944 | tf_op jit(solution)/shard_map/ppermute | solution.py:55
  22.3 3.5 %collective-permute-done = bf16[1152,128]{1,0:T(8,128)(2,1)S(1)} collective-permute-done((bf16[1152,128]{1,0:T(8,128)(2,1)}, bf16[1152,128]{1,0:T(8,128)(2,1)S(1)}, u32[]{:S(2)}, u32[]{:S(2)}) %collective-permute-start) | collective-permute-done | bytes 294944 | tf_op jit(solution)/shard_map/ppermute | solution.py:55
  25.9 0.1 collective-permute-start.2
  26.0 2.1 %collective-permute-start.3 = (bf16[864,128]{1,0:T(8,128)(2,1)S(1)}, bf16[864,128]{1,0:T(8,128)(2,1)S(1)}, u32[]{:S(2)}, u32[]{:S(2)}) collective-permute-start(bf16[864,128]{1,0:T(8,128)(2,1)S(1)} %bitcast.121), channel_id=1, source_target_pairs={{0,3},{1,0},{2,1},{3,2},{4,7},{5,4},{6,5},{7,6},{8,11},{9,8},{10,9... | collective-permute-start | bytes 663560 | tf_op jit(solution)/shard_map/ppermute | solution.py:55
  28.1 0.1 pad_maximum_fusion.2
  28.1 1.7 %collective-permute-start.6 = (bf16[1152,128]{1,0:T(8,128)(2,1)S(1)}, bf16[1152,128]{1,0:T(8,128)(2,1)S(1)}, u32[]{:S(2)}, u32[]{:S(2)}) collective-permute-start(bf16[1152,128]{1,0:T(8,128)(2,1)S(1)} %bitcast.118), channel_id=1, source_target_pairs={{0,64},{64,128},{128,192},{192,0},{1,65},{65,129},{129,193},{193,1... | collective-permute-start | bytes 884744 | tf_op jit(solution)/shard_map/ppermute | solution.py:55
  29.8 5.7 %inside_pairs.1 = (bf16[6,8,128,768]{3,2,1,0:T(8,128)(2,1)}, f32[2,4,128,128]{3,2,1,0:T(8,128)S(1)}) custom-call(bf16[2,4,144,128]{3,2,1,0:T(8,128)(2,1)S(1)} %bitcast.82, bf16[2,4,144,128]{3,2,1,0:T(8,128)(2,1)S(1)} %bitcast.92, bf16[2,4,144,128]{3,2,1,0:T(8,128)(2,1)S(1)} %bitcast.88, bf16[8,128,128]{2,1,0:T(8,128)(2,1)S(1)} %bitcast.96, ...), custom_call_target="tpu_custom_call" | custom-call | flops 5000000000 | bytes 9000000 | tf_op jit(solution)/shard_map/inside_pairs/pallas_call | solution.py:232
  35.6 0.0 collective-permute-done.2
  35.6 1.7 %collective-permute-start.7 = (bf16[1152,128]{1,0:T(8,128)(2,1)S(1)}, bf16[1152,128]{1,0:T(8,128)(2,1)S(1)}, u32[]{:S(2)}, u32[]{:S(2)}) collective-permute-start(bf16[1152,128]{1,0:T(8,128)(2,1)S(1)} %bitcast.117), channel_id=1, source_target_pairs={{0,192},{64,0},{128,64},{192,128},{1,193},{65,1},{129,65},{193,129... | collective-permute-start | bytes 884744 | tf_op jit(solution)/shard_map/ppermute | solution.py:55
  37.3 0.0 collective-permute-done.3
  37.3 0.5 collective-permute-start.8
  37.9 0.0 collective-permute-done.4
  37.9 3.1 %collective-permute-start.9 = (bf16[864,128]{1,0:T(8,128)(2,1)S(1)}, bf16[864,128]{1,0:T(8,128)(2,1)S(1)}, u32[]{:S(2)}, u32[]{:S(2)}) collective-permute-start(bf16[864,128]{1,0:T(8,128)(2,1)S(1)} %bitcast.120), channel_id=1, source_target_pairs={{0,192},{64,0},{128,64},{192,128},{1,193},{65,1},{129,65},{193,129... | collective-permute-start | bytes 663560 | tf_op jit(solution)/shard_map/ppermute | solution.py:55
  41.0 5.2 %ends_pairs.1 = (bf16[6,8,128,768]{3,2,1,0:T(8,128)(2,1)}, f32[2,4,128,128]{3,2,1,0:T(8,128)S(1)}) custom-call(bf16[2,4,144,128]{3,2,1,0:T(8,128)(2,1)S(1)} %bitcast.83, bf16[2,4,144,128]{3,2,1,0:T(8,128)(2,1)S(1)} %bitcast.93, bf16[2,4,144,128]{3,2,1,0:T(8,128)(2,1)S(1)} %bitcast.89, ...), custom_call_target="tpu_custom_call", output_to_operand_aliasing={{0}: (6, {})} | custom-call | flops 6000000000 | bytes 9000000 | tf_op jit(solution)/shard_map/ends_pairs/pallas_call | solution.py:300
  46.2 0.0 collective-permute-done.5
  46.2 0.0 collective-permute-done.6
  46.2 0.0 collective-permute-done.7
  46.2 0.0 collective-permute-done.8
  46.2 0.0 collective-permute-done.9
  46.2 5.8 %message.1 = (bf16[6,8,128,768]{3,2,1,0:T(8,128)(2,1)}, f32[2,4,128,128]{3,2,1,0:T(8,128)S(1)}, bf16[16,16,128]{2,1,0:T(8,128)(2,1)}, f32[4,6,8,128]{3,2,1,0:T(8,128)S(1)}) custom-call(bf16[2,4,144,128]{3,2,1,0:T(8,128)(2,1)S(1)} %bitcast.84, bf16[3,2,1,144,128]{4,3,2,1,0:T(8,128)(2,1)S(1)} %bitcast.100, ...), custom_call_target="tpu_custom_call", output_to_operand_aliasing={{0}: (11, {})} | custom-call | flops 5000000000 | bytes 6000000 | tf_op jit(solution)/shard_map/message/pallas_call | solution.py:417
  52.0 0.0 copy-start.4
  52.0 0.0 copy-start.7
  52.0 0.2 slope.1
  52.3 0.0 copy-start.3
  52.3 3.2 %collective-permute-start.11 = (bf16[256,128]{1,0:T(8,128)(2,1)S(1)}, bf16[256,128]{1,0:T(8,128)(2,1)S(1)}, u32[]{:S(2)}, u32[]{:S(2)}) collective-permute-start(bf16[256,128]{1,0:T(8,128)(2,1)S(1)} %bitcast.128), channel_id=1, source_target_pairs={{0,3},{1,0},{2,1},{3,2},{4,7},{5,4},{6,5},{7,6},{8,11},{9,8},{10,9... | collective-permute-start | bytes 196616 | tf_op jit(solution)/shard_map/ppermute | solution.py:55
  55.5 0.0 collective-permute-start.10
  55.5 6.5 %all-to-all-start = ((bf16[16,16,128]{2,1,0:T(8,128)(2,1)}), bf16[16,16,128]{2,1,0:T(8,128)(2,1)S(1)}, u32[]{:S(2)}, u32[]{:S(2)}) async-start(bf16[16,16,128]{2,1,0:T(8,128)(2,1)} %get-tuple-element.27), calls=%async_computation | async-start | bytes 131072 | tf_op jit(solution)/shard_map/all_to_all | solution.py:801
  62.0 0.0 collective-permute-done.10
  62.0 0.1 fusion.8
  62.1 4.7 %collective-permute-start.13 = (bf16[1536,128]{1,0:T(8,128)(2,1)S(1)}, bf16[1536,128]{1,0:T(8,128)(2,1)S(1)}, u32[]{:S(2)}, u32[]{:S(2)}) collective-permute-start(bf16[1536,128]{1,0:T(8,128)(2,1)S(1)} %bitcast.115), channel_id=1, source_target_pairs={{0,60},{4,0},{8,4},{12,8},{16,12},{20,16},{24,20},{28,24},{32,28},... | collective-permute-start | bytes 1179656 | tf_op jit(solution)/shard_map/ppermute | solution.py:55
  66.8 2.0 %all-to-all-done = bf16[16,16,128]{2,1,0:T(8,128)(2,1)S(1)} async-done(((bf16[16,16,128]{2,1,0:T(8,128)(2,1)}), bf16[16,16,128]{2,1,0:T(8,128)(2,1)S(1)}, u32[]{:S(2)}, u32[]{:S(2)}) %all-to-all-start) | async-done | bytes 65568 | tf_op jit(solution)/shard_map/all_to_all | solution.py:801
  68.8 1.0 forward_xz.1
  69.8 18.5 %all-to-all-start.1 = ((f32[256,1,128]{2,1,0:T(1,128)}), f32[256,1,128]{2,1,0:T(1,128)S(1)}, u32[]{:S(2)}, u32[]{:S(2)}) async-start(f32[256,1,128]{2,1,0:T(1,128)} %bitcast.46), calls=%async_computation.1 | async-start | bytes 262144 | tf_op jit(solution)/shard_map/all_to_all | solution.py:801
  88.4 0.1 fusion.1.influence_ref
  88.5 12.6 %all-to-all-done.1 = f32[256,1,128]{2,1,0:T(1,128)S(1)} async-done(((f32[256,1,128]{2,1,0:T(1,128)}), f32[256,1,128]{2,1,0:T(1,128)S(1)}, u32[]{:S(2)}, u32[]{:S(2)}) %all-to-all-start.1) | async-done | bytes 131104 | tf_op jit(solution)/shard_map/all_to_all | solution.py:801
  101.1 1.1 filter_y.1
  102.2 6.2 %all-to-all-start.2 = ((f32[256,2,128]{2,1,0:T(2,128)}), f32[256,2,128]{2,1,0:T(2,128)S(1)}, u32[]{:S(2)}, u32[]{:S(2)}) async-start(f32[256,2,128]{2,1,0:T(2,128)} %bitcast.48), calls=%async_computation.2 | async-start | bytes 524288 | tf_op jit(solution)/shard_map/all_to_all | solution.py:801
  108.3 0.0 collective-permute-done.12
  108.4 0.1 pad_maximum_fusion.rows_ref
  108.5 0.0 copy-start.2
  108.5 0.0 copy-start.5
  108.5 1.1 fusion.9
  109.6 1.5 collective-permute-start.14
  111.1 1.7 %collective-permute-start.15 = (bf16[2304,128]{1,0:T(8,128)(2,1)}, bf16[2304,128]{1,0:T(8,128)(2,1)S(1)}, u32[]{:S(2)}, u32[]{:S(2)}) collective-permute-start(bf16[2304,128]{1,0:T(8,128)(2,1)} %bitcast.42), channel_id=1, source_target_pairs={{0,192},{64,0},{128,64},{192,128},{1,193},{65,1},{129,65},{193,129... | collective-permute-start | bytes 1769480 | tf_op jit(solution)/shard_map/ppermute | solution.py:55
  112.9 10.8 %all-to-all-done.2 = f32[256,2,128]{2,1,0:T(2,128)S(1)} async-done(((f32[256,2,128]{2,1,0:T(2,128)}), f32[256,2,128]{2,1,0:T(2,128)S(1)}, u32[]{:S(2)}, u32[]{:S(2)}) %all-to-all-start.2) | async-done | bytes 262176 | tf_op jit(solution)/shard_map/all_to_all | solution.py:801
  123.7 1.0 inverse_xz.1
  124.7 4.4 %all-to-all-start.3 = ((bf16[16,64,128]{2,1,0:T(8,128)(2,1)}), bf16[16,64,128]{2,1,0:T(8,128)(2,1)S(1)}, u32[]{:S(2)}, u32[]{:S(2)}) async-start(bf16[16,64,128]{2,1,0:T(8,128)(2,1)} %bitcast.50), calls=%async_computation.3 | async-start | bytes 524288 | tf_op jit(solution)/shard_map/all_to_all | solution.py:801
  129.1 0.5 slice.77
  129.6 0.0 collective-permute-done.14
  129.6 0.0 collective-permute-done.15
  129.6 9.1 %all-to-all-done.3.field_ref = bf16[16,64,128]{2,1,0:T(8,128)(2,1)S(1)} async-done(((bf16[16,64,128]{2,1,0:T(8,128)(2,1)}), bf16[16,64,128]{2,1,0:T(8,128)(2,1)S(1)}, u32[]{:S(2)}, u32[]{:S(2)}) %all-to-all-start.3) | async-done | bytes 262176 | tf_op jit(solution)/shard_map/all_to_all | solution.py:801
  138.7 3.2 %interpolate.1 = (f32[24,128]{1,0:T(8,128)S(1)}, f32[8,128]{1,0:T(8,128)}, bf16[6,8,128,256]{3,2,1,0:T(8,128)(2,1)S(1)}, bf16[4,6,128,128]{3,2,1,0:T(8,128)(2,1)S(1)}) custom-call(bf16[16,64,128]{2,1,0:T(8,128)(2,1)S(1)} %all-to-all-done.3.field_ref, f32[24,8,128]{2,1,0:T(8,128)S(1)} %bitcast.104, bf16[6,8,128,768]{3,2,1,0:T(8,128)(2,1)} %get-tuple-element.25.stored_ref, ...), custom_call_target="tpu_custom_call" | custom-call | flops 201326592 | bytes 400000 | tf_op jit(solution)/shard_map/interpolate/pallas_call | solution.py:605
  141.9 0.1 collective-permute-start.17
  142.0 2.1 %collective-permute-start.16 = (f32[24,128]{1,0:T(8,128)S(1)}, f32[24,128]{1,0:T(8,128)S(1)}, u32[]{:S(2)}, u32[]{:S(2)}) collective-permute-start(f32[24,128]{1,0:T(8,128)S(1)} %get-tuple-element.32.potential_ref), channel_id=1, source_target_pairs={{0,60},{4,8},{8,4},{12,16},{16,12},{20,24},{24,20},{28,32},{32,28}... | collective-permute-start | bytes 36872 | tf_op jit(solution)/shard_map/ppermute | solution.py:62
  144.1 3.4 %beside.1 = (bf16[6,8,128,512]{3,2,1,0:T(8,128)(2,1)S(1)}, bf16[2,4,6,128,128]{4,3,2,1,0:T(8,128)(2,1)S(1)}, f32[2,4,128,128]{3,2,1,0:T(8,128)S(1)}, bf16[2,4,128,128]{3,2,1,0:T(8,128)(2,1)S(1)}) custom-call(bf16[6,8,128,768]{3,2,1,0:T(8,128)(2,1)} %get-tuple-element.25.stored_ref, bf16[3,2,6,128,128]{4,3,2,1,0:T(8,128)(2,1)S(1)} %pad_maximum_fusion.rows_ref, ...), custom_call_target="tpu_custom_call" | custom-call | flops 3000000000 | bytes 12000000 | tf_op jit(solution)/shard_map/beside/pallas_call | solution.py:675
  147.5 3.7 %collective-permute-done.16.across_ref = f32[24,128]{1,0:T(8,128)S(1)} collective-permute-done((f32[24,128]{1,0:T(8,128)S(1)}, f32[24,128]{1,0:T(8,128)S(1)}, u32[]{:S(2)}, u32[]{:S(2)}) %collective-permute-start.16) | collective-permute-done | bytes 12320 | tf_op jit(solution)/shard_map/ppermute | solution.py:62
  151.3 4.3 %backward.1 = f32[2,4,128,128]{3,2,1,0:T(8,128)} custom-call(bf16[6,8,128,512]{3,2,1,0:T(8,128)(2,1)S(1)} %get-tuple-element.33.weight_ref, bf16[2,4,6,128,128]{4,3,2,1,0:T(8,128)(2,1)S(1)} %get-tuple-element.34.slope_ref, f32[2,4,128,128]{3,2,1,0:T(8,128)S(1)} %get-tuple-element.35.part_ref, bf16[2,4,128,128]{3,2,1,0:T(8,128)(2,1)S(1)} %get-tuple-element.36.own_ref, ...), custom_call_target="tpu_custom_call" | custom-call | flops 4000000000 | bytes 12000000 | tf_op jit(solution)/shard_map/backward/pallas_call | solution.py:741
  (31 shorter events, 0.2 us)
Async XLA Ops:
  2.5 19.8 %collective-permute-start.1 = (bf16[1152,128]{1,0:T(8,128)(2,1)}, bf16[1152,128]{1,0:T(8,128)(2,1)S(1)}, u32[]{:S(2)}, u32[]{:S(2)}) collective-permute-start(bf16[1152,128]{1,0:T(8,128)(2,1)} %bitcast.79), channel_id=1, source_target_pairs={{0,60},{4,0},{8,4},{12,8},{16,12},{20,16},{24,20},{28,24},{32,28},... | collective-permute-start | bytes 884744 | tf_op jit(solution)/shard_map/ppermute | solution.py:55
  10.5 15.4 %collective-permute-start = (bf16[1152,128]{1,0:T(8,128)(2,1)}, bf16[1152,128]{1,0:T(8,128)(2,1)S(1)}, u32[]{:S(2)}, u32[]{:S(2)}) collective-permute-start(bf16[1152,128]{1,0:T(8,128)(2,1)} %bitcast.80), channel_id=1, source_target_pairs={{0,4},{4,8},{8,12},{12,16},{16,20},{20,24},{24,28},{28,32},{32,36}... | collective-permute-start | bytes 884744 | tf_op jit(solution)/shard_map/ppermute | solution.py:55
  11.5 26.4 %collective-permute-start.4 = (bf16[576,128]{1,0:T(8,128)(2,1)S(1)}, bf16[576,128]{1,0:T(8,128)(2,1)S(1)}, u32[]{:S(2)}, u32[]{:S(2)}) collective-permute-start(bf16[576,128]{1,0:T(8,128)(2,1)S(1)} %bitcast.124), channel_id=1, source_target_pairs={{0,64},{64,128},{128,192},{192,0},{1,65},{65,129},{129,193},{193,1... | collective-permute-start | bytes 442376 | tf_op jit(solution)/shard_map/ppermute | solution.py:55
  13.1 33.0 %collective-permute-start.5 = (bf16[576,128]{1,0:T(8,128)(2,1)S(1)}, bf16[576,128]{1,0:T(8,128)(2,1)S(1)}, u32[]{:S(2)}, u32[]{:S(2)}) collective-permute-start(bf16[576,128]{1,0:T(8,128)(2,1)S(1)} %bitcast.123), channel_id=1, source_target_pairs={{0,192},{64,0},{128,64},{192,128},{1,193},{65,1},{129,65},{193,129... | collective-permute-start | bytes 442376 | tf_op jit(solution)/shard_map/ppermute | solution.py:55
  25.8 4.0 %copy-start = (bf16[8,144,128]{2,1,0:T(8,128)(2,1)S(1)}, bf16[8,144,128]{2,1,0:T(8,128)(2,1)}, u32[]{:S(2)}) copy-start(bf16[8,144,128]{2,1,0:T(8,128)(2,1)} %project.1) | copy-start | bytes 884740
  25.8 4.0 %copy-start.1 = (bf16[2,1,4,128,128]{4,3,2,1,0:T(8,128)(2,1)S(1)}, bf16[2,1,4,128,128]{4,3,2,1,0:T(8,128)(2,1)}, u32[]{:S(2)}) copy-start(bf16[2,1,4,128,128]{4,3,2,1,0:T(8,128)(2,1)} %param.11) | copy-start | bytes 786436
  25.8 4.0 %copy-start.9 = (bf16[128,128]{1,0:T(8,128)(2,1)S(1)}, bf16[128,128]{1,0:T(8,128)(2,1)}, u32[]{:S(2)}) copy-start(bf16[128,128]{1,0:T(8,128)(2,1)} %self_ref.3) | copy-start | bytes 98308
  25.9 9.7 %collective-permute-start.2 = (bf16[864,128]{1,0:T(8,128)(2,1)S(1)}, bf16[864,128]{1,0:T(8,128)(2,1)S(1)}, u32[]{:S(2)}, u32[]{:S(2)}) collective-permute-start(bf16[864,128]{1,0:T(8,128)(2,1)S(1)} %bitcast.122), channel_id=1, source_target_pairs={{0,1},{1,2},{2,3},{3,0},{4,5},{5,6},{6,7},{7,4},{8,9},{9,10},{10,1... | collective-permute-start | bytes 663560 | tf_op jit(solution)/shard_map/ppermute | solution.py:55
  26.0 11.3 %collective-permute-start.3 = (bf16[864,128]{1,0:T(8,128)(2,1)S(1)}, bf16[864,128]{1,0:T(8,128)(2,1)S(1)}, u32[]{:S(2)}, u32[]{:S(2)}) collective-permute-start(bf16[864,128]{1,0:T(8,128)(2,1)S(1)} %bitcast.121), channel_id=1, source_target_pairs={{0,3},{1,0},{2,1},{3,2},{4,7},{5,4},{6,5},{7,6},{8,11},{9,8},{10,9... | collective-permute-start | bytes 663560 | tf_op jit(solution)/shard_map/ppermute | solution.py:55
  28.1 18.0 %collective-permute-start.6 = (bf16[1152,128]{1,0:T(8,128)(2,1)S(1)}, bf16[1152,128]{1,0:T(8,128)(2,1)S(1)}, u32[]{:S(2)}, u32[]{:S(2)}) collective-permute-start(bf16[1152,128]{1,0:T(8,128)(2,1)S(1)} %bitcast.118), channel_id=1, source_target_pairs={{0,64},{64,128},{128,192},{192,0},{1,65},{65,129},{129,193},{193,1... | collective-permute-start | bytes 884744 | tf_op jit(solution)/shard_map/ppermute | solution.py:55
  35.6 10.6 %collective-permute-start.7 = (bf16[1152,128]{1,0:T(8,128)(2,1)S(1)}, bf16[1152,128]{1,0:T(8,128)(2,1)S(1)}, u32[]{:S(2)}, u32[]{:S(2)}) collective-permute-start(bf16[1152,128]{1,0:T(8,128)(2,1)S(1)} %bitcast.117), channel_id=1, source_target_pairs={{0,192},{64,0},{128,64},{192,128},{1,193},{65,1},{129,65},{193,129... | collective-permute-start | bytes 884744 | tf_op jit(solution)/shard_map/ppermute | solution.py:55
  37.3 8.8 %collective-permute-start.8 = (bf16[864,128]{1,0:T(8,128)(2,1)S(1)}, bf16[864,128]{1,0:T(8,128)(2,1)S(1)}, u32[]{:S(2)}, u32[]{:S(2)}) collective-permute-start(bf16[864,128]{1,0:T(8,128)(2,1)S(1)} %bitcast.119), channel_id=1, source_target_pairs={{0,64},{64,128},{128,192},{192,0},{1,65},{65,129},{129,193},{193,1... | collective-permute-start | bytes 663560 | tf_op jit(solution)/shard_map/ppermute | solution.py:55
  37.9 8.3 %collective-permute-start.9 = (bf16[864,128]{1,0:T(8,128)(2,1)S(1)}, bf16[864,128]{1,0:T(8,128)(2,1)S(1)}, u32[]{:S(2)}, u32[]{:S(2)}) collective-permute-start(bf16[864,128]{1,0:T(8,128)(2,1)S(1)} %bitcast.120), channel_id=1, source_target_pairs={{0,192},{64,0},{128,64},{192,128},{1,193},{65,1},{129,65},{193,129... | collective-permute-start | bytes 663560 | tf_op jit(solution)/shard_map/ppermute | solution.py:55
  41.0 5.3 %copy-start.8 = (bf16[128]{0:T(256)(128)(2,1)S(1)}, bf16[128]{0:T(256)(128)(2,1)}, u32[]{:S(2)}) copy-start(bf16[128]{0:T(256)(128)(2,1)} %param.14) | copy-start | bytes 772
  52.0 16.8 %copy-start.4 = (bf16[256,256]{1,0:T(8,128)(2,1)S(1)}, bf16[256,256]{1,0:T(8,128)(2,1)}, u32[]{:S(2)}) copy-start(bf16[256,256]{1,0:T(8,128)(2,1)} %constant.86.clone.along_z_ref) | copy-start | bytes 393220
  52.0 16.8 %copy-start.7 = (bf16[128,128]{1,0:T(8,128)(2,1)S(1)}, bf16[128,128]{1,0:T(8,128)(2,1)}, u32[]{:S(2)}) copy-start(bf16[128,128]{1,0:T(8,128)(2,1)} %constant.87.clone.along_x_ref) | copy-start | bytes 98308
  52.3 48.8 %copy-start.3 = (bf16[256,256]{1,0:T(8,128)(2,1)S(1)}, bf16[256,256]{1,0:T(8,128)(2,1)}, u32[]{:S(2)}) copy-start(bf16[256,256]{1,0:T(8,128)(2,1)} %constant.88.clone.into_ref) | copy-start | bytes 393220
  52.3 9.7 %collective-permute-start.11 = (bf16[256,128]{1,0:T(8,128)(2,1)S(1)}, bf16[256,128]{1,0:T(8,128)(2,1)S(1)}, u32[]{:S(2)}, u32[]{:S(2)}) collective-permute-start(bf16[256,128]{1,0:T(8,128)(2,1)S(1)} %bitcast.128), channel_id=1, source_target_pairs={{0,3},{1,0},{2,1},{3,2},{4,7},{5,4},{6,5},{7,6},{8,11},{9,8},{10,9... | collective-permute-start | bytes 196616 | tf_op jit(solution)/shard_map/ppermute | solution.py:55
  55.5 6.5 %collective-permute-start.10 = (bf16[256,128]{1,0:T(8,128)(2,1)S(1)}, bf16[256,128]{1,0:T(8,128)(2,1)S(1)}, u32[]{:S(2)}, u32[]{:S(2)}) collective-permute-start(bf16[256,128]{1,0:T(8,128)(2,1)S(1)} %bitcast.127), channel_id=1, source_target_pairs={{0,1},{1,2},{2,3},{3,0},{4,5},{5,6},{6,7},{7,4},{8,9},{9,10},{10,1... | collective-permute-start | bytes 196616 | tf_op jit(solution)/shard_map/ppermute | solution.py:55
  55.5 13.3 %all-to-all-start = ((bf16[16,16,128]{2,1,0:T(8,128)(2,1)}), bf16[16,16,128]{2,1,0:T(8,128)(2,1)S(1)}, u32[]{:S(2)}, u32[]{:S(2)}) async-start(bf16[16,16,128]{2,1,0:T(8,128)(2,1)} %get-tuple-element.27), calls=%async_computation | async-start | bytes 131072 | tf_op jit(solution)/shard_map/all_to_all | solution.py:801
  62.1 46.2 %collective-permute-start.13 = (bf16[1536,128]{1,0:T(8,128)(2,1)S(1)}, bf16[1536,128]{1,0:T(8,128)(2,1)S(1)}, u32[]{:S(2)}, u32[]{:S(2)}) collective-permute-start(bf16[1536,128]{1,0:T(8,128)(2,1)S(1)} %bitcast.115), channel_id=1, source_target_pairs={{0,60},{4,0},{8,4},{12,8},{16,12},{20,16},{24,20},{28,24},{32,28},... | collective-permute-start | bytes 1179656 | tf_op jit(solution)/shard_map/ppermute | solution.py:55
  66.8 41.6 %collective-permute-start.12 = (bf16[1536,128]{1,0:T(8,128)(2,1)S(1)}, bf16[1536,128]{1,0:T(8,128)(2,1)S(1)}, u32[]{:S(2)}, u32[]{:S(2)}) collective-permute-start(bf16[1536,128]{1,0:T(8,128)(2,1)S(1)} %bitcast.116), channel_id=1, source_target_pairs={{0,4},{4,8},{8,12},{12,16},{16,20},{20,24},{24,28},{28,32},{32,36}... | collective-permute-start | bytes 1179656 | tf_op jit(solution)/shard_map/ppermute | solution.py:55
  69.8 31.2 %all-to-all-start.1 = ((f32[256,1,128]{2,1,0:T(1,128)}), f32[256,1,128]{2,1,0:T(1,128)S(1)}, u32[]{:S(2)}, u32[]{:S(2)}) async-start(f32[256,1,128]{2,1,0:T(1,128)} %bitcast.46), calls=%async_computation.1 | async-start | bytes 262144 | tf_op jit(solution)/shard_map/all_to_all | solution.py:801
  102.2 21.5 %all-to-all-start.2 = ((f32[256,2,128]{2,1,0:T(2,128)}), f32[256,2,128]{2,1,0:T(2,128)S(1)}, u32[]{:S(2)}, u32[]{:S(2)}) async-start(f32[256,2,128]{2,1,0:T(2,128)} %bitcast.48), calls=%async_computation.2 | async-start | bytes 524288 | tf_op jit(solution)/shard_map/all_to_all | solution.py:801
  108.5 15.2 %copy-start.2 = (bf16[256,512]{1,0:T(8,128)(2,1)S(1)}, bf16[256,512]{1,0:T(8,128)(2,1)}, u32[]{:S(2)}) copy-start(bf16[256,512]{1,0:T(8,128)(2,1)} %constant.90.clone.along_z_ref) | copy-start | bytes 786436
  108.5 15.1 %copy-start.5 = (bf16[256,128]{1,0:T(8,128)(2,1)S(1)}, bf16[256,128]{1,0:T(8,128)(2,1)}, u32[]{:S(2)}) copy-start(bf16[256,128]{1,0:T(8,128)(2,1)} %constant.89.clone.along_x_ref) | copy-start | bytes 196612
  109.6 20.0 %collective-permute-start.14 = (bf16[2304,128]{1,0:T(8,128)(2,1)}, bf16[2304,128]{1,0:T(8,128)(2,1)S(1)}, u32[]{:S(2)}, u32[]{:S(2)}) collective-permute-start(bf16[2304,128]{1,0:T(8,128)(2,1)} %bitcast.40), channel_id=1, source_target_pairs={{0,64},{64,128},{128,192},{192,0},{1,65},{65,129},{129,193},{193,1... | collective-permute-start | bytes 1769480 | tf_op jit(solution)/shard_map/ppermute | solution.py:55
  111.1 18.4 %collective-permute-start.15 = (bf16[2304,128]{1,0:T(8,128)(2,1)}, bf16[2304,128]{1,0:T(8,128)(2,1)S(1)}, u32[]{:S(2)}, u32[]{:S(2)}) collective-permute-start(bf16[2304,128]{1,0:T(8,128)(2,1)} %bitcast.42), channel_id=1, source_target_pairs={{0,192},{64,0},{128,64},{192,128},{1,193},{65,1},{129,65},{193,129... | collective-permute-start | bytes 1769480 | tf_op jit(solution)/shard_map/ppermute | solution.py:55
  124.7 14.0 %all-to-all-start.3 = ((bf16[16,64,128]{2,1,0:T(8,128)(2,1)}), bf16[16,64,128]{2,1,0:T(8,128)(2,1)S(1)}, u32[]{:S(2)}, u32[]{:S(2)}) async-start(bf16[16,64,128]{2,1,0:T(8,128)(2,1)} %bitcast.50), calls=%async_computation.3 | async-start | bytes 524288 | tf_op jit(solution)/shard_map/all_to_all | solution.py:801
  141.9 5.6 %collective-permute-start.17 = (f32[24,128]{1,0:T(8,128)S(1)}, f32[24,128]{1,0:T(8,128)S(1)}, u32[]{:S(2)}, u32[]{:S(2)}) collective-permute-start(f32[24,128]{1,0:T(8,128)S(1)} %get-tuple-element.32.potential_ref), channel_id=1, source_target_pairs={{0,4},{4,0},{8,12},{12,8},{16,20},{20,16},{24,28},{28,24},{32,36},... | collective-permute-start | bytes 36872 | tf_op jit(solution)/shard_map/ppermute | solution.py:62
  142.0 9.2 %collective-permute-start.16 = (f32[24,128]{1,0:T(8,128)S(1)}, f32[24,128]{1,0:T(8,128)S(1)}, u32[]{:S(2)}, u32[]{:S(2)}) collective-permute-start(f32[24,128]{1,0:T(8,128)S(1)} %get-tuple-element.32.potential_ref), channel_id=1, source_target_pairs={{0,60},{4,8},{8,4},{12,16},{16,12},{20,24},{24,20},{28,32},{32,28}... | collective-permute-start | bytes 36872 | tf_op jit(solution)/shard_map/ppermute | solution.py:62
  144.1 7.1 %copy-start.6 = (bf16[128,128]{1,0:T(8,128)(2,1)S(1)}, bf16[128,128]{1,0:T(8,128)(2,1)}, u32[]{:S(2)}) copy-start(bf16[128,128]{1,0:T(8,128)(2,1)} %msg_ref.1) | copy-start | bytes 98308
